TPU v7x, 32 devices: a whole 2x2x4 slice. The times are simulated.
32 devices in a mesh: dp: 4 (over y, core), seq: 8 (over z, x).
Axes of the slice: x: 2, y: 2, z: 4, core: 2. Of those that a mesh axis runs over, the one named last changes fastest.
Arguments:
- activations: bfloat16 [16, 2048, 1280], P('dp', 'seq'), may hold values from -6 to 6
- segment_ids: int32 [16, 2048], P('dp'), may hold values from 0 to 3, never falling along the last dimension, each value on 1 to 1024 neighbouring positions
- norm1_gain: bfloat16 [1280], P('dp'), may hold values from 0.25 to 1.75
- w_qkv: bfloat16 [1280, 16, 3, 80], P('dp'), may hold values from -0.15625 to 0.15625
- per_dim_scale: float32 [80], replicated, may hold values from -1 to 1
- w_out: bfloat16 [1280, 1280], P('dp'), may hold values from -0.625 to 0.625
- norm2_gain: bfloat16 [1280], P('dp'), may hold values from 0.25 to 1.75
- w_up: bfloat16 [1280, 1280], P('dp'), may hold values from -0.15625 to 0.15625
- b_up: bfloat16 [1280], P('dp'), may hold values from -3 to 3
- w_down: bfloat16 [1280, 1280], P('dp'), may hold values from -0.15625 to 0.15625
- b_down: bfloat16 [1280], P('dp'), may hold values from -2 to 2
- cotangent: float32 [16, 2048, 1280], P('dp', 'seq'), may hold values from -6 to 6
Outputs:
- layer_out: bfloat16 [16, 2048, 1280], P('dp', 'seq')
- input_grad: float32 [16, 2048, 1280], P('dp', 'seq')
- grad_norm1_gain: float32 [1280], P('dp')
- grad_w_qkv: float32 [1280, 16, 3, 80], P('dp')
- grad_per_dim_scale: float32 [80], replicated
- grad_w_out: float32 [1280, 1280], P('dp')
- grad_norm2_gain: float32 [1280], P('dp')
- grad_w_up: float32 [1280, 1280], P('dp')
- grad_b_up: float32 [1280], P('dp')
- grad_w_down: float32 [1280, 1280], P('dp')
- grad_b_down: float32 [1280], P('dp')
Inputs may be any that keep to these rules, and one draw needn't show every extreme that they name: `segment_ids`: ids never fall along a sequence, and every id from 0 to 3 occurs in each sequence.
All inputs are finite; a program needn't handle non-finite values.
Results may differ from a plain program's by a relative error of at most 0.028.
Values may be sent and summed in bfloat16 or wider, within the bound.
No kernel may reach another device: no remote copies, remote signals or barrier semaphores. Data moves between devices by JAX's collectives and lax.ppermute only.
A program may use at most 320 MiB of HBM per device.

v0:
```python
import math

import jax
import jax.numpy as jnp
from jax import lax
from jax.sharding import PartitionSpec as P

epsilon = 1e-06
scale_base = 1.442695041
masked_value = -1e30


def shortened(shard):

    def short(part):
        return part.astype(jnp.bfloat16) if part.dtype == jnp.float32 else part

    return jax.tree.map(short, shard)


def query_factor(per_dim_scale):
    head_size = per_dim_scale.shape[0]
    return scale_base / math.sqrt(head_size) * jax.nn.softplus(per_dim_scale)


def rms_factor(inputs):
    return lax.rsqrt(jnp.mean(inputs * inputs, axis=-1, keepdims=True) + epsilon)


def visible(segs, first, count):
    length = segs.shape[0]
    places = jnp.arange(length)
    row_places = places[first : first + count]
    row_segs = segs[first : first + count]
    return (places[None, :] <= row_places[:, None]) & (segs[None, :] == row_segs[:, None])


def block_scores(queries, keys, visible_mask):
    scores = jnp.einsum("qhe,khe->hqk", queries, keys, preferred_element_type=jnp.float32)
    return jnp.where(visible_mask[None], scores, masked_value)


def attend_forward(sequence_item):
    packed, segs = sequence_item
    length = packed.shape[0]
    step_rows = min(512, length)
    queries = packed[:, :, 0, :]
    keys = packed[:, :, 1, :]
    values_in = packed[:, :, 2, :]
    outputs = []
    log_sums = []
    for first in range(0, length, step_rows):
        visible_mask = visible(segs, first, step_rows)
        scores = block_scores(queries[first : first + step_rows], keys, visible_mask)
        peak = jnp.max(scores, axis=-1, keepdims=True)
        raised = jnp.exp(scores - peak)
        total = jnp.sum(raised, axis=-1, keepdims=True)
        attention_weights = (raised / total).astype(jnp.bfloat16)
        log_sums.append((peak + jnp.log(total))[..., 0])
        block_out = jnp.einsum(
            "hqk,khe->qhe", attention_weights, values_in, preferred_element_type=jnp.float32
        )
        outputs.append(block_out.astype(jnp.bfloat16))
    return (jnp.concatenate(outputs, axis=0), jnp.concatenate(log_sums, axis=1))


def attend_backward(sequence_item):
    packed, segs, log_sums, grad_out = sequence_item
    length = packed.shape[0]
    step_rows = min(512, length)
    queries = packed[:, :, 0, :]
    keys = packed[:, :, 1, :]
    values_in = packed[:, :, 2, :]
    grad_keys = jnp.zeros(keys.shape, jnp.float32)
    grad_values = jnp.zeros(values_in.shape, jnp.float32)
    query_grads = []
    for first in range(0, length, step_rows):
        visible_mask = visible(segs, first, step_rows)
        query_block = queries[first : first + step_rows]
        grad_block = grad_out[first : first + step_rows]
        scores = block_scores(query_block, keys, visible_mask)
        attention_weights = jnp.exp(scores - log_sums[:, first : first + step_rows, None])
        grad_values = grad_values + jnp.einsum(
            "hqk,qhe->khe",
            attention_weights.astype(jnp.bfloat16),
            grad_block,
            preferred_element_type=jnp.float32,
        )
        grad_weights = jnp.einsum(
            "qhe,khe->hqk", grad_block, values_in, preferred_element_type=jnp.float32
        )
        inner = jnp.sum(attention_weights * grad_weights, axis=-1, keepdims=True)
        grad_scores = (attention_weights * (grad_weights - inner)).astype(jnp.bfloat16)
        query_grads.append(
            jnp.einsum("hqk,khe->qhe", grad_scores, keys, preferred_element_type=jnp.float32)
        )
        grad_keys = grad_keys + jnp.einsum(
            "hqk,qhe->khe", grad_scores, query_block, preferred_element_type=jnp.float32
        )
    grad_queries = jnp.concatenate(query_grads, axis=0)
    return jnp.stack([grad_queries, grad_keys, grad_values], axis=2).astype(jnp.bfloat16)


def collect(norm_in, w_qkv, w_out, norm_mid, w_up, b_up, w_down, b_down):
    return (
        lax.all_gather(norm_in, "dp", axis=0, tiled=True),
        lax.all_gather(w_qkv, "dp", axis=0, tiled=True),
        lax.all_gather(w_out, "dp", axis=0, tiled=True),
        lax.all_gather(norm_mid, "dp", axis=0, tiled=True),
        lax.all_gather(w_up, "dp", axis=0, tiled=True),
        lax.all_gather(b_up, "dp", axis=0, tiled=True),
        lax.all_gather(w_down, "dp", axis=0, tiled=True),
        lax.all_gather(b_down, "dp", axis=0, tiled=True),
    )


def forward(tokens, segment_ids, full, per_dim_scale):
    norm_in, w_qkv, w_out, norm_mid, w_up, b_up, w_down, b_down = full
    seqs, span, width = tokens.shape
    heads = w_qkv.shape[1]
    head_size = w_qkv.shape[3]
    length = segment_ids.shape[1]
    local_heads = heads // lax.axis_size("seq")
    x_float = tokens.astype(jnp.float32)
    rms_in = rms_factor(x_float)
    normed_in = (x_float * rms_in * norm_in.astype(jnp.float32)).astype(jnp.bfloat16)
    projected = jnp.einsum(
        "scd,df->scf",
        normed_in,
        w_qkv.reshape(width, heads * 3 * head_size),
        preferred_element_type=jnp.float32,
    )
    unit_scale = jnp.ones((head_size,), jnp.float32)
    factors = jnp.stack([query_factor(per_dim_scale), unit_scale, unit_scale])
    scaled = projected.reshape(seqs, span, heads, 3, head_size) * factors
    outgoing = scaled.astype(jnp.bfloat16).reshape(seqs, span, heads * 3 * head_size)
    by_head = lax.all_to_all(outgoing, "seq", split_axis=2, concat_axis=1, tiled=True).reshape(
        seqs, length, local_heads, 3, head_size
    )
    attended_heads, log_sums = lax.map(attend_forward, (by_head, segment_ids))
    attended = lax.all_to_all(
        shortened(attended_heads.reshape(seqs, length, local_heads * head_size)),
        "seq",
        split_axis=1,
        concat_axis=2,
        tiled=True,
    )
    mid = x_float + jnp.einsum("scf,fd->scd", attended, w_out, preferred_element_type=jnp.float32)
    rms_mid = rms_factor(mid)
    normed_mid = (mid * rms_mid * norm_mid.astype(jnp.float32)).astype(jnp.bfloat16)
    pre_act = jnp.einsum(
        "scd,df->scf", normed_mid, w_up, preferred_element_type=jnp.float32
    ) + b_up.astype(jnp.float32)
    activated = jax.nn.silu(pre_act).astype(jnp.bfloat16)
    result = (
        mid
        + jnp.einsum("scf,fd->scd", activated, w_down, preferred_element_type=jnp.float32)
        + b_down.astype(jnp.float32)
    )
    kept = (
        x_float,
        rms_in,
        normed_in,
        projected,
        by_head,
        log_sums,
        attended,
        mid,
        rms_mid,
        normed_mid,
        pre_act,
        activated,
        factors,
    )
    return (result, kept)


def on_device(
    activations,
    segment_ids,
    norm1_gain,
    w_qkv,
    per_dim_scale,
    w_out,
    norm2_gain,
    w_up,
    b_up,
    w_down,
    b_down,
    cotangent,
):
    seqs, span, width = activations.shape
    heads = w_qkv.shape[1]
    head_size = w_qkv.shape[3]
    length = segment_ids.shape[1]
    local_heads = heads // lax.axis_size("seq")
    data_groups = lax.axis_size("dp")
    full = collect(norm1_gain, w_qkv, w_out, norm2_gain, w_up, b_up, w_down, b_down)
    result, kept = forward(activations, segment_ids, full, per_dim_scale)
    (
        x_float,
        rms_in,
        normed_in,
        projected,
        by_head,
        log_sums,
        attended,
        mid,
        rms_mid,
        normed_mid,
        pre_act,
        activated,
        factors,
    ) = kept
    gain_in, w_qkv_all, w_out_all, gain_mid, w_up_all, b_up_all, w_down_all, b_down_all = full
    grad_branch = cotangent.astype(jnp.bfloat16)
    grad_bias_down = jnp.sum(grad_branch.astype(jnp.float32), axis=(0, 1))
    grad_down = jnp.einsum(
        "scf,scd->fd", activated, grad_branch, preferred_element_type=jnp.float32
    )
    grad_act = jnp.einsum(
        "scd,fd->scf", grad_branch, w_down_all, preferred_element_type=jnp.float32
    )
    sigmoid_pre = jax.nn.sigmoid(pre_act)
    grad_pre = (grad_act * sigmoid_pre * (1.0 + pre_act * (1.0 - sigmoid_pre))).astype(jnp.bfloat16)
    grad_bias_up = jnp.sum(grad_pre.astype(jnp.float32), axis=(0, 1))
    grad_up = jnp.einsum("scd,scf->df", normed_mid, grad_pre, preferred_element_type=jnp.float32)
    grad_normed_mid = jnp.einsum(
        "scf,df->scd", grad_pre, w_up_all, preferred_element_type=jnp.float32
    )
    grad_gain_mid = jnp.sum(grad_normed_mid * mid * rms_mid, axis=(0, 1))
    scaled_mid = grad_normed_mid * gain_mid.astype(jnp.float32)
    grad_mid = cotangent + rms_mid * (
        scaled_mid - mid * rms_mid * rms_mid * jnp.mean(scaled_mid * mid, axis=-1, keepdims=True)
    )
    grad_attn = grad_mid.astype(jnp.bfloat16)
    grad_wout = jnp.einsum("scf,scd->fd", attended, grad_attn, preferred_element_type=jnp.float32)
    grad_att_tokens = jnp.einsum(
        "scd,fd->scf", grad_attn, w_out_all, preferred_element_type=jnp.float32
    ).astype(jnp.bfloat16)
    grad_att_heads = lax.all_to_all(
        grad_att_tokens, "seq", split_axis=2, concat_axis=1, tiled=True
    ).reshape(seqs, length, local_heads, head_size)
    grad_packed = lax.map(attend_backward, (by_head, segment_ids, log_sums, grad_att_heads))
    grad_tokens = lax.all_to_all(
        shortened(grad_packed.reshape(seqs, length, local_heads * 3 * head_size)),
        "seq",
        split_axis=1,
        concat_axis=2,
        tiled=True,
    )
    grad_float = grad_tokens.reshape(seqs, span, heads, 3, head_size).astype(jnp.float32)
    query_float = projected.reshape(seqs, span, heads, 3, head_size)[:, :, :, 0, :]
    grad_factor = jnp.sum(query_float * grad_float[:, :, :, 0, :], axis=(0, 1, 2))
    grad_scale = grad_factor * (scale_base / math.sqrt(head_size)) * jax.nn.sigmoid(per_dim_scale)
    grad_proj = (
        (grad_float * factors).astype(jnp.bfloat16).reshape(seqs, span, heads * 3 * head_size)
    )
    grad_qkv = jnp.einsum("scd,scf->df", normed_in, grad_proj, preferred_element_type=jnp.float32)
    grad_normed_in = jnp.einsum(
        "scf,df->scd",
        grad_proj,
        w_qkv_all.reshape(width, heads * 3 * head_size),
        preferred_element_type=jnp.float32,
    )
    grad_gain_in = jnp.sum(grad_normed_in * x_float * rms_in, axis=(0, 1))
    scaled_in = grad_normed_in * gain_in.astype(jnp.float32)
    input_grad = grad_mid + rms_in * (
        scaled_in
        - x_float * rms_in * rms_in * jnp.mean(scaled_in * x_float, axis=-1, keepdims=True)
    )
    gain_in_rows = grad_gain_in.reshape(data_groups, -1)
    gain_mid_rows = grad_gain_mid.reshape(data_groups, -1)
    bias_up_rows = grad_bias_up.reshape(data_groups, -1)
    bias_down_rows = grad_bias_down.reshape(data_groups, -1)
    scale_tiled = jnp.broadcast_to(grad_scale[None, :], (data_groups, head_size))
    (
        part_gain_in,
        part_qkv,
        part_out,
        part_gain_mid,
        part_up,
        part_bias_up,
        part_down,
        part_bias_down,
        part_scale,
    ) = (
        lax.psum_scatter(
            gain_in_rows.astype(jnp.bfloat16), "dp", scatter_dimension=0, tiled=True
        ).astype(jnp.float32),
        lax.psum_scatter(
            grad_qkv.astype(jnp.bfloat16), "dp", scatter_dimension=0, tiled=True
        ).astype(jnp.float32),
        lax.psum_scatter(
            grad_wout.astype(jnp.bfloat16), "dp", scatter_dimension=0, tiled=True
        ).astype(jnp.float32),
        lax.psum_scatter(
            gain_mid_rows.astype(jnp.bfloat16), "dp", scatter_dimension=0, tiled=True
        ).astype(jnp.float32),
        lax.psum_scatter(
            grad_up.astype(jnp.bfloat16), "dp", scatter_dimension=0, tiled=True
        ).astype(jnp.float32),
        lax.psum_scatter(
            bias_up_rows.astype(jnp.bfloat16), "dp", scatter_dimension=0, tiled=True
        ).astype(jnp.float32),
        lax.psum_scatter(
            grad_down.astype(jnp.bfloat16), "dp", scatter_dimension=0, tiled=True
        ).astype(jnp.float32),
        lax.psum_scatter(
            bias_down_rows.astype(jnp.bfloat16), "dp", scatter_dimension=0, tiled=True
        ).astype(jnp.float32),
        lax.psum_scatter(
            scale_tiled.astype(jnp.bfloat16), "dp", scatter_dimension=0, tiled=True
        ).astype(jnp.float32),
    )
    (
        part_gain_in,
        part_qkv,
        part_out,
        part_gain_mid,
        part_up,
        part_bias_up,
        part_down,
        part_bias_down,
        part_scale,
    ) = (
        lax.psum(part_gain_in.astype(jnp.bfloat16), "seq").astype(jnp.float32),
        lax.psum(part_qkv.astype(jnp.bfloat16), "seq").astype(jnp.float32),
        lax.psum(part_out.astype(jnp.bfloat16), "seq").astype(jnp.float32),
        lax.psum(part_gain_mid.astype(jnp.bfloat16), "seq").astype(jnp.float32),
        lax.psum(part_up.astype(jnp.bfloat16), "seq").astype(jnp.float32),
        lax.psum(part_bias_up.astype(jnp.bfloat16), "seq").astype(jnp.float32),
        lax.psum(part_down.astype(jnp.bfloat16), "seq").astype(jnp.float32),
        lax.psum(part_bias_down.astype(jnp.bfloat16), "seq").astype(jnp.float32),
        lax.psum(part_scale.astype(jnp.bfloat16), "seq").astype(jnp.float32),
    )
    return (
        result.astype(jnp.bfloat16),
        input_grad,
        part_gain_in.reshape(-1),
        part_qkv.reshape(-1, heads, 3, head_size),
        part_scale.reshape(-1),
        part_out,
        part_gain_mid.reshape(-1),
        part_up,
        part_bias_up.reshape(-1),
        part_down,
        part_bias_down.reshape(-1),
    )


def solution(mesh):
    in_specs = (
        P("dp", "seq", None),
        P("dp", None),
        P("dp"),
        P("dp", None, None, None),
        P(),
        P("dp", None),
        P("dp"),
        P("dp", None),
        P("dp"),
        P("dp", None),
        P("dp"),
        P("dp", "seq", None),
    )
    out_specs = (
        P("dp", "seq", None),
        P("dp", "seq", None),
        P("dp"),
        P("dp", None, None, None),
        P(),
        P("dp", None),
        P("dp"),
        P("dp", None),
        P("dp"),
        P("dp", None),
        P("dp"),
    )
    return jax.shard_map(
        on_device, mesh=mesh, in_specs=in_specs, out_specs=out_specs, check_vma=False
    )
```

profile of v0, /device:TPU:12, one launch (start us, length us, event | category | flops | bytes accessed | tf_op | source)
XLA Modules:
  0.0 1920.8 jit_solution(3033586279104093381)
XLA Ops:
  7.3 6.4 copy.110
  15.7 10.7 all-reduce.13
  27.1 86.9 %all-gather.5.cloned.1.call-done = bf16[1280,16,3,80]{3,1,2,0:T(8,128)(2,1)} async-done(((bf16[320,16,3,80]{3,1,2,0:T(8,128)(2,1)}), bf16[1280,16,3,80]{3,1,2,0:T(8,128)(2,1)}) %all-gather.5.cloned.1.call-update) | async-done | bytes 9830416 | tf_op jit(solution)/shard_map/all_gather | solution.py:107
  114.0 19.1 copy.111
  133.1 16.6 multiply_convert_fusion.5
  149.7 31.2 %copy.112 = bf16[4,256,3840]{1,0,2:T(4,128)(2,1)} copy(bf16[4,256,3840]{1,2,0:T(8,128)(2,1)S(1)} %bitcast.440) | data formatting | bytes 15728640 | tf_op jit(solution)/shard_map/reshape | solution.py:136
  188.4 168.3 %all-to-all-done = bf16[4,256,3840]{1,0,2:T(4,128)(2,1)} async-done(((bf16[4,256,3840]{1,0,2:T(4,128)(2,1)}), bf16[4,256,3840]{1,0,2:T(4,128)(2,1)}, u32[]{:S(2)}, u32[]{:S(2)}) %all-to-all-start) | async-done | bytes 7864352 | tf_op jit(solution)/shard_map/all_to_all | solution.py:137
  361.0 7.8 copy.114
  368.8 12.8 reshape.636
  381.6 8.1 copy.115
  389.7 132.5 %while.22 = (s32[]{:T(128)}, bf16[4,2048,2,80]{1,3,2,0:T(8,128)(2,1)S(1)}, f32[4,2,2048]{2,1,0:T(2,128)S(1)}, bf16[4,2048,2,3,80]{1,4,2,3,0:T(8,128)(2,1)}, s32[...) while((s32[]{:T(128)}, bf16[4,2048,2,80]{1,3,2,0:T(8,128)(2,1)S(1)}, ...), condition=%wide.region_10.11_spmd, body=%wide.region_1.10_spmd.sunk | while | flops 2775394304 | bytes 129466536 | solution.py:140
  526.9 7.1 all-to-all-start.1
  534.7 89.7 %all-to-all-done.1 = bf16[4,2048,160]{2,0,1:T(4,128)(2,1)} async-done(((bf16[4,2048,160]{2,0,1:T(4,128)(2,1)}), bf16[4,2048,160]{2,0,1:T(4,128)(2,1)}, u32[]{:S(2)}, u32[]{:S(2)}) %all-to-all-start.1) | async-done | bytes 2621472 | tf_op jit(solution)/shard_map/all_to_all | solution.py:141
  624.4 7.1 copy.145
  631.5 8.9 multiply_reduce_fusion.6
  640.4 9.4 fusion.126
  649.9 10.4 fusion.144
  677.9 6.2 all-to-all-start.2
  684.0 57.2 %all-to-all-done.2 = bf16[4,256,1280]{1,0,2:T(4,128)(2,1)S(1)} async-done(((bf16[4,256,1280]{1,0,2:T(4,128)(2,1)}), bf16[4,256,1280]{1,0,2:T(4,128)(2,1)S(1)}, u32[]{:S(2)}, u32[]{:S(2)}) %all-to-all-start.2) | async-done | bytes 2621472 | tf_op jit(solution)/shard_map/all_to_all | solution.py:241
  746.2 474.4 %while.23 = (s32[]{:T(128)}, bf16[4,2048,2,3,80]{1,4,3,2,0:T(8,128)(2,1)}, bf16[4,2048,2,3,80]{1,4,2,3,0:T(8,128)(2,1)}, s32[4,2048]{1,0:T(4,128)S(1)}, f32[4,2,...) while((s32[]{:T(128)}, ...), condition=%wide.region_18.19_spmd, body=%wide.region_13.18_spmd.sunk | while | flops 6831667200 | bytes 568672896 | solution.py:244
  777.6 6.9 fusion.221
  800.0 7.2 multiply_reduce_fusion.11
  813.3 17.0 multiply_convert_fusion.16
  837.1 6.2 multiply_reduce_fusion.13
  849.4 16.8 multiply_convert_fusion.17
  888.7 6.9 fusion.221
  911.0 7.2 multiply_reduce_fusion.11
  924.3 17.0 multiply_convert_fusion.16
  948.1 6.2 multiply_reduce_fusion.13
  960.4 16.8 multiply_convert_fusion.17
  999.7 6.9 fusion.221
  1022.1 7.2 multiply_reduce_fusion.11
  1035.4 17.0 multiply_convert_fusion.16
  1059.2 6.2 multiply_reduce_fusion.13
  1065.4 6.1 multiply_reduce_fusion.14
  1071.5 16.8 multiply_convert_fusion.17
  1110.8 6.9 fusion.221
  1133.2 7.2 multiply_reduce_fusion.11
  1146.4 17.0 multiply_convert_fusion.16
  1170.2 6.2 multiply_reduce_fusion.13
  1176.5 6.1 multiply_reduce_fusion.14
  1182.6 16.8 multiply_convert_fusion.17
  1220.6 14.4 copy.125
  1235.1 7.4 all-to-all-start.3
  1242.6 179.9 %all-to-all-done.3 = bf16[4,2048,480]{2,0,1:T(4,128)(2,1)} async-done(((bf16[4,2048,480]{2,0,1:T(4,128)(2,1)}), bf16[4,2048,480]{2,0,1:T(4,128)(2,1)}, u32[]{:S(2)}, u32[]{:S(2)}) %all-to-all-start.3) | async-done | bytes 7864352 | tf_op jit(solution)/shard_map/all_to_all | solution.py:245
  1422.5 14.7 copy.126
  1437.3 10.7 convert_element_type.249
  1448.0 18.7 copy.152
  1466.7 16.0 copy.127
  1482.7 9.5 fusion.102
  1492.2 16.6 bitcast_convert_fusion
  1508.9 8.6 fusion.107
  1518.0 11.1 fusion.108
  1529.2 9.5 fusion.109
  1542.3 47.1 %reduce-scatter.5.cloned.1.call-done = bf16[320,3840]{1,0:T(8,128)(2,1)} async-done(((bf16[1280,3840]{1,0:T(8,128)(2,1)}), bf16[320,3840]{1,0:T(8,128)(2,1)}) %reduce-scatter.5.cloned.1.call-update) | async-done | bytes 2457616 | tf_op jit(solution)/shard_map/reduce_scatter | solution.py:291
  1593.8 37.3 %reduce-scatter.7.cloned.1.call-done = bf16[320,1280]{1,0:T(8,128)(2,1)} async-done(((bf16[1280,1280]{1,0:T(8,128)(2,1)}), bf16[320,1280]{1,0:T(8,128)(2,1)}) %reduce-scatter.7.cloned.1.call-update) | async-done | bytes 819216 | tf_op jit(solution)/shard_map/reduce_scatter | solution.py:294
  1631.2 41.3 %reduce-scatter.9.cloned.1.call-done = bf16[320,1280]{1,0:T(8,128)(2,1)} async-done(((bf16[1280,1280]{1,0:T(8,128)(2,1)}), bf16[320,1280]{1,0:T(8,128)(2,1)}) %reduce-scatter.9.cloned.1.call-update) | async-done | bytes 819216 | tf_op jit(solution)/shard_map/reduce_scatter | solution.py:300
  1672.5 41.3 %reduce-scatter.11.cloned.1.call-done = bf16[320,1280]{1,0:T(8,128)(2,1)} async-done(((bf16[1280,1280]{1,0:T(8,128)(2,1)}), bf16[320,1280]{1,0:T(8,128)(2,1)}) %reduce-scatter.11.cloned.1.call-update) | async-done | bytes 819216 | tf_op jit(solution)/shard_map/reduce_scatter | solution.py:306
  1713.8 27.4 %fusion.120 = (bf16[1280]{0:T(1024)(128)(2,1)S(1)}, f32[4,256]{1,0:T(4,128)S(1)}, f32[4,256,1280,1,1]{2,1,4,3,0:T(8,128)}) fusion(bf16[4,256,1280]{2,1,0:T(8,128)(2,1)S(1)} %copy-done.16, f32[4,256]{1,0:T(4,128)S(1)} %copy-done.32, f32[1280]{0:T(1024)S(1)} %copy-done.26, bf16[1280,16,3,80,1]{3,1,2,0,4:T(8,128)(2,1)} %bitcast.434, ...), kind=kOutput, calls=%fused_computation.197 | convolution fusion | flops 10083366912 | bytes 33440192 | tf_op jit(solution)/shard_map/scf,df->scd/dot_general | solution.py:260
  1746.2 10.8 all-reduce.12
  1759.0 20.8 %all-reduce.10 = (bf16[320]{0:T(512)(128)(2,1)S(1)}, bf16[80]{0:T(256)(128)(2,1)S(1)}, bf16[320]{0:T(512)(128)(2,1)S(1)}, bf16[320]{0:T(512)(128)(2,1)S(1)}, bf16[320]{0:T(512)(128)(2,1)S(1)}) all-reduce(bf16[320]{0:T(512)(128)(2,1)S(1)} %get-tuple-element.230, ...), channel_id=1, replica_groups=mesh['dp'=4,'seq'=8] {'seq'}, use_global_device_ids=true, to_apply=%region_22.23 | all-reduce | flops 1360 | bytes 5440 | tf_op jit(solution)/shard_map/psum | solution.py:327
  1782.6 6.5 fusion.116
  1789.1 9.1 add_convert_fusion
  1798.2 107.1 %all-reduce.16.cloned.1.call-done = (bf16[320,16,3,80]{0,3,2,1:T(8,128)(2,1)}, bf16[320,1280]{1,0:T(8,128)(2,1)}, bf16[320,1280]{1,0:T(8,128)(2,1)}, bf16[320,1280]{1,0:T(8,128)(2,1)}) async-done(((bf16[320,16,3,80]{0,3,2,1:T(8,128)(2,1)}, bf16[320,1280]{1,0:T(8,128)(2,1)}, bf16[320,1280]{1,0:T(8,128)(2,1)}, bf16[320,1280]{1,0:T(8,128)(2,1)}), (bf16[320,16,3,80]{0,3,2,1:T(8,128)(2,1)}, ...) | async-done | bytes 4915216 | tf_op jit(solution)/shard_map/psum | solution.py:328
  (493 shorter events, 415.9 us)
Async XLA Ops:
  7.2 6.5 copy-start.41
  7.2 7.7 copy-start.42
  7.2 8.0 copy-start.43
  7.2 8.2 copy-start.44
  7.2 19.2 %copy-start.48 = (f32[80]{0:T(128)S(1)}, f32[80]{0:T(128)}, u32[]{:S(2)}) copy-start(f32[80]{0:T(128)} %param.20) | copy-start | bytes 964
  7.2 19.2 %copy-start.14 = (bf16[4,256,1280]{2,1,0:T(8,128)(2,1)S(1)}, bf16[4,256,1280]{2,1,0:T(8,128)(2,1)}, u32[]{:S(2)}) copy-start(bf16[4,256,1280]{2,1,0:T(8,128)(2,1)} %param.16) | copy-start | bytes 7864324
  7.2 106.7 %all-gather.5.cloned.1.call-start = ((), (), s32[]{:S(2)}) async-start(), calls=%async_computation.8 | async-start | bytes 19660800 | tf_op jit(solution)/shard_map/all_gather | solution.py:107
  26.5 106.6 %copy-start.25 = (f32[1280]{0:T(1024)}, f32[1280]{0:T(1024)S(1)}, u32[]{:S(2)}) copy-start(f32[1280]{0:T(1024)S(1)} %convert_element_type.210) | copy-start | bytes 15364
  26.5 106.6 %copy-start.33 = (f32[3,80]{1,0:T(4,128)}, f32[3,80]{1,0:T(4,128)S(1)}, u32[]{:S(2)}) copy-start(f32[3,80]{1,0:T(4,128)S(1)} %stack.20) | copy-start | bytes 2884
  27.1 106.0 %copy-start.31 = (f32[4,256]{1,0:T(4,128)}, f32[4,256]{1,0:T(4,128)S(1)}, u32[]{:S(2)}) copy-start(f32[4,256]{1,0:T(4,128)S(1)} %add_rsqrt_fusion.1) | copy-start | bytes 12292
  180.9 175.8 %all-to-all-start = ((bf16[4,256,3840]{1,0,2:T(4,128)(2,1)}), bf16[4,256,3840]{1,0,2:T(4,128)(2,1)}, u32[]{:S(2)}, u32[]{:S(2)}) async-start(bf16[4,256,3840]{1,0,2:T(4,128)(2,1)} %copy.112), calls=%async_computation | async-start | bytes 15728640 | tf_op jit(solution)/shard_map/all_to_all | solution.py:137
  186.9 444.6 %all-gather.7.cloned.1.call-start = ((), (), s32[]{:S(2)}) async-start(), calls=%async_computation.9 | async-start | bytes 4096000 | tf_op jit(solution)/shard_map/all_gather | solution.py:108
  187.7 452.7 %all-gather.9.cloned.1.call-start = ((), (), s32[]{:S(2)}) async-start(), calls=%async_computation.10 | async-start | bytes 4096000 | tf_op jit(solution)/shard_map/all_gather | solution.py:110
  381.6 8.1 copy-start.20
  381.6 8.1 copy-start.24
  526.9 7.7 copy-start.38
  526.9 7.7 copy-start.37
  526.9 97.5 %all-to-all-start.1 = ((bf16[4,2048,160]{2,0,1:T(4,128)(2,1)}), bf16[4,2048,160]{2,0,1:T(4,128)(2,1)}, u32[]{:S(2)}, u32[]{:S(2)}) async-start(bf16[4,2048,160]{2,0,1:T(4,128)(2,1)} %copy.116), calls=%async_computation.1 | async-start | bytes 8388608 | tf_op jit(solution)/shard_map/all_to_all | solution.py:141
  534.1 97.5 %copy-start.15 = (bf16[4,256,1280]{2,1,0:T(8,128)(2,1)S(1)}, bf16[4,256,1280]{2,1,0:T(8,128)(2,1)}, u32[]{:S(2)}) copy-start(bf16[4,256,1280]{2,1,0:T(8,128)(2,1)} %param.16) | copy-start | bytes 7864324
  534.1 115.8 %all-gather.11.cloned.1.call-start = ((), (), s32[]{:S(2)}) async-start(), calls=%async_computation.11 | async-start | bytes 4096000 | tf_op jit(solution)/shard_map/all_gather | solution.py:112
  534.6 130.4 %copy-start.27 = (f32[1280]{0:T(1024)}, f32[1280]{0:T(1024)S(1)}, u32[]{:S(2)}) copy-start(f32[1280]{0:T(1024)S(1)} %convert_element_type.213) | copy-start | bytes 15364
  534.7 115.2 %copy-start.35 = (f32[1280]{0:T(1024)}, f32[1280]{0:T(1024)S(1)}, u32[]{:S(2)}) copy-start(f32[1280]{0:T(1024)S(1)} %convert_element_type.215) | copy-start | bytes 15364
  640.4 24.6 %copy-start.29 = (f32[4,256]{1,0:T(4,128)}, f32[4,256]{1,0:T(4,128)S(1)}, u32[]{:S(2)}) copy-start(f32[4,256]{1,0:T(4,128)S(1)} %add_rsqrt_fusion) | copy-start | bytes 12292
  649.9 10.4 copy-start.17
  649.9 10.4 copy-start.47
  677.9 63.4 %all-to-all-start.2 = ((bf16[4,256,1280]{1,0,2:T(4,128)(2,1)}), bf16[4,256,1280]{1,0,2:T(4,128)(2,1)S(1)}, u32[]{:S(2)}, u32[]{:S(2)}) async-start(bf16[4,256,1280]{1,0,2:T(4,128)(2,1)} %copy.120), calls=%async_computation.2 | async-start | bytes 5242880 | tf_op jit(solution)/shard_map/all_to_all | solution.py:241
  777.6 18.0 copy-start.10
  777.6 22.4 %copy-start.12 = (pred[512,2048]{1,0:T(8,128)(4,1)}, pred[512,2048]{1,0:T(8,128)(4,1)S(1)}, u32[]{:S(2)}) copy-start(pred[512,2048]{1,0:T(8,128)(4,1)S(1)} %get-tuple-element.368) | copy-start | bytes 3145732 | tf_op jit(solution)/shard_map/while
  777.6 29.6 %copy-start.9 = (pred[512,2048]{1,0:T(8,128)(4,1)}, pred[512,2048]{1,0:T(8,128)(4,1)S(1)}, u32[]{:S(2)}) copy-start(pred[512,2048]{1,0:T(8,128)(4,1)S(1)} %get-tuple-element.370) | copy-start | bytes 3145732 | tf_op jit(solution)/shard_map/while
  785.8 21.4 %copy-start.3 = (f32[2,512,2048]{2,1,0:T(8,128)}, f32[2,512,2048]{2,1,0:T(8,128)S(1)}, u32[]{:S(2)}) copy-start(f32[2,512,2048]{2,1,0:T(8,128)S(1)} %fusion.222) | copy-start | bytes 25165828 | tf_op jit(solution)/shard_map/while
  830.2 6.4 copy-start.2
  833.7 9.6 slice-start
  888.6 18.0 copy-start.10
  888.6 22.4 %copy-start.12 = (pred[512,2048]{1,0:T(8,128)(4,1)}, pred[512,2048]{1,0:T(8,128)(4,1)S(1)}, u32[]{:S(2)}) copy-start(pred[512,2048]{1,0:T(8,128)(4,1)S(1)} %get-tuple-element.368) | copy-start | bytes 3145732 | tf_op jit(solution)/shard_map/while
  888.6 29.6 %copy-start.9 = (pred[512,2048]{1,0:T(8,128)(4,1)}, pred[512,2048]{1,0:T(8,128)(4,1)S(1)}, u32[]{:S(2)}) copy-start(pred[512,2048]{1,0:T(8,128)(4,1)S(1)} %get-tuple-element.370) | copy-start | bytes 3145732 | tf_op jit(solution)/shard_map/while
  896.8 21.4 %copy-start.3 = (f32[2,512,2048]{2,1,0:T(8,128)}, f32[2,512,2048]{2,1,0:T(8,128)S(1)}, u32[]{:S(2)}) copy-start(f32[2,512,2048]{2,1,0:T(8,128)S(1)} %fusion.222) | copy-start | bytes 25165828 | tf_op jit(solution)/shard_map/while
  941.3 6.4 copy-start.2
  944.7 9.6 slice-start
  999.7 18.0 copy-start.10
  999.7 22.4 %copy-start.12 = (pred[512,2048]{1,0:T(8,128)(4,1)}, pred[512,2048]{1,0:T(8,128)(4,1)S(1)}, u32[]{:S(2)}) copy-start(pred[512,2048]{1,0:T(8,128)(4,1)S(1)} %get-tuple-element.368) | copy-start | bytes 3145732 | tf_op jit(solution)/shard_map/while
  999.7 29.6 %copy-start.9 = (pred[512,2048]{1,0:T(8,128)(4,1)}, pred[512,2048]{1,0:T(8,128)(4,1)S(1)}, u32[]{:S(2)}) copy-start(pred[512,2048]{1,0:T(8,128)(4,1)S(1)} %get-tuple-element.370) | copy-start | bytes 3145732 | tf_op jit(solution)/shard_map/while
  1007.9 21.4 %copy-start.3 = (f32[2,512,2048]{2,1,0:T(8,128)}, f32[2,512,2048]{2,1,0:T(8,128)S(1)}, u32[]{:S(2)}) copy-start(f32[2,512,2048]{2,1,0:T(8,128)S(1)} %fusion.222) | copy-start | bytes 25165828 | tf_op jit(solution)/shard_map/while
  1052.4 6.4 copy-start.2
  1055.8 9.6 slice-start
  1110.7 18.0 copy-start.10
  1110.8 22.4 %copy-start.12 = (pred[512,2048]{1,0:T(8,128)(4,1)}, pred[512,2048]{1,0:T(8,128)(4,1)S(1)}, u32[]{:S(2)}) copy-start(pred[512,2048]{1,0:T(8,128)(4,1)S(1)} %get-tuple-element.368) | copy-start | bytes 3145732 | tf_op jit(solution)/shard_map/while
  1110.8 29.6 %copy-start.9 = (pred[512,2048]{1,0:T(8,128)(4,1)}, pred[512,2048]{1,0:T(8,128)(4,1)S(1)}, u32[]{:S(2)}) copy-start(pred[512,2048]{1,0:T(8,128)(4,1)S(1)} %get-tuple-element.370) | copy-start | bytes 3145732 | tf_op jit(solution)/shard_map/while
  1118.9 21.4 %copy-start.3 = (f32[2,512,2048]{2,1,0:T(8,128)}, f32[2,512,2048]{2,1,0:T(8,128)S(1)}, u32[]{:S(2)}) copy-start(f32[2,512,2048]{2,1,0:T(8,128)S(1)} %fusion.222) | copy-start | bytes 25165828 | tf_op jit(solution)/shard_map/while
  1166.9 9.6 slice-start
  1235.1 7.5 copy-start.34
  1235.1 187.4 %all-to-all-start.3 = ((bf16[4,2048,480]{2,0,1:T(4,128)(2,1)}), bf16[4,2048,480]{2,0,1:T(4,128)(2,1)}, u32[]{:S(2)}, u32[]{:S(2)}) async-start(bf16[4,2048,480]{2,0,1:T(4,128)(2,1)} %copy.125), calls=%async_computation.3 | async-start | bytes 16777216 | tf_op jit(solution)/shard_map/all_to_all | solution.py:245
  1242.5 346.9 %reduce-scatter.5.cloned.1.call-start = ((), (), s32[]{:S(2)}) async-start(), calls=%async_computation.12 | async-start | bytes 12288000 | tf_op jit(solution)/shard_map/reduce_scatter | solution.py:291
  1482.7 9.5 copy-start.16
  1482.7 9.5 copy-start.26
  1482.7 9.5 copy-start.32
  1508.8 9.1 copy-start.28
  1508.9 9.1 copy-start.30
  1508.9 122.3 %reduce-scatter.7.cloned.1.call-start = ((), (), s32[]{:S(2)}) async-start(), calls=%async_computation.13 | async-start | bytes 4096000 | tf_op jit(solution)/shard_map/reduce_scatter | solution.py:294
  1517.5 11.7 copy-start.36
  1517.5 155.0 %reduce-scatter.9.cloned.1.call-start = ((), (), s32[]{:S(2)}) async-start(), calls=%async_computation.14 | async-start | bytes 4096000 | tf_op jit(solution)/shard_map/reduce_scatter | solution.py:300
  1529.1 184.6 %reduce-scatter.11.cloned.1.call-start = ((), (), s32[]{:S(2)}) async-start(), calls=%async_computation.15 | async-start | bytes 4096000 | tf_op jit(solution)/shard_map/reduce_scatter | solution.py:306
  1538.8 366.5 %all-reduce.16.cloned.1.call-start = ((), (), s32[]{:S(2)}) async-start(), calls=%async_computation.16 | async-start | bytes 10813440 | tf_op jit(solution)/shard_map/psum | solution.py:328
  1782.6 6.5 copy-start.46
  1905.3 7.5 copy-start.21
  (50 other events, 189.3 us)
Sparse Core Ops, SparseCore 0:
  13.8 100.1 all-gather.4
  189.3 29.1 all-gather.6
  220.1 29.2 all-gather.8
  536.1 29.2 all-gather.10
  1509.0 80.3 reduce-scatter.4
  1592.4 38.7 reduce-scatter.6
  1633.7 38.6 reduce-scatter.8
  1675.0 38.6 reduce-scatter.10
  1717.8 187.4 all-reduce.15
where the time goes:
time: 1940 us; the launch traced here: 1920 us
  waiting for transfers between devices  858 us (44%)
  matrix products  477 us (25%)
  other arithmetic  262 us (14%)
  local copies, waits for them, and re-layouts  207 us (11%)
  blocking collectives  42.2 us (2%)
  loops' own time  31.9 us (2%)
  starting transfers between devices  28.1 us (1%)
    all_to_all x1, waiting for transfers between devices, on_device(): lax.all_to_all(shortened(grad_packed.reshape(seqs, length, local_heads *...  180 us
    all_to_all x1, waiting for transfers between devices, forward(): lax.all_to_all(outgoing, 'seq', split_axis=2, concat_axis=1, tiled=True)  168 us
    convert_element_type x8, other arithmetic, attend_backward(): (attention_weights * (grad_weights - inner)).astype(jnp.bfloat16)  135 us
    psum x1, waiting for transfers between devices, on_device(): lax.psum(part_qkv.astype(jnp.bfloat16), 'seq').astype(jnp.float32)  107 us
    dot_general x16, matrix products, attend_backward(): jnp.einsum('qhe,khe->hqk', grad_block, values_in, preferred_element_type=...  102 us
    all_to_all x1, waiting for transfers between devices, forward(): lax.all_to_all(shortened(attended_heads.reshape(seqs, length, local_heads...  89.7 us
    all_gather x1, waiting for transfers between devices, collect(): lax.all_gather(w_qkv, 'dp', axis=0, tiled=True)  86.9 us
    dot_general x16, matrix products, attend_backward(): jnp.einsum('hqk,qhe->khe', attention_weights.astype(jnp.bfloat16), grad_b...  73.8 us
  transfers between devices with their start and end apart: 13, of which 10 were waited for; matrix products, arithmetic and copies ran while one was open for 15% of the time, Pallas kernels for 0%

commit v1 on v0

v1 whole, which is shorter than its diff:
```python
import functools
import math

import jax
import jax.numpy as jnp
from jax import lax
from jax.experimental import pallas as pl
from jax.experimental.pallas import tpu as pltpu
from jax.sharding import PartitionSpec as P

epsilon = 1e-06
scale_base = 1.442695041
log2e = 1.4426950408889634
masked_value = -1e30
score_limit = 100.0
bf16 = jnp.bfloat16
f32 = jnp.float32
axes = ("dp", "seq")
nt = (((1,), (1,)), ((), ()))
nn = (((1,), (0,)), ((), ()))


def mm(a, b, dims=nn):
    return lax.dot_general(a, b, dims, preferred_element_type=f32)


class Team:
    def __init__(self, dp, seq, seqs):
        self.dp, self.seq, self.seqs = dp, seq, seqs
        self.size = seq // seqs
        assert seq % seqs == 0 and self.size % 2 == 0 and dp % 2 == 0
        self.half = self.size // 2
        self.rows = dp // 2

    def places(self):
        for row in range(self.rows):
            for core in range(2):
                for place in range(self.seq):
                    yield row, core, place

    def rank(self, row, core, place):
        return (row * 2 + core) * self.seq + place

    def here(self):
        d = lax.axis_index("dp")
        p = lax.axis_index("seq")
        row, core = d // 2, d % 2
        group = p // self.size
        side = (p % self.size) // self.half
        member = (p % self.half) * 2 + core
        return row, core, group, side, member

    def spread(self, step):
        pairs = []
        for row, core, place in self.places():
            z, u = place // self.size, place % self.size
            s = (z + step) % self.seqs
            pairs.append(
                (
                    self.rank(row, core, place),
                    self.rank(row, u % 2, s * self.size + core * self.half + u // 2),
                )
            )
        return pairs

    def back(self, step):
        return [(b, a) for a, b in self.spread(step)]

    def rotate(self, step):
        pairs = []
        for row, core, place in self.places():
            base = place - place % self.half
            m = (place % self.half) * 2 + core
            to = (m + step) % self.size
            pairs.append((self.rank(row, core, place), self.rank(row, to % 2, base + to // 2)))
        return pairs

    def swap_core(self):
        return [(d, d ^ 1) for d in range(self.dp)]

    def turn_rows(self, step):
        return [(d, (d + 2 * step) % self.dp) for d in range(self.dp)]


def place_in(pieces, count):
    first = pieces[0][0]
    out = jnp.zeros((count,) + first.shape, first.dtype)
    for piece, index in pieces:
        out = lax.dynamic_update_index_in_dim(out, piece, index, 0)
    return out


def gather_dp(team, shard, row, core):
    mine = [(shard, row)]
    for step in range(1, team.rows):
        got = lax.ppermute(shard, "dp", team.turn_rows(step))
        mine.append((got, (row - step) % team.rows))
    mine = place_in(mine, team.rows)
    theirs = lax.ppermute(mine, "dp", team.swap_core())
    first = jnp.where(core == 0, mine, theirs)
    second = jnp.where(core == 0, theirs, mine)
    return jnp.stack([first, second], axis=1).reshape((team.dp,) + shard.shape)


def qkv_kernel(head_size, x_ref, gain_ref, w_ref, factor_ref, out_ref, normed_ref):
    x = x_ref[...].astype(f32)
    rms = lax.rsqrt(jnp.mean(x * x, axis=-1, keepdims=True) + epsilon)
    normed = (x * rms * gain_ref[...]).astype(bf16)
    normed_ref[...] = normed
    packed = (mm(normed, w_ref[...]) * factor_ref[...]).astype(bf16)
    for i in range(packed.shape[1] // head_size):
        out_ref[i // 3, i % 3] = packed[:, i * head_size : (i + 1) * head_size]


def project_qkv(x, gain, w, factor_row, heads, head_size, block):
    tokens, width = x.shape
    wide = w.shape[1]
    return pl.pallas_call(
        functools.partial(qkv_kernel, head_size),
        grid=(tokens // block,),
        in_specs=[
            pl.BlockSpec((block, width), lambda i: (i, 0)),
            pl.BlockSpec((1, width), lambda i: (0, 0)),
            pl.BlockSpec((width, wide), lambda i: (0, 0)),
            pl.BlockSpec((1, wide), lambda i: (0, 0)),
        ],
        out_specs=[
            pl.BlockSpec((heads, 3, block, head_size), lambda i: (0, 0, i, 0)),
            pl.BlockSpec((block, width), lambda i: (i, 0)),
        ],
        out_shape=[
            jax.ShapeDtypeStruct((heads, 3, tokens, head_size), bf16),
            jax.ShapeDtypeStruct((tokens, width), bf16),
        ],
        compiler_params=pltpu.CompilerParams(vmem_limit_bytes=56 << 20),
        cost_estimate=pl.CostEstimate(
            flops=2 * tokens * width * wide,
            bytes_accessed=tokens * width * 4 + width * wide * 2 + tokens * wide * 4,
            transcendentals=0,
        ),
        name="qkv",
    )(x, gain, w, factor_row)


def eye_rows(rows, columns):
    a = lax.broadcasted_iota(jnp.int32, (rows, columns), 0)
    b = lax.broadcasted_iota(jnp.int32, (rows, columns), 1)
    return (a == b).astype(bf16)


def attend_kernel(count, block, pair, table, qkv_ref, start_ref, att_ref, lse_ref, vt_ref, acc_ref):
    size = qkv_ref.shape[3]
    rows = vt_ref.shape[1]
    unit = eye_rows(rows, size)
    one_row = (lax.broadcasted_iota(jnp.int32, (rows, block), 0) == size).astype(f32)
    for h in range(pair):
        for b in range(count):
            here = slice(b * block, (b + 1) * block)
            vt_ref[h, :, here] = (mm(unit, qkv_ref[h, 2, here, :], nt) + one_row).astype(bf16)
    key_index = lax.broadcasted_iota(jnp.int32, (block, block), 0)
    lane_index = lax.broadcasted_iota(jnp.int32, (1, block), 1)
    ones = jnp.ones((8, size), bf16)

    def longest(part):
        best = jnp.zeros((8, block), f32)
        for h in range(pair):
            for b in range(count):
                x = qkv_ref[h, part, b * block : (b + 1) * block, :]
                best = jnp.maximum(best, mm(ones, x * x, nt))
        return jnp.max(best)

    small = longest(0) * longest(1) * 1.1 < score_limit * score_limit

    def query_block(raised, i, carry):
        at = pl.multiple_of(table[0, i] * block, block)
        starts = start_ref[pl.ds(i, 1), :]
        places = lane_index + i * block
        queries = [qkv_ref[h, 0, pl.ds(at, block), :] for h in range(pair)]
        acc_ref[...] = jnp.zeros_like(acc_ref)

        def step(masked, j, peaks):
            key_at = pl.multiple_of(table[0, j] * block, block)
            if masked:
                keys_here = key_index + j * block
                seen = (keys_here >= starts) & (keys_here <= places)
            out = []
            for h in range(pair):
                s = mm(qkv_ref[h, 1, pl.ds(key_at, block), :], queries[h], nt)
                if masked:
                    s = jnp.where(seen, s, masked_value)
                values = vt_ref[h, :, pl.ds(key_at, block)]
                if raised:
                    peak = jnp.maximum(peaks[h], jnp.max(s, axis=0, keepdims=True))
                    p = jnp.exp2(s - peak).astype(bf16)
                    acc_ref[h] = acc_ref[h] * jnp.exp2(peaks[h] - peak) + mm(values, p)
                    out.append(peak)
                else:
                    acc_ref[h] += mm(values, jnp.exp2(s).astype(bf16))
            return tuple(out)

        peaks = ()
        if raised:
            peaks = tuple(jnp.full((1, block), masked_value, f32) for _ in range(pair))
        peaks = lax.fori_loop(table[1, i], table[2, i], functools.partial(step, True), peaks)
        peaks = lax.fori_loop(table[2, i], i, functools.partial(step, False), peaks)
        peaks = step(True, i, peaks)
        for h in range(pair):
            total = acc_ref[h, size : size + 1, :]
            att_ref[h * size : (h + 1) * size, pl.ds(at, block)] = (
                acc_ref[h, :size, :] / total
            ).astype(bf16)
            low = jnp.log2(total)
            lse_ref[h, :, pl.ds(at, block)] = peaks[h] + low if raised else low
        return carry

    @pl.when(small)
    def plain():
        lax.fori_loop(0, count, functools.partial(query_block, False), 0)

    @pl.when(jnp.logical_not(small))
    def careful():
        lax.fori_loop(0, count, functools.partial(query_block, True), 0)


def attend(table, qkv, starts, pair=2):
    heads, _, length, size = qkv.shape
    count, block = starts.shape
    rows = (size // 16 + 1) * 16
    return pl.pallas_call(
        functools.partial(attend_kernel, count, block, pair),
        grid_spec=pltpu.PrefetchScalarGridSpec(
            num_scalar_prefetch=1,
            grid=(heads // pair,),
            in_specs=[
                pl.BlockSpec((pair, 3, length, size), lambda g, t: (g, 0, 0, 0)),
                pl.BlockSpec((count, block), lambda g, t: (0, 0)),
            ],
            out_specs=[
                pl.BlockSpec((pair * size, length), lambda g, t: (g, 0)),
                pl.BlockSpec((pair, 1, length), lambda g, t: (g, 0, 0)),
            ],
            scratch_shapes=[
                pltpu.VMEM((pair, rows, length), bf16),
                pltpu.VMEM((pair, rows, block), f32),
            ],
        ),
        out_shape=[
            jax.ShapeDtypeStruct((heads * size, length), bf16),
            jax.ShapeDtypeStruct((heads, 1, length), f32),
        ],
        compiler_params=pltpu.CompilerParams(vmem_limit_bytes=56 << 20),
        cost_estimate=pl.CostEstimate(
            flops=heads * length * length * size * 2,
            bytes_accessed=heads * length * size * 10,
            transcendentals=heads * length * length // 4,
        ),
        name="attend",
    )(table, qkv, starts)


def attend_back_kernel(
    count,
    block,
    pair,
    table,
    qkv_ref,
    att_ref,
    grad_ref,
    lse_ref,
    start_ref,
    factor_ref,
    out_ref,
    dots_ref,
    qt_ref,
    kt_ref,
    delta_ref,
    dq_ref,
    dk_ref,
    dv_ref,
):
    size = qkv_ref.shape[3]
    unit = eye_rows(size, size)
    for h in range(pair):
        for b in range(count):
            here = slice(b * block, (b + 1) * block)
            qt_ref[h, :, here] = mm(unit, qkv_ref[h, 0, here, :], nt).astype(bf16)
            kt_ref[h, :, here] = mm(unit, qkv_ref[h, 1, here, :], nt).astype(bf16)
        rows = slice(h * size, (h + 1) * size)
        delta_ref[h] = jnp.sum(
            att_ref[rows, :].astype(f32) * grad_ref[rows, :].astype(f32), axis=0, keepdims=True
        )
    dq_ref[...] = jnp.zeros_like(dq_ref)
    key_index = lax.broadcasted_iota(jnp.int32, (block, block), 0)
    lane_index = lax.broadcasted_iota(jnp.int32, (1, block), 1)

    def key_block(j, carry):
        key_at = pl.multiple_of(table[0, j] * block, block)
        keys_here = key_index + j * block
        dk_ref[...] = jnp.zeros_like(dk_ref)
        dv_ref[...] = jnp.zeros_like(dv_ref)

        def step(masked, i, inner):
            at = pl.multiple_of(table[0, i] * block, block)
            if masked:
                seen = (keys_here >= start_ref[pl.ds(i, 1), :]) & (
                    keys_here <= lane_index + i * block
                )
            for h in range(pair):
                grads = grad_ref[h * size : (h + 1) * size, pl.ds(at, block)]
                s = mm(qkv_ref[h, 1, pl.ds(key_at, block), :], qt_ref[h, :, pl.ds(at, block)])
                p = jnp.exp2(s - lse_ref[h, :, pl.ds(at, block)])
                if masked:
                    p = jnp.where(seen, p, 0.0)
                dp = mm(qkv_ref[h, 2, pl.ds(key_at, block), :], grads)
                ds = (p * (dp - delta_ref[h, :, pl.ds(at, block)])).astype(bf16)
                dv_ref[h] += mm(grads, p.astype(bf16), nt)
                dk_ref[h] += mm(qt_ref[h, :, pl.ds(at, block)], ds, nt)
                dq_ref[h, :, pl.ds(at, block)] += mm(kt_ref[h, :, pl.ds(key_at, block)], ds)
            return inner

        step(True, j, 0)
        lax.fori_loop(j + 1, table[3, j], functools.partial(step, False), 0)
        lax.fori_loop(table[3, j], table[4, j], functools.partial(step, True), 0)
        for h in range(pair):
            base = h * 3 * size
            out_ref[base + size : base + 2 * size, pl.ds(key_at, block)] = (
                dk_ref[h] * (1.0 / log2e)
            ).astype(bf16)
            out_ref[base + 2 * size : base + 3 * size, pl.ds(key_at, block)] = dv_ref[h].astype(bf16)
        return carry

    lax.fori_loop(0, count, key_block, 0)

    @pl.when(pl.program_id(0) == 0)
    def clear():
        dots_ref[...] = jnp.zeros_like(dots_ref)

    for h in range(pair):
        base = h * 3 * size
        rounded = dq_ref[h].astype(bf16).astype(f32)
        dots_ref[...] += jnp.sum(qt_ref[h].astype(f32) * rounded, axis=1, keepdims=True)
        out_ref[base : base + size, :] = (rounded * factor_ref[...]).astype(bf16)


def attend_back(chunk, table, qkv, att, grad, lse, starts, factor, pair=2):
    heads, _, length, size = qkv.shape
    count, block = starts.shape
    return pl.pallas_call(
        functools.partial(attend_back_kernel, count, block, pair),
        grid_spec=pltpu.PrefetchScalarGridSpec(
            num_scalar_prefetch=1,
            grid=(1,),
            in_specs=[
                pl.BlockSpec((pair, 3, length, size), lambda g, t: (chunk, 0, 0, 0)),
                pl.BlockSpec((pair * size, length), lambda g, t: (chunk, 0)),
                pl.BlockSpec((pair * size, length), lambda g, t: (chunk, 0)),
                pl.BlockSpec((pair, 1, length), lambda g, t: (chunk, 0, 0)),
                pl.BlockSpec((count, block), lambda g, t: (0, 0)),
                pl.BlockSpec((size, 1), lambda g, t: (0, 0)),
            ],
            out_specs=[
                pl.BlockSpec((pair * 3 * size, length), lambda g, t: (0, 0)),
                pl.BlockSpec((size, 1), lambda g, t: (0, 0)),
            ],
            scratch_shapes=[
                pltpu.VMEM((pair, size, length), bf16),
                pltpu.VMEM((pair, size, length), bf16),
                pltpu.VMEM((pair, 1, length), f32),
                pltpu.VMEM((pair, size, length), f32),
                pltpu.VMEM((pair, size, block), f32),
                pltpu.VMEM((pair, size, block), f32),
            ],
        ),
        out_shape=[
            jax.ShapeDtypeStruct((pair * 3 * size, length), bf16),
            jax.ShapeDtypeStruct((size, 1), f32),
        ],
        compiler_params=pltpu.CompilerParams(vmem_limit_bytes=56 << 20),
        cost_estimate=pl.CostEstimate(
            flops=pair * length * length * size * 5,
            bytes_accessed=pair * length * size * 20,
            transcendentals=pair * length * length // 4,
        ),
        name="attend_back",
    )(table, qkv, att, grad, lse, starts, factor)


def input_side_kernel(count, *refs):
    w_ref, out_ref = refs[count], refs[count + 1]
    grads = jnp.concatenate([ref[...] for ref in refs[:count]], axis=0)
    out_ref[...] = mm(grads.T, w_ref[...], nt).astype(bf16)


def input_side(grads, w, block):
    width, wide = w.shape
    rows, tokens = grads[0].shape
    return pl.pallas_call(
        functools.partial(input_side_kernel, len(grads)),
        grid=(tokens // block,),
        in_specs=[pl.BlockSpec((rows, block), lambda i: (0, i)) for _ in grads]
        + [pl.BlockSpec((width, wide), lambda i: (0, 0))],
        out_specs=pl.BlockSpec((block, width), lambda i: (i, 0)),
        out_shape=jax.ShapeDtypeStruct((tokens, width), bf16),
        compiler_params=pltpu.CompilerParams(vmem_limit_bytes=56 << 20),
        cost_estimate=pl.CostEstimate(
            flops=2 * tokens * width * wide,
            bytes_accessed=tokens * width * 2 + width * wide * 2 + tokens * wide * 2,
            transcendentals=0,
        ),
        name="input_side",
    )(*grads, w)


def reduce_places(buf, places):
    place = lax.axis_index("seq")
    rows = buf.shape[0]
    bits = places.bit_length() - 1
    assert places == 1 << bits and rows % places == 0
    for b in range(bits):
        bit = (place >> b) & 1
        halves = buf.reshape((2, -1) + buf.shape[1:])
        keep = lax.dynamic_index_in_dim(halves, bit, 0, keepdims=False)
        send = lax.dynamic_index_in_dim(halves, 1 - bit, 0, keepdims=False)
        got = lax.ppermute(send, "seq", [(i, i ^ (1 << b)) for i in range(places)])
        buf = (keep.astype(f32) + got.astype(f32)).astype(bf16)
    for b in reversed(range(bits)):
        bit = (place >> b) & 1
        got = lax.ppermute(buf, "seq", [(i, i ^ (1 << b)) for i in range(places)])
        buf = jnp.where(
            bit == 0, jnp.concatenate([buf, got], axis=0), jnp.concatenate([got, buf], axis=0)
        )
    return buf


def sum_everywhere(team, vector):
    vector = vector + lax.ppermute(vector, "dp", team.swap_core())
    total = vector
    for step in range(1, team.rows):
        total = total + lax.ppermute(vector, "dp", team.turn_rows(step))
    for b in range(team.seq.bit_length() - 1):
        total = total + lax.ppermute(
            total, "seq", [(i, i ^ (1 << b)) for i in range(team.seq)]
        )
    return total


def on_device(
    activations,
    segment_ids,
    norm1_gain,
    w_qkv,
    per_dim_scale,
    w_out,
    norm2_gain,
    w_up,
    b_up,
    w_down,
    b_down,
    cotangent,
):
    seqs, span, width = activations.shape
    rows_here, heads, _, head_size = w_qkv.shape
    length = segment_ids.shape[1]
    team = Team(lax.axis_size("dp"), lax.axis_size("seq"), seqs)
    size = team.size
    row, core, group, side, member = team.here()
    local_heads = heads // size
    wide = local_heads * 3 * head_size
    own = seqs * span

    def spread(array):
        out = []
        for step in range(seqs):
            block = lax.dynamic_index_in_dim(array, (group + step) % seqs, 0, keepdims=False)
            out.append(lax.ppermute(block, axes, team.spread(step)))
        return jnp.concatenate(out, axis=0)

    def unspread(array):
        out = []
        for step in range(seqs):
            got = lax.ppermute(array[step * span : (step + 1) * span], axes, team.back(step))
            out.append((got, (group + step) % seqs))
        return place_in(out, seqs)

    other_ids = lax.ppermute(segment_ids, "dp", team.swap_core())
    x_own = spread(activations)
    w_local = w_qkv.reshape(rows_here, heads * 3 * head_size)
    small = jnp.concatenate([norm1_gain, norm2_gain, b_up, b_down])
    small = jnp.pad(small, (0, wide * 16 - small.shape[0])).reshape(16, wide)

    def columns(first):
        part = lax.dynamic_slice_in_dim(w_local, first * wide, wide, 1)
        return jnp.concatenate([part, small], axis=0)

    mine = columns(member)
    got = lax.ppermute(columns(member + 1 - 2 * core), "dp", team.swap_core())
    both = jnp.stack([jnp.where(core == 0, mine, got), jnp.where(core == 0, got, mine)])
    pieces = [(both, row)]
    for step in range(1, team.rows):
        pieces.append(
            (lax.ppermute(both, "dp", team.turn_rows(step)), (row - step) % team.rows)
        )
    w_parts = place_in(pieces, team.rows).reshape(team.dp, rows_here + 16, wide)
    w_half = w_parts[:, :rows_here].reshape(width, wide)
    small = w_parts[:, rows_here:].reshape(team.dp, -1)[:, : 4 * rows_here]
    small = small.reshape(team.dp, 4, rows_here).transpose(1, 0, 2).reshape(4, width).astype(f32)
    gain_in, gain_mid, bias_up, bias_down = (small[i : i + 1] for i in range(4))
    three = jnp.stack([w_out, w_up, w_down])
    three, _ = lax.optimization_barrier((three, w_parts))
    three = gather_dp(team, three, row, core)
    w_out_all, w_up_all, w_down_all = (three[:, i].reshape(-1, width) for i in range(3))
    x_all = jnp.concatenate(
        [x_own] + [lax.ppermute(x_own, axes, team.rotate(-j)) for j in range(1, size)], axis=0
    )
    cot_in, _ = lax.optimization_barrier((cotangent, x_own))
    cot_own = spread(cot_in.astype(bf16))

    ids = lax.dynamic_index_in_dim(
        jnp.where(side == core, segment_ids, other_ids), group, 0, keepdims=False
    )
    starts = jnp.sum((ids[None, :] < ids[:, None]).astype(jnp.int32), axis=1)
    ends = jnp.sum((ids[None, :] <= ids[:, None]).astype(jnp.int32), axis=1) - 1
    count = length // span
    starts = starts.reshape(count, span)
    ends = ends.reshape(count, span)
    index = jnp.arange(count)
    z_of, u_of = index // size, index % size
    at = ((u_of - member) % size) * seqs + (group - z_of) % seqs
    first = starts[:, 0] // span
    last_start = starts[:, -1]
    open_from = jnp.minimum((last_start + span - 1) // span, index)
    open_to = jnp.sum((last_start[None, :] <= index[:, None] * span).astype(jnp.int32), axis=1)
    open_to = jnp.maximum(open_to, index + 1)
    stop = ends[:, -1] // span + 1
    table = jnp.stack([at, first, open_from, open_to, stop]).astype(jnp.int32)

    factor = scale_base / math.sqrt(head_size) * jax.nn.softplus(per_dim_scale)
    unit = jnp.ones((head_size,), f32)
    factor_row = jnp.tile(jnp.concatenate([factor * log2e, unit, unit]), local_heads)[None, :]

    qkv, normed_in = project_qkv(
        x_all, gain_in, w_half, factor_row, local_heads, head_size, span
    )
    att, lse = attend(table, qkv, starts)

    pieces = [(att[:, :own], member)]
    for j in range(1, size):
        got = lax.ppermute(att[:, j * own : (j + 1) * own], axes, team.rotate(j))
        pieces.append((got, (member - j) % size))
    att_own = place_in(pieces, size).reshape(heads * head_size, own)

    x_float = x_own.astype(f32)
    mid = x_float + lax.dot_general(
        att_own, w_out_all, (((0,), (0,)), ((), ())), preferred_element_type=f32
    )
    rms_mid = lax.rsqrt(jnp.mean(mid * mid, axis=-1, keepdims=True) + epsilon)
    normed_mid = (mid * rms_mid * gain_mid).astype(bf16)
    pre_act = mm(normed_mid, w_up_all) + bias_up
    activated = jax.nn.silu(pre_act).astype(bf16)
    result_own = (mid + mm(activated, w_down_all) + bias_down).astype(bf16)

    grad_bias_down = jnp.sum(cot_own.astype(f32), axis=0)
    tn = (((0,), (0,)), ((), ()))
    grad_act = mm(cot_own, w_down_all, nt)
    sig = jax.nn.sigmoid(pre_act)
    grad_pre = (grad_act * sig * (1.0 + pre_act * (1.0 - sig))).astype(bf16)
    grad_bias_up = jnp.sum(grad_pre.astype(f32), axis=0)
    grad_normed_mid = mm(grad_pre, w_up_all, nt)
    grad_gain_mid = jnp.sum(grad_normed_mid * mid * rms_mid, axis=0)
    scaled_mid = grad_normed_mid * gain_mid
    grad_mid = cot_own.astype(f32) + rms_mid * (
        scaled_mid - mid * rms_mid * rms_mid * jnp.mean(scaled_mid * mid, axis=-1, keepdims=True)
    )
    grad_attn = grad_mid.astype(bf16)
    grad_att = mm(w_out_all, grad_attn, nt).astype(bf16).reshape(size, -1, own)
    pieces = [(lax.dynamic_index_in_dim(grad_att, member, 0, keepdims=False), 0)]
    for j in range(1, size):
        out = lax.dynamic_index_in_dim(grad_att, (member + j) % size, 0, keepdims=False)
        pieces.append((lax.ppermute(out, axes, team.rotate(j)), (-j) % size))
    pieces.sort(key=lambda item: item[1])
    grad_heads = jnp.concatenate([piece for piece, _ in pieces], axis=1)

    grad_down = mm(activated, cot_own, tn)
    grad_up = mm(normed_mid, grad_pre, tn)
    grad_out = mm(att_own, grad_attn)

    chunks = [
        attend_back(c, table, qkv, att, grad_heads, lse, starts, factor[:, None])
        for c in range(local_heads // 2)
    ]
    dots = sum(d for _, d in chunks)
    chunks = [g for g, _ in chunks]
    partial = input_side(chunks, w_half, span)
    grad_normed_in = partial[:own].astype(f32)
    for j in range(1, size):
        grad_normed_in = grad_normed_in + lax.ppermute(
            partial[j * own : (j + 1) * own], axes, team.rotate(j)
        ).astype(f32)
    rms_in = lax.rsqrt(jnp.mean(x_float * x_float, axis=-1, keepdims=True) + epsilon)
    grad_gain_in = jnp.sum(grad_normed_in * x_float * rms_in, axis=0)
    scaled_in = grad_normed_in * gain_in
    input_grad_own = grad_mid + rms_in * (
        scaled_in
        - x_float * rms_in * rms_in * jnp.mean(scaled_in * x_float, axis=-1, keepdims=True)
    )
    input_grad = unspread(input_grad_own.astype(bf16)).astype(f32)
    result = unspread(result_own)

    def shared(parts):
        parts = parts.reshape((team.rows, 2) + parts.shape[1:])
        keep = lax.dynamic_index_in_dim(parts, core, 1, keepdims=False)
        send = lax.dynamic_index_in_dim(parts, 1 - core, 1, keepdims=False)
        got = lax.ppermute(send, "dp", team.swap_core())
        both = (keep.astype(f32) + got.astype(f32)).astype(bf16)
        return over_rows(both)

    def over_rows(both):
        total = lax.dynamic_index_in_dim(both, row, 0, keepdims=False).astype(f32)
        for step in range(1, team.rows):
            out = lax.dynamic_index_in_dim(both, (row + step) % team.rows, 0, keepdims=False)
            total = total + lax.ppermute(out, "dp", team.turn_rows(step)).astype(f32)
        return total.astype(bf16)

    vectors = jnp.stack([grad_gain_mid, grad_bias_up, grad_bias_down]).reshape(3, team.dp, -1)
    vectors = vectors.transpose(1, 0, 2).reshape(team.dp, 1, -1).astype(bf16)
    lines = -(-(3 * rows_here + 1) // (16 * team.seq)) * 16 * team.seq
    vectors = jnp.pad(
        vectors, ((0, 0), (0, lines - 3 * rows_here - 1), (0, width - vectors.shape[2]))
    )
    three = jnp.concatenate(
        [g.astype(bf16).reshape(team.dp, rows_here, width) for g in (grad_out, grad_up, grad_down)]
        + [vectors],
        axis=1,
    )
    three = reduce_places(shared(three), team.seq)
    part_out, part_up, part_down = (
        three[i * rows_here : (i + 1) * rows_here].astype(f32) for i in range(3)
    )
    part_gain_mid, part_bias_up, part_bias_down = (
        three[3 * rows_here, i * rows_here : (i + 1) * rows_here].astype(f32) for i in range(3)
    )
    heads_of = []
    for grads in chunks:
        part = mm(grads, normed_in).astype(bf16)
        part = part.reshape(-1, team.rows, 2, rows_here).transpose(1, 2, 0, 3)
        keep = lax.dynamic_index_in_dim(part, core, 1, keepdims=False)
        send = lax.dynamic_index_in_dim(part, 1 - core, 1, keepdims=False)
        got = lax.ppermute(send, "dp", team.swap_core())
        both = jnp.stack(
            [jnp.where(core == 0, keep, got), jnp.where(core == 0, got, keep)], axis=1
        )
        total = over_rows(both)
        total = place_in([(total, member // 2)], team.half)
        lines = total.size // rows_here
        total = reduce_places(total.reshape(lines, rows_here), team.seq)
        heads_of.append(total.reshape(size, -1, rows_here))
    full = jnp.stack(heads_of, axis=1).reshape(heads, 3, head_size, rows_here)
    vectors = sum_everywhere(team, jnp.concatenate([grad_gain_in, dots[:, 0]]))
    d = lax.axis_index("dp")

    def slice_of(i):
        return lax.dynamic_slice_in_dim(vectors, i * width + d * rows_here, rows_here, 0)

    grad_scale = vectors[width:] / (factor * log2e) * (
        scale_base / math.sqrt(head_size)
    ) * jax.nn.sigmoid(per_dim_scale)
    return (
        result,
        input_grad,
        slice_of(0),
        full.astype(f32).transpose(3, 0, 1, 2),
        grad_scale,
        part_out,
        part_gain_mid,
        part_up,
        part_bias_up,
        part_down,
        part_bias_down,
    )


def solution(mesh):
    in_specs = (
        P("dp", "seq", None),
        P("dp", None),
        P("dp"),
        P("dp", None, None, None),
        P(),
        P("dp", None),
        P("dp"),
        P("dp", None),
        P("dp"),
        P("dp", None),
        P("dp"),
        P("dp", "seq", None),
    )
    out_specs = (
        P("dp", "seq", None),
        P("dp", "seq", None),
        P("dp"),
        P("dp", None, None, None),
        P(),
        P("dp", None),
        P("dp"),
        P("dp", None),
        P("dp"),
        P("dp", None),
        P("dp"),
    )
    return jax.shard_map(
        on_device, mesh=mesh, in_specs=in_specs, out_specs=out_specs, check_vma=False
    )
```

time: 1940 us -> 918 us (0.47)
  waiting for transfers between devices: 858 us -> 306 us
  matrix products: 477 us -> 81.5 us
  Pallas kernels: 0 us -> 177 us
  other arithmetic: 262 us -> 96.4 us
  starting transfers between devices: 28.1 us -> 94.1 us
  local copies, waits for them, and re-layouts: 207 us -> 146 us
  blocking collectives: 42.2 us -> 0 us
  loops' own time: 31.9 us -> 0 us
    all_to_all x4 -> x0, waiting for transfers between devices: 495 us -> none  [the longest x1 180 us: on_device(): lax.all_to_all(shortened(grad_packed.reshape(seqs, length, local_heads *...]
    dot_general x124 -> x13, matrix products: 477 us -> 81.5 us  [the longest x12 75.5 us: mm(): return lax.dot_general(a, b, dims, preferred_element_type=f32)]
    ppermute x0 -> x70, waiting for transfers between devices: none -> 306 us  [the longest x15 126 us: reduce_places(): got = lax.ppermute(buf, 'seq', [(i, i ^ 1 << b) for i in range(places)])]
    pallas_call x0 -> x7, Pallas kernels: none -> 177 us  [the longest x4 79.5 us: attend_back(): pl.pallas_call(functools.partial(attend_back_kernel, count, block, pair),...]
    reduce_scatter x4 -> x0, waiting for transfers between devices: 167 us -> none  [the longest x1 47.1 us: on_device(): lax.psum_scatter(grad_qkv.astype(jnp.bfloat16), 'dp', scatter_dimension=0...]
    convert_element_type x18 -> x28, other arithmetic: 159 us -> 33.5 us  [the longest x15 10.9 us: reduce_places(): buf = (keep.astype(f32) + got.astype(f32)).astype(bf16)]
    psum x1 -> x0, waiting for transfers between devices: 107 us -> none  [on_device(): lax.psum(part_qkv.astype(jnp.bfloat16), 'seq').astype(jnp.float32)]
    ppermute x0 -> x70, starting transfers between devices: none -> 94.1 us  [the longest x8 22.3 us: spread(): out.append(lax.ppermute(block, axes, team.spread(step)))]
  transfers between devices with their start and end apart: 13 -> 70, of which waited for: 10 -> 20; matrix products, arithmetic and copies ran while one was open for 15% -> 24% of each run, Pallas kernels for 0% -> 20%
where the time goes in v1:
time: 918 us; the launch traced here: 903 us
  waiting for transfers between devices  306 us (33%)
  Pallas kernels  177 us (19%)
  local copies, waits for them, and re-layouts  146 us (16%)
  other arithmetic  96.4 us (11%)
  starting transfers between devices  94.1 us (10%)
  matrix products  81.5 us (9%)
    ppermute x15, waiting for transfers between devices, reduce_places(): got = lax.ppermute(buf, 'seq', [(i, i ^ 1 << b) for i in range(places)])  126 us
    pallas_call x4, Pallas kernels, attend_back(): pl.pallas_call(functools.partial(attend_back_kernel, count, block, pair),...  79.5 us
    dot_general x12, matrix products, mm(): return lax.dot_general(a, b, dims, preferred_element_type=f32)  75.5 us
    ppermute x5, waiting for transfers between devices, over_rows(): total = total + lax.ppermute(out, 'dp', team.turn_rows(step)).astype(f32)  64.8 us
    pallas_call x1, Pallas kernels, attend(): pl.pallas_call(functools.partial(attend_kernel, count, block, pair), grid...  61.6 us
    ppermute x1, waiting for transfers between devices, gather_dp(): got = lax.ppermute(shard, 'dp', team.turn_rows(step))  34.4 us
    ppermute x1, waiting for transfers between devices, on_device(): lax.ppermute(both, 'dp', team.turn_rows(step))  32.9 us
    ppermute x8, waiting for transfers between devices, unspread(): lax.ppermute(array[step * span:(step + 1) * span], axes, team.back(step))  32.4 us
  transfers between devices with their start and end apart: 70, of which 20 were waited for; matrix products, arithmetic and copies ran while one was open for 24% of the time, Pallas kernels for 20%

profile of v1, /device:TPU:12, one launch (start us, length us, event | category | flops | bytes accessed | tf_op | source)
XLA Modules:
  0.0 902.6 jit_solution(13749370135202103967)
XLA Ops:
  9.0 3.2 dynamic-slice_bitcast_fusion.14
  14.2 6.5 collective-permute-start
  26.1 3.8 copy.282
  30.4 3.4 pad_maximum_fusion.4
  35.2 4.4 collective-permute-start.2
  39.6 4.1 convert_reduce_fusion
  46.2 4.5 copy.281
  52.8 32.9 %collective-permute-done.7 = bf16[2,336,1920]{2,1,0:T(8,128)(2,1)} collective-permute-done((bf16[2,336,1920]{2,1,0:T(8,128)(2,1)}, bf16[2,336,1920]{2,1,0:T(8,128)(2,1)}, u32[]{:S(2)}, u32[]{:S(2)}) %collective-permute-start.7) | collective-permute-done | bytes 2580512 | tf_op jit(solution)/shard_map/ppermute | solution.py:501
  102.5 3.3 bitcast_dynamic-update-slice_fusion.2
  105.8 34.4 %collective-permute-done.9 = bf16[3,320,1280]{2,1,0:T(8,128)(2,1)} collective-permute-done((bf16[3,320,1280]{2,1,0:T(8,128)(2,1)}, bf16[3,320,1280]{2,1,0:T(8,128)(2,1)}, u32[]{:S(2)}, u32[]{:S(2)}) %collective-permute-start.9) | collective-permute-done | bytes 2457632 | tf_op jit(solution)/shard_map/ppermute | solution.py:96
  140.2 3.4 bitcast_dynamic-update-slice_fusion.1
  144.3 4.5 collective-permute-start.17
  154.2 3.4 constant_dynamic-update-slice_fusion.4.x_ref
  161.2 18.9 %qkv.1 = (bf16[8,3,2048,80]{3,2,1,0:T(8,128)(2,1)}, bf16[2048,1280]{1,0:T(8,128)(2,1)}) custom-call(bf16[2048,1280]{1,0:T(8,128)(2,1)} %constant_dynamic-update-slice_fusion.4.x_ref, f32[1,1280]{1,0:T(1,128)} %slice.108.gain_ref, bf16[1280,1920]{1,0:T(8,128)(2,1)} %bitcast.406, f32[1,1920]{1,0:T(1,128)} %broadcast_in_dim_tile.3.factor_ref), custom_call_target="tpu_custom_call" | custom-call | flops 10066329600 | bytes 31129600 | tf_op jit(solution)/shard_map/qkv/pallas_call | solution.py:118
  180.1 61.6 %attend.1 = (bf16[640,2048]{1,0:T(8,128)(2,1)}, f32[8,1,2048]{2,1,0:T(1,128)}) custom-call(s32[5,8]{1,0:T(8,128)} %stack.89.table, bf16[8,3,2048,80]{3,2,1,0:T(8,128)(2,1)} %get-tuple-element.25.qkv_ref, s32[8,256]{1,0:T(8,128)} %copy-done.24), custom_call_target="tpu_custom_call" | custom-call | flops 5368709120 | bytes 13107200 | tf_op jit(solution)/shard_map/attend/pallas_call | solution.py:229
  244.1 3.1 collective-permute-start.8
  260.9 8.4 select_bitcast_fusion.1
  269.3 8.5 pad_maximum_fusion.1
  277.8 4.9 fusion.70
  282.8 6.0 multiply_reduce_fusion.2
  288.7 3.7 fusion.68
  292.4 7.9 convolution_convert_fusion
  300.3 7.9 fusion.77
  308.2 5.9 multiply_reduce_fusion
  314.0 5.3 convolution_convert_fusion.1
  319.3 3.1 multiply_add_fusion
  322.4 5.0 convolution_convert_fusion.3
  327.5 7.9 convolution_convert_fusion.2
  335.3 8.3 add_convert_fusion
  343.8 3.2 fusion.72
  349.1 6.5 collective-permute-start.11
  358.5 3.8 pad_maximum_fusion
  373.5 32.4 %collective-permute-done.12 = bf16[256,1280]{1,0:T(8,128)(2,1)} collective-permute-done((bf16[256,1280]{1,0:T(8,128)(2,1)}, bf16[256,1280]{1,0:T(8,128)(2,1)}, u32[]{:S(2)}, u32[]{:S(2)}) %collective-permute-start.12) | collective-permute-done | bytes 655392 | tf_op jit(solution)/shard_map/ppermute | solution.py:481
  413.6 19.8 %attend_back.7 = (bf16[480,2048]{1,0:T(8,128)(2,1)}, f32[80,1]{1,0:T(8,128)}) custom-call(s32[5,8]{1,0:T(8,128)} %stack.89.table, bf16[8,3,2048,80]{3,2,1,0:T(8,128)(2,1)} %get-tuple-element.25.qkv_ref, bf16[640,2048]{1,0:T(8,128)(2,1)} %get-tuple-element.26.att_ref, bf16[640,2048]{1,0:T(8,128)(2,1)} %pad_maximum_fusion.3.grad_ref, ...), custom_call_target="tpu_custom_call" | custom-call | flops 3355443200 | bytes 6553600 | tf_op jit(solution)/shard_map/attend_back/pallas_call | solution.py:348
  433.4 19.8 %attend_back.6 = (bf16[480,2048]{1,0:T(8,128)(2,1)}, f32[80,1]{1,0:T(8,128)}) custom-call(s32[5,8]{1,0:T(8,128)} %stack.89.table, bf16[8,3,2048,80]{3,2,1,0:T(8,128)(2,1)} %get-tuple-element.25.qkv_ref, bf16[640,2048]{1,0:T(8,128)(2,1)} %get-tuple-element.26.att_ref, bf16[640,2048]{1,0:T(8,128)(2,1)} %pad_maximum_fusion.3.grad_ref, ...), custom_call_target="tpu_custom_call" | custom-call | flops 3355443200 | bytes 6553600 | tf_op jit(solution)/shard_map/attend_back/pallas_call | solution.py:348
  453.2 19.8 %attend_back.5 = (bf16[480,2048]{1,0:T(8,128)(2,1)}, f32[80,1]{1,0:T(8,128)}) custom-call(s32[5,8]{1,0:T(8,128)} %stack.89.table, bf16[8,3,2048,80]{3,2,1,0:T(8,128)(2,1)} %get-tuple-element.25.qkv_ref, bf16[640,2048]{1,0:T(8,128)(2,1)} %get-tuple-element.26.att_ref, bf16[640,2048]{1,0:T(8,128)(2,1)} %pad_maximum_fusion.3.grad_ref, ...), custom_call_target="tpu_custom_call" | custom-call | flops 3355443200 | bytes 6553600 | tf_op jit(solution)/shard_map/attend_back/pallas_call | solution.py:348
  473.0 20.1 %attend_back.4 = (bf16[480,2048]{1,0:T(8,128)(2,1)}, f32[80,1]{1,0:T(8,128)}) custom-call(s32[5,8]{1,0:T(8,128)} %stack.89.table, bf16[8,3,2048,80]{3,2,1,0:T(8,128)(2,1)} %get-tuple-element.25.qkv_ref, bf16[640,2048]{1,0:T(8,128)(2,1)} %get-tuple-element.26.att_ref, bf16[640,2048]{1,0:T(8,128)(2,1)} %pad_maximum_fusion.3.grad_ref, ...), custom_call_target="tpu_custom_call" | custom-call | flops 3355443200 | bytes 6553600 | tf_op jit(solution)/shard_map/attend_back/pallas_call | solution.py:348
  493.1 5.2 convolution_convert_fusion.4
  499.1 6.1 convolution_convert_fusion.5
  505.3 6.2 convolution_convert_fusion.7
  511.5 16.7 %input_side.1 = bf16[2048,1280]{1,0:T(8,128)(2,1)} custom-call(bf16[480,2048]{1,0:T(8,128)(2,1)} %get-tuple-element.30.refs_0_, bf16[480,2048]{1,0:T(8,128)(2,1)} %get-tuple-element.31.refs_1_, bf16[480,2048]{1,0:T(8,128)(2,1)} %get-tuple-element.32.refs_2_, bf16[480,2048]{1,0:T(8,128)(2,1)} %get-tuple-element.33.refs_3_, bf16[1280,1920]{1,0:T(8,128)(2,1)} %bitcast.407), custom_call_target="tpu_custom_call" | custom-call | flops 10066329600 | bytes 18022400 | tf_op jit(solution)/shard_map/input_side/pallas_call | solution.py:397
  528.2 6.2 convolution_convert_fusion.6
  540.5 3.5 slice.153
  545.7 3.9 collective-permute-start.55
  553.4 11.8 %collective-permute-done.55 = bf16[2,480,320]{1,2,0:T(8,128)(2,1)S(1)} collective-permute-done((bf16[2,480,320]{1,2,0:T(8,128)(2,1)S(1)}, bf16[2,480,320]{1,2,0:T(8,128)(2,1)S(1)}, u32[]{:S(2)}, u32[]{:S(2)}) %collective-permute-start.55) | collective-permute-done | bytes 614432 | tf_op jit(solution)/shard_map/ppermute | solution.py:621
  567.5 11.8 %collective-permute-done.47 = bf16[2,480,320]{1,2,0:T(8,128)(2,1)S(1)} collective-permute-done((bf16[2,480,320]{1,2,0:T(8,128)(2,1)S(1)}, bf16[2,480,320]{1,2,0:T(8,128)(2,1)S(1)}, u32[]{:S(2)}, u32[]{:S(2)}) %collective-permute-start.47) | collective-permute-done | bytes 614432 | tf_op jit(solution)/shard_map/ppermute | solution.py:621
  580.2 13.1 %collective-permute-done.39 = bf16[2,480,320]{1,2,0:T(8,128)(2,1)S(1)} collective-permute-done((bf16[2,480,320]{1,2,0:T(8,128)(2,1)S(1)}, bf16[2,480,320]{1,2,0:T(8,128)(2,1)S(1)}, u32[]{:S(2)}, u32[]{:S(2)}) %collective-permute-start.39) | collective-permute-done | bytes 614432 | tf_op jit(solution)/shard_map/ppermute | solution.py:621
  594.3 12.7 %collective-permute-done.31 = bf16[2,480,320]{1,2,0:T(8,128)(2,1)S(1)} collective-permute-done((bf16[2,480,320]{1,2,0:T(8,128)(2,1)S(1)}, bf16[2,480,320]{1,2,0:T(8,128)(2,1)S(1)}, u32[]{:S(2)}, u32[]{:S(2)}) %collective-permute-start.31) | collective-permute-done | bytes 614432 | tf_op jit(solution)/shard_map/ppermute | solution.py:621
  619.4 4.0 collective-permute-done.32
  628.3 5.3 fusion
  663.2 5.1 collective-permute-start.43
  678.6 15.5 %collective-permute-done.63 = bf16[1024,1280]{1,0:T(8,128)(2,1)S(1)} collective-permute-done((bf16[1024,1280]{1,0:T(8,128)(2,1)}, bf16[1024,1280]{1,0:T(8,128)(2,1)S(1)}, u32[]{:S(2)}, u32[]{:S(2)}) %collective-permute-start.63) | collective-permute-done | bytes 2621472 | tf_op jit(solution)/shard_map/ppermute | solution.py:621
  701.7 3.0 collective-permute-done.61
  705.6 34.2 %collective-permute-done.53 = bf16[480,320]{0,1:T(8,128)(2,1)S(1)} collective-permute-done((bf16[480,320]{0,1:T(8,128)(2,1)S(1)}, bf16[480,320]{0,1:T(8,128)(2,1)S(1)}, u32[]{:S(2)}, u32[]{:S(2)}) %collective-permute-start.53) | collective-permute-done | bytes 307232 | tf_op jit(solution)/shard_map/ppermute | solution.py:428
  741.0 5.8 collective-permute-done.45
  748.1 3.8 fusion.10
  759.3 3.5 select_n.582
  777.0 5.3 fusion.7
  784.2 6.4 collective-permute-done.66
  790.7 3.5 collective-permute-start.67
  799.0 6.2 copy.315
  807.8 3.7 collective-permute-start.23
  815.6 51.5 %collective-permute-done.68 = bf16[256,1280]{1,0:T(8,128)(2,1)S(1)} collective-permute-done((bf16[256,1280]{1,0:T(8,128)(2,1)S(1)}, bf16[256,1280]{1,0:T(8,128)(2,1)S(1)}, u32[]{:S(2)}, u32[]{:S(2)}) %collective-permute-start.68) | collective-permute-done | bytes 655392 | tf_op jit(solution)/shard_map/ppermute | solution.py:428
  870.8 27.9 %collective-permute-done.69 = bf16[512,1280]{1,0:T(8,128)(2,1)S(1)} collective-permute-done((bf16[512,1280]{1,0:T(8,128)(2,1)S(1)}, bf16[512,1280]{1,0:T(8,128)(2,1)S(1)}, u32[]{:S(2)}, u32[]{:S(2)}) %collective-permute-start.69) | collective-permute-done | bytes 1310752 | tf_op jit(solution)/shard_map/ppermute | solution.py:428
  (396 shorter events, 215.1 us)
Async XLA Ops:
  8.4 12.3 %collective-permute-start.6 = (bf16[336,1920]{1,0:T(8,128)(2,1)}, bf16[336,1920]{1,0:T(8,128)(2,1)}, u32[]{:S(2)}, u32[]{:S(2)}) collective-permute-start(bf16[336,1920]{1,0:T(8,128)(2,1)} %copy.278), channel_id=1, source_target_pairs={{0,8},{8,0},{16,24},{24,16},{1,9},{9,1},{17,25},{25,17},{2,10},{10... | collective-permute-start | bytes 3870728 | tf_op jit(solution)/shard_map/ppermute | solution.py:496
  8.4 26.8 %collective-permute-start.4 = (s32[4,2048]{1,0:T(4,128)S(1)}, s32[4,2048]{1,0:T(4,128)S(1)}, u32[]{:S(2)}, u32[]{:S(2)}) collective-permute-start(s32[4,2048]{1,0:T(4,128)S(1)} %copy-done.31), channel_id=1, source_target_pairs={{0,8},{8,0},{16,24},{24,16},{1,9},{9,1},{17,25},{25,17},{2,10},{10... | collective-permute-start | bytes 98312 | tf_op jit(solution)/shard_map/ppermute | solution.py:485
  12.2 80.7 %collective-permute-start.3 = (bf16[256,1280]{1,0:T(8,128)(2,1)}, bf16[256,1280]{1,0:T(8,128)(2,1)}, u32[]{:S(2)}, u32[]{:S(2)}) collective-permute-start(bf16[256,1280]{1,0:T(8,128)(2,1)} %get-tuple-element.85), channel_id=1, source_target_pairs={{0,6},{1,14},{2,0},{3,8},{4,2},{5,10},{6,4},{7,12},{8,7},{9,15},{1... | collective-permute-start | bytes 1966088 | tf_op jit(solution)/shard_map/ppermute | solution.py:475
  12.6 75.7 %collective-permute-start.1 = (bf16[256,1280]{1,0:T(8,128)(2,1)}, bf16[256,1280]{1,0:T(8,128)(2,1)}, u32[]{:S(2)}, u32[]{:S(2)}) collective-permute-start(bf16[256,1280]{1,0:T(8,128)(2,1)} %get-tuple-element.86), channel_id=1, source_target_pairs={{0,2},{1,10},{2,4},{3,12},{4,6},{5,14},{6,0},{7,8},{8,3},{9,11},{1... | collective-permute-start | bytes 1966088 | tf_op jit(solution)/shard_map/ppermute | solution.py:475
  14.2 30.0 %collective-permute-start = (bf16[256,1280]{1,0:T(8,128)(2,1)}, bf16[256,1280]{1,0:T(8,128)(2,1)}, u32[]{:S(2)}, u32[]{:S(2)}) collective-permute-start(bf16[256,1280]{1,0:T(8,128)(2,1)} %get-tuple-element.87), channel_id=1, source_target_pairs={{0,0},{1,8},{2,2},{3,10},{4,4},{5,12},{6,6},{7,14},{8,1},{9,9},{10... | collective-permute-start | bytes 1966088 | tf_op jit(solution)/shard_map/ppermute | solution.py:475
  29.8 55.8 %collective-permute-start.7 = (bf16[2,336,1920]{2,1,0:T(8,128)(2,1)}, bf16[2,336,1920]{2,1,0:T(8,128)(2,1)}, u32[]{:S(2)}, u32[]{:S(2)}) collective-permute-start(bf16[2,336,1920]{2,1,0:T(8,128)(2,1)} %copy.282), channel_id=1, source_target_pairs={{0,16},{8,24},{16,0},{24,8},{1,17},{9,25},{17,1},{25,9},{2,18},{10... | collective-permute-start | bytes 7741448 | tf_op jit(solution)/shard_map/ppermute | solution.py:501
  35.2 55.7 %collective-permute-start.2 = (bf16[256,1280]{1,0:T(8,128)(2,1)S(1)}, bf16[256,1280]{1,0:T(8,128)(2,1)}, u32[]{:S(2)}, u32[]{:S(2)}) collective-permute-start(bf16[256,1280]{1,0:T(8,128)(2,1)S(1)} %copy-done.21), channel_id=1, source_target_pairs={{0,4},{1,12},{2,6},{3,14},{4,0},{5,8},{6,2},{7,10},{8,5},{9,13},{1... | collective-permute-start | bytes 1966088 | tf_op jit(solution)/shard_map/ppermute | solution.py:475
  87.8 52.4 %collective-permute-start.9 = (bf16[3,320,1280]{2,1,0:T(8,128)(2,1)}, bf16[3,320,1280]{2,1,0:T(8,128)(2,1)}, u32[]{:S(2)}, u32[]{:S(2)}) collective-permute-start(bf16[3,320,1280]{2,1,0:T(8,128)(2,1)} %pad_maximum_fusion.4), channel_id=1, source_target_pairs={{0,16},{8,24},{16,0},{24,8},{1,17},{9,25},{17,1},{25,9},{2,18},{10... | collective-permute-start | bytes 7372808 | tf_op jit(solution)/shard_map/ppermute | solution.py:96
  94.9 57.3 %collective-permute-start.5 = (bf16[1024,1280]{1,0:T(8,128)(2,1)S(1)}, bf16[1024,1280]{1,0:T(8,128)(2,1)}, u32[]{:S(2)}, u32[]{:S(2)}) collective-permute-start(bf16[1024,1280]{1,0:T(8,128)(2,1)S(1)} %get-tuple-element.106), channel_id=1, source_target_pairs={{0,8},{1,9},{2,10},{3,11},{4,12},{5,13},{6,14},{7,15},{8,0},{9,1},... | collective-permute-start | bytes 7864328 | tf_op jit(solution)/shard_map/ppermute | solution.py:513
  143.6 117.3 %collective-permute-start.10 = (bf16[2,3,320,1280]{3,2,1,0:T(8,128)(2,1)}, bf16[2,3,320,1280]{3,2,1,0:T(8,128)(2,1)}, u32[]{:S(2)}, u32[]{:S(2)}) collective-permute-start(bf16[2,3,320,1280]{3,2,1,0:T(8,128)(2,1)} %bitcast_dynamic-update-slice_fusion.1), channel_id=1, source_target_pairs={{0,8},{8,0},{16,24},{24,16},{1,9},{9,1},{17,25},{25,17},{2,10},{10... | collective-permute-start | bytes 14745608 | tf_op jit(solution)/shard_map/ppermute | solution.py:99
  144.2 108.2 %collective-permute-start.18 = (bf16[256,1280]{1,0:T(8,128)(2,1)S(1)}, bf16[256,1280]{1,0:T(8,128)(2,1)}, u32[]{:S(2)}, u32[]{:S(2)}) collective-permute-start(bf16[256,1280]{1,0:T(8,128)(2,1)S(1)} %get-tuple-element.77), channel_id=1, source_target_pairs={{0,6},{1,14},{2,0},{3,8},{4,2},{5,10},{6,4},{7,12},{8,7},{9,15},{1... | collective-permute-start | bytes 1966088 | tf_op jit(solution)/shard_map/ppermute | solution.py:475
  144.3 105.9 %collective-permute-start.17 = (bf16[256,1280]{1,0:T(8,128)(2,1)}, bf16[256,1280]{1,0:T(8,128)(2,1)}, u32[]{:S(2)}, u32[]{:S(2)}) collective-permute-start(bf16[256,1280]{1,0:T(8,128)(2,1)} %get-tuple-element.78), channel_id=1, source_target_pairs={{0,4},{1,12},{2,6},{3,14},{4,0},{5,8},{6,2},{7,10},{8,5},{9,13},{1... | collective-permute-start | bytes 1966088 | tf_op jit(solution)/shard_map/ppermute | solution.py:475
  148.7 99.4 %collective-permute-start.16 = (bf16[256,1280]{1,0:T(8,128)(2,1)}, bf16[256,1280]{1,0:T(8,128)(2,1)}, u32[]{:S(2)}, u32[]{:S(2)}) collective-permute-start(bf16[256,1280]{1,0:T(8,128)(2,1)} %get-tuple-element.79), channel_id=1, source_target_pairs={{0,2},{1,10},{2,4},{3,12},{4,6},{5,14},{6,0},{7,8},{8,3},{9,11},{1... | collective-permute-start | bytes 1966088 | tf_op jit(solution)/shard_map/ppermute | solution.py:475
  152.2 92.0 %collective-permute-start.15 = (bf16[256,1280]{1,0:T(8,128)(2,1)}, bf16[256,1280]{1,0:T(8,128)(2,1)S(1)}, u32[]{:S(2)}, u32[]{:S(2)}) collective-permute-start(bf16[256,1280]{1,0:T(8,128)(2,1)} %get-tuple-element.80), channel_id=1, source_target_pairs={{0,0},{1,8},{2,2},{3,10},{4,4},{5,12},{6,6},{7,14},{8,1},{9,9},{10... | collective-permute-start | bytes 1966088 | tf_op jit(solution)/shard_map/ppermute | solution.py:475
  244.1 14.3 %collective-permute-start.8 = (bf16[640,1024]{1,0:T(8,128)(2,1)}, bf16[640,1024]{1,0:T(8,128)(2,1)}, u32[]{:S(2)}, u32[]{:S(2)}) collective-permute-start(bf16[640,1024]{1,0:T(8,128)(2,1)} %slice.111), channel_id=1, source_target_pairs={{0,8},{1,9},{2,10},{3,11},{4,12},{5,13},{6,14},{7,15},{8,0},{9,1},... | collective-permute-start | bytes 3932168 | tf_op jit(solution)/shard_map/ppermute | solution.py:548
  347.0 62.9 %collective-permute-start.14 = (bf16[256,1280]{1,0:T(8,128)(2,1)}, bf16[256,1280]{1,0:T(8,128)(2,1)}, u32[]{:S(2)}, u32[]{:S(2)}) collective-permute-start(bf16[256,1280]{1,0:T(8,128)(2,1)} %get-tuple-element.81), channel_id=1, source_target_pairs={{6,0},{14,1},{0,2},{8,3},{2,4},{10,5},{4,6},{12,7},{7,8},{15,9},{1... | collective-permute-start | bytes 1966088 | tf_op jit(solution)/shard_map/ppermute | solution.py:481
  347.0 60.9 %collective-permute-start.13 = (bf16[256,1280]{1,0:T(8,128)(2,1)}, bf16[256,1280]{1,0:T(8,128)(2,1)}, u32[]{:S(2)}, u32[]{:S(2)}) collective-permute-start(bf16[256,1280]{1,0:T(8,128)(2,1)} %get-tuple-element.82), channel_id=1, source_target_pairs={{4,0},{12,1},{6,2},{14,3},{0,4},{8,5},{2,6},{10,7},{5,8},{13,9},{7... | collective-permute-start | bytes 1966088 | tf_op jit(solution)/shard_map/ppermute | solution.py:481
  349.1 56.8 %collective-permute-start.12 = (bf16[256,1280]{1,0:T(8,128)(2,1)}, bf16[256,1280]{1,0:T(8,128)(2,1)}, u32[]{:S(2)}, u32[]{:S(2)}) collective-permute-start(bf16[256,1280]{1,0:T(8,128)(2,1)} %get-tuple-element.83), channel_id=1, source_target_pairs={{2,0},{10,1},{4,2},{12,3},{6,4},{14,5},{0,6},{8,7},{3,8},{11,9},{5... | collective-permute-start | bytes 1966088 | tf_op jit(solution)/shard_map/ppermute | solution.py:481
  349.1 18.8 %collective-permute-start.11 = (bf16[256,1280]{1,0:T(8,128)(2,1)}, bf16[256,1280]{1,0:T(8,128)(2,1)}, u32[]{:S(2)}, u32[]{:S(2)}) collective-permute-start(bf16[256,1280]{1,0:T(8,128)(2,1)} %get-tuple-element.84), channel_id=1, source_target_pairs={{0,0},{8,1},{2,2},{10,3},{4,4},{12,5},{6,6},{14,7},{1,8},{9,9},{3,... | collective-permute-start | bytes 1966088 | tf_op jit(solution)/shard_map/ppermute | solution.py:481
  357.9 53.9 %collective-permute-start.19 = (bf16[640,1024]{1,0:T(8,128)(2,1)S(1)}, bf16[640,1024]{1,0:T(8,128)(2,1)S(1)}, u32[]{:S(2)}, u32[]{:S(2)}) collective-permute-start(bf16[640,1024]{1,0:T(8,128)(2,1)S(1)} %get-tuple-element.76), channel_id=1, source_target_pairs={{0,8},{1,9},{2,10},{3,11},{4,12},{5,13},{6,14},{7,15},{8,0},{9,1},... | collective-permute-start | bytes 3932168 | tf_op jit(solution)/shard_map/ppermute | solution.py:579
  367.8 260.4 %collective-permute-start.62 = (bf16[2,1024,1280]{2,1,0:T(8,128)(2,1)}, bf16[2,1024,1280]{2,1,0:T(8,128)(2,1)}, u32[]{:S(2)}, u32[]{:S(2)}) collective-permute-start(bf16[2,1024,1280]{2,1,0:T(8,128)(2,1)} %dynamic-slice_bitcast_fusion), channel_id=1, source_target_pairs={{0,8},{8,0},{16,24},{24,16},{1,9},{9,1},{17,25},{25,17},{2,10},{10... | collective-permute-start | bytes 15728648 | tf_op jit(solution)/shard_map/ppermute | solution.py:613
  499.0 45.1 %collective-permute-start.54 = (bf16[2,480,320]{1,2,0:T(8,128)(2,1)S(1)}, bf16[2,480,320]{1,2,0:T(8,128)(2,1)}, u32[]{:S(2)}, u32[]{:S(2)}) collective-permute-start(bf16[2,480,320]{1,2,0:T(8,128)(2,1)S(1)} %dynamic-slice_bitcast_fusion.6), channel_id=1, source_target_pairs={{0,8},{8,0},{16,24},{24,16},{1,9},{9,1},{17,25},{25,17},{2,10},{10... | collective-permute-start | bytes 1843208 | tf_op jit(solution)/shard_map/ppermute | solution.py:648
  536.0 9.7 %collective-permute-start.46 = (bf16[2,480,320]{1,2,0:T(8,128)(2,1)}, bf16[2,480,320]{1,2,0:T(8,128)(2,1)}, u32[]{:S(2)}, u32[]{:S(2)}) collective-permute-start(bf16[2,480,320]{1,2,0:T(8,128)(2,1)} %dynamic-slice_bitcast_fusion.7), channel_id=1, source_target_pairs={{0,8},{8,0},{16,24},{24,16},{1,9},{9,1},{17,25},{25,17},{2,10},{10... | collective-permute-start | bytes 1843208 | tf_op jit(solution)/shard_map/ppermute | solution.py:648
  539.7 11.2 %collective-permute-start.38 = (bf16[2,480,320]{1,2,0:T(8,128)(2,1)S(1)}, bf16[2,480,320]{1,2,0:T(8,128)(2,1)S(1)}, u32[]{:S(2)}, u32[]{:S(2)}) collective-permute-start(bf16[2,480,320]{1,2,0:T(8,128)(2,1)S(1)} %dynamic-slice_bitcast_fusion.8), channel_id=1, source_target_pairs={{0,8},{8,0},{16,24},{24,16},{1,9},{9,1},{17,25},{25,17},{2,10},{10... | collective-permute-start | bytes 1843208 | tf_op jit(solution)/shard_map/ppermute | solution.py:648
  540.2 11.0 %collective-permute-start.30 = (bf16[2,480,320]{1,2,0:T(8,128)(2,1)S(1)}, bf16[2,480,320]{1,2,0:T(8,128)(2,1)S(1)}, u32[]{:S(2)}, u32[]{:S(2)}) collective-permute-start(bf16[2,480,320]{1,2,0:T(8,128)(2,1)S(1)} %dynamic-slice_bitcast_fusion.9), channel_id=1, source_target_pairs={{0,8},{8,0},{16,24},{24,16},{1,9},{9,1},{17,25},{25,17},{2,10},{10... | collective-permute-start | bytes 1843208 | tf_op jit(solution)/shard_map/ppermute | solution.py:648
  544.1 204.0 %collective-permute-start.20 = (bf16[1024,1280]{1,0:T(8,128)(2,1)}, bf16[1024,1280]{1,0:T(8,128)(2,1)}, u32[]{:S(2)}, u32[]{:S(2)}) collective-permute-start(bf16[1024,1280]{1,0:T(8,128)(2,1)} %slice.153), channel_id=1, source_target_pairs={{0,8},{1,9},{2,10},{3,11},{4,12},{5,13},{6,14},{7,15},{8,0},{9,1},... | collective-permute-start | bytes 7864328 | tf_op jit(solution)/shard_map/ppermute | solution.py:596
  545.7 19.5 %collective-permute-start.55 = (bf16[2,480,320]{1,2,0:T(8,128)(2,1)S(1)}, bf16[2,480,320]{1,2,0:T(8,128)(2,1)S(1)}, u32[]{:S(2)}, u32[]{:S(2)}) collective-permute-start(bf16[2,480,320]{1,2,0:T(8,128)(2,1)S(1)} %fusion.22), channel_id=1, source_target_pairs={{0,16},{8,24},{16,0},{24,8},{1,17},{9,25},{17,1},{25,9},{2,18},{10... | collective-permute-start | bytes 1843208 | tf_op jit(solution)/shard_map/ppermute | solution.py:621
  550.9 28.4 %collective-permute-start.47 = (bf16[2,480,320]{1,2,0:T(8,128)(2,1)S(1)}, bf16[2,480,320]{1,2,0:T(8,128)(2,1)S(1)}, u32[]{:S(2)}, u32[]{:S(2)}) collective-permute-start(bf16[2,480,320]{1,2,0:T(8,128)(2,1)S(1)} %fusion.26), channel_id=1, source_target_pairs={{0,16},{8,24},{16,0},{24,8},{1,17},{9,25},{17,1},{25,9},{2,18},{10... | collective-permute-start | bytes 1843208 | tf_op jit(solution)/shard_map/ppermute | solution.py:621
  551.2 42.1 %collective-permute-start.39 = (bf16[2,480,320]{1,2,0:T(8,128)(2,1)S(1)}, bf16[2,480,320]{1,2,0:T(8,128)(2,1)S(1)}, u32[]{:S(2)}, u32[]{:S(2)}) collective-permute-start(bf16[2,480,320]{1,2,0:T(8,128)(2,1)S(1)} %fusion.30), channel_id=1, source_target_pairs={{0,16},{8,24},{16,0},{24,8},{1,17},{9,25},{17,1},{25,9},{2,18},{10... | collective-permute-start | bytes 1843208 | tf_op jit(solution)/shard_map/ppermute | solution.py:621
  565.2 41.7 %collective-permute-start.31 = (bf16[2,480,320]{1,2,0:T(8,128)(2,1)S(1)}, bf16[2,480,320]{1,2,0:T(8,128)(2,1)S(1)}, u32[]{:S(2)}, u32[]{:S(2)}) collective-permute-start(bf16[2,480,320]{1,2,0:T(8,128)(2,1)S(1)} %fusion.34), channel_id=1, source_target_pairs={{0,16},{8,24},{16,0},{24,8},{1,17},{9,25},{17,1},{25,9},{2,18},{10... | collective-permute-start | bytes 1843208 | tf_op jit(solution)/shard_map/ppermute | solution.py:621
  579.3 28.6 %collective-permute-start.56 = (bf16[480,320]{0,1:T(8,128)(2,1)S(1)}, bf16[480,320]{0,1:T(8,128)(2,1)S(1)}, u32[]{:S(2)}, u32[]{:S(2)}) collective-permute-start(bf16[480,320]{0,1:T(8,128)(2,1)S(1)} %dynamic-slice_bitcast_fusion.19), channel_id=1, source_target_pairs={{0,1},{1,0},{2,3},{3,2},{4,5},{5,4},{6,7},{7,6},{8,9},{9,8},{10,11... | collective-permute-start | bytes 921608 | tf_op jit(solution)/shard_map/ppermute | solution.py:424
  593.3 19.0 %collective-permute-start.48 = (bf16[480,320]{0,1:T(8,128)(2,1)}, bf16[480,320]{0,1:T(8,128)(2,1)}, u32[]{:S(2)}, u32[]{:S(2)}) collective-permute-start(bf16[480,320]{0,1:T(8,128)(2,1)} %dynamic-slice_bitcast_fusion.20), channel_id=1, source_target_pairs={{0,1},{1,0},{2,3},{3,2},{4,5},{5,4},{6,7},{7,6},{8,9},{9,8},{10,11... | collective-permute-start | bytes 921608 | tf_op jit(solution)/shard_map/ppermute | solution.py:424
  606.9 10.8 %collective-permute-start.40 = (bf16[480,320]{0,1:T(8,128)(2,1)}, bf16[480,320]{0,1:T(8,128)(2,1)S(1)}, u32[]{:S(2)}, u32[]{:S(2)}) collective-permute-start(bf16[480,320]{0,1:T(8,128)(2,1)} %dynamic-slice_bitcast_fusion.21), channel_id=1, source_target_pairs={{0,1},{1,0},{2,3},{3,2},{4,5},{5,4},{6,7},{7,6},{8,9},{9,8},{10,11... | collective-permute-start | bytes 921608 | tf_op jit(solution)/shard_map/ppermute | solution.py:424
  607.9 15.6 %collective-permute-start.32 = (bf16[480,320]{0,1:T(8,128)(2,1)}, bf16[480,320]{0,1:T(8,128)(2,1)S(1)}, u32[]{:S(2)}, u32[]{:S(2)}) collective-permute-start(bf16[480,320]{0,1:T(8,128)(2,1)} %dynamic-slice_bitcast_fusion.22), channel_id=1, source_target_pairs={{0,1},{1,0},{2,3},{3,2},{4,5},{5,4},{6,7},{7,6},{8,9},{9,8},{10,11... | collective-permute-start | bytes 921608 | tf_op jit(solution)/shard_map/ppermute | solution.py:424
  612.3 12.8 %collective-permute-start.57 = (bf16[240,320]{0,1:T(8,128)(2,1)}, bf16[240,320]{0,1:T(8,128)(2,1)}, u32[]{:S(2)}, u32[]{:S(2)}) collective-permute-start(bf16[240,320]{0,1:T(8,128)(2,1)} %bitcast.376), channel_id=1, source_target_pairs={{0,2},{1,3},{2,0},{3,1},{4,6},{5,7},{6,4},{7,5},{8,10},{9,11},{10,... | collective-permute-start | bytes 460808 | tf_op jit(solution)/shard_map/ppermute | solution.py:424
  617.7 22.1 %collective-permute-start.49 = (bf16[240,320]{0,1:T(8,128)(2,1)}, bf16[240,320]{0,1:T(8,128)(2,1)}, u32[]{:S(2)}, u32[]{:S(2)}) collective-permute-start(bf16[240,320]{0,1:T(8,128)(2,1)} %bitcast.377), channel_id=1, source_target_pairs={{0,2},{1,3},{2,0},{3,1},{4,6},{5,7},{6,4},{7,5},{8,10},{9,11},{10,... | collective-permute-start | bytes 460808 | tf_op jit(solution)/shard_map/ppermute | solution.py:424
  623.5 20.7 %collective-permute-start.41 = (bf16[240,320]{0,1:T(8,128)(2,1)}, bf16[240,320]{0,1:T(8,128)(2,1)}, u32[]{:S(2)}, u32[]{:S(2)}) collective-permute-start(bf16[240,320]{0,1:T(8,128)(2,1)} %bitcast.378), channel_id=1, source_target_pairs={{0,2},{1,3},{2,0},{3,1},{4,6},{5,7},{6,4},{7,5},{8,10},{9,11},{10,... | collective-permute-start | bytes 460808 | tf_op jit(solution)/shard_map/ppermute | solution.py:424
  625.2 26.4 %collective-permute-start.33 = (bf16[240,320]{0,1:T(8,128)(2,1)}, bf16[240,320]{0,1:T(8,128)(2,1)}, u32[]{:S(2)}, u32[]{:S(2)}) collective-permute-start(bf16[240,320]{0,1:T(8,128)(2,1)} %bitcast.379), channel_id=1, source_target_pairs={{0,2},{1,3},{2,0},{3,1},{4,6},{5,7},{6,4},{7,5},{8,10},{9,11},{10,... | collective-permute-start | bytes 460808 | tf_op jit(solution)/shard_map/ppermute | solution.py:424
  636.7 57.4 %collective-permute-start.63 = (bf16[1024,1280]{1,0:T(8,128)(2,1)}, bf16[1024,1280]{1,0:T(8,128)(2,1)S(1)}, u32[]{:S(2)}, u32[]{:S(2)}) collective-permute-start(bf16[1024,1280]{1,0:T(8,128)(2,1)} %dynamic-slice_bitcast_fusion.1), channel_id=1, source_target_pairs={{0,16},{8,24},{16,0},{24,8},{1,17},{9,25},{17,1},{25,9},{2,18},{10... | collective-permute-start | bytes 7864328 | tf_op jit(solution)/shard_map/ppermute | solution.py:621
  639.9 14.7 %collective-permute-start.58 = (bf16[120,320]{0,1:T(8,128)(2,1)}, bf16[120,320]{0,1:T(8,128)(2,1)S(1)}, u32[]{:S(2)}, u32[]{:S(2)}) collective-permute-start(bf16[120,320]{0,1:T(8,128)(2,1)} %bitcast.381), channel_id=1, source_target_pairs={{0,4},{1,5},{2,6},{3,7},{4,0},{5,1},{6,2},{7,3},{8,12},{9,13},{10,... | collective-permute-start | bytes 230408 | tf_op jit(solution)/shard_map/ppermute | solution.py:424
  644.2 13.4 %collective-permute-start.50 = (bf16[120,320]{0,1:T(8,128)(2,1)}, bf16[120,320]{0,1:T(8,128)(2,1)}, u32[]{:S(2)}, u32[]{:S(2)}) collective-permute-start(bf16[120,320]{0,1:T(8,128)(2,1)} %bitcast.382), channel_id=1, source_target_pairs={{0,4},{1,5},{2,6},{3,7},{4,0},{5,1},{6,2},{7,3},{8,12},{9,13},{10,... | collective-permute-start | bytes 230408 | tf_op jit(solution)/shard_map/ppermute | solution.py:424
  654.6 8.6 collective-permute-start.34
  657.6 10.8 %collective-permute-start.59 = (bf16[120,320]{0,1:T(8,128)(2,1)S(1)}, bf16[120,320]{0,1:T(8,128)(2,1)S(1)}, u32[]{:S(2)}, u32[]{:S(2)}) collective-permute-start(bf16[120,320]{0,1:T(8,128)(2,1)S(1)} %fusion.54), channel_id=1, source_target_pairs={{0,4},{1,5},{2,6},{3,7},{4,0},{5,1},{6,2},{7,3},{8,12},{9,13},{10,... | collective-permute-start | bytes 230408 | tf_op jit(solution)/shard_map/ppermute | solution.py:428
  658.6 11.6 %collective-permute-start.51 = (bf16[120,320]{0,1:T(8,128)(2,1)S(1)}, bf16[120,320]{0,1:T(8,128)(2,1)S(1)}, u32[]{:S(2)}, u32[]{:S(2)}) collective-permute-start(bf16[120,320]{0,1:T(8,128)(2,1)S(1)} %fusion.55), channel_id=1, source_target_pairs={{0,4},{1,5},{2,6},{3,7},{4,0},{5,1},{6,2},{7,3},{8,12},{9,13},{10,... | collective-permute-start | bytes 230408 | tf_op jit(solution)/shard_map/ppermute | solution.py:428
  671.7 25.5 %collective-permute-start.52 = (bf16[240,320]{0,1:T(8,128)(2,1)S(1)}, bf16[240,320]{0,1:T(8,128)(2,1)S(1)}, u32[]{:S(2)}, u32[]{:S(2)}) collective-permute-start(bf16[240,320]{0,1:T(8,128)(2,1)S(1)} %maximum_select_fusion.13), channel_id=1, source_target_pairs={{0,2},{1,3},{2,0},{3,1},{4,6},{5,7},{6,4},{7,5},{8,10},{9,11},{10,... | collective-permute-start | bytes 460808 | tf_op jit(solution)/shard_map/ppermute | solution.py:428
  674.6 24.3 %collective-permute-start.44 = (bf16[240,320]{0,1:T(8,128)(2,1)S(1)}, bf16[240,320]{0,1:T(8,128)(2,1)S(1)}, u32[]{:S(2)}, u32[]{:S(2)}) collective-permute-start(bf16[240,320]{0,1:T(8,128)(2,1)S(1)} %maximum_select_fusion.12), channel_id=1, source_target_pairs={{0,2},{1,3},{2,0},{3,1},{4,6},{5,7},{6,4},{7,5},{8,10},{9,11},{10,... | collective-permute-start | bytes 460808 | tf_op jit(solution)/shard_map/ppermute | solution.py:428
  677.4 22.5 %collective-permute-start.36 = (bf16[240,320]{0,1:T(8,128)(2,1)S(1)}, bf16[240,320]{0,1:T(8,128)(2,1)S(1)}, u32[]{:S(2)}, u32[]{:S(2)}) collective-permute-start(bf16[240,320]{0,1:T(8,128)(2,1)S(1)} %maximum_select_fusion.11), channel_id=1, source_target_pairs={{0,2},{1,3},{2,0},{3,1},{4,6},{5,7},{6,4},{7,5},{8,10},{9,11},{10,... | collective-permute-start | bytes 460808 | tf_op jit(solution)/shard_map/ppermute | solution.py:428
  694.1 10.6 %collective-permute-start.61 = (bf16[480,320]{0,1:T(8,128)(2,1)S(1)}, bf16[480,320]{0,1:T(8,128)(2,1)S(1)}, u32[]{:S(2)}, u32[]{:S(2)}) collective-permute-start(bf16[480,320]{0,1:T(8,128)(2,1)S(1)} %maximum_select_fusion.10), channel_id=1, source_target_pairs={{0,1},{1,0},{2,3},{3,2},{4,5},{5,4},{6,7},{7,6},{8,9},{9,8},{10,11... | collective-permute-start | bytes 921608 | tf_op jit(solution)/shard_map/ppermute | solution.py:428
  697.2 54.7 %collective-permute-start.64 = (bf16[512,1280]{1,0:T(8,128)(2,1)S(1)}, bf16[512,1280]{1,0:T(8,128)(2,1)S(1)}, u32[]{:S(2)}, u32[]{:S(2)}) collective-permute-start(bf16[512,1280]{1,0:T(8,128)(2,1)S(1)} %dynamic-slice_bitcast_fusion.2), channel_id=1, source_target_pairs={{0,1},{1,0},{2,3},{3,2},{4,5},{5,4},{6,7},{7,6},{8,9},{9,8},{10,11... | collective-permute-start | bytes 3932168 | tf_op jit(solution)/shard_map/ppermute | solution.py:424
  699.0 40.8 %collective-permute-start.53 = (bf16[480,320]{0,1:T(8,128)(2,1)S(1)}, bf16[480,320]{0,1:T(8,128)(2,1)S(1)}, u32[]{:S(2)}, u32[]{:S(2)}) collective-permute-start(bf16[480,320]{0,1:T(8,128)(2,1)S(1)} %maximum_select_fusion.9), channel_id=1, source_target_pairs={{0,1},{1,0},{2,3},{3,2},{4,5},{5,4},{6,7},{7,6},{8,9},{9,8},{10,11... | collective-permute-start | bytes 921608 | tf_op jit(solution)/shard_map/ppermute | solution.py:428
  699.9 46.9 %collective-permute-start.45 = (bf16[480,320]{0,1:T(8,128)(2,1)S(1)}, bf16[480,320]{0,1:T(8,128)(2,1)S(1)}, u32[]{:S(2)}, u32[]{:S(2)}) collective-permute-start(bf16[480,320]{0,1:T(8,128)(2,1)S(1)} %maximum_select_fusion.8), channel_id=1, source_target_pairs={{0,1},{1,0},{2,3},{3,2},{4,5},{5,4},{6,7},{7,6},{8,9},{9,8},{10,11... | collective-permute-start | bytes 921608 | tf_op jit(solution)/shard_map/ppermute | solution.py:428
  704.7 49.8 %collective-permute-start.37 = (bf16[480,320]{0,1:T(8,128)(2,1)S(1)}, bf16[480,320]{0,1:T(8,128)(2,1)S(1)}, u32[]{:S(2)}, u32[]{:S(2)}) collective-permute-start(bf16[480,320]{0,1:T(8,128)(2,1)S(1)} %maximum_select_fusion.7), channel_id=1, source_target_pairs={{0,1},{1,0},{2,3},{3,2},{4,5},{5,4},{6,7},{7,6},{8,9},{9,8},{10,11... | collective-permute-start | bytes 921608 | tf_op jit(solution)/shard_map/ppermute | solution.py:428
  754.2 21.3 %collective-permute-start.65 = (bf16[256,1280]{1,0:T(8,128)(2,1)}, bf16[256,1280]{1,0:T(8,128)(2,1)}, u32[]{:S(2)}, u32[]{:S(2)}) collective-permute-start(bf16[256,1280]{1,0:T(8,128)(2,1)} %dynamic-slice_bitcast_fusion.5), channel_id=1, source_target_pairs={{0,2},{1,3},{2,0},{3,1},{4,6},{5,7},{6,4},{7,5},{8,10},{9,11},{10,... | collective-permute-start | bytes 1966088 | tf_op jit(solution)/shard_map/ppermute | solution.py:424
  754.5 16.7 %collective-permute-start.25 = (f32[1360]{0:T(1024)S(1)}, f32[1360]{0:T(1024)S(1)}, u32[]{:S(2)}, u32[]{:S(2)}) collective-permute-start(f32[1360]{0:T(1024)S(1)} %pad_maximum_fusion.7), channel_id=1, source_target_pairs={{0,8},{8,0},{16,24},{24,16},{1,9},{9,1},{17,25},{25,17},{2,10},{10... | collective-permute-start | bytes 16328 | tf_op jit(solution)/shard_map/ppermute | solution.py:436
  777.0 13.6 %collective-permute-start.66 = (bf16[128,1280]{1,0:T(8,128)(2,1)S(1)}, bf16[128,1280]{1,0:T(8,128)(2,1)S(1)}, u32[]{:S(2)}, u32[]{:S(2)}) collective-permute-start(bf16[128,1280]{1,0:T(8,128)(2,1)S(1)} %dynamic-slice_bitcast_fusion.18), channel_id=1, source_target_pairs={{0,4},{1,5},{2,6},{3,7},{4,0},{5,1},{6,2},{7,3},{8,12},{9,13},{10,... | collective-permute-start | bytes 983048 | tf_op jit(solution)/shard_map/ppermute | solution.py:424
  782.4 13.5 %collective-permute-start.28 = (f32[1360]{0:T(1024)S(1)}, f32[1360]{0:T(1024)S(1)}, u32[]{:S(2)}, u32[]{:S(2)}) collective-permute-start(f32[1360]{0:T(1024)S(1)} %add.555), channel_id=1, source_target_pairs={{0,2},{1,3},{2,0},{3,1},{4,6},{5,7},{6,4},{7,5},{8,10},{9,11},{10,... | collective-permute-start | bytes 16328 | tf_op jit(solution)/shard_map/ppermute | solution.py:441
  790.7 21.4 %collective-permute-start.67 = (bf16[128,1280]{1,0:T(8,128)(2,1)S(1)}, bf16[128,1280]{1,0:T(8,128)(2,1)S(1)}, u32[]{:S(2)}, u32[]{:S(2)}) collective-permute-start(bf16[128,1280]{1,0:T(8,128)(2,1)S(1)} %fusion.43), channel_id=1, source_target_pairs={{0,4},{1,5},{2,6},{3,7},{4,0},{5,1},{6,2},{7,3},{8,12},{9,13},{10,... | collective-permute-start | bytes 983048 | tf_op jit(solution)/shard_map/ppermute | solution.py:428
  794.4 20.0 %collective-permute-start.21 = (bf16[256,1280]{1,0:T(8,128)(2,1)S(1)}, bf16[256,1280]{1,0:T(8,128)(2,1)}, u32[]{:S(2)}, u32[]{:S(2)}) collective-permute-start(bf16[256,1280]{1,0:T(8,128)(2,1)S(1)} %get-tuple-element.74), channel_id=1, source_target_pairs={{0,0},{8,1},{2,2},{10,3},{4,4},{12,5},{6,6},{14,7},{1,8},{9,9},{3,... | collective-permute-start | bytes 1966088 | tf_op jit(solution)/shard_map/ppermute | solution.py:481
  795.9 15.6 %collective-permute-start.29 = (f32[1360]{0:T(1024)S(1)}, f32[1360]{0:T(1024)S(1)}, u32[]{:S(2)}, u32[]{:S(2)}) collective-permute-start(f32[1360]{0:T(1024)S(1)} %add.556), channel_id=1, source_target_pairs={{0,4},{1,5},{2,6},{3,7},{4,0},{5,1},{6,2},{7,3},{8,12},{9,13},{10,... | collective-permute-start | bytes 16328 | tf_op jit(solution)/shard_map/ppermute | solution.py:441
  805.2 62.7 %collective-permute-start.24 = (bf16[256,1280]{1,0:T(8,128)(2,1)S(1)}, bf16[256,1280]{1,0:T(8,128)(2,1)S(1)}, u32[]{:S(2)}, u32[]{:S(2)}) collective-permute-start(bf16[256,1280]{1,0:T(8,128)(2,1)S(1)} %get-tuple-element.71), channel_id=1, source_target_pairs={{6,0},{14,1},{0,2},{8,3},{2,4},{10,5},{4,6},{12,7},{7,8},{15,9},{1... | collective-permute-start | bytes 1966088 | tf_op jit(solution)/shard_map/ppermute | solution.py:481
  807.8 60.1 %collective-permute-start.23 = (bf16[256,1280]{1,0:T(8,128)(2,1)S(1)}, bf16[256,1280]{1,0:T(8,128)(2,1)S(1)}, u32[]{:S(2)}, u32[]{:S(2)}) collective-permute-start(bf16[256,1280]{1,0:T(8,128)(2,1)S(1)} %get-tuple-element.72), channel_id=1, source_target_pairs={{4,0},{12,1},{6,2},{14,3},{0,4},{8,5},{2,6},{10,7},{5,8},{13,9},{7... | collective-permute-start | bytes 1966088 | tf_op jit(solution)/shard_map/ppermute | solution.py:481
  811.5 56.3 %collective-permute-start.22 = (bf16[256,1280]{1,0:T(8,128)(2,1)S(1)}, bf16[256,1280]{1,0:T(8,128)(2,1)S(1)}, u32[]{:S(2)}, u32[]{:S(2)}) collective-permute-start(bf16[256,1280]{1,0:T(8,128)(2,1)S(1)} %get-tuple-element.73), channel_id=1, source_target_pairs={{2,0},{10,1},{4,2},{12,3},{6,4},{14,5},{0,6},{8,7},{3,8},{11,9},{5... | collective-permute-start | bytes 1966088 | tf_op jit(solution)/shard_map/ppermute | solution.py:481
  812.3 54.9 %collective-permute-start.68 = (bf16[256,1280]{1,0:T(8,128)(2,1)S(1)}, bf16[256,1280]{1,0:T(8,128)(2,1)S(1)}, u32[]{:S(2)}, u32[]{:S(2)}) collective-permute-start(bf16[256,1280]{1,0:T(8,128)(2,1)S(1)} %maximum_select_fusion.6), channel_id=1, source_target_pairs={{0,2},{1,3},{2,0},{3,1},{4,6},{5,7},{6,4},{7,5},{8,10},{9,11},{10,... | collective-permute-start | bytes 1966088 | tf_op jit(solution)/shard_map/ppermute | solution.py:428
  867.7 31.1 %collective-permute-start.69 = (bf16[512,1280]{1,0:T(8,128)(2,1)S(1)}, bf16[512,1280]{1,0:T(8,128)(2,1)S(1)}, u32[]{:S(2)}, u32[]{:S(2)}) collective-permute-start(bf16[512,1280]{1,0:T(8,128)(2,1)S(1)} %maximum_select_fusion.1), channel_id=1, source_target_pairs={{0,1},{1,0},{2,3},{3,2},{4,5},{5,4},{6,7},{7,6},{8,9},{9,8},{10,11... | collective-permute-start | bytes 3932168 | tf_op jit(solution)/shard_map/ppermute | solution.py:428
  (51 other events, 660.6 us)

commit v2 on v1

--- a/solution.py
+++ b/solution.py
@@ -16,6 +16,7 @@
 bf16 = jnp.bfloat16
 f32 = jnp.float32
 axes = ("dp", "seq")
+brief = pl.CostEstimate(flops=1, bytes_accessed=1, transcendentals=0)
 nt = (((1,), (1,)), ((), ()))
 nn = (((1,), (0,)), ((), ()))
 
@@ -78,8 +79,12 @@
     def swap_core(self):
         return [(d, d ^ 1) for d in range(self.dp)]
 
-    def turn_rows(self, step):
-        return [(d, (d + 2 * step) % self.dp) for d in range(self.dp)]
+    def turn_rows(self, step, flip=0):
+        return [(d, ((d + 2 * step) % self.dp) ^ flip) for d in range(self.dp)]
+
+
+def after(value, *first):
+    return lax.optimization_barrier((value, first))[0]
 
 
 def place_in(pieces, count):
@@ -90,56 +95,173 @@
     return out
 
 
-def gather_dp(team, shard, row, core):
-    mine = [(shard, row)]
-    for step in range(1, team.rows):
-        got = lax.ppermute(shard, "dp", team.turn_rows(step))
-        mine.append((got, (row - step) % team.rows))
-    mine = place_in(mine, team.rows)
-    theirs = lax.ppermute(mine, "dp", team.swap_core())
-    first = jnp.where(core == 0, mine, theirs)
-    second = jnp.where(core == 0, theirs, mine)
-    return jnp.stack([first, second], axis=1).reshape((team.dp,) + shard.shape)
-
-
-def qkv_kernel(head_size, x_ref, gain_ref, w_ref, factor_ref, out_ref, normed_ref):
-    x = x_ref[...].astype(f32)
+def join_kernel(count, ends, slots_ref, *refs):
+    outs = refs[count:]
+    for k in range(count):
+        start = 0
+        for out_ref, end in zip(outs, ends):
+            out_ref[slots_ref[k]] = refs[k][start:end, :].astype(out_ref.dtype)
+            start = end
+
+
+def join(pieces, slots, ends=None, dtype=None):
+    count = len(pieces)
+    rows, columns = pieces[0].shape
+    dtype = dtype or pieces[0].dtype
+    ends = ends or (rows,)
+    heights = [b - a for a, b in zip((0,) + tuple(ends[:-1]), ends)]
+    wide = columns
+    if columns % 128 == 0:
+        wide = max(b for b in range(128, min(columns, 640) + 1, 128) if columns % b == 0)
+    outs = pl.pallas_call(
+        functools.partial(join_kernel, count, ends),
+        grid_spec=pltpu.PrefetchScalarGridSpec(
+            num_scalar_prefetch=1,
+            grid=(columns // wide,),
+            in_specs=[pl.BlockSpec((rows, wide), lambda i, s: (0, i)) for _ in pieces],
+            out_specs=[pl.BlockSpec((count, h, wide), lambda i, s: (0, 0, i)) for h in heights],
+        ),
+        out_shape=[jax.ShapeDtypeStruct((count, h, columns), dtype) for h in heights],
+        compiler_params=pltpu.CompilerParams(vmem_limit_bytes=56 << 20),
+        cost_estimate=brief,
+        name="join",
+    )(jnp.stack(slots).astype(jnp.int32), *pieces)
+    return outs if len(ends) > 1 else outs[0]
+
+
+def qkv_kernel(count, blocks, parts, head_size, *refs):
+    x_refs = refs[:count]
+    gain_ref, w_ref, factor_ref, out_ref, normed_ref = refs[count:]
+    i = pl.program_id(0)
+    x = x_refs[0][...]
+    for j in range(1, count):
+        x = jnp.where(i >= j * blocks, x_refs[j][...], x)
+    x = x.astype(f32)
     rms = lax.rsqrt(jnp.mean(x * x, axis=-1, keepdims=True) + epsilon)
     normed = (x * rms * gain_ref[...]).astype(bf16)
-    normed_ref[...] = normed
+    part = x.shape[1] // parts
+    for d in range(parts):
+        normed_ref[d % 2, :, d // 2 * part : (d // 2 + 1) * part] = normed[
+            :, d * part : (d + 1) * part
+        ]
     packed = (mm(normed, w_ref[...]) * factor_ref[...]).astype(bf16)
-    for i in range(packed.shape[1] // head_size):
-        out_ref[i // 3, i % 3] = packed[:, i * head_size : (i + 1) * head_size]
-
-
-def project_qkv(x, gain, w, factor_row, heads, head_size, block):
-    tokens, width = x.shape
+    for h in range(packed.shape[1] // head_size):
+        out_ref[h // 3, h % 3] = packed[:, h * head_size : (h + 1) * head_size]
+
+
+def project_qkv(xs, gain, w, factor_row, heads, head_size, parts, block):
+    own, width = xs[0].shape
+    count, blocks = len(xs), own // block
+    tokens = own * count
     wide = w.shape[1]
+
+    def x_spec(j):
+        return pl.BlockSpec(
+            (block, width), lambda i: (jnp.clip(i - j * blocks, 0, blocks - 1), 0)
+        )
+
     return pl.pallas_call(
-        functools.partial(qkv_kernel, head_size),
+        functools.partial(qkv_kernel, count, blocks, parts, head_size),
         grid=(tokens // block,),
-        in_specs=[
-            pl.BlockSpec((block, width), lambda i: (i, 0)),
+        in_specs=[x_spec(j) for j in range(count)]
+        + [
             pl.BlockSpec((1, width), lambda i: (0, 0)),
             pl.BlockSpec((width, wide), lambda i: (0, 0)),
             pl.BlockSpec((1, wide), lambda i: (0, 0)),
         ],
         out_specs=[
             pl.BlockSpec((heads, 3, block, head_size), lambda i: (0, 0, i, 0)),
-            pl.BlockSpec((block, width), lambda i: (i, 0)),
+            pl.BlockSpec((2, block, width // 2), lambda i: (0, i, 0)),
         ],
         out_shape=[
             jax.ShapeDtypeStruct((heads, 3, tokens, head_size), bf16),
-            jax.ShapeDtypeStruct((tokens, width), bf16),
+            jax.ShapeDtypeStruct((2, tokens, width // 2), bf16),
         ],
         compiler_params=pltpu.CompilerParams(vmem_limit_bytes=56 << 20),
-        cost_estimate=pl.CostEstimate(
-            flops=2 * tokens * width * wide,
-            bytes_accessed=tokens * width * 4 + width * wide * 2 + tokens * wide * 4,
-            transcendentals=0,
+        cost_estimate=brief,
+        name="qkv",
+    )(*xs, gain, w, factor_row)
+
+
+def head_grad_kernel(rows, fold, place_ref, grads_ref, normed_ref, *out_refs):
+    result = mm(grads_ref[...], normed_ref[0]).astype(bf16)
+    part = result.shape[1] // rows
+    lines = result.shape[0] // fold
+    for side in range(2):
+        for row in range(rows):
+
+            @pl.when((pl.program_id(0) == side) & (place_ref[2] == row))
+            def store(side=side, row=row):
+                for step in range(rows):
+                    at = (row + step) % rows * part
+                    for k in range(fold):
+                        out_refs[side * rows + step][:, k * part : (k + 1) * part] = result[
+                            k * lines : (k + 1) * lines, at : at + part
+                        ]
+
+
+def head_grad(grads, normed, rows, row, core):
+    _, tokens, width = normed.shape
+    lines = grads.shape[0]
+    part = width // rows
+    fold = 128 // math.gcd(part, 128)
+    shape = (lines // fold, fold * part)
+    outs = pl.pallas_call(
+        functools.partial(head_grad_kernel, rows, fold),
+        grid_spec=pltpu.PrefetchScalarGridSpec(
+            num_scalar_prefetch=1,
+            grid=(2,),
+            in_specs=[
+                pl.BlockSpec((lines, tokens), lambda i, o: (0, 0)),
+                pl.BlockSpec((1, tokens, width), lambda i, o: (o[i], 0, 0)),
+            ],
+            out_specs=[pl.BlockSpec(shape, lambda i, o: (0, 0)) for _ in range(2 * rows)],
         ),
-        name="qkv",
-    )(x, gain, w, factor_row)
+        out_shape=[jax.ShapeDtypeStruct(shape, bf16) for _ in range(2 * rows)],
+        compiler_params=pltpu.CompilerParams(vmem_limit_bytes=56 << 20),
+        cost_estimate=brief,
+        name="head_grad",
+    )(jnp.stack([1 - core, core, row]).astype(jnp.int32), grads, normed)
+    return outs[:rows], outs[rows:]
+
+
+def unfold_kernel(count, fold, core_ref, *refs):
+    out_ref = refs[count]
+    part = out_ref.shape[1]
+    lines = out_ref.shape[0] // fold
+    for c in range(count):
+
+        @pl.when(pl.program_id(0) % count == c)
+        def store(c=c):
+            for k in range(fold):
+                out_ref[k * lines : (k + 1) * lines, :] = refs[c][
+                    :, k * part : (k + 1) * part
+                ].astype(f32)
+
+
+def unfold(chunks, groups, part, core):
+    count = len(chunks)
+    lines = chunks[0].shape[0] // (2 * groups)
+    wide = chunks[0].shape[1]
+    fold = wide // part
+
+    def source(i, o):
+        g = i // count
+        return (g // 2 * 2 + (g % 2 + o[0]) % 2, 0)
+
+    return pl.pallas_call(
+        functools.partial(unfold_kernel, count, fold),
+        grid_spec=pltpu.PrefetchScalarGridSpec(
+            num_scalar_prefetch=1,
+            grid=(2 * groups * count,),
+            in_specs=[pl.BlockSpec((lines, wide), source) for _ in chunks],
+            out_specs=pl.BlockSpec((lines * fold, part), lambda i, o: (i, 0)),
+        ),
+        out_shape=jax.ShapeDtypeStruct((2 * groups * count * lines * fold, part), f32),
+        compiler_params=pltpu.CompilerParams(vmem_limit_bytes=56 << 20),
+        cost_estimate=brief,
+        name="unfold",
+    )(core.reshape(1).astype(jnp.int32), *chunks)
 
 
 def eye_rows(rows, columns):
@@ -183,19 +305,24 @@
             if masked:
                 keys_here = key_index + j * block
                 seen = (keys_here >= starts) & (keys_here <= places)
+            scores = [
+                mm(qkv_ref[h, 1, pl.ds(key_at, block), :], queries[h], nt) for h in range(pair)
+            ]
+            if masked:
+                scores = [jnp.where(seen, s, masked_value) for s in scores]
+            values = [vt_ref[h, :, pl.ds(key_at, block)] for h in range(pair)]
+            if not raised:
+                probs = [jnp.exp2(s).astype(bf16) for s in scores]
+                sums = [mm(values[h], probs[h]) for h in range(pair)]
+                for h in range(pair):
+                    acc_ref[h] += sums[h]
+                return ()
             out = []
             for h in range(pair):
-                s = mm(qkv_ref[h, 1, pl.ds(key_at, block), :], queries[h], nt)
-                if masked:
-                    s = jnp.where(seen, s, masked_value)
-                values = vt_ref[h, :, pl.ds(key_at, block)]
-                if raised:
-                    peak = jnp.maximum(peaks[h], jnp.max(s, axis=0, keepdims=True))
-                    p = jnp.exp2(s - peak).astype(bf16)
-                    acc_ref[h] = acc_ref[h] * jnp.exp2(peaks[h] - peak) + mm(values, p)
-                    out.append(peak)
-                else:
-                    acc_ref[h] += mm(values, jnp.exp2(s).astype(bf16))
+                peak = jnp.maximum(peaks[h], jnp.max(scores[h], axis=0, keepdims=True))
+                p = jnp.exp2(scores[h] - peak).astype(bf16)
+                acc_ref[h] = acc_ref[h] * jnp.exp2(peaks[h] - peak) + mm(values[h], p)
+                out.append(peak)
             return tuple(out)
 
         peaks = ()
@@ -222,8 +349,9 @@
         lax.fori_loop(0, count, functools.partial(query_block, True), 0)
 
 
-def attend(table, qkv, starts, pair=2):
+def attend(table, qkv, starts):
     heads, _, length, size = qkv.shape
+    pair = math.gcd(heads, 8)
     count, block = starts.shape
     rows = (size // 16 + 1) * 16
     return pl.pallas_call(
@@ -249,11 +377,7 @@
             jax.ShapeDtypeStruct((heads, 1, length), f32),
         ],
         compiler_params=pltpu.CompilerParams(vmem_limit_bytes=56 << 20),
-        cost_estimate=pl.CostEstimate(
-            flops=heads * length * length * size * 2,
-            bytes_accessed=heads * length * size * 10,
-            transcendentals=heads * length * length // 4,
-        ),
+        cost_estimate=brief,
         name="attend",
     )(table, qkv, starts)
 
@@ -305,17 +429,24 @@
                 seen = (keys_here >= start_ref[pl.ds(i, 1), :]) & (
                     keys_here <= lane_index + i * block
                 )
-            for h in range(pair):
-                grads = grad_ref[h * size : (h + 1) * size, pl.ds(at, block)]
-                s = mm(qkv_ref[h, 1, pl.ds(key_at, block), :], qt_ref[h, :, pl.ds(at, block)])
-                p = jnp.exp2(s - lse_ref[h, :, pl.ds(at, block)])
-                if masked:
-                    p = jnp.where(seen, p, 0.0)
-                dp = mm(qkv_ref[h, 2, pl.ds(key_at, block), :], grads)
-                ds = (p * (dp - delta_ref[h, :, pl.ds(at, block)])).astype(bf16)
-                dv_ref[h] += mm(grads, p.astype(bf16), nt)
-                dk_ref[h] += mm(qt_ref[h, :, pl.ds(at, block)], ds, nt)
-                dq_ref[h, :, pl.ds(at, block)] += mm(kt_ref[h, :, pl.ds(key_at, block)], ds)
+            both = range(pair)
+            grads = [grad_ref[h * size : (h + 1) * size, pl.ds(at, block)] for h in both]
+            queries = [qt_ref[h, :, pl.ds(at, block)] for h in both]
+            s = [mm(qkv_ref[h, 1, pl.ds(key_at, block), :], queries[h]) for h in both]
+            dp = [mm(qkv_ref[h, 2, pl.ds(key_at, block), :], grads[h]) for h in both]
+            p = [jnp.exp2(s[h] - lse_ref[h, :, pl.ds(at, block)]) for h in both]
+            if masked:
+                p = [jnp.where(seen, x, 0.0) for x in p]
+            ds = [
+                (p[h] * (dp[h] - delta_ref[h, :, pl.ds(at, block)])).astype(bf16) for h in both
+            ]
+            dv = [mm(grads[h], p[h].astype(bf16), nt) for h in both]
+            dk = [mm(queries[h], ds[h], nt) for h in both]
+            dq = [mm(kt_ref[h, :, pl.ds(key_at, block)], ds[h]) for h in both]
+            for h in both:
+                dv_ref[h] += dv[h]
+                dk_ref[h] += dk[h]
+                dq_ref[h, :, pl.ds(at, block)] += dq[h]
             return inner
 
         step(True, j, 0)
@@ -342,7 +473,7 @@
         out_ref[base : base + size, :] = (rounded * factor_ref[...]).astype(bf16)
 
 
-def attend_back(chunk, table, qkv, att, grad, lse, starts, factor, pair=2):
+def attend_back(chunk, pair, table, qkv, att, grad, lse, starts, factor):
     heads, _, length, size = qkv.shape
     count, block = starts.shape
     return pl.pallas_call(
@@ -376,11 +507,7 @@
             jax.ShapeDtypeStruct((size, 1), f32),
         ],
         compiler_params=pltpu.CompilerParams(vmem_limit_bytes=56 << 20),
-        cost_estimate=pl.CostEstimate(
-            flops=pair * length * length * size * 5,
-            bytes_accessed=pair * length * size * 20,
-            transcendentals=pair * length * length // 4,
-        ),
+        cost_estimate=brief,
         name="attend_back",
     )(table, qkv, att, grad, lse, starts, factor)
 
@@ -391,45 +518,50 @@
     out_ref[...] = mm(grads.T, w_ref[...], nt).astype(bf16)
 
 
-def input_side(grads, w, block):
+def input_side(grads, w, block, first, blocks):
     width, wide = w.shape
-    rows, tokens = grads[0].shape
+    rows = grads[0].shape[0]
+    tokens = blocks * block
     return pl.pallas_call(
         functools.partial(input_side_kernel, len(grads)),
-        grid=(tokens // block,),
-        in_specs=[pl.BlockSpec((rows, block), lambda i: (0, i)) for _ in grads]
+        grid=(blocks,),
+        in_specs=[pl.BlockSpec((rows, block), lambda i: (0, i + first)) for _ in grads]
         + [pl.BlockSpec((width, wide), lambda i: (0, 0))],
         out_specs=pl.BlockSpec((block, width), lambda i: (i, 0)),
         out_shape=jax.ShapeDtypeStruct((tokens, width), bf16),
         compiler_params=pltpu.CompilerParams(vmem_limit_bytes=56 << 20),
-        cost_estimate=pl.CostEstimate(
-            flops=2 * tokens * width * wide,
-            bytes_accessed=tokens * width * 2 + width * wide * 2 + tokens * wide * 2,
-            transcendentals=0,
-        ),
+        cost_estimate=brief,
         name="input_side",
     )(*grads, w)
 
 
 def reduce_places(buf, places):
     place = lax.axis_index("seq")
-    rows = buf.shape[0]
+    lines, wide = buf.shape
     bits = places.bit_length() - 1
-    assert places == 1 << bits and rows % places == 0
+    assert places == 1 << bits and lines % places == 0
     for b in range(bits):
         bit = (place >> b) & 1
-        halves = buf.reshape((2, -1) + buf.shape[1:])
+        halves = buf.reshape(2, -1, wide)
         keep = lax.dynamic_index_in_dim(halves, bit, 0, keepdims=False)
         send = lax.dynamic_index_in_dim(halves, 1 - bit, 0, keepdims=False)
+        yield send
         got = lax.ppermute(send, "seq", [(i, i ^ (1 << b)) for i in range(places)])
         buf = (keep.astype(f32) + got.astype(f32)).astype(bf16)
     for b in reversed(range(bits)):
         bit = (place >> b) & 1
+        yield buf
         got = lax.ppermute(buf, "seq", [(i, i ^ (1 << b)) for i in range(places)])
         buf = jnp.where(
             bit == 0, jnp.concatenate([buf, got], axis=0), jnp.concatenate([got, buf], axis=0)
         )
-    return buf
+    yield buf
+
+
+def last(steps):
+    for value in steps:
+        pass
+    return value
 
 
 def sum_everywhere(team, vector):
@@ -473,17 +605,22 @@
         for step in range(seqs):
             block = lax.dynamic_index_in_dim(array, (group + step) % seqs, 0, keepdims=False)
             out.append(lax.ppermute(block, axes, team.spread(step)))
-        return jnp.concatenate(out, axis=0)
+        return join(out, [jnp.int32(k) for k in range(seqs)]).reshape(own, width)
 
     def unspread(array):
-        out = []
-        for step in range(seqs):
-            got = lax.ppermute(array[step * span : (step + 1) * span], axes, team.back(step))
-            out.append((got, (group + step) % seqs))
-        return place_in(out, seqs)
-
-    other_ids = lax.ppermute(segment_ids, "dp", team.swap_core())
-    x_own = spread(activations)
+        return [
+            lax.ppermute(array[step * span : (step + 1) * span], axes, team.back(step))
+            for step in range(seqs)
+        ]
+
+    def unspread_done(pieces, dtype):
+        return join(pieces, [(group + step) % seqs for step in range(seqs)], dtype=dtype)
+
+    def shard_of(step, flip):
+        return (row - step) % team.rows * 2 + (core ^ flip)
+
+    shifts = [(step, flip) for step in range(team.rows) for flip in range(2)]
+
     w_local = w_qkv.reshape(rows_here, heads * 3 * head_size)
     small = jnp.concatenate([norm1_gain, norm2_gain, b_up, b_down])
     small = jnp.pad(small, (0, wide * 16 - small.shape[0])).reshape(16, wide)
@@ -492,28 +629,28 @@
         part = lax.dynamic_slice_in_dim(w_local, first * wide, wide, 1)
         return jnp.concatenate([part, small], axis=0)
 
-    mine = columns(member)
-    got = lax.ppermute(columns(member + 1 - 2 * core), "dp", team.swap_core())
-    both = jnp.stack([jnp.where(core == 0, mine, got), jnp.where(core == 0, got, mine)])
-    pieces = [(both, row)]
-    for step in range(1, team.rows):
-        pieces.append(
-            (lax.ppermute(both, "dp", team.turn_rows(step)), (row - step) % team.rows)
-        )
-    w_parts = place_in(pieces, team.rows).reshape(team.dp, rows_here + 16, wide)
-    w_half = w_parts[:, :rows_here].reshape(width, wide)
-    small = w_parts[:, rows_here:].reshape(team.dp, -1)[:, : 4 * rows_here]
+    parts = [columns(member), columns(member + 1 - 2 * core)]
+    far = [
+        lax.ppermute(parts[flip], "dp", team.turn_rows(step, flip)) for step, flip in shifts[2:]
+    ]
+    near = lax.ppermute(parts[1], "dp", team.swap_core())
+    x_own = spread(after(activations, *parts))
+    other_ids = lax.ppermute(segment_ids, "dp", team.swap_core())
+    w_half, small = join(
+        [parts[0], near] + far,
+        [shard_of(*s) for s in shifts],
+        ends=(rows_here, rows_here + 16),
+    )
+    w_half = w_half.reshape(width, wide)
+    small = small.reshape(team.dp, -1)[:, : 4 * rows_here]
     small = small.reshape(team.dp, 4, rows_here).transpose(1, 0, 2).reshape(4, width).astype(f32)
     gain_in, gain_mid, bias_up, bias_down = (small[i : i + 1] for i in range(4))
-    three = jnp.stack([w_out, w_up, w_down])
-    three, _ = lax.optimization_barrier((three, w_parts))
-    three = gather_dp(team, three, row, core)
-    w_out_all, w_up_all, w_down_all = (three[:, i].reshape(-1, width) for i in range(3))
-    x_all = jnp.concatenate(
-        [x_own] + [lax.ppermute(x_own, axes, team.rotate(-j)) for j in range(1, size)], axis=0
-    )
-    cot_in, _ = lax.optimization_barrier((cotangent, x_own))
-    cot_own = spread(cot_in.astype(bf16))
+    xs = [x_own] + [lax.ppermute(x_own, axes, team.rotate(-j)) for j in range(1, size)]
+    three = after(jnp.concatenate([w_out, w_up, w_down]), *far)
+    three = [three] + [
+        lax.ppermute(three, "dp", team.turn_rows(step)) for step in range(1, team.rows)
+    ]
+    cot_own = spread(after(cotangent, x_own).astype(bf16))
 
     ids = lax.dynamic_index_in_dim(
         jnp.where(side == core, segment_ids, other_ids), group, 0, keepdims=False
@@ -539,15 +676,27 @@
     factor_row = jnp.tile(jnp.concatenate([factor * log2e, unit, unit]), local_heads)[None, :]
 
     qkv, normed_in = project_qkv(
-        x_all, gain_in, w_half, factor_row, local_heads, head_size, span
+        xs, gain_in, w_half, factor_row, local_heads, head_size, team.dp, span
     )
     att, lse = attend(table, qkv, starts)
+    three = after(three, att)
+    swapped = [lax.ppermute(piece, "dp", team.swap_core()) for piece in three]
+    w_out_all, w_up_all, w_down_all = (
+        w.reshape(-1, width)
+        for w in join(
+            three + swapped,
+            [shard_of(step, 0) for step in range(team.rows)]
+            + [shard_of(step, 1) for step in range(team.rows)],
+            ends=(rows_here, 2 * rows_here, 3 * rows_here),
+        )
+    )
 
     pieces = [(att[:, :own], member)]
     for j in range(1, size):
         got = lax.ppermute(att[:, j * own : (j + 1) * own], axes, team.rotate(j))
         pieces.append((got, (member - j) % size))
-    att_own = place_in(pieces, size).reshape(heads * head_size, own)
+    att_own = join([p for p, _ in pieces], [s for _, s in pieces])
+    att_own = att_own.reshape(heads * head_size, own)
 
     x_float = x_own.astype(f32)
     mid = x_float + lax.dot_general(
@@ -558,6 +707,8 @@
     pre_act = mm(normed_mid, w_up_all) + bias_up
     activated = jax.nn.silu(pre_act).astype(bf16)
     result_own = (mid + mm(activated, w_down_all) + bias_down).astype(bf16)
+    result = unspread(result_own)
+    cot_own = after(cot_own, result_own)
 
     grad_bias_down = jnp.sum(cot_own.astype(f32), axis=0)
     tn = (((0,), (0,)), ((), ()))
@@ -580,22 +731,81 @@
     pieces.sort(key=lambda item: item[1])
     grad_heads = jnp.concatenate([piece for piece, _ in pieces], axis=1)
 
-    grad_down = mm(activated, cot_own, tn)
-    grad_up = mm(normed_mid, grad_pre, tn)
-    grad_out = mm(att_own, grad_attn)
-
-    chunks = [
-        attend_back(c, table, qkv, att, grad_heads, lse, starts, factor[:, None])
-        for c in range(local_heads // 2)
+    def by_core(grad):
+        parts = grad.astype(bf16).reshape(team.rows, 2, rows_here, width)
+        keep = lax.dynamic_index_in_dim(parts, core, 1, keepdims=False)
+        send = lax.dynamic_index_in_dim(parts, 1 - core, 1, keepdims=False)
+        return keep, lax.ppermute(send, "dp", team.swap_core())
+
+    three = [
+        by_core(grad)
+        for grad in (mm(activated, cot_own, tn), mm(normed_mid, grad_pre, tn), mm(att_own, grad_attn))
     ]
-    dots = sum(d for _, d in chunks)
-    chunks = [g for g, _ in chunks]
-    partial = input_side(chunks, w_half, span)
-    grad_normed_in = partial[:own].astype(f32)
-    for j in range(1, size):
-        grad_normed_in = grad_normed_in + lax.ppermute(
-            partial[j * own : (j + 1) * own], axes, team.rotate(j)
-        ).astype(f32)
+
+    def both_cores(step):
+        at = (row + step) % team.rows
+        return jnp.concatenate(
+            [
+                lax.dynamic_index_in_dim(keep, at, 0, keepdims=False).astype(f32)
+                + lax.dynamic_index_in_dim(got, at, 0, keepdims=False).astype(f32)
+                for keep, got in three
+            ]
+        ).astype(bf16)
+
+    three_rows = [both_cores(step) for step in range(team.rows)]
+    three_far = [
+        lax.ppermute(three_rows[step], "dp", team.turn_rows(step)) for step in range(1, team.rows)
+    ]
+
+    def add(first, *more):
+        total = first.astype(f32)
+        for piece in more:
+            total = total + piece.astype(f32)
+        return total.astype(bf16)
+
+    pair = math.gcd(local_heads, 4)
+    grad_in = after(grad_heads, *three_rows)
+    chunks, dots, heads_of = [], 0.0, []
+    steps = None
+    for c in range(local_heads // pair):
+        grads, dot = attend_back(
+            c, pair, table, qkv, att, grad_in, lse, starts, factor[:, None]
+        )
+        chunks.append(grads)
+        dots = dots + dot
+        if c == 0:
+            result = after(result, grads)
+            grads = after(grads, *result)
+        else:
+            if steps is None:
+                three_far = after(three_far, grads)
+                steps = reduce_places(add(three_rows[0], *three_far), team.seq)
+            grads = after(grads, next(steps))
+        send, keep = head_grad(grads, normed_in, team.rows, row, core)
+        near = [lax.ppermute(piece, "dp", team.swap_core()) for piece in send]
+        far = [
+            [
+                lax.ppermute(source, "dp", team.turn_rows(step))
+                for source in (keep[step], near[step])
+            ]
+            for step in range(1, team.rows)
+        ]
+        heads_of.append((keep[0], near[0], far))
+        grad_in = after(grad_in, *send, *keep)
+    steps = steps or reduce_places(add(three_rows[0], *three_far), team.seq)
+    blocks = own // span
+    chunks = after(chunks, *send, *keep)
+    partial = [
+        input_side(chunks, w_half, span, j * blocks, blocks) for j in range(1, size)
+    ]
+    chunks = after(chunks, *partial)
+    grad_normed_in = sum(
+        [
+            lax.ppermute(p, axes, team.rotate(j + 1)).astype(f32)
+            for j, p in enumerate(partial)
+        ],
+        input_side(chunks, w_half, span, 0, blocks).astype(f32),
+    )
     rms_in = lax.rsqrt(jnp.mean(x_float * x_float, axis=-1, keepdims=True) + epsilon)
     grad_gain_in = jnp.sum(grad_normed_in * x_float * rms_in, axis=0)
     scaled_in = grad_normed_in * gain_in
@@ -603,79 +813,45 @@
         scaled_in
         - x_float * rms_in * rms_in * jnp.mean(scaled_in * x_float, axis=-1, keepdims=True)
     )
-    input_grad = unspread(input_grad_own.astype(bf16)).astype(f32)
-    result = unspread(result_own)
-
-    def shared(parts):
-        parts = parts.reshape((team.rows, 2) + parts.shape[1:])
-        keep = lax.dynamic_index_in_dim(parts, core, 1, keepdims=False)
-        send = lax.dynamic_index_in_dim(parts, 1 - core, 1, keepdims=False)
-        got = lax.ppermute(send, "dp", team.swap_core())
-        both = (keep.astype(f32) + got.astype(f32)).astype(bf16)
-        return over_rows(both)
-
-    def over_rows(both):
-        total = lax.dynamic_index_in_dim(both, row, 0, keepdims=False).astype(f32)
-        for step in range(1, team.rows):
-            out = lax.dynamic_index_in_dim(both, (row + step) % team.rows, 0, keepdims=False)
-            total = total + lax.ppermute(out, "dp", team.turn_rows(step)).astype(f32)
-        return total.astype(bf16)
-
-    vectors = jnp.stack([grad_gain_mid, grad_bias_up, grad_bias_down]).reshape(3, team.dp, -1)
-    vectors = vectors.transpose(1, 0, 2).reshape(team.dp, 1, -1).astype(bf16)
-    lines = -(-(3 * rows_here + 1) // (16 * team.seq)) * 16 * team.seq
-    vectors = jnp.pad(
-        vectors, ((0, 0), (0, lines - 3 * rows_here - 1), (0, width - vectors.shape[2]))
-    )
-    three = jnp.concatenate(
-        [g.astype(bf16).reshape(team.dp, rows_here, width) for g in (grad_out, grad_up, grad_down)]
-        + [vectors],
-        axis=1,
-    )
-    three = reduce_places(shared(three), team.seq)
+    input_grad = unspread_done(unspread(input_grad_own.astype(bf16)), f32)
+    result = unspread_done(result, bf16)
+
+    three = last(steps).astype(f32)
     part_out, part_up, part_down = (
-        three[i * rows_here : (i + 1) * rows_here].astype(f32) for i in range(3)
-    )
-    part_gain_mid, part_bias_up, part_bias_down = (
-        three[3 * rows_here, i * rows_here : (i + 1) * rows_here].astype(f32) for i in range(3)
-    )
-    heads_of = []
-    for grads in chunks:
-        part = mm(grads, normed_in).astype(bf16)
-        part = part.reshape(-1, team.rows, 2, rows_here).transpose(1, 2, 0, 3)
-        keep = lax.dynamic_index_in_dim(part, core, 1, keepdims=False)
-        send = lax.dynamic_index_in_dim(part, 1 - core, 1, keepdims=False)
-        got = lax.ppermute(send, "dp", team.swap_core())
-        both = jnp.stack(
-            [jnp.where(core == 0, keep, got), jnp.where(core == 0, got, keep)], axis=1
+        three[i * rows_here : (i + 1) * rows_here] for i in (2, 1, 0)
+    )
+    full = []
+    for mine, theirs, far in heads_of:
+        total = jnp.concatenate(
+            [add(mine, *[f[0] for f in far]), add(theirs, *[f[1] for f in far])]
         )
-        total = over_rows(both)
-        total = place_in([(total, member // 2)], team.half)
-        lines = total.size // rows_here
-        total = reduce_places(total.reshape(lines, rows_here), team.seq)
-        heads_of.append(total.reshape(size, -1, rows_here))
-    full = jnp.stack(heads_of, axis=1).reshape(heads, 3, head_size, rows_here)
-    vectors = sum_everywhere(team, jnp.concatenate([grad_gain_in, dots[:, 0]]))
+        total = place_in([(total, member // 2)], team.half) if team.half > 1 else total
+        full.append(last(reduce_places(total.reshape(-1, total.shape[-1]), team.seq)))
+    full = unfold(full, team.half, rows_here, core).reshape(heads, 3, head_size, rows_here)
+    vectors = sum_everywhere(
+        team,
+        jnp.concatenate([grad_gain_in, grad_gain_mid, grad_bias_up, grad_bias_down, dots[:, 0]]),
+    )
     d = lax.axis_index("dp")
 
     def slice_of(i):
         return lax.dynamic_slice_in_dim(vectors, i * width + d * rows_here, rows_here, 0)
 
-    grad_scale = vectors[width:] / (factor * log2e) * (
+    grad_scale = vectors[4 * width :] / (factor * log2e) * (
         scale_base / math.sqrt(head_size)
     ) * jax.nn.sigmoid(per_dim_scale)
     return (
         result,
         input_grad,
         slice_of(0),
-        full.astype(f32).transpose(3, 0, 1, 2),
+        full.transpose(3, 0, 1, 2),
         grad_scale,
         part_out,
-        part_gain_mid,
+        slice_of(1),
         part_up,
-        part_bias_up,
+        slice_of(2),
         part_down,
-        part_bias_down,
+        slice_of(3),
     )
 
 

time: 918 us -> 689 us (0.75)
  local copies, waits for them, and re-layouts: 146 us -> 45.7 us
  waiting for transfers between devices: 306 us -> 251 us
  other arithmetic: 96.4 us -> 57.1 us
  matrix products: 81.5 us -> 59.2 us
    ppermute x15 -> x19, waiting for transfers between devices: 132 us -> 34.7 us  [the longest x4 28 us: on_device(): lax.ppermute(source, 'dp', team.turn_rows(step))]
    ppermute x15 -> x9, waiting for transfers between devices: 126 us -> 30.5 us  [reduce_places(): got = lax.ppermute(buf, 'seq', [(i, i ^ 1 << b) for i in range(places)])]
    ppermute x8, waiting for transfers between devices: 0.02 us -> 88.5 us  [spread(): out.append(lax.ppermute(block, axes, team.spread(step)))]
    pallas_call x2 -> x13, Pallas kernels: 35.6 us -> 102 us  [the longest x7 33.1 us: join(): pl.pallas_call(functools.partial(join_kernel, count, ends), grid_spec=plt...]
    pallas_call x1, Pallas kernels: 61.6 us -> 23.6 us  [attend(): pl.pallas_call(functools.partial(attend_kernel, count, block, pair), grid...]
    pallas_call x4 -> x2, Pallas kernels: 79.5 us -> 45.2 us  [attend_back(): pl.pallas_call(functools.partial(attend_back_kernel, count, block, pair),...]
    dot_general x12 -> x8, matrix products: 75.5 us -> 52.9 us  [mm(): return lax.dot_general(a, b, dims, preferred_element_type=f32)]
    ppermute x15 -> x9, waiting for transfers between devices: 13.1 us -> 35.3 us  [reduce_places(): got = lax.ppermute(send, 'seq', [(i, i ^ 1 << b) for i in range(places)])]
  transfers between devices with their start and end apart: 70 -> 62, of which waited for: 20 -> 26; matrix products, arithmetic and copies ran while one was open for 24% -> 11% of each run, Pallas kernels for 20% -> 21%
where the time goes in v2:
time: 689 us; the launch traced here: 678 us
  waiting for transfers between devices  251 us (36%)
  Pallas kernels  171 us (25%)
  starting transfers between devices  92 us (13%)
  matrix products  59.2 us (9%)
  other arithmetic  57.1 us (8%)
  local copies, waits for them, and re-layouts  45.7 us (7%)
    ppermute x8, waiting for transfers between devices, spread(): out.append(lax.ppermute(block, axes, team.spread(step)))  88.5 us
    dot_general x8, matrix products, mm(): return lax.dot_general(a, b, dims, preferred_element_type=f32)  52.9 us
    ppermute x8, waiting for transfers between devices, unspread(): lax.ppermute(array[step * span:(step + 1) * span], axes, team.back(step))  46 us
    pallas_call x2, Pallas kernels, attend_back(): pl.pallas_call(functools.partial(attend_back_kernel, count, block, pair),...  45.2 us
    ppermute x9, waiting for transfers between devices, reduce_places(): got = lax.ppermute(send, 'seq', [(i, i ^ 1 << b) for i in range(places)])  35.3 us
    pallas_call x7, Pallas kernels, join(): pl.pallas_call(functools.partial(join_kernel, count, ends), grid_spec=plt...  33.1 us
    ppermute x9, waiting for transfers between devices, reduce_places(): got = lax.ppermute(buf, 'seq', [(i, i ^ 1 << b) for i in range(places)])  30.5 us
    ppermute x4, waiting for transfers between devices, on_device(): lax.ppermute(source, 'dp', team.turn_rows(step))  28 us
  transfers between devices with their start and end apart: 62, of which 26 were waited for; matrix products, arithmetic and copies ran while one was open for 11% of the time, Pallas kernels for 21%

profile of v2, /device:TPU:12, one launch (start us, length us, event | category | flops | bytes accessed | tf_op | source)
XLA Modules:
  0.0 678.3 jit_solution(3390004124540736019)
XLA Ops:
  0.8 2.8 concatenate.90
  12.4 3.7 dynamic-slice_bitcast_fusion.10
  24.4 9.3 %collective-permute-done.3.refs_3_ = bf16[256,1280]{1,0:T(8,128)(2,1)} collective-permute-done((bf16[256,1280]{1,0:T(8,128)(2,1)}, bf16[256,1280]{1,0:T(8,128)(2,1)}, u32[]{:S(2)}, u32[]{:S(2)}) %collective-permute-start.3) | collective-permute-done | bytes 655392 | tf_op jit(solution)/shard_map/ppermute | solution.py:607
  33.7 6.5 collective-permute-start
  40.2 3.0 pad_maximum_fusion.1.refs_0_
  43.3 20.1 %collective-permute-done.2.refs_2_ = bf16[256,1280]{1,0:T(8,128)(2,1)} collective-permute-done((bf16[256,1280]{1,0:T(8,128)(2,1)}, bf16[256,1280]{1,0:T(8,128)(2,1)}, u32[]{:S(2)}, u32[]{:S(2)}) %collective-permute-start.2) | collective-permute-done | bytes 655392 | tf_op jit(solution)/shard_map/ppermute | solution.py:607
  64.6 12.6 %collective-permute-done.1.refs_1_ = bf16[256,1280]{1,0:T(8,128)(2,1)} collective-permute-done((bf16[256,1280]{1,0:T(8,128)(2,1)}, bf16[256,1280]{1,0:T(8,128)(2,1)}, u32[]{:S(2)}, u32[]{:S(2)}) %collective-permute-start.1) | collective-permute-done | bytes 655392 | tf_op jit(solution)/shard_map/ppermute | solution.py:607
  77.8 3.5 join.7
  82.4 4.1 convert_reduce_fusion
  87.6 6.4 join.8
  95.9 19.7 %qkv.1 = (bf16[8,3,2048,80]{3,2,1,0:T(8,128)(2,1)}, bf16[2,2048,640]{2,1,0:T(8,128)(2,1)}) custom-call(bf16[1024,1280]{1,0:T(8,128)(2,1)} %bitcast.198, bf16[1024,1280]{1,0:T(8,128)(2,1)} %collective-permute-done.5.refs_1_, f32[1,1280]{1,0:T(1,128)} %slice.77.refs_2_, bf16[1280,1920]{1,0:T(8,128)(2,1)} %bitcast.200, f32[1,1920]{1,0:T(1,128)} %broadcast_in_dim_tile.3.refs_4_), custom_call_target="tpu_custom_call" | custom-call | flops 1 | bytes 1 | tf_op jit(solution)/shard_map/qkv/pallas_call | solution.py:163
  115.6 23.6 %attend.1 = (bf16[640,2048]{1,0:T(8,128)(2,1)}, f32[8,1,2048]{2,1,0:T(1,128)}) custom-call(s32[5,8]{1,0:T(8,128)} %stack.81.table, bf16[8,3,2048,80]{3,2,1,0:T(8,128)(2,1)} %get-tuple-element.54.qkv_ref, s32[8,256]{1,0:T(8,128)} %copy-done.38), custom_call_target="tpu_custom_call" | custom-call | flops 1 | bytes 1 | tf_op jit(solution)/shard_map/attend/pallas_call | solution.py:357
  143.0 5.2 collective-permute-start.19
  150.2 40.2 %collective-permute-done.20.refs_3_ = bf16[256,1280]{1,0:T(8,128)(2,1)S(1)} collective-permute-done((bf16[256,1280]{1,0:T(8,128)(2,1)S(1)}, bf16[256,1280]{1,0:T(8,128)(2,1)S(1)}, u32[]{:S(2)}, u32[]{:S(2)}) %collective-permute-start.20) | collective-permute-done | bytes 655392 | tf_op jit(solution)/shard_map/ppermute | solution.py:607
  195.1 6.3 collective-permute-done.18.refs_1_
  201.8 3.6 join.11
  206.5 3.6 join.9
  210.1 7.9 %join.10 = (bf16[4,320,1280]{2,1,0:T(8,128)(2,1)}, bf16[4,320,1280]{2,1,0:T(8,128)(2,1)}, bf16[4,320,1280]{2,1,0:T(8,128)(2,1)}) custom-call(s32[4]{0:T(128)} %add_add_fusion.1.slots_ref, bf16[960,1280]{1,0:T(8,128)(2,1)} %pad_maximum_fusion.1.refs_0_, bf16[960,1280]{1,0:T(8,128)(2,1)} %collective-permute-done.10.refs_1_, ...), custom_call_target="tpu_custom_call" | custom-call | flops 1 | bytes 1 | tf_op jit(solution)/shard_map/join/pallas_call | solution.py:116
  218.0 6.3 multiply_reduce_fusion.3
  224.3 3.6 fusion.35
  228.0 5.7 add_convert_fusion
  233.7 14.6 %convert_reduce_fusion.3 = (f32[1280]{0:T(1024)}, bf16[1024,1280]{1,0:T(8,128)(2,1)}) fusion(f32[1024,1280]{1,0:T(8,128)S(1)} %fusion.35, f32[1280]{0:T(1024)S(1)} %add.541, bf16[1024,1280]{1,0:T(8,128)(2,1)S(1)} %bitcast.205, bf16[1280,1280]{1,0:T(8,128)(2,1)S(1)} %bitcast.250), kind=kOutput, calls=%fused_computation.20 | convolution fusion | flops 3371170560 | bytes 13772800 | tf_op jit(solution)/shard_map/dot_general | solution.py:25
  248.3 6.3 convolution_convert_fusion.2
  254.6 7.5 %multiply_reduce_fusion = (f32[1280]{0:T(1024)}, f32[1024]{0:T(1024)S(1)}, f32[1024,1280]{1,0:T(8,128)S(1)}) fusion(f32[1024,1280]{1,0:T(8,128)S(1)} %get-tuple-element.146, f32[1024]{0:T(1024)S(1)} %add_rsqrt_fusion, f32[1280]{0:T(1024)S(1)} %mul.203, bf16[1024,1280]{1,0:T(8,128)(2,1)} %get-tuple-element.149, bf16[1280,1280]{1,0:T(8,128)(2,1)S(1)} %bitcast.248), kind=kOutput, calls=%fused_computation.21 | convolution fusion | flops 3363305216 | bytes 16402432 | tf_op jit(solution)/shard_map/dot_general | solution.py:25
  262.1 7.1 %convolution_convert_fusion.1 = bf16[1280,1280]{1,0:T(8,128)(2,1)} fusion(bf16[1024,1280]{1,0:T(8,128)(2,1)} %get-tuple-element.149, f32[1024,1280]{1,0:T(8,128)S(1)} %get-tuple-element.146, f32[1280]{0:T(1024)S(1)} %mul.203, f32[1024]{0:T(1024)S(1)} %add_rsqrt_fusion), kind=kOutput, calls=%fused_computation.7 | convolution fusion | flops 3361013760 | bytes 11150336 | tf_op jit(solution)/shard_map/dot_general | solution.py:25
  273.0 3.9 convolution_convert_fusion.3
  281.5 4.2 convolution_convert_fusion
  291.9 14.4 %collective-permute-start.16 = (bf16[256,1280]{1,0:T(8,128)(2,1)S(1)}, bf16[256,1280]{1,0:T(8,128)(2,1)S(1)}, u32[]{:S(2)}, u32[]{:S(2)}) collective-permute-start(bf16[256,1280]{1,0:T(8,128)(2,1)S(1)} %get-tuple-element.129), channel_id=1, source_target_pairs={{6,0},{14,1},{0,2},{8,3},{2,4},{10,5},{4,6},{12,7},{7,8},{15,9},{1... | collective-permute-start | bytes 1966088 | tf_op jit(solution)/shard_map/ppermute | solution.py:612
  306.3 4.0 collective-permute-start.15
  310.3 3.2 pad_maximum_fusion.grad_ref
  324.4 22.5 %attend_back.2 = (bf16[960,2048]{1,0:T(8,128)(2,1)}, f32[80,1]{1,0:T(8,128)}) custom-call(s32[5,8]{1,0:T(8,128)} %stack.81.table, bf16[8,3,2048,80]{3,2,1,0:T(8,128)(2,1)} %get-tuple-element.54.qkv_ref, bf16[640,2048]{1,0:T(8,128)(2,1)} %get-tuple-element.55.att_ref, bf16[640,2048]{1,0:T(8,128)(2,1)} %pad_maximum_fusion.grad_ref, ...), custom_call_target="tpu_custom_call" | custom-call | flops 1 | bytes 1 | tf_op jit(solution)/shard_map/attend_back/pallas_call | solution.py:479
  346.9 15.4 %collective-permute-done.15.refs_2_ = bf16[256,1280]{1,0:T(8,128)(2,1)S(1)} collective-permute-done((bf16[256,1280]{1,0:T(8,128)(2,1)S(1)}, bf16[256,1280]{1,0:T(8,128)(2,1)S(1)}, u32[]{:S(2)}, u32[]{:S(2)}) %collective-permute-start.15) | collective-permute-done | bytes 655392 | tf_op jit(solution)/shard_map/ppermute | solution.py:612
  362.4 4.4 collective-permute-done.14.refs_1_
  366.8 12.2 %head_grad.2 = (bf16[480,640]{1,0:T(8,128)(2,1)}, bf16[480,640]{1,0:T(8,128)(2,1)}, bf16[480,640]{1,0:T(8,128)(2,1)}, bf16[480,640]{1,0:T(8,128)(2,1)}) custom-call(s32[3]{0:T(128)} %pad_add_fusion.2.place_ref, bf16[960,2048]{1,0:T(8,128)(2,1)} %get-tuple-element.87.grads_ref.refs_0_, bf16[2,2048,640]{2,1,0:T(8,128)(2,1)} %get-tuple-element.72.normed_ref), custom_call_target="tpu_custom_call" | custom-call | flops 1 | bytes 1 | tf_op jit(solution)/shard_map/head_grad/pallas_call | solution.py:209
  379.8 2.9 collective-permute-start.36
  384.7 13.0 %collective-permute-done.36 = bf16[480,640]{1,0:T(8,128)(2,1)} collective-permute-done((bf16[480,640]{1,0:T(8,128)(2,1)}, bf16[480,640]{1,0:T(8,128)(2,1)}, u32[]{:S(2)}, u32[]{:S(2)}) %collective-permute-start.36) | collective-permute-done | bytes 614432 | tf_op jit(solution)/shard_map/ppermute | solution.py:788
  399.1 11.7 %collective-permute-done.39 = bf16[480,640]{1,0:T(8,128)(2,1)} collective-permute-done((bf16[480,640]{1,0:T(8,128)(2,1)}, bf16[480,640]{1,0:T(8,128)(2,1)}, u32[]{:S(2)}, u32[]{:S(2)}) %collective-permute-start.39) | collective-permute-done | bytes 614432 | tf_op jit(solution)/shard_map/ppermute | solution.py:788
  415.6 13.9 %collective-permute-done.40 = bf16[480,640]{1,0:T(8,128)(2,1)} collective-permute-done((bf16[480,640]{1,0:T(8,128)(2,1)}, bf16[480,640]{1,0:T(8,128)(2,1)}, u32[]{:S(2)}, u32[]{:S(2)}) %collective-permute-start.40) | collective-permute-done | bytes 614432 | tf_op jit(solution)/shard_map/ppermute | solution.py:549
  432.5 22.7 %attend_back.3 = (bf16[960,2048]{1,0:T(8,128)(2,1)}, f32[80,1]{1,0:T(8,128)}) custom-call(s32[5,8]{1,0:T(8,128)} %stack.81.table, bf16[8,3,2048,80]{3,2,1,0:T(8,128)(2,1)} %get-tuple-element.54.qkv_ref, bf16[640,2048]{1,0:T(8,128)(2,1)} %get-tuple-element.55.att_ref, bf16[640,2048]{1,0:T(8,128)(2,1)} %pad_maximum_fusion.grad_ref, ...), custom_call_target="tpu_custom_call" | custom-call | flops 1 | bytes 1 | tf_op jit(solution)/shard_map/attend_back/pallas_call | solution.py:479
  456.2 6.7 collective-permute-done.25
  467.9 12.2 %head_grad.3 = (bf16[480,640]{1,0:T(8,128)(2,1)}, bf16[480,640]{1,0:T(8,128)(2,1)}, bf16[480,640]{1,0:T(8,128)(2,1)}, bf16[480,640]{1,0:T(8,128)(2,1)}) custom-call(s32[3]{0:T(128)} %pad_add_fusion.2.place_ref, bf16[960,2048]{1,0:T(8,128)(2,1)} %get-tuple-element.88.grads_ref.refs_1_, bf16[2,2048,640]{2,1,0:T(8,128)(2,1)} %get-tuple-element.72.normed_ref), custom_call_target="tpu_custom_call" | custom-call | flops 1 | bytes 1 | tf_op jit(solution)/shard_map/head_grad/pallas_call | solution.py:209
  484.2 3.4 collective-permute-done.42
  487.7 3.4 collective-permute-start.43
  495.5 10.0 %input_side.2 = bf16[1024,1280]{1,0:T(8,128)(2,1)} custom-call(bf16[960,2048]{1,0:T(8,128)(2,1)} %get-tuple-element.87.grads_ref.refs_0_, bf16[960,2048]{1,0:T(8,128)(2,1)} %get-tuple-element.88.grads_ref.refs_1_, bf16[1280,1920]{1,0:T(8,128)(2,1)} %bitcast.201), custom_call_target="tpu_custom_call" | custom-call | flops 1 | bytes 1 | tf_op jit(solution)/shard_map/input_side/pallas_call | solution.py:525
  506.7 3.3 collective-permute-done.49
  511.6 3.0 collective-permute-start.50
  518.3 9.9 %input_side.3 = bf16[1024,1280]{1,0:T(8,128)(2,1)} custom-call(bf16[960,2048]{1,0:T(8,128)(2,1)} %get-tuple-element.87.grads_ref.refs_0_, bf16[960,2048]{1,0:T(8,128)(2,1)} %get-tuple-element.88.grads_ref.refs_1_, bf16[1280,1920]{1,0:T(8,128)(2,1)} %bitcast.202), custom_call_target="tpu_custom_call" | custom-call | flops 1 | bytes 1 | tf_op jit(solution)/shard_map/input_side/pallas_call | solution.py:525
  536.2 6.9 %collective-permute-done.51 = bf16[240,640]{1,0:T(8,128)(2,1)S(1)} collective-permute-done((bf16[240,640]{1,0:T(8,128)(2,1)S(1)}, bf16[240,640]{1,0:T(8,128)(2,1)S(1)}, u32[]{:S(2)}, u32[]{:S(2)}) %collective-permute-start.51) | collective-permute-done | bytes 307232 | tf_op jit(solution)/shard_map/ppermute | solution.py:549
  543.3 3.7 collective-permute-start.52
  546.9 6.8 %collective-permute-done.58 = bf16[120,1280]{1,0:T(8,128)(2,1)S(1)} collective-permute-done((bf16[120,1280]{1,0:T(8,128)(2,1)S(1)}, bf16[120,1280]{1,0:T(8,128)(2,1)S(1)}, u32[]{:S(2)}, u32[]{:S(2)}) %collective-permute-start.58) | collective-permute-done | bytes 307232 | tf_op jit(solution)/shard_map/ppermute | solution.py:549
  553.8 3.4 collective-permute-start.59
  559.9 3.4 collective-permute-start.53
  563.4 2.9 fusion.8
  566.5 8.6 %collective-permute-done.53 = bf16[120,640]{1,0:T(8,128)(2,1)S(1)} collective-permute-done((bf16[120,640]{1,0:T(8,128)(2,1)S(1)}, bf16[120,640]{1,0:T(8,128)(2,1)S(1)}, u32[]{:S(2)}, u32[]{:S(2)}) %collective-permute-start.53) | collective-permute-done | bytes 153632 | tf_op jit(solution)/shard_map/ppermute | solution.py:554
  575.2 3.7 collective-permute-start.54
  579.2 3.6 collective-permute-done.32
  583.8 2.8 collective-permute-done.33
  589.1 9.6 %collective-permute-done.34 = f32[5200]{0:T(1024)S(1)} collective-permute-done((f32[5200]{0:T(1024)S(1)}, f32[5200]{0:T(1024)S(1)}, u32[]{:S(2)}, u32[]{:S(2)}) %collective-permute-start.34) | collective-permute-done | bytes 20832 | tf_op jit(solution)/shard_map/ppermute | solution.py:573
  607.9 19.5 %collective-permute-done.55 = bf16[480,640]{1,0:T(8,128)(2,1)S(1)} collective-permute-done((bf16[480,640]{1,0:T(8,128)(2,1)S(1)}, bf16[480,640]{1,0:T(8,128)(2,1)S(1)}, u32[]{:S(2)}, u32[]{:S(2)}) %collective-permute-start.55) | collective-permute-done | bytes 614432 | tf_op jit(solution)/shard_map/ppermute | solution.py:554
  629.6 3.7 join.12
  637.5 12.1 %collective-permute-done.30.refs_3_ = bf16[256,1280]{1,0:T(8,128)(2,1)} collective-permute-done((bf16[256,1280]{1,0:T(8,128)(2,1)}, bf16[256,1280]{1,0:T(8,128)(2,1)}, u32[]{:S(2)}, u32[]{:S(2)}) %collective-permute-start.30) | collective-permute-done | bytes 655392 | tf_op jit(solution)/shard_map/ppermute | solution.py:612
  649.6 13.0 %collective-permute-done.29.refs_2_ = bf16[256,1280]{1,0:T(8,128)(2,1)} collective-permute-done((bf16[256,1280]{1,0:T(8,128)(2,1)}, bf16[256,1280]{1,0:T(8,128)(2,1)}, u32[]{:S(2)}, u32[]{:S(2)}) %collective-permute-start.29) | collective-permute-done | bytes 655392 | tf_op jit(solution)/shard_map/ppermute | solution.py:612
  663.7 4.5 join.13
  668.2 5.4 unfold.1
  (318 shorter events, 129.0 us)
Async XLA Ops:
  16.2 47.2 %copy-start.45 = (s32[4,2048]{1,0:T(4,128)S(1)}, s32[4,2048]{1,0:T(4,128)}, u32[]{:S(2)}) copy-start(s32[4,2048]{1,0:T(4,128)} %param.13) | copy-start | bytes 98308
  16.2 17.6 %collective-permute-start.3 = (bf16[256,1280]{1,0:T(8,128)(2,1)}, bf16[256,1280]{1,0:T(8,128)(2,1)}, u32[]{:S(2)}, u32[]{:S(2)}) collective-permute-start(bf16[256,1280]{1,0:T(8,128)(2,1)} %get-tuple-element.135), channel_id=1, source_target_pairs={{0,6},{1,14},{2,0},{3,8},{4,2},{5,10},{6,4},{7,12},{8,7},{9,15},{1... | collective-permute-start | bytes 1966088 | tf_op jit(solution)/shard_map/ppermute | solution.py:607
  16.6 65.2 %collective-permute-start.8 = (bf16[336,1920]{1,0:T(8,128)(2,1)S(1)}, bf16[336,1920]{1,0:T(8,128)(2,1)}, u32[]{:S(2)}, u32[]{:S(2)}) collective-permute-start(bf16[336,1920]{1,0:T(8,128)(2,1)S(1)} %copy-done.26), channel_id=1, source_target_pairs={{0,24},{8,16},{16,8},{24,0},{1,25},{9,17},{17,9},{25,1},{2,26},{10... | collective-permute-start | bytes 3870728 | tf_op jit(solution)/shard_map/ppermute | solution.py:634
  17.8 64.1 %collective-permute-start.7 = (bf16[336,1920]{1,0:T(8,128)(2,1)S(1)}, bf16[336,1920]{1,0:T(8,128)(2,1)}, u32[]{:S(2)}, u32[]{:S(2)}) collective-permute-start(bf16[336,1920]{1,0:T(8,128)(2,1)S(1)} %get-tuple-element.140.refs_0_), channel_id=1, source_target_pairs={{0,16},{8,24},{16,0},{24,8},{1,17},{9,25},{17,1},{25,9},{2,18},{10... | collective-permute-start | bytes 3870728 | tf_op jit(solution)/shard_map/ppermute | solution.py:634
  19.3 44.0 %collective-permute-start.2 = (bf16[256,1280]{1,0:T(8,128)(2,1)}, bf16[256,1280]{1,0:T(8,128)(2,1)}, u32[]{:S(2)}, u32[]{:S(2)}) collective-permute-start(bf16[256,1280]{1,0:T(8,128)(2,1)} %get-tuple-element.136), channel_id=1, source_target_pairs={{0,4},{1,12},{2,6},{3,14},{4,0},{5,8},{6,2},{7,10},{8,5},{9,13},{1... | collective-permute-start | bytes 1966088 | tf_op jit(solution)/shard_map/ppermute | solution.py:607
  21.9 55.4 %collective-permute-start.1 = (bf16[256,1280]{1,0:T(8,128)(2,1)}, bf16[256,1280]{1,0:T(8,128)(2,1)}, u32[]{:S(2)}, u32[]{:S(2)}) collective-permute-start(bf16[256,1280]{1,0:T(8,128)(2,1)} %get-tuple-element.137), channel_id=1, source_target_pairs={{0,2},{1,10},{2,4},{3,12},{4,6},{5,14},{6,0},{7,8},{8,3},{9,11},{1... | collective-permute-start | bytes 1966088 | tf_op jit(solution)/shard_map/ppermute | solution.py:607
  33.7 43.6 %collective-permute-start = (bf16[256,1280]{1,0:T(8,128)(2,1)}, bf16[256,1280]{1,0:T(8,128)(2,1)}, u32[]{:S(2)}, u32[]{:S(2)}) collective-permute-start(bf16[256,1280]{1,0:T(8,128)(2,1)} %get-tuple-element.138), channel_id=1, source_target_pairs={{0,0},{1,8},{2,2},{3,10},{4,4},{5,12},{6,6},{7,14},{8,1},{9,9},{10... | collective-permute-start | bytes 1966088 | tf_op jit(solution)/shard_map/ppermute | solution.py:607
  63.3 19.0 %collective-permute-start.4 = (s32[4,2048]{1,0:T(4,128)S(1)}, s32[4,2048]{1,0:T(4,128)S(1)}, u32[]{:S(2)}, u32[]{:S(2)}) collective-permute-start(s32[4,2048]{1,0:T(4,128)S(1)} %copy-done.45), channel_id=1, source_target_pairs={{0,8},{8,0},{16,24},{24,16},{1,9},{9,1},{17,25},{25,17},{2,10},{10... | collective-permute-start | bytes 98312 | tf_op jit(solution)/shard_map/ppermute | solution.py:638
  77.3 10.3 %collective-permute-start.6 = (bf16[336,1920]{1,0:T(8,128)(2,1)S(1)}, bf16[336,1920]{1,0:T(8,128)(2,1)}, u32[]{:S(2)}, u32[]{:S(2)}) collective-permute-start(bf16[336,1920]{1,0:T(8,128)(2,1)S(1)} %copy-done.26), channel_id=1, source_target_pairs={{0,8},{8,0},{16,24},{24,16},{1,9},{9,1},{17,25},{25,17},{2,10},{10... | collective-permute-start | bytes 3870728 | tf_op jit(solution)/shard_map/ppermute | solution.py:636
  81.3 14.6 %collective-permute-start.5 = (bf16[1024,1280]{1,0:T(8,128)(2,1)}, bf16[1024,1280]{1,0:T(8,128)(2,1)}, u32[]{:S(2)}, u32[]{:S(2)}) collective-permute-start(bf16[1024,1280]{1,0:T(8,128)(2,1)} %bitcast.197), channel_id=1, source_target_pairs={{0,8},{1,9},{2,10},{3,11},{4,12},{5,13},{6,14},{7,15},{8,0},{9,1},... | collective-permute-start | bytes 7864328 | tf_op jit(solution)/shard_map/ppermute | solution.py:648
  81.8 57.4 %collective-permute-start.10 = (bf16[960,1280]{1,0:T(8,128)(2,1)}, bf16[960,1280]{1,0:T(8,128)(2,1)}, u32[]{:S(2)}, u32[]{:S(2)}) collective-permute-start(bf16[960,1280]{1,0:T(8,128)(2,1)} %pad_maximum_fusion.1.refs_0_), channel_id=1, source_target_pairs={{0,16},{8,24},{16,0},{24,8},{1,17},{9,25},{17,1},{25,9},{2,18},{10... | collective-permute-start | bytes 7372808 | tf_op jit(solution)/shard_map/ppermute | solution.py:651
  139.2 70.9 %collective-permute-start.11 = (bf16[960,1280]{1,0:T(8,128)(2,1)}, bf16[960,1280]{1,0:T(8,128)(2,1)}, u32[]{:S(2)}, u32[]{:S(2)}) collective-permute-start(bf16[960,1280]{1,0:T(8,128)(2,1)} %pad_maximum_fusion.1.refs_0_), channel_id=1, source_target_pairs={{0,8},{8,0},{16,24},{24,16},{1,9},{9,1},{17,25},{25,17},{2,10},{10... | collective-permute-start | bytes 7372808 | tf_op jit(solution)/shard_map/ppermute | solution.py:683
  139.2 70.9 %collective-permute-start.12 = (bf16[960,1280]{1,0:T(8,128)(2,1)}, bf16[960,1280]{1,0:T(8,128)(2,1)}, u32[]{:S(2)}, u32[]{:S(2)}) collective-permute-start(bf16[960,1280]{1,0:T(8,128)(2,1)} %collective-permute-done.10.refs_1_), channel_id=1, source_target_pairs={{0,8},{8,0},{16,24},{24,16},{1,9},{9,1},{17,25},{25,17},{2,10},{10... | collective-permute-start | bytes 7372808 | tf_op jit(solution)/shard_map/ppermute | solution.py:683
  141.0 49.4 %collective-permute-start.20 = (bf16[256,1280]{1,0:T(8,128)(2,1)S(1)}, bf16[256,1280]{1,0:T(8,128)(2,1)S(1)}, u32[]{:S(2)}, u32[]{:S(2)}) collective-permute-start(bf16[256,1280]{1,0:T(8,128)(2,1)S(1)} %get-tuple-element.125), channel_id=1, source_target_pairs={{0,6},{1,14},{2,0},{3,8},{4,2},{5,10},{6,4},{7,12},{8,7},{9,15},{1... | collective-permute-start | bytes 1966088 | tf_op jit(solution)/shard_map/ppermute | solution.py:607
  143.0 47.4 %collective-permute-start.19 = (bf16[256,1280]{1,0:T(8,128)(2,1)S(1)}, bf16[256,1280]{1,0:T(8,128)(2,1)S(1)}, u32[]{:S(2)}, u32[]{:S(2)}) collective-permute-start(bf16[256,1280]{1,0:T(8,128)(2,1)S(1)} %get-tuple-element.126), channel_id=1, source_target_pairs={{0,4},{1,12},{2,6},{3,14},{4,0},{5,8},{6,2},{7,10},{8,5},{9,13},{1... | collective-permute-start | bytes 1966088 | tf_op jit(solution)/shard_map/ppermute | solution.py:607
  149.5 55.9 %collective-permute-start.9 = (bf16[640,1024]{1,0:T(8,128)(2,1)S(1)}, bf16[640,1024]{1,0:T(8,128)(2,1)S(1)}, u32[]{:S(2)}, u32[]{:S(2)}) collective-permute-start(bf16[640,1024]{1,0:T(8,128)(2,1)S(1)} %get-tuple-element.133), channel_id=1, source_target_pairs={{0,8},{1,9},{2,10},{3,11},{4,12},{5,13},{6,14},{7,15},{8,0},{9,1},... | collective-permute-start | bytes 3932168 | tf_op jit(solution)/shard_map/ppermute | solution.py:696
  190.4 10.9 %collective-permute-start.18 = (bf16[256,1280]{1,0:T(8,128)(2,1)}, bf16[256,1280]{1,0:T(8,128)(2,1)}, u32[]{:S(2)}, u32[]{:S(2)}) collective-permute-start(bf16[256,1280]{1,0:T(8,128)(2,1)} %get-tuple-element.127), channel_id=1, source_target_pairs={{0,2},{1,10},{2,4},{3,12},{4,6},{5,14},{6,0},{7,8},{8,3},{9,11},{1... | collective-permute-start | bytes 1966088 | tf_op jit(solution)/shard_map/ppermute | solution.py:607
  192.1 9.2 %collective-permute-start.17 = (bf16[256,1280]{1,0:T(8,128)(2,1)S(1)}, bf16[256,1280]{1,0:T(8,128)(2,1)}, u32[]{:S(2)}, u32[]{:S(2)}) collective-permute-start(bf16[256,1280]{1,0:T(8,128)(2,1)S(1)} %get-tuple-element.128), channel_id=1, source_target_pairs={{0,0},{1,8},{2,2},{3,10},{4,4},{5,12},{6,6},{7,14},{8,1},{9,9},{10... | collective-permute-start | bytes 1966088 | tf_op jit(solution)/shard_map/ppermute | solution.py:607
  270.5 43.1 %collective-permute-start.22 = (bf16[2,320,1280]{2,1,0:T(8,128)(2,1)}, bf16[2,320,1280]{2,1,0:T(8,128)(2,1)}, u32[]{:S(2)}, u32[]{:S(2)}) collective-permute-start(bf16[2,320,1280]{2,1,0:T(8,128)(2,1)} %dynamic-slice_bitcast_fusion.2), channel_id=1, source_target_pairs={{0,8},{8,0},{16,24},{24,16},{1,9},{9,1},{17,25},{25,17},{2,10},{10... | collective-permute-start | bytes 4915208 | tf_op jit(solution)/shard_map/ppermute | solution.py:738
  278.6 27.7 %collective-permute-start.21 = (bf16[640,1024]{1,0:T(8,128)(2,1)}, bf16[640,1024]{1,0:T(8,128)(2,1)}, u32[]{:S(2)}, u32[]{:S(2)}) collective-permute-start(bf16[640,1024]{1,0:T(8,128)(2,1)} %get-tuple-element.124), channel_id=1, source_target_pairs={{0,8},{1,9},{2,10},{3,11},{4,12},{5,13},{6,14},{7,15},{8,0},{9,1},... | collective-permute-start | bytes 3932168 | tf_op jit(solution)/shard_map/ppermute | solution.py:730
  281.0 34.6 %collective-permute-start.23 = (bf16[2,320,1280]{2,1,0:T(8,128)(2,1)}, bf16[2,320,1280]{2,1,0:T(8,128)(2,1)}, u32[]{:S(2)}, u32[]{:S(2)}) collective-permute-start(bf16[2,320,1280]{2,1,0:T(8,128)(2,1)} %dynamic-slice_bitcast_fusion.1), channel_id=1, source_target_pairs={{0,8},{8,0},{16,24},{24,16},{1,9},{9,1},{17,25},{25,17},{2,10},{10... | collective-permute-start | bytes 4915208 | tf_op jit(solution)/shard_map/ppermute | solution.py:738
  288.7 31.3 %collective-permute-start.24 = (bf16[2,320,1280]{2,1,0:T(8,128)(2,1)}, bf16[2,320,1280]{2,1,0:T(8,128)(2,1)}, u32[]{:S(2)}, u32[]{:S(2)}) collective-permute-start(bf16[2,320,1280]{2,1,0:T(8,128)(2,1)} %dynamic-slice_bitcast_fusion), channel_id=1, source_target_pairs={{0,8},{8,0},{16,24},{24,16},{1,9},{9,1},{17,25},{25,17},{2,10},{10... | collective-permute-start | bytes 4915208 | tf_op jit(solution)/shard_map/ppermute | solution.py:738
  291.9 55.0 %collective-permute-start.16 = (bf16[256,1280]{1,0:T(8,128)(2,1)S(1)}, bf16[256,1280]{1,0:T(8,128)(2,1)S(1)}, u32[]{:S(2)}, u32[]{:S(2)}) collective-permute-start(bf16[256,1280]{1,0:T(8,128)(2,1)S(1)} %get-tuple-element.129), channel_id=1, source_target_pairs={{6,0},{14,1},{0,2},{8,3},{2,4},{10,5},{4,6},{12,7},{7,8},{15,9},{1... | collective-permute-start | bytes 1966088 | tf_op jit(solution)/shard_map/ppermute | solution.py:612
  306.3 56.0 %collective-permute-start.15 = (bf16[256,1280]{1,0:T(8,128)(2,1)S(1)}, bf16[256,1280]{1,0:T(8,128)(2,1)S(1)}, u32[]{:S(2)}, u32[]{:S(2)}) collective-permute-start(bf16[256,1280]{1,0:T(8,128)(2,1)S(1)} %get-tuple-element.130), channel_id=1, source_target_pairs={{4,0},{12,1},{6,2},{14,3},{0,4},{8,5},{2,6},{10,7},{5,8},{13,9},{7... | collective-permute-start | bytes 1966088 | tf_op jit(solution)/shard_map/ppermute | solution.py:612
  313.6 53.2 %collective-permute-start.14 = (bf16[256,1280]{1,0:T(8,128)(2,1)S(1)}, bf16[256,1280]{1,0:T(8,128)(2,1)S(1)}, u32[]{:S(2)}, u32[]{:S(2)}) collective-permute-start(bf16[256,1280]{1,0:T(8,128)(2,1)S(1)} %get-tuple-element.131), channel_id=1, source_target_pairs={{2,0},{10,1},{4,2},{12,3},{6,4},{14,5},{0,6},{8,7},{3,8},{11,9},{5... | collective-permute-start | bytes 1966088 | tf_op jit(solution)/shard_map/ppermute | solution.py:612
  315.6 51.1 %collective-permute-start.13 = (bf16[256,1280]{1,0:T(8,128)(2,1)S(1)}, bf16[256,1280]{1,0:T(8,128)(2,1)}, u32[]{:S(2)}, u32[]{:S(2)}) collective-permute-start(bf16[256,1280]{1,0:T(8,128)(2,1)S(1)} %get-tuple-element.132), channel_id=1, source_target_pairs={{0,0},{8,1},{2,2},{10,3},{4,4},{12,5},{6,6},{14,7},{1,8},{9,9},{3,... | collective-permute-start | bytes 1966088 | tf_op jit(solution)/shard_map/ppermute | solution.py:612
  379.0 3.8 collective-permute-start.38
  379.8 17.9 %collective-permute-start.36 = (bf16[480,640]{1,0:T(8,128)(2,1)}, bf16[480,640]{1,0:T(8,128)(2,1)}, u32[]{:S(2)}, u32[]{:S(2)}) collective-permute-start(bf16[480,640]{1,0:T(8,128)(2,1)} %get-tuple-element.76), channel_id=1, source_target_pairs={{0,16},{8,24},{16,0},{24,8},{1,17},{9,25},{17,1},{25,9},{2,18},{10... | collective-permute-start | bytes 1843208 | tf_op jit(solution)/shard_map/ppermute | solution.py:788
  382.7 16.4 %collective-permute-start.37 = (bf16[480,640]{1,0:T(8,128)(2,1)}, bf16[480,640]{1,0:T(8,128)(2,1)}, u32[]{:S(2)}, u32[]{:S(2)}) collective-permute-start(bf16[480,640]{1,0:T(8,128)(2,1)} %get-tuple-element.73), channel_id=1, source_target_pairs={{0,8},{8,0},{16,24},{24,16},{1,9},{9,1},{17,25},{25,17},{2,10},{10... | collective-permute-start | bytes 1843208 | tf_op jit(solution)/shard_map/ppermute | solution.py:785
  382.7 28.2 %collective-permute-start.39 = (bf16[480,640]{1,0:T(8,128)(2,1)}, bf16[480,640]{1,0:T(8,128)(2,1)}, u32[]{:S(2)}, u32[]{:S(2)}) collective-permute-start(bf16[480,640]{1,0:T(8,128)(2,1)} %collective-permute-done.38), channel_id=1, source_target_pairs={{0,16},{8,24},{16,0},{24,8},{1,17},{9,25},{17,1},{25,9},{2,18},{10... | collective-permute-start | bytes 1843208 | tf_op jit(solution)/shard_map/ppermute | solution.py:788
  384.7 78.2 %collective-permute-start.25 = (bf16[960,1280]{1,0:T(8,128)(2,1)}, bf16[960,1280]{1,0:T(8,128)(2,1)}, u32[]{:S(2)}, u32[]{:S(2)}) collective-permute-start(bf16[960,1280]{1,0:T(8,128)(2,1)} %pad_maximum_fusion.3), channel_id=1, source_target_pairs={{0,16},{8,24},{16,0},{24,8},{1,17},{9,25},{17,1},{25,9},{2,18},{10... | collective-permute-start | bytes 7372808 | tf_op jit(solution)/shard_map/ppermute | solution.py:757
  414.3 15.2 %collective-permute-start.40 = (bf16[480,640]{1,0:T(8,128)(2,1)}, bf16[480,640]{1,0:T(8,128)(2,1)}, u32[]{:S(2)}, u32[]{:S(2)}) collective-permute-start(bf16[480,640]{1,0:T(8,128)(2,1)} %dynamic-slice_bitcast_fusion.16), channel_id=1, source_target_pairs={{0,1},{1,0},{2,3},{3,2},{4,5},{5,4},{6,7},{7,6},{8,9},{9,8},{10,11... | collective-permute-start | bytes 1843208 | tf_op jit(solution)/shard_map/ppermute | solution.py:549
  432.4 22.7 %collective-permute-start.41 = (bf16[240,640]{1,0:T(8,128)(2,1)}, bf16[240,640]{1,0:T(8,128)(2,1)}, u32[]{:S(2)}, u32[]{:S(2)}) collective-permute-start(bf16[240,640]{1,0:T(8,128)(2,1)} %dynamic-slice_bitcast_fusion.19), channel_id=1, source_target_pairs={{0,2},{1,3},{2,0},{3,1},{4,6},{5,7},{6,4},{7,5},{8,10},{9,11},{10,... | collective-permute-start | bytes 921608 | tf_op jit(solution)/shard_map/ppermute | solution.py:549
  480.1 11.0 %collective-permute-start.48 = (bf16[480,640]{1,0:T(8,128)(2,1)}, bf16[480,640]{1,0:T(8,128)(2,1)}, u32[]{:S(2)}, u32[]{:S(2)}) collective-permute-start(bf16[480,640]{1,0:T(8,128)(2,1)} %get-tuple-element.82), channel_id=1, source_target_pairs={{0,8},{8,0},{16,24},{24,16},{1,9},{9,1},{17,25},{25,17},{2,10},{10... | collective-permute-start | bytes 1843208 | tf_op jit(solution)/shard_map/ppermute | solution.py:785
  480.1 7.5 %collective-permute-start.42 = (bf16[120,640]{1,0:T(8,128)(2,1)S(1)}, bf16[120,640]{1,0:T(8,128)(2,1)S(1)}, u32[]{:S(2)}, u32[]{:S(2)}) collective-permute-start(bf16[120,640]{1,0:T(8,128)(2,1)S(1)} %dynamic-slice_bitcast_fusion.21), channel_id=1, source_target_pairs={{0,4},{1,5},{2,6},{3,7},{4,0},{5,1},{6,2},{7,3},{8,12},{9,13},{10,... | collective-permute-start | bytes 460808 | tf_op jit(solution)/shard_map/ppermute | solution.py:549
  480.2 25.3 %collective-permute-start.46 = (bf16[480,640]{1,0:T(8,128)(2,1)}, bf16[480,640]{1,0:T(8,128)(2,1)}, u32[]{:S(2)}, u32[]{:S(2)}) collective-permute-start(bf16[480,640]{1,0:T(8,128)(2,1)} %get-tuple-element.84), channel_id=1, source_target_pairs={{0,16},{8,24},{16,0},{24,8},{1,17},{9,25},{17,1},{25,9},{2,18},{10... | collective-permute-start | bytes 1843208 | tf_op jit(solution)/shard_map/ppermute | solution.py:788
  482.6 32.1 %collective-permute-start.56 = (bf16[480,1280]{1,0:T(8,128)(2,1)}, bf16[480,1280]{1,0:T(8,128)(2,1)}, u32[]{:S(2)}, u32[]{:S(2)}) collective-permute-start(bf16[480,1280]{1,0:T(8,128)(2,1)} %dynamic-slice_bitcast_fusion.5), channel_id=1, source_target_pairs={{0,1},{1,0},{2,3},{3,2},{4,5},{5,4},{6,7},{7,6},{8,9},{9,8},{10,11... | collective-permute-start | bytes 3686408 | tf_op jit(solution)/shard_map/ppermute | solution.py:549
  487.7 7.7 %collective-permute-start.43 = (bf16[120,640]{1,0:T(8,128)(2,1)S(1)}, bf16[120,640]{1,0:T(8,128)(2,1)S(1)}, u32[]{:S(2)}, u32[]{:S(2)}) collective-permute-start(bf16[120,640]{1,0:T(8,128)(2,1)S(1)} %fusion.27), channel_id=1, source_target_pairs={{0,4},{1,5},{2,6},{3,7},{4,0},{5,1},{6,2},{7,3},{8,12},{9,13},{10,... | collective-permute-start | bytes 460808 | tf_op jit(solution)/shard_map/ppermute | solution.py:554
  491.1 15.6 %collective-permute-start.47 = (bf16[480,640]{1,0:T(8,128)(2,1)}, bf16[480,640]{1,0:T(8,128)(2,1)}, u32[]{:S(2)}, u32[]{:S(2)}) collective-permute-start(bf16[480,640]{1,0:T(8,128)(2,1)} %get-tuple-element.81), channel_id=1, source_target_pairs={{0,8},{8,0},{16,24},{24,16},{1,9},{9,1},{17,25},{25,17},{2,10},{10... | collective-permute-start | bytes 1843208 | tf_op jit(solution)/shard_map/ppermute | solution.py:785
  491.1 18.9 %collective-permute-start.49 = (bf16[480,640]{1,0:T(8,128)(2,1)}, bf16[480,640]{1,0:T(8,128)(2,1)}, u32[]{:S(2)}, u32[]{:S(2)}) collective-permute-start(bf16[480,640]{1,0:T(8,128)(2,1)} %collective-permute-done.48), channel_id=1, source_target_pairs={{0,16},{8,24},{16,0},{24,8},{1,17},{9,25},{17,1},{25,9},{2,18},{10... | collective-permute-start | bytes 1843208 | tf_op jit(solution)/shard_map/ppermute | solution.py:788
  495.4 32.9 %collective-permute-start.44 = (bf16[240,640]{1,0:T(8,128)(2,1)S(1)}, bf16[240,640]{1,0:T(8,128)(2,1)}, u32[]{:S(2)}, u32[]{:S(2)}) collective-permute-start(bf16[240,640]{1,0:T(8,128)(2,1)S(1)} %maximum_select_fusion.7), channel_id=1, source_target_pairs={{0,2},{1,3},{2,0},{3,1},{4,6},{5,7},{6,4},{7,5},{8,10},{9,11},{10,... | collective-permute-start | bytes 921608 | tf_op jit(solution)/shard_map/ppermute | solution.py:554
  505.5 57.9 %collective-permute-start.26 = (bf16[1024,1280]{1,0:T(8,128)(2,1)}, bf16[1024,1280]{1,0:T(8,128)(2,1)S(1)}, u32[]{:S(2)}, u32[]{:S(2)}) collective-permute-start(bf16[1024,1280]{1,0:T(8,128)(2,1)} %input_side.2), channel_id=1, source_target_pairs={{0,8},{1,9},{2,10},{3,11},{4,12},{5,13},{6,14},{7,15},{8,0},{9,1},... | collective-permute-start | bytes 7864328 | tf_op jit(solution)/shard_map/ppermute | solution.py:804
  511.6 18.2 %collective-permute-start.50 = (bf16[480,640]{1,0:T(8,128)(2,1)S(1)}, bf16[480,640]{1,0:T(8,128)(2,1)}, u32[]{:S(2)}, u32[]{:S(2)}) collective-permute-start(bf16[480,640]{1,0:T(8,128)(2,1)S(1)} %dynamic-slice_bitcast_fusion.15), channel_id=1, source_target_pairs={{0,1},{1,0},{2,3},{3,2},{4,5},{5,4},{6,7},{7,6},{8,9},{9,8},{10,11... | collective-permute-start | bytes 1843208 | tf_op jit(solution)/shard_map/ppermute | solution.py:549
  518.2 16.7 %collective-permute-start.57 = (bf16[240,1280]{1,0:T(8,128)(2,1)}, bf16[240,1280]{1,0:T(8,128)(2,1)}, u32[]{:S(2)}, u32[]{:S(2)}) collective-permute-start(bf16[240,1280]{1,0:T(8,128)(2,1)} %dynamic-slice_bitcast_fusion.14), channel_id=1, source_target_pairs={{0,2},{1,3},{2,0},{3,1},{4,6},{5,7},{6,4},{7,5},{8,10},{9,11},{10,... | collective-permute-start | bytes 1843208 | tf_op jit(solution)/shard_map/ppermute | solution.py:549
  529.6 76.5 %collective-permute-start.45 = (bf16[480,640]{1,0:T(8,128)(2,1)S(1)}, bf16[480,640]{1,0:T(8,128)(2,1)S(1)}, u32[]{:S(2)}, u32[]{:S(2)}) collective-permute-start(bf16[480,640]{1,0:T(8,128)(2,1)S(1)} %maximum_select_fusion.4), channel_id=1, source_target_pairs={{0,1},{1,0},{2,3},{3,2},{4,5},{5,4},{6,7},{7,6},{8,9},{9,8},{10,11... | collective-permute-start | bytes 1843208 | tf_op jit(solution)/shard_map/ppermute | solution.py:554
  531.1 32.2 %copy-start.1 = (bf16[1024,1280]{1,0:T(8,128)(2,1)S(1)}, bf16[1024,1280]{1,0:T(8,128)(2,1)}, u32[]{:S(2)}) copy-start(bf16[1024,1280]{1,0:T(8,128)(2,1)} %input_side.3) | copy-start | bytes 7864324
  531.1 12.0 %collective-permute-start.51 = (bf16[240,640]{1,0:T(8,128)(2,1)S(1)}, bf16[240,640]{1,0:T(8,128)(2,1)S(1)}, u32[]{:S(2)}, u32[]{:S(2)}) collective-permute-start(bf16[240,640]{1,0:T(8,128)(2,1)S(1)} %dynamic-slice_bitcast_fusion.18), channel_id=1, source_target_pairs={{0,2},{1,3},{2,0},{3,1},{4,6},{5,7},{6,4},{7,5},{8,10},{9,11},{10,... | collective-permute-start | bytes 921608 | tf_op jit(solution)/shard_map/ppermute | solution.py:549
  536.1 17.6 %collective-permute-start.58 = (bf16[120,1280]{1,0:T(8,128)(2,1)S(1)}, bf16[120,1280]{1,0:T(8,128)(2,1)S(1)}, u32[]{:S(2)}, u32[]{:S(2)}) collective-permute-start(bf16[120,1280]{1,0:T(8,128)(2,1)S(1)} %dynamic-slice_bitcast_fusion.17), channel_id=1, source_target_pairs={{0,4},{1,5},{2,6},{3,7},{4,0},{5,1},{6,2},{7,3},{8,12},{9,13},{10,... | collective-permute-start | bytes 921608 | tf_op jit(solution)/shard_map/ppermute | solution.py:549
  543.3 16.6 %collective-permute-start.52 = (bf16[120,640]{1,0:T(8,128)(2,1)S(1)}, bf16[120,640]{1,0:T(8,128)(2,1)S(1)}, u32[]{:S(2)}, u32[]{:S(2)}) collective-permute-start(bf16[120,640]{1,0:T(8,128)(2,1)S(1)} %dynamic-slice_bitcast_fusion.20), channel_id=1, source_target_pairs={{0,4},{1,5},{2,6},{3,7},{4,0},{5,1},{6,2},{7,3},{8,12},{9,13},{10,... | collective-permute-start | bytes 460808 | tf_op jit(solution)/shard_map/ppermute | solution.py:549
  553.8 25.1 %collective-permute-start.59 = (bf16[120,1280]{1,0:T(8,128)(2,1)S(1)}, bf16[120,1280]{1,0:T(8,128)(2,1)S(1)}, u32[]{:S(2)}, u32[]{:S(2)}) collective-permute-start(bf16[120,1280]{1,0:T(8,128)(2,1)S(1)} %fusion.23), channel_id=1, source_target_pairs={{0,4},{1,5},{2,6},{3,7},{4,0},{5,1},{6,2},{7,3},{8,12},{9,13},{10,... | collective-permute-start | bytes 921608 | tf_op jit(solution)/shard_map/ppermute | solution.py:554
  559.9 15.2 %collective-permute-start.53 = (bf16[120,640]{1,0:T(8,128)(2,1)S(1)}, bf16[120,640]{1,0:T(8,128)(2,1)S(1)}, u32[]{:S(2)}, u32[]{:S(2)}) collective-permute-start(bf16[120,640]{1,0:T(8,128)(2,1)S(1)} %fusion.26), channel_id=1, source_target_pairs={{0,4},{1,5},{2,6},{3,7},{4,0},{5,1},{6,2},{7,3},{8,12},{9,13},{10,... | collective-permute-start | bytes 460808 | tf_op jit(solution)/shard_map/ppermute | solution.py:554
  566.4 12.4 %collective-permute-start.31 = (f32[5200]{0:T(1024)S(1)}, f32[5200]{0:T(1024)S(1)}, u32[]{:S(2)}, u32[]{:S(2)}) collective-permute-start(f32[5200]{0:T(1024)S(1)} %constant_dynamic-update-slice_fusion), channel_id=1, source_target_pairs={{0,8},{8,0},{16,24},{24,16},{1,9},{9,1},{17,25},{25,17},{2,10},{10... | collective-permute-start | bytes 62408 | tf_op jit(solution)/shard_map/ppermute | solution.py:568
  575.2 25.2 %collective-permute-start.54 = (bf16[240,640]{1,0:T(8,128)(2,1)S(1)}, bf16[240,640]{1,0:T(8,128)(2,1)S(1)}, u32[]{:S(2)}, u32[]{:S(2)}) collective-permute-start(bf16[240,640]{1,0:T(8,128)(2,1)S(1)} %maximum_select_fusion.8), channel_id=1, source_target_pairs={{0,2},{1,3},{2,0},{3,1},{4,6},{5,7},{6,4},{7,5},{8,10},{9,11},{10,... | collective-permute-start | bytes 921608 | tf_op jit(solution)/shard_map/ppermute | solution.py:554
  578.8 3.9 collective-permute-start.32
  579.1 21.6 %collective-permute-start.60 = (bf16[240,1280]{1,0:T(8,128)(2,1)S(1)}, bf16[240,1280]{1,0:T(8,128)(2,1)S(1)}, u32[]{:S(2)}, u32[]{:S(2)}) collective-permute-start(bf16[240,1280]{1,0:T(8,128)(2,1)S(1)} %maximum_select_fusion.6), channel_id=1, source_target_pairs={{0,2},{1,3},{2,0},{3,1},{4,6},{5,7},{6,4},{7,5},{8,10},{9,11},{10,... | collective-permute-start | bytes 1843208 | tf_op jit(solution)/shard_map/ppermute | solution.py:554
  582.7 3.8 collective-permute-start.33
  586.6 12.2 %collective-permute-start.34 = (f32[5200]{0:T(1024)S(1)}, f32[5200]{0:T(1024)S(1)}, u32[]{:S(2)}, u32[]{:S(2)}) collective-permute-start(f32[5200]{0:T(1024)S(1)} %add.573), channel_id=1, source_target_pairs={{0,2},{1,3},{2,0},{3,1},{4,6},{5,7},{6,4},{7,5},{8,10},{9,11},{10,... | collective-permute-start | bytes 62408 | tf_op jit(solution)/shard_map/ppermute | solution.py:573
  598.8 8.4 %collective-permute-start.35 = (f32[5200]{0:T(1024)S(1)}, f32[5200]{0:T(1024)S(1)}, u32[]{:S(2)}, u32[]{:S(2)}) collective-permute-start(f32[5200]{0:T(1024)S(1)} %add.574), channel_id=1, source_target_pairs={{0,4},{1,5},{2,6},{3,7},{4,0},{5,1},{6,2},{7,3},{8,12},{9,13},{10,... | collective-permute-start | bytes 62408 | tf_op jit(solution)/shard_map/ppermute | solution.py:573
  600.6 26.8 %collective-permute-start.55 = (bf16[480,640]{1,0:T(8,128)(2,1)S(1)}, bf16[480,640]{1,0:T(8,128)(2,1)S(1)}, u32[]{:S(2)}, u32[]{:S(2)}) collective-permute-start(bf16[480,640]{1,0:T(8,128)(2,1)S(1)} %maximum_select_fusion.5), channel_id=1, source_target_pairs={{0,1},{1,0},{2,3},{3,2},{4,5},{5,4},{6,7},{7,6},{8,9},{9,8},{10,11... | collective-permute-start | bytes 1843208 | tf_op jit(solution)/shard_map/ppermute | solution.py:554
  601.2 72.5 %collective-permute-start.61 = (bf16[480,1280]{1,0:T(8,128)(2,1)S(1)}, bf16[480,1280]{1,0:T(8,128)(2,1)}, u32[]{:S(2)}, u32[]{:S(2)}) collective-permute-start(bf16[480,1280]{1,0:T(8,128)(2,1)S(1)} %maximum_select_fusion.3), channel_id=1, source_target_pairs={{0,1},{1,0},{2,3},{3,2},{4,5},{5,4},{6,7},{7,6},{8,9},{9,8},{10,11... | collective-permute-start | bytes 3686408 | tf_op jit(solution)/shard_map/ppermute | solution.py:554
  604.5 45.1 %collective-permute-start.30 = (bf16[256,1280]{1,0:T(8,128)(2,1)}, bf16[256,1280]{1,0:T(8,128)(2,1)}, u32[]{:S(2)}, u32[]{:S(2)}) collective-permute-start(bf16[256,1280]{1,0:T(8,128)(2,1)} %get-tuple-element.119), channel_id=1, source_target_pairs={{6,0},{14,1},{0,2},{8,3},{2,4},{10,5},{4,6},{12,7},{7,8},{15,9},{1... | collective-permute-start | bytes 1966088 | tf_op jit(solution)/shard_map/ppermute | solution.py:612
  606.1 56.5 %collective-permute-start.29 = (bf16[256,1280]{1,0:T(8,128)(2,1)}, bf16[256,1280]{1,0:T(8,128)(2,1)}, u32[]{:S(2)}, u32[]{:S(2)}) collective-permute-start(bf16[256,1280]{1,0:T(8,128)(2,1)} %get-tuple-element.120), channel_id=1, source_target_pairs={{4,0},{12,1},{6,2},{14,3},{0,4},{8,5},{2,6},{10,7},{5,8},{13,9},{7... | collective-permute-start | bytes 1966088 | tf_op jit(solution)/shard_map/ppermute | solution.py:612
  607.2 56.5 %collective-permute-start.28 = (bf16[256,1280]{1,0:T(8,128)(2,1)}, bf16[256,1280]{1,0:T(8,128)(2,1)}, u32[]{:S(2)}, u32[]{:S(2)}) collective-permute-start(bf16[256,1280]{1,0:T(8,128)(2,1)} %get-tuple-element.121), channel_id=1, source_target_pairs={{2,0},{10,1},{4,2},{12,3},{6,4},{14,5},{0,6},{8,7},{3,8},{11,9},{5... | collective-permute-start | bytes 1966088 | tf_op jit(solution)/shard_map/ppermute | solution.py:612
  627.4 36.3 %collective-permute-start.27 = (bf16[256,1280]{1,0:T(8,128)(2,1)S(1)}, bf16[256,1280]{1,0:T(8,128)(2,1)}, u32[]{:S(2)}, u32[]{:S(2)}) collective-permute-start(bf16[256,1280]{1,0:T(8,128)(2,1)S(1)} %get-tuple-element.122), channel_id=1, source_target_pairs={{0,0},{8,1},{2,2},{10,3},{4,4},{12,5},{6,6},{14,7},{1,8},{9,9},{3,... | collective-permute-start | bytes 1966088 | tf_op jit(solution)/shard_map/ppermute | solution.py:612
  (55 other events, 525.1 us)

commit v3 on v2

--- a/solution.py
+++ b/solution.py
@@ -530,7 +530,9 @@
         out_specs=pl.BlockSpec((block, width), lambda i: (i, 0)),
         out_shape=jax.ShapeDtypeStruct((tokens, width), bf16),
         compiler_params=pltpu.CompilerParams(vmem_limit_bytes=56 << 20),
-        cost_estimate=brief,
+        cost_estimate=pl.CostEstimate(
+            flops=4 * tokens * width * wide, bytes_accessed=1, transcendentals=0
+        ),
         name="input_side",
     )(*grads, w)
 
@@ -600,12 +602,16 @@
     wide = local_heads * 3 * head_size
     own = seqs * span
 
-    def spread(array):
+    def spread(array, *near):
         out = []
         for step in range(seqs):
-            block = lax.dynamic_index_in_dim(array, (group + step) % seqs, 0, keepdims=False)
+            source = after(array, *near) if near and step < seqs // 2 else array
+            block = lax.dynamic_index_in_dim(source, (group + step) % seqs, 0, keepdims=False)
             out.append(lax.ppermute(block, axes, team.spread(step)))
-        return join(out, [jnp.int32(k) for k in range(seqs)]).reshape(own, width)
+        return out
+
+    def spread_done(pieces):
+        return join(pieces, [jnp.int32(k) for k in range(seqs)]).reshape(own, width)
 
     def unspread(array):
         return [
@@ -634,7 +640,7 @@
         lax.ppermute(parts[flip], "dp", team.turn_rows(step, flip)) for step, flip in shifts[2:]
     ]
     near = lax.ppermute(parts[1], "dp", team.swap_core())
-    x_own = spread(after(activations, *parts))
+    x_own = spread_done(spread(after(activations, *parts), near))
     other_ids = lax.ppermute(segment_ids, "dp", team.swap_core())
     w_half, small = join(
         [parts[0], near] + far,
@@ -678,6 +684,8 @@
     qkv, normed_in = project_qkv(
         xs, gain_in, w_half, factor_row, local_heads, head_size, team.dp, span
     )
+    early = seqs // 2
+    qkv, cot_own[early:] = after((qkv, cot_own[early:]), *cot_own[early:])
     att, lse = attend(table, qkv, starts)
     three = after(three, att)
     swapped = [lax.ppermute(piece, "dp", team.swap_core()) for piece in three]
@@ -708,7 +716,7 @@
     activated = jax.nn.silu(pre_act).astype(bf16)
     result_own = (mid + mm(activated, w_down_all) + bias_down).astype(bf16)
     result = unspread(result_own)
-    cot_own = after(cot_own, result_own)
+    cot_own = spread_done(after(cot_own, result_own))
 
     grad_bias_down = jnp.sum(cot_own.astype(f32), axis=0)
     tn = (((0,), (0,)), ((), ()))
@@ -799,6 +807,7 @@
         input_side(chunks, w_half, span, j * blocks, blocks) for j in range(1, size)
     ]
     chunks = after(chunks, *partial)
+    heads_of = after(heads_of, *partial)
     grad_normed_in = sum(
         [
             lax.ppermute(p, axes, team.rotate(j + 1)).astype(f32)

time: 689 us -> 637 us (0.925)
  the two profiles are of different devices: /device:TPU:12 before, /device:TPU:1 now
where the time goes in v3:
time: 637 us; the launch traced here: 626 us
  Pallas kernels  187 us (29%)
  waiting for transfers between devices  150 us (24%)
  starting transfers between devices  145 us (23%)
  matrix products  50.9 us (8%)
  other arithmetic  47.9 us (8%)
  local copies, waits for them, and re-layouts  42.1 us (7%)
    pallas_call x2, Pallas kernels, attend_back(): pl.pallas_call(functools.partial(attend_back_kernel, count, block, pair),...  57 us
    ppermute x9, starting transfers between devices, reduce_places(): got = lax.ppermute(send, 'seq', [(i, i ^ 1 << b) for i in range(places)])  56.9 us
    ppermute x8, starting transfers between devices, unspread(): lax.ppermute(array[step * span:(step + 1) * span], axes, team.back(step))  47 us
    dot_general x8, matrix products, mm(): return lax.dot_general(a, b, dims, preferred_element_type=f32)  44.7 us
    ppermute x2, waiting for transfers between devices, on_device(): lax.ppermute(parts[flip], 'dp', team.turn_rows(step, flip))  39.3 us
    pallas_call x7, Pallas kernels, join(): pl.pallas_call(functools.partial(join_kernel, count, ends), grid_spec=plt...  33.4 us
    pallas_call x1, Pallas kernels, attend(): pl.pallas_call(functools.partial(attend_kernel, count, block, pair), grid...  27.5 us
    ppermute x9, waiting for transfers between devices, reduce_places(): got = lax.ppermute(send, 'seq', [(i, i ^ 1 << b) for i in range(places)])  27.2 us
  transfers between devices with their start and end apart: 62, of which 15 were waited for; matrix products, arithmetic and copies ran while one was open for 14% of the time, Pallas kernels for 29%

profile of v3, /device:TPU:1, one launch (start us, length us, event | category | flops | bytes accessed | tf_op | source)
XLA Modules:
  0.0 625.8 jit_solution(6082118505239968227)
XLA Ops:
  0.7 2.8 concatenate.90
  9.8 2.5 pad_maximum_fusion.4
  12.4 2.7 collective-permute-start.8
  15.5 2.5 dynamic-slice_bitcast_fusion.10
  18.0 4.7 collective-permute-start.4
  27.1 17.3 %collective-permute-done.8.refs_3_ = bf16[336,1920]{1,0:T(8,128)(2,1)} collective-permute-done((bf16[336,1920]{1,0:T(8,128)(2,1)}, bf16[336,1920]{1,0:T(8,128)(2,1)}, u32[]{:S(2)}, u32[]{:S(2)}) %collective-permute-start.8) | collective-permute-done | bytes 1290272 | tf_op jit(solution)/shard_map/ppermute | solution.py:640
  44.4 3.1 collective-permute-start.1
  49.8 21.9 %collective-permute-done.7.refs_2_ = bf16[336,1920]{1,0:T(8,128)(2,1)} collective-permute-done((bf16[336,1920]{1,0:T(8,128)(2,1)S(1)}, bf16[336,1920]{1,0:T(8,128)(2,1)}, u32[]{:S(2)}, u32[]{:S(2)}) %collective-permute-start.7) | collective-permute-done | bytes 1290272 | tf_op jit(solution)/shard_map/ppermute | solution.py:640
  72.7 6.2 collective-permute-done.3.refs_2_
  80.2 3.5 join.7
  84.0 4.1 convert_reduce_fusion
  88.6 2.7 convert_element_type.313
  92.7 4.2 collective-permute-start.9
  97.5 6.4 %join.8 = (bf16[4,320,1920]{2,1,0:T(8,128)(2,1)}, bf16[4,16,1920]{2,1,0:T(8,128)(2,1)}) custom-call(s32[4]{0:T(128)} %add_add_fusion.slots_ref, bf16[336,1920]{1,0:T(8,128)(2,1)} %copy-done.7, bf16[336,1920]{1,0:T(8,128)(2,1)} %copy-done.17, bf16[336,1920]{1,0:T(8,128)(2,1)} %collective-permute-done.7.refs_2_, bf16[336,1920]{1,0:T(8,128)(2,1)} %collective-permute-done.8.refs_3_), custom_call_target="tpu_custom_call" | custom-call | flops 1 | bytes 1 | tf_op jit(solution)/shard_map/join/pallas_call | solution.py:116
  107.3 19.7 %qkv.1 = (bf16[8,3,2048,80]{3,2,1,0:T(8,128)(2,1)}, bf16[2,2048,640]{2,1,0:T(8,128)(2,1)}) custom-call(bf16[1024,1280]{1,0:T(8,128)(2,1)} %bitcast.199, bf16[1024,1280]{1,0:T(8,128)(2,1)} %copy-done.15, f32[1,1280]{1,0:T(1,128)} %slice.77.refs_2_, bf16[1280,1920]{1,0:T(8,128)(2,1)} %bitcast.212, f32[1,1920]{1,0:T(1,128)} %broadcast_in_dim_tile.3.refs_4_), custom_call_target="tpu_custom_call" | custom-call | flops 1 | bytes 1 | tf_op jit(solution)/shard_map/qkv/pallas_call | solution.py:163
  126.9 13.4 %collective-permute-done.9.refs_2_ = bf16[256,1280]{1,0:T(8,128)(2,1)} collective-permute-done((bf16[256,1280]{1,0:T(8,128)(2,1)}, bf16[256,1280]{1,0:T(8,128)(2,1)}, u32[]{:S(2)}, u32[]{:S(2)}) %collective-permute-start.9) | collective-permute-done | bytes 655392 | tf_op jit(solution)/shard_map/ppermute | solution.py:610
  140.3 27.5 %attend.1 = (bf16[640,2048]{1,0:T(8,128)(2,1)}, f32[8,1,2048]{2,1,0:T(1,128)}) custom-call(s32[5,8]{1,0:T(8,128)} %stack.81.table, bf16[8,3,2048,80]{3,2,1,0:T(8,128)(2,1)} %get-tuple-element.72.qkv_ref, s32[8,256]{1,0:T(8,128)} %copy-done.35), custom_call_target="tpu_custom_call" | custom-call | flops 1 | bytes 1 | tf_op jit(solution)/shard_map/attend/pallas_call | solution.py:357
  168.3 3.0 fusion.39
  174.8 3.3 collective-permute-done.11.refs_1_
  179.2 3.5 join.9
  182.7 7.9 %join.10 = (bf16[4,320,1280]{2,1,0:T(8,128)(2,1)}, bf16[4,320,1280]{2,1,0:T(8,128)(2,1)}, bf16[4,320,1280]{2,1,0:T(8,128)(2,1)}) custom-call(s32[4]{0:T(128)} %add_add_fusion.1.slots_ref, bf16[960,1280]{1,0:T(8,128)(2,1)} %pad_maximum_fusion.1.refs_0_, bf16[960,1280]{1,0:T(8,128)(2,1)} %collective-permute-done.12.refs_1_, ...), custom_call_target="tpu_custom_call" | custom-call | flops 1 | bytes 1 | tf_op jit(solution)/shard_map/join/pallas_call | solution.py:116
  190.6 6.3 %multiply_reduce_fusion.3 = (f32[1024]{0:T(1024)S(1)}, f32[1024,1280]{1,0:T(8,128)S(1)}) fusion(bf16[1280,1024]{1,0:T(8,128)(2,1)S(1)} %bitcast.207, bf16[1280,1280]{1,0:T(8,128)(2,1)} %bitcast.221, bf16[1024,1280]{1,0:T(8,128)(2,1)S(1)} %bitcast.200), kind=kOutput, calls=%fused_computation.30 | convolution fusion | flops 3360685056 | bytes 13766656 | tf_op jit(solution)/shard_map/dot_general | solution.py:710
  197.0 3.7 fusion.35
  200.8 5.7 add_convert_fusion
  207.9 3.9 join.11
  211.8 10.4 %convert_reduce_fusion.3 = (f32[1280]{0:T(1024)S(1)}, bf16[1024,1280]{1,0:T(8,128)(2,1)}) fusion(f32[1024,1280]{1,0:T(8,128)} %copy-done.47, f32[1280]{0:T(1024)S(1)} %add.541, bf16[1024,1280]{1,0:T(8,128)(2,1)} %bitcast.201, bf16[1280,1280]{1,0:T(8,128)(2,1)} %bitcast.249), kind=kOutput, calls=%fused_computation.19 | convolution fusion | flops 3371170560 | bytes 13772800 | tf_op jit(solution)/shard_map/dot_general | solution.py:25
  222.2 4.0 convolution_convert_fusion.2
  226.3 6.9 %multiply_reduce_fusion = (f32[1280]{0:T(1024)S(1)}, f32[1024]{0:T(1024)S(1)}, f32[1024,1280]{1,0:T(8,128)S(1)}) fusion(f32[1024,1280]{1,0:T(8,128)S(1)} %bitcast.204, f32[1024]{0:T(1024)S(1)} %add_rsqrt_fusion, f32[1280]{0:T(1024)S(1)} %mul.203, bf16[1024,1280]{1,0:T(8,128)(2,1)} %get-tuple-element.177, bf16[1280,1280]{1,0:T(8,128)(2,1)S(1)} %bitcast.248), kind=kOutput, calls=%fused_computation.20 | convolution fusion | flops 3363305216 | bytes 16402432 | tf_op jit(solution)/shard_map/dot_general | solution.py:25
  233.2 5.8 convolution_convert_fusion.1
  242.5 4.2 convolution_convert_fusion
  248.7 3.9 convolution_convert_fusion.3
  263.7 2.7 collective-permute-start.17
  271.5 3.5 pad_maximum_fusion.grad_ref
  275.0 28.3 %attend_back.2 = (bf16[960,2048]{1,0:T(8,128)(2,1)}, f32[80,1]{1,0:T(8,128)}) custom-call(s32[5,8]{1,0:T(8,128)} %stack.81.table, bf16[8,3,2048,80]{3,2,1,0:T(8,128)(2,1)} %get-tuple-element.72.qkv_ref, bf16[640,2048]{1,0:T(8,128)(2,1)} %get-tuple-element.73.att_ref, bf16[640,2048]{1,0:T(8,128)(2,1)} %pad_maximum_fusion.grad_ref, ...), custom_call_target="tpu_custom_call" | custom-call | flops 1 | bytes 1 | tf_op jit(solution)/shard_map/attend_back/pallas_call | solution.py:479
  303.3 6.6 %collective-permute-done.17.refs_2_ = bf16[256,1280]{1,0:T(8,128)(2,1)} collective-permute-done((bf16[256,1280]{1,0:T(8,128)(2,1)}, bf16[256,1280]{1,0:T(8,128)(2,1)}, u32[]{:S(2)}, u32[]{:S(2)}) %collective-permute-start.17) | collective-permute-done | bytes 655392 | tf_op jit(solution)/shard_map/ppermute | solution.py:618
  309.9 12.2 %head_grad.2 = (bf16[480,640]{1,0:T(8,128)(2,1)}, bf16[480,640]{1,0:T(8,128)(2,1)}, bf16[480,640]{1,0:T(8,128)(2,1)}, bf16[480,640]{1,0:T(8,128)(2,1)}) custom-call(s32[3]{0:T(128)} %pad_add_fusion.2.place_ref, bf16[960,2048]{1,0:T(8,128)(2,1)} %get-tuple-element.109.grads_ref.refs_0_, bf16[2,2048,640]{2,1,0:T(8,128)(2,1)} %get-tuple-element.94.normed_ref), custom_call_target="tpu_custom_call" | custom-call | flops 1 | bytes 1 | tf_op jit(solution)/shard_map/head_grad/pallas_call | solution.py:209
  325.9 28.7 %attend_back.3 = (bf16[960,2048]{1,0:T(8,128)(2,1)}, f32[80,1]{1,0:T(8,128)}) custom-call(s32[5,8]{1,0:T(8,128)} %stack.81.table, bf16[8,3,2048,80]{3,2,1,0:T(8,128)(2,1)} %get-tuple-element.72.qkv_ref, bf16[640,2048]{1,0:T(8,128)(2,1)} %get-tuple-element.73.att_ref, bf16[640,2048]{1,0:T(8,128)(2,1)} %pad_maximum_fusion.grad_ref, ...), custom_call_target="tpu_custom_call" | custom-call | flops 1 | bytes 1 | tf_op jit(solution)/shard_map/attend_back/pallas_call | solution.py:479
  359.0 12.2 %head_grad.3 = (bf16[480,640]{1,0:T(8,128)(2,1)}, bf16[480,640]{1,0:T(8,128)(2,1)}, bf16[480,640]{1,0:T(8,128)(2,1)}, bf16[480,640]{1,0:T(8,128)(2,1)}) custom-call(s32[3]{0:T(128)} %pad_add_fusion.2.place_ref, bf16[960,2048]{1,0:T(8,128)(2,1)} %get-tuple-element.110.grads_ref.refs_1_, bf16[2,2048,640]{2,1,0:T(8,128)(2,1)} %get-tuple-element.94.normed_ref), custom_call_target="tpu_custom_call" | custom-call | flops 1 | bytes 1 | tf_op jit(solution)/shard_map/head_grad/pallas_call | solution.py:209
  371.6 9.9 %input_side.2 = bf16[1024,1280]{1,0:T(8,128)(2,1)} custom-call(bf16[960,2048]{1,0:T(8,128)(2,1)} %get-tuple-element.109.grads_ref.refs_0_, bf16[960,2048]{1,0:T(8,128)(2,1)} %get-tuple-element.110.grads_ref.refs_1_, bf16[1280,1920]{1,0:T(8,128)(2,1)} %bitcast.213), custom_call_target="tpu_custom_call" | custom-call | flops 10066329600 | bytes 1 | tf_op jit(solution)/shard_map/input_side/pallas_call | solution.py:525
  381.5 10.0 %input_side.3 = bf16[1024,1280]{1,0:T(8,128)(2,1)} custom-call(bf16[960,2048]{1,0:T(8,128)(2,1)} %get-tuple-element.109.grads_ref.refs_0_, bf16[960,2048]{1,0:T(8,128)(2,1)} %get-tuple-element.110.grads_ref.refs_1_, bf16[1280,1920]{1,0:T(8,128)(2,1)} %bitcast.214), custom_call_target="tpu_custom_call" | custom-call | flops 10066329600 | bytes 1 | tf_op jit(solution)/shard_map/input_side/pallas_call | solution.py:525
  396.8 14.8 %collective-permute-start.57 = (bf16[240,1280]{1,0:T(8,128)(2,1)S(1)}, bf16[240,1280]{1,0:T(8,128)(2,1)S(1)}, u32[]{:S(2)}, u32[]{:S(2)}) collective-permute-start(bf16[240,1280]{1,0:T(8,128)(2,1)S(1)} %dynamic-slice_bitcast_fusion.14), channel_id=1, source_target_pairs={{0,2},{1,3},{2,0},{3,1},{4,6},{5,7},{6,4},{7,5},{8,10},{9,11},{10,... | collective-permute-start | bytes 1843208 | tf_op jit(solution)/shard_map/ppermute | solution.py:551
  411.7 8.6 %collective-permute-done.43 = bf16[480,640]{1,0:T(8,128)(2,1)S(1)} collective-permute-done((bf16[480,640]{1,0:T(8,128)(2,1)}, bf16[480,640]{1,0:T(8,128)(2,1)S(1)}, u32[]{:S(2)}, u32[]{:S(2)}) %collective-permute-start.43) | collective-permute-done | bytes 614432 | tf_op jit(solution)/shard_map/ppermute | solution.py:796
  426.2 13.0 %collective-permute-start.58 = (bf16[120,1280]{1,0:T(8,128)(2,1)S(1)}, bf16[120,1280]{1,0:T(8,128)(2,1)S(1)}, u32[]{:S(2)}, u32[]{:S(2)}) collective-permute-start(bf16[120,1280]{1,0:T(8,128)(2,1)S(1)} %dynamic-slice_bitcast_fusion.17), channel_id=1, source_target_pairs={{0,4},{1,5},{2,6},{3,7},{4,0},{5,1},{6,2},{7,3},{8,12},{9,13},{10,... | collective-permute-start | bytes 921608 | tf_op jit(solution)/shard_map/ppermute | solution.py:551
  439.4 10.3 %collective-permute-start.51 = (bf16[240,640]{1,0:T(8,128)(2,1)S(1)}, bf16[240,640]{1,0:T(8,128)(2,1)S(1)}, u32[]{:S(2)}, u32[]{:S(2)}) collective-permute-start(bf16[240,640]{1,0:T(8,128)(2,1)S(1)} %dynamic-slice_bitcast_fusion.18), channel_id=1, source_target_pairs={{0,2},{1,3},{2,0},{3,1},{4,6},{5,7},{6,4},{7,5},{8,10},{9,11},{10,... | collective-permute-start | bytes 921608 | tf_op jit(solution)/shard_map/ppermute | solution.py:551
  449.8 13.0 %collective-permute-start.45 = (bf16[240,640]{1,0:T(8,128)(2,1)S(1)}, bf16[240,640]{1,0:T(8,128)(2,1)S(1)}, u32[]{:S(2)}, u32[]{:S(2)}) collective-permute-start(bf16[240,640]{1,0:T(8,128)(2,1)S(1)} %dynamic-slice_bitcast_fusion.19), channel_id=1, source_target_pairs={{0,2},{1,3},{2,0},{3,1},{4,6},{5,7},{6,4},{7,5},{8,10},{9,11},{10,... | collective-permute-start | bytes 921608 | tf_op jit(solution)/shard_map/ppermute | solution.py:551
  463.1 2.4 collective-permute-start.52
  465.5 6.5 %collective-permute-done.45 = bf16[240,640]{1,0:T(8,128)(2,1)S(1)} collective-permute-done((bf16[240,640]{1,0:T(8,128)(2,1)S(1)}, bf16[240,640]{1,0:T(8,128)(2,1)S(1)}, u32[]{:S(2)}, u32[]{:S(2)}) %collective-permute-start.45) | collective-permute-done | bytes 307232 | tf_op jit(solution)/shard_map/ppermute | solution.py:551
  473.1 14.2 %collective-permute-done.52 = bf16[120,640]{1,0:T(8,128)(2,1)S(1)} collective-permute-done((bf16[120,640]{1,0:T(8,128)(2,1)S(1)}, bf16[120,640]{1,0:T(8,128)(2,1)S(1)}, u32[]{:S(2)}, u32[]{:S(2)}) %collective-permute-start.52) | collective-permute-done | bytes 153632 | tf_op jit(solution)/shard_map/ppermute | solution.py:551
  487.4 6.5 %collective-permute-done.46 = bf16[120,640]{1,0:T(8,128)(2,1)S(1)} collective-permute-done((bf16[120,640]{1,0:T(8,128)(2,1)S(1)}, bf16[120,640]{1,0:T(8,128)(2,1)S(1)}, u32[]{:S(2)}, u32[]{:S(2)}) %collective-permute-start.46) | collective-permute-done | bytes 153632 | tf_op jit(solution)/shard_map/ppermute | solution.py:551
  494.2 2.9 fusion.8
  497.2 8.4 %collective-permute-start.31 = (f32[5200]{0:T(1024)S(1)}, f32[5200]{0:T(1024)S(1)}, u32[]{:S(2)}, u32[]{:S(2)}) collective-permute-start(f32[5200]{0:T(1024)S(1)} %constant_dynamic-update-slice_fusion), channel_id=1, source_target_pairs={{0,8},{8,0},{16,24},{24,16},{1,9},{9,1},{17,25},{25,17},{2,10},{10... | collective-permute-start | bytes 62408 | tf_op jit(solution)/shard_map/ppermute | solution.py:570
  510.5 3.0 collective-permute-done.33
  514.1 2.4 fusion.5
  516.5 10.9 %collective-permute-done.34 = f32[5200]{0:T(1024)S(1)} collective-permute-done((f32[5200]{0:T(1024)S(1)}, f32[5200]{0:T(1024)S(1)}, u32[]{:S(2)}, u32[]{:S(2)}) %collective-permute-start.34) | collective-permute-done | bytes 20832 | tf_op jit(solution)/shard_map/ppermute | solution.py:575
  531.3 4.9 collective-permute-start.30
  536.2 3.4 collective-permute-start.29
  539.6 16.1 %collective-permute-start.28 = (bf16[256,1280]{1,0:T(8,128)(2,1)}, bf16[256,1280]{1,0:T(8,128)(2,1)}, u32[]{:S(2)}, u32[]{:S(2)}) collective-permute-start(bf16[256,1280]{1,0:T(8,128)(2,1)} %get-tuple-element.149), channel_id=1, source_target_pairs={{2,0},{10,1},{4,2},{12,3},{6,4},{14,5},{0,6},{8,7},{3,8},{11,9},{5... | collective-permute-start | bytes 1966088 | tf_op jit(solution)/shard_map/ppermute | solution.py:618
  555.7 11.5 %collective-permute-done.49 = bf16[480,640]{1,0:T(8,128)(2,1)S(1)} collective-permute-done((bf16[480,640]{1,0:T(8,128)(2,1)S(1)}, bf16[480,640]{1,0:T(8,128)(2,1)S(1)}, u32[]{:S(2)}, u32[]{:S(2)}) %collective-permute-start.49) | collective-permute-done | bytes 614432 | tf_op jit(solution)/shard_map/ppermute | solution.py:556
  567.3 16.2 %collective-permute-start.27 = (bf16[256,1280]{1,0:T(8,128)(2,1)S(1)}, bf16[256,1280]{1,0:T(8,128)(2,1)}, u32[]{:S(2)}, u32[]{:S(2)}) collective-permute-start(bf16[256,1280]{1,0:T(8,128)(2,1)S(1)} %get-tuple-element.150), channel_id=1, source_target_pairs={{0,0},{8,1},{2,2},{10,3},{4,4},{12,5},{6,6},{14,7},{1,8},{9,9},{3,... | collective-permute-start | bytes 1966088 | tf_op jit(solution)/shard_map/ppermute | solution.py:618
  584.2 3.7 join.12
  592.1 18.9 %collective-permute-done.27.refs_0_ = bf16[256,1280]{1,0:T(8,128)(2,1)} collective-permute-done((bf16[256,1280]{1,0:T(8,128)(2,1)S(1)}, bf16[256,1280]{1,0:T(8,128)(2,1)}, u32[]{:S(2)}, u32[]{:S(2)}) %collective-permute-start.27) | collective-permute-done | bytes 655392 | tf_op jit(solution)/shard_map/ppermute | solution.py:618
  611.0 4.5 join.13
  615.5 5.4 unfold.1
  623.0 2.4 fusion.36
  (312 shorter events, 87.9 us)
Async XLA Ops:
  12.4 11.6 %collective-permute-start = (bf16[336,1920]{1,0:T(8,128)(2,1)}, bf16[336,1920]{1,0:T(8,128)(2,1)S(1)}, u32[]{:S(2)}, u32[]{:S(2)}) collective-permute-start(bf16[336,1920]{1,0:T(8,128)(2,1)} %get-tuple-element.167), channel_id=1, source_target_pairs={{0,8},{8,0},{16,24},{24,16},{1,9},{9,1},{17,25},{25,17},{2,10},{10... | collective-permute-start | bytes 3870728 | tf_op jit(solution)/shard_map/ppermute | solution.py:642
  12.4 32.1 %collective-permute-start.8 = (bf16[336,1920]{1,0:T(8,128)(2,1)}, bf16[336,1920]{1,0:T(8,128)(2,1)}, u32[]{:S(2)}, u32[]{:S(2)}) collective-permute-start(bf16[336,1920]{1,0:T(8,128)(2,1)} %get-tuple-element.167), channel_id=1, source_target_pairs={{0,24},{8,16},{16,8},{24,0},{1,25},{9,17},{17,9},{25,1},{2,26},{10... | collective-permute-start | bytes 3870728 | tf_op jit(solution)/shard_map/ppermute | solution.py:640
  15.0 10.9 %collective-permute-start.5 = (s32[4,2048]{1,0:T(4,128)S(1)}, s32[4,2048]{1,0:T(4,128)S(1)}, u32[]{:S(2)}, u32[]{:S(2)}) collective-permute-start(s32[4,2048]{1,0:T(4,128)S(1)} %copy-done.37), channel_id=1, source_target_pairs={{0,8},{8,0},{16,24},{24,16},{1,9},{9,1},{17,25},{25,17},{2,10},{10... | collective-permute-start | bytes 98312 | tf_op jit(solution)/shard_map/ppermute | solution.py:644
  15.5 56.2 %collective-permute-start.7 = (bf16[336,1920]{1,0:T(8,128)(2,1)S(1)}, bf16[336,1920]{1,0:T(8,128)(2,1)}, u32[]{:S(2)}, u32[]{:S(2)}) collective-permute-start(bf16[336,1920]{1,0:T(8,128)(2,1)S(1)} %get-tuple-element.168.refs_0_), channel_id=1, source_target_pairs={{0,16},{8,24},{16,0},{24,8},{1,17},{9,25},{17,1},{25,9},{2,18},{10... | collective-permute-start | bytes 3870728 | tf_op jit(solution)/shard_map/ppermute | solution.py:640
  18.0 54.7 %collective-permute-start.4 = (bf16[256,1280]{1,0:T(8,128)(2,1)}, bf16[256,1280]{1,0:T(8,128)(2,1)}, u32[]{:S(2)}, u32[]{:S(2)}) collective-permute-start(bf16[256,1280]{1,0:T(8,128)(2,1)} %get-tuple-element.163), channel_id=1, source_target_pairs={{0,6},{1,14},{2,0},{3,8},{4,2},{5,10},{6,4},{7,12},{8,7},{9,15},{1... | collective-permute-start | bytes 1966088 | tf_op jit(solution)/shard_map/ppermute | solution.py:610
  24.0 55.0 %collective-permute-start.3 = (bf16[256,1280]{1,0:T(8,128)(2,1)}, bf16[256,1280]{1,0:T(8,128)(2,1)S(1)}, u32[]{:S(2)}, u32[]{:S(2)}) collective-permute-start(bf16[256,1280]{1,0:T(8,128)(2,1)} %get-tuple-element.164), channel_id=1, source_target_pairs={{0,4},{1,12},{2,6},{3,14},{4,0},{5,8},{6,2},{7,10},{8,5},{9,13},{1... | collective-permute-start | bytes 1966088 | tf_op jit(solution)/shard_map/ppermute | solution.py:610
  26.0 53.0 %collective-permute-start.2 = (bf16[256,1280]{1,0:T(8,128)(2,1)S(1)}, bf16[256,1280]{1,0:T(8,128)(2,1)S(1)}, u32[]{:S(2)}, u32[]{:S(2)}) collective-permute-start(bf16[256,1280]{1,0:T(8,128)(2,1)S(1)} %get-tuple-element.165), channel_id=1, source_target_pairs={{0,2},{1,10},{2,4},{3,12},{4,6},{5,14},{6,0},{7,8},{8,3},{9,11},{1... | collective-permute-start | bytes 1966088 | tf_op jit(solution)/shard_map/ppermute | solution.py:610
  44.4 34.5 %collective-permute-start.1 = (bf16[256,1280]{1,0:T(8,128)(2,1)S(1)}, bf16[256,1280]{1,0:T(8,128)(2,1)S(1)}, u32[]{:S(2)}, u32[]{:S(2)}) collective-permute-start(bf16[256,1280]{1,0:T(8,128)(2,1)S(1)} %get-tuple-element.166), channel_id=1, source_target_pairs={{0,0},{1,8},{2,2},{3,10},{4,4},{5,12},{6,6},{7,14},{8,1},{9,9},{10... | collective-permute-start | bytes 1966088 | tf_op jit(solution)/shard_map/ppermute | solution.py:610
  71.7 96.1 %collective-permute-start.12 = (bf16[960,1280]{1,0:T(8,128)(2,1)}, bf16[960,1280]{1,0:T(8,128)(2,1)}, u32[]{:S(2)}, u32[]{:S(2)}) collective-permute-start(bf16[960,1280]{1,0:T(8,128)(2,1)} %pad_maximum_fusion.1.refs_0_), channel_id=1, source_target_pairs={{0,16},{8,24},{16,0},{24,8},{1,17},{9,25},{17,1},{25,9},{2,18},{10... | collective-permute-start | bytes 7372808 | tf_op jit(solution)/shard_map/ppermute | solution.py:657
  83.8 22.0 %collective-permute-start.6 = (bf16[1024,1280]{1,0:T(8,128)(2,1)}, bf16[1024,1280]{1,0:T(8,128)(2,1)S(1)}, u32[]{:S(2)}, u32[]{:S(2)}) collective-permute-start(bf16[1024,1280]{1,0:T(8,128)(2,1)} %bitcast.198), channel_id=1, source_target_pairs={{0,8},{1,9},{2,10},{3,11},{4,12},{5,13},{6,14},{7,15},{8,0},{9,1},... | collective-permute-start | bytes 7864328 | tf_op jit(solution)/shard_map/ppermute | solution.py:654
  92.6 34.3 %collective-permute-start.10 = (bf16[256,1280]{1,0:T(8,128)(2,1)}, bf16[256,1280]{1,0:T(8,128)(2,1)}, u32[]{:S(2)}, u32[]{:S(2)}) collective-permute-start(bf16[256,1280]{1,0:T(8,128)(2,1)} %get-tuple-element.155), channel_id=1, source_target_pairs={{0,6},{1,14},{2,0},{3,8},{4,2},{5,10},{6,4},{7,12},{8,7},{9,15},{1... | collective-permute-start | bytes 1966088 | tf_op jit(solution)/shard_map/ppermute | solution.py:610
  92.7 47.7 %collective-permute-start.9 = (bf16[256,1280]{1,0:T(8,128)(2,1)}, bf16[256,1280]{1,0:T(8,128)(2,1)}, u32[]{:S(2)}, u32[]{:S(2)}) collective-permute-start(bf16[256,1280]{1,0:T(8,128)(2,1)} %get-tuple-element.156), channel_id=1, source_target_pairs={{0,4},{1,12},{2,6},{3,14},{4,0},{5,8},{6,2},{7,10},{8,5},{9,13},{1... | collective-permute-start | bytes 1966088 | tf_op jit(solution)/shard_map/ppermute | solution.py:610
  167.8 14.9 %collective-permute-start.13 = (bf16[960,1280]{1,0:T(8,128)(2,1)}, bf16[960,1280]{1,0:T(8,128)(2,1)}, u32[]{:S(2)}, u32[]{:S(2)}) collective-permute-start(bf16[960,1280]{1,0:T(8,128)(2,1)} %pad_maximum_fusion.1.refs_0_), channel_id=1, source_target_pairs={{0,8},{8,0},{16,24},{24,16},{1,9},{9,1},{17,25},{25,17},{2,10},{10... | collective-permute-start | bytes 7372808 | tf_op jit(solution)/shard_map/ppermute | solution.py:691
  167.8 14.9 %collective-permute-start.14 = (bf16[960,1280]{1,0:T(8,128)(2,1)}, bf16[960,1280]{1,0:T(8,128)(2,1)}, u32[]{:S(2)}, u32[]{:S(2)}) collective-permute-start(bf16[960,1280]{1,0:T(8,128)(2,1)} %collective-permute-done.12.refs_1_), channel_id=1, source_target_pairs={{0,8},{8,0},{16,24},{24,16},{1,9},{9,1},{17,25},{25,17},{2,10},{10... | collective-permute-start | bytes 7372808 | tf_op jit(solution)/shard_map/ppermute | solution.py:691
  171.4 6.8 %collective-permute-start.11 = (bf16[640,1024]{1,0:T(8,128)(2,1)S(1)}, bf16[640,1024]{1,0:T(8,128)(2,1)S(1)}, u32[]{:S(2)}, u32[]{:S(2)}) collective-permute-start(bf16[640,1024]{1,0:T(8,128)(2,1)S(1)} %get-tuple-element.161), channel_id=1, source_target_pairs={{0,8},{1,9},{2,10},{3,11},{4,12},{5,13},{6,14},{7,15},{8,0},{9,1},... | collective-permute-start | bytes 3932168 | tf_op jit(solution)/shard_map/ppermute | solution.py:704
  172.9 33.6 %collective-permute-start.20 = (bf16[256,1280]{1,0:T(8,128)(2,1)}, bf16[256,1280]{1,0:T(8,128)(2,1)S(1)}, u32[]{:S(2)}, u32[]{:S(2)}) collective-permute-start(bf16[256,1280]{1,0:T(8,128)(2,1)} %get-tuple-element.153), channel_id=1, source_target_pairs={{0,2},{1,10},{2,4},{3,12},{4,6},{5,14},{6,0},{7,8},{8,3},{9,11},{1... | collective-permute-start | bytes 1966088 | tf_op jit(solution)/shard_map/ppermute | solution.py:610
  172.9 33.6 %collective-permute-start.19 = (bf16[256,1280]{1,0:T(8,128)(2,1)S(1)}, bf16[256,1280]{1,0:T(8,128)(2,1)S(1)}, u32[]{:S(2)}, u32[]{:S(2)}) collective-permute-start(bf16[256,1280]{1,0:T(8,128)(2,1)S(1)} %get-tuple-element.154), channel_id=1, source_target_pairs={{0,0},{1,8},{2,2},{3,10},{4,4},{5,12},{6,6},{7,14},{8,1},{9,9},{10... | collective-permute-start | bytes 1966088 | tf_op jit(solution)/shard_map/ppermute | solution.py:610
  240.3 14.0 %collective-permute-start.22 = (bf16[2,320,1280]{2,1,0:T(8,128)(2,1)}, bf16[2,320,1280]{2,1,0:T(8,128)(2,1)}, u32[]{:S(2)}, u32[]{:S(2)}) collective-permute-start(bf16[2,320,1280]{2,1,0:T(8,128)(2,1)} %dynamic-slice_bitcast_fusion.2), channel_id=1, source_target_pairs={{0,8},{8,0},{16,24},{24,16},{1,9},{9,1},{17,25},{25,17},{2,10},{10... | collective-permute-start | bytes 4915208 | tf_op jit(solution)/shard_map/ppermute | solution.py:746
  246.9 9.9 %collective-permute-start.23 = (bf16[2,320,1280]{2,1,0:T(8,128)(2,1)S(1)}, bf16[2,320,1280]{2,1,0:T(8,128)(2,1)S(1)}, u32[]{:S(2)}, u32[]{:S(2)}) collective-permute-start(bf16[2,320,1280]{2,1,0:T(8,128)(2,1)S(1)} %dynamic-slice_bitcast_fusion.1), channel_id=1, source_target_pairs={{0,8},{8,0},{16,24},{24,16},{1,9},{9,1},{17,25},{25,17},{2,10},{10... | collective-permute-start | bytes 4915208 | tf_op jit(solution)/shard_map/ppermute | solution.py:746
  247.4 10.7 %collective-permute-start.24 = (bf16[2,320,1280]{2,1,0:T(8,128)(2,1)S(1)}, bf16[2,320,1280]{2,1,0:T(8,128)(2,1)S(1)}, u32[]{:S(2)}, u32[]{:S(2)}) collective-permute-start(bf16[2,320,1280]{2,1,0:T(8,128)(2,1)S(1)} %dynamic-slice_bitcast_fusion), channel_id=1, source_target_pairs={{0,8},{8,0},{16,24},{24,16},{1,9},{9,1},{17,25},{25,17},{2,10},{10... | collective-permute-start | bytes 4915208 | tf_op jit(solution)/shard_map/ppermute | solution.py:746
  253.9 14.3 %collective-permute-start.21 = (bf16[640,1024]{1,0:T(8,128)(2,1)S(1)}, bf16[640,1024]{1,0:T(8,128)(2,1)}, u32[]{:S(2)}, u32[]{:S(2)}) collective-permute-start(bf16[640,1024]{1,0:T(8,128)(2,1)S(1)} %get-tuple-element.152), channel_id=1, source_target_pairs={{0,8},{1,9},{2,10},{3,11},{4,12},{5,13},{6,14},{7,15},{8,0},{9,1},... | collective-permute-start | bytes 3932168 | tf_op jit(solution)/shard_map/ppermute | solution.py:738
  261.2 94.4 %collective-permute-start.25 = (bf16[960,1280]{1,0:T(8,128)(2,1)}, bf16[960,1280]{1,0:T(8,128)(2,1)}, u32[]{:S(2)}, u32[]{:S(2)}) collective-permute-start(bf16[960,1280]{1,0:T(8,128)(2,1)} %pad_maximum_fusion.3), channel_id=1, source_target_pairs={{0,16},{8,24},{16,0},{24,8},{1,17},{9,25},{17,1},{25,9},{2,18},{10... | collective-permute-start | bytes 7372808 | tf_op jit(solution)/shard_map/ppermute | solution.py:765
  263.7 39.6 %collective-permute-start.18 = (bf16[256,1280]{1,0:T(8,128)(2,1)}, bf16[256,1280]{1,0:T(8,128)(2,1)}, u32[]{:S(2)}, u32[]{:S(2)}) collective-permute-start(bf16[256,1280]{1,0:T(8,128)(2,1)} %get-tuple-element.157), channel_id=1, source_target_pairs={{6,0},{14,1},{0,2},{8,3},{2,4},{10,5},{4,6},{12,7},{7,8},{15,9},{1... | collective-permute-start | bytes 1966088 | tf_op jit(solution)/shard_map/ppermute | solution.py:618
  263.7 46.2 %collective-permute-start.17 = (bf16[256,1280]{1,0:T(8,128)(2,1)}, bf16[256,1280]{1,0:T(8,128)(2,1)}, u32[]{:S(2)}, u32[]{:S(2)}) collective-permute-start(bf16[256,1280]{1,0:T(8,128)(2,1)} %get-tuple-element.158), channel_id=1, source_target_pairs={{4,0},{12,1},{6,2},{14,3},{0,4},{8,5},{2,6},{10,7},{5,8},{13,9},{7... | collective-permute-start | bytes 1966088 | tf_op jit(solution)/shard_map/ppermute | solution.py:618
  266.5 43.4 %collective-permute-start.16 = (bf16[256,1280]{1,0:T(8,128)(2,1)}, bf16[256,1280]{1,0:T(8,128)(2,1)}, u32[]{:S(2)}, u32[]{:S(2)}) collective-permute-start(bf16[256,1280]{1,0:T(8,128)(2,1)} %get-tuple-element.159), channel_id=1, source_target_pairs={{2,0},{10,1},{4,2},{12,3},{6,4},{14,5},{0,6},{8,7},{3,8},{11,9},{5... | collective-permute-start | bytes 1966088 | tf_op jit(solution)/shard_map/ppermute | solution.py:618
  268.2 41.7 %collective-permute-start.15 = (bf16[256,1280]{1,0:T(8,128)(2,1)}, bf16[256,1280]{1,0:T(8,128)(2,1)}, u32[]{:S(2)}, u32[]{:S(2)}) collective-permute-start(bf16[256,1280]{1,0:T(8,128)(2,1)} %get-tuple-element.160), channel_id=1, source_target_pairs={{0,0},{8,1},{2,2},{10,3},{4,4},{12,5},{6,6},{14,7},{1,8},{9,9},{3,... | collective-permute-start | bytes 1966088 | tf_op jit(solution)/shard_map/ppermute | solution.py:618
  322.1 33.4 %collective-permute-start.38 = (bf16[480,640]{1,0:T(8,128)(2,1)}, bf16[480,640]{1,0:T(8,128)(2,1)}, u32[]{:S(2)}, u32[]{:S(2)}) collective-permute-start(bf16[480,640]{1,0:T(8,128)(2,1)} %get-tuple-element.96), channel_id=1, source_target_pairs={{0,8},{8,0},{16,24},{24,16},{1,9},{9,1},{17,25},{25,17},{2,10},{10... | collective-permute-start | bytes 1843208 | tf_op jit(solution)/shard_map/ppermute | solution.py:793
  324.3 67.2 %collective-permute-start.36 = (bf16[480,640]{1,0:T(8,128)(2,1)}, bf16[480,640]{1,0:T(8,128)(2,1)S(1)}, u32[]{:S(2)}, u32[]{:S(2)}) collective-permute-start(bf16[480,640]{1,0:T(8,128)(2,1)} %get-tuple-element.95), channel_id=1, source_target_pairs={{0,8},{8,0},{16,24},{24,16},{1,9},{9,1},{17,25},{25,17},{2,10},{10... | collective-permute-start | bytes 1843208 | tf_op jit(solution)/shard_map/ppermute | solution.py:793
  325.3 70.7 %collective-permute-start.37 = (bf16[480,640]{1,0:T(8,128)(2,1)}, bf16[480,640]{1,0:T(8,128)(2,1)}, u32[]{:S(2)}, u32[]{:S(2)}) collective-permute-start(bf16[480,640]{1,0:T(8,128)(2,1)} %get-tuple-element.98), channel_id=1, source_target_pairs={{0,16},{8,24},{16,0},{24,8},{1,17},{9,25},{17,1},{25,9},{2,18},{10... | collective-permute-start | bytes 1843208 | tf_op jit(solution)/shard_map/ppermute | solution.py:796
  355.5 41.4 %collective-permute-start.39 = (bf16[480,640]{1,0:T(8,128)(2,1)}, bf16[480,640]{1,0:T(8,128)(2,1)}, u32[]{:S(2)}, u32[]{:S(2)}) collective-permute-start(bf16[480,640]{1,0:T(8,128)(2,1)} %collective-permute-done.38), channel_id=1, source_target_pairs={{0,16},{8,24},{16,0},{24,8},{1,17},{9,25},{17,1},{25,9},{2,18},{10... | collective-permute-start | bytes 1843208 | tf_op jit(solution)/shard_map/ppermute | solution.py:796
  359.0 34.3 %collective-permute-start.56 = (bf16[480,1280]{1,0:T(8,128)(2,1)}, bf16[480,1280]{1,0:T(8,128)(2,1)S(1)}, u32[]{:S(2)}, u32[]{:S(2)}) collective-permute-start(bf16[480,1280]{1,0:T(8,128)(2,1)} %dynamic-slice_bitcast_fusion.5), channel_id=1, source_target_pairs={{0,1},{1,0},{2,3},{3,2},{4,5},{5,4},{6,7},{7,6},{8,9},{9,8},{10,11... | collective-permute-start | bytes 3686408 | tf_op jit(solution)/shard_map/ppermute | solution.py:551
  371.2 20.5 %collective-permute-start.42 = (bf16[480,640]{1,0:T(8,128)(2,1)}, bf16[480,640]{1,0:T(8,128)(2,1)}, u32[]{:S(2)}, u32[]{:S(2)}) collective-permute-start(bf16[480,640]{1,0:T(8,128)(2,1)} %get-tuple-element.104), channel_id=1, source_target_pairs={{0,8},{8,0},{16,24},{24,16},{1,9},{9,1},{17,25},{25,17},{2,10},{10... | collective-permute-start | bytes 1843208 | tf_op jit(solution)/shard_map/ppermute | solution.py:793
  391.5 20.2 %collective-permute-start.40 = (bf16[480,640]{1,0:T(8,128)(2,1)}, bf16[480,640]{1,0:T(8,128)(2,1)S(1)}, u32[]{:S(2)}, u32[]{:S(2)}) collective-permute-start(bf16[480,640]{1,0:T(8,128)(2,1)} %get-tuple-element.103), channel_id=1, source_target_pairs={{0,8},{8,0},{16,24},{24,16},{1,9},{9,1},{17,25},{25,17},{2,10},{10... | collective-permute-start | bytes 1843208 | tf_op jit(solution)/shard_map/ppermute | solution.py:793
  391.7 20.0 %collective-permute-start.41 = (bf16[480,640]{1,0:T(8,128)(2,1)S(1)}, bf16[480,640]{1,0:T(8,128)(2,1)S(1)}, u32[]{:S(2)}, u32[]{:S(2)}) collective-permute-start(bf16[480,640]{1,0:T(8,128)(2,1)S(1)} %copy-done.46), channel_id=1, source_target_pairs={{0,16},{8,24},{16,0},{24,8},{1,17},{9,25},{17,1},{25,9},{2,18},{10... | collective-permute-start | bytes 1843208 | tf_op jit(solution)/shard_map/ppermute | solution.py:796
  394.4 25.9 %collective-permute-start.43 = (bf16[480,640]{1,0:T(8,128)(2,1)}, bf16[480,640]{1,0:T(8,128)(2,1)S(1)}, u32[]{:S(2)}, u32[]{:S(2)}) collective-permute-start(bf16[480,640]{1,0:T(8,128)(2,1)} %collective-permute-done.42), channel_id=1, source_target_pairs={{0,16},{8,24},{16,0},{24,8},{1,17},{9,25},{17,1},{25,9},{2,18},{10... | collective-permute-start | bytes 1843208 | tf_op jit(solution)/shard_map/ppermute | solution.py:796
  396.0 98.1 %collective-permute-start.26 = (bf16[1024,1280]{1,0:T(8,128)(2,1)S(1)}, bf16[1024,1280]{1,0:T(8,128)(2,1)S(1)}, u32[]{:S(2)}, u32[]{:S(2)}) collective-permute-start(bf16[1024,1280]{1,0:T(8,128)(2,1)S(1)} %copy-done.45), channel_id=1, source_target_pairs={{0,8},{1,9},{2,10},{3,11},{4,12},{5,13},{6,14},{7,15},{8,0},{9,1},... | collective-permute-start | bytes 7864328 | tf_op jit(solution)/shard_map/ppermute | solution.py:813
  396.8 29.1 %collective-permute-start.57 = (bf16[240,1280]{1,0:T(8,128)(2,1)S(1)}, bf16[240,1280]{1,0:T(8,128)(2,1)S(1)}, u32[]{:S(2)}, u32[]{:S(2)}) collective-permute-start(bf16[240,1280]{1,0:T(8,128)(2,1)S(1)} %dynamic-slice_bitcast_fusion.14), channel_id=1, source_target_pairs={{0,2},{1,3},{2,0},{3,1},{4,6},{5,7},{6,4},{7,5},{8,10},{9,11},{10,... | collective-permute-start | bytes 1843208 | tf_op jit(solution)/shard_map/ppermute | solution.py:551
  420.8 18.4 %collective-permute-start.50 = (bf16[480,640]{1,0:T(8,128)(2,1)S(1)}, bf16[480,640]{1,0:T(8,128)(2,1)S(1)}, u32[]{:S(2)}, u32[]{:S(2)}) collective-permute-start(bf16[480,640]{1,0:T(8,128)(2,1)S(1)} %dynamic-slice_bitcast_fusion.15), channel_id=1, source_target_pairs={{0,1},{1,0},{2,3},{3,2},{4,5},{5,4},{6,7},{7,6},{8,9},{9,8},{10,11... | collective-permute-start | bytes 1843208 | tf_op jit(solution)/shard_map/ppermute | solution.py:551
  425.3 24.4 %collective-permute-start.44 = (bf16[480,640]{1,0:T(8,128)(2,1)S(1)}, bf16[480,640]{1,0:T(8,128)(2,1)S(1)}, u32[]{:S(2)}, u32[]{:S(2)}) collective-permute-start(bf16[480,640]{1,0:T(8,128)(2,1)S(1)} %dynamic-slice_bitcast_fusion.16), channel_id=1, source_target_pairs={{0,1},{1,0},{2,3},{3,2},{4,5},{5,4},{6,7},{7,6},{8,9},{9,8},{10,11... | collective-permute-start | bytes 1843208 | tf_op jit(solution)/shard_map/ppermute | solution.py:551
  426.2 36.6 %collective-permute-start.58 = (bf16[120,1280]{1,0:T(8,128)(2,1)S(1)}, bf16[120,1280]{1,0:T(8,128)(2,1)S(1)}, u32[]{:S(2)}, u32[]{:S(2)}) collective-permute-start(bf16[120,1280]{1,0:T(8,128)(2,1)S(1)} %dynamic-slice_bitcast_fusion.17), channel_id=1, source_target_pairs={{0,4},{1,5},{2,6},{3,7},{4,0},{5,1},{6,2},{7,3},{8,12},{9,13},{10,... | collective-permute-start | bytes 921608 | tf_op jit(solution)/shard_map/ppermute | solution.py:551
  439.4 23.6 %collective-permute-start.51 = (bf16[240,640]{1,0:T(8,128)(2,1)S(1)}, bf16[240,640]{1,0:T(8,128)(2,1)S(1)}, u32[]{:S(2)}, u32[]{:S(2)}) collective-permute-start(bf16[240,640]{1,0:T(8,128)(2,1)S(1)} %dynamic-slice_bitcast_fusion.18), channel_id=1, source_target_pairs={{0,2},{1,3},{2,0},{3,1},{4,6},{5,7},{6,4},{7,5},{8,10},{9,11},{10,... | collective-permute-start | bytes 921608 | tf_op jit(solution)/shard_map/ppermute | solution.py:551
  449.8 44.3 %copy-start.5 = (bf16[1024,1280]{1,0:T(8,128)(2,1)S(1)}, bf16[1024,1280]{1,0:T(8,128)(2,1)}, u32[]{:S(2)}) copy-start(bf16[1024,1280]{1,0:T(8,128)(2,1)} %input_side.3) | copy-start | bytes 7864324
  449.8 22.2 %collective-permute-start.45 = (bf16[240,640]{1,0:T(8,128)(2,1)S(1)}, bf16[240,640]{1,0:T(8,128)(2,1)S(1)}, u32[]{:S(2)}, u32[]{:S(2)}) collective-permute-start(bf16[240,640]{1,0:T(8,128)(2,1)S(1)} %dynamic-slice_bitcast_fusion.19), channel_id=1, source_target_pairs={{0,2},{1,3},{2,0},{3,1},{4,6},{5,7},{6,4},{7,5},{8,10},{9,11},{10,... | collective-permute-start | bytes 921608 | tf_op jit(solution)/shard_map/ppermute | solution.py:551
  462.9 31.1 %collective-permute-start.59 = (bf16[120,1280]{1,0:T(8,128)(2,1)S(1)}, bf16[120,1280]{1,0:T(8,128)(2,1)S(1)}, u32[]{:S(2)}, u32[]{:S(2)}) collective-permute-start(bf16[120,1280]{1,0:T(8,128)(2,1)S(1)} %fusion.23), channel_id=1, source_target_pairs={{0,4},{1,5},{2,6},{3,7},{4,0},{5,1},{6,2},{7,3},{8,12},{9,13},{10,... | collective-permute-start | bytes 921608 | tf_op jit(solution)/shard_map/ppermute | solution.py:556
  463.1 24.1 %collective-permute-start.52 = (bf16[120,640]{1,0:T(8,128)(2,1)S(1)}, bf16[120,640]{1,0:T(8,128)(2,1)S(1)}, u32[]{:S(2)}, u32[]{:S(2)}) collective-permute-start(bf16[120,640]{1,0:T(8,128)(2,1)S(1)} %dynamic-slice_bitcast_fusion.20), channel_id=1, source_target_pairs={{0,4},{1,5},{2,6},{3,7},{4,0},{5,1},{6,2},{7,3},{8,12},{9,13},{10,... | collective-permute-start | bytes 460808 | tf_op jit(solution)/shard_map/ppermute | solution.py:551
  472.2 21.7 %collective-permute-start.46 = (bf16[120,640]{1,0:T(8,128)(2,1)S(1)}, bf16[120,640]{1,0:T(8,128)(2,1)S(1)}, u32[]{:S(2)}, u32[]{:S(2)}) collective-permute-start(bf16[120,640]{1,0:T(8,128)(2,1)S(1)} %dynamic-slice_bitcast_fusion.21), channel_id=1, source_target_pairs={{0,4},{1,5},{2,6},{3,7},{4,0},{5,1},{6,2},{7,3},{8,12},{9,13},{10,... | collective-permute-start | bytes 460808 | tf_op jit(solution)/shard_map/ppermute | solution.py:551
  487.3 18.3 %collective-permute-start.53 = (bf16[120,640]{1,0:T(8,128)(2,1)S(1)}, bf16[120,640]{1,0:T(8,128)(2,1)S(1)}, u32[]{:S(2)}, u32[]{:S(2)}) collective-permute-start(bf16[120,640]{1,0:T(8,128)(2,1)S(1)} %fusion.26), channel_id=1, source_target_pairs={{0,4},{1,5},{2,6},{3,7},{4,0},{5,1},{6,2},{7,3},{8,12},{9,13},{10,... | collective-permute-start | bytes 460808 | tf_op jit(solution)/shard_map/ppermute | solution.py:556
  493.9 14.5 %collective-permute-start.47 = (bf16[120,640]{1,0:T(8,128)(2,1)S(1)}, bf16[120,640]{1,0:T(8,128)(2,1)S(1)}, u32[]{:S(2)}, u32[]{:S(2)}) collective-permute-start(bf16[120,640]{1,0:T(8,128)(2,1)S(1)} %fusion.27), channel_id=1, source_target_pairs={{0,4},{1,5},{2,6},{3,7},{4,0},{5,1},{6,2},{7,3},{8,12},{9,13},{10,... | collective-permute-start | bytes 460808 | tf_op jit(solution)/shard_map/ppermute | solution.py:556
  494.1 35.4 %collective-permute-start.60 = (bf16[240,1280]{1,0:T(8,128)(2,1)S(1)}, bf16[240,1280]{1,0:T(8,128)(2,1)S(1)}, u32[]{:S(2)}, u32[]{:S(2)}) collective-permute-start(bf16[240,1280]{1,0:T(8,128)(2,1)S(1)} %maximum_select_fusion.6), channel_id=1, source_target_pairs={{0,2},{1,3},{2,0},{3,1},{4,6},{5,7},{6,4},{7,5},{8,10},{9,11},{10,... | collective-permute-start | bytes 1843208 | tf_op jit(solution)/shard_map/ppermute | solution.py:556
  497.2 10.2 %collective-permute-start.31 = (f32[5200]{0:T(1024)S(1)}, f32[5200]{0:T(1024)S(1)}, u32[]{:S(2)}, u32[]{:S(2)}) collective-permute-start(f32[5200]{0:T(1024)S(1)} %constant_dynamic-update-slice_fusion), channel_id=1, source_target_pairs={{0,8},{8,0},{16,24},{24,16},{1,9},{9,1},{17,25},{25,17},{2,10},{10... | collective-permute-start | bytes 62408 | tf_op jit(solution)/shard_map/ppermute | solution.py:570
  505.6 21.8 %collective-permute-start.54 = (bf16[240,640]{1,0:T(8,128)(2,1)S(1)}, bf16[240,640]{1,0:T(8,128)(2,1)S(1)}, u32[]{:S(2)}, u32[]{:S(2)}) collective-permute-start(bf16[240,640]{1,0:T(8,128)(2,1)S(1)} %maximum_select_fusion.8), channel_id=1, source_target_pairs={{0,2},{1,3},{2,0},{3,1},{4,6},{5,7},{6,4},{7,5},{8,10},{9,11},{10,... | collective-permute-start | bytes 921608 | tf_op jit(solution)/shard_map/ppermute | solution.py:556
  507.4 3.0 collective-permute-start.32
  508.4 19.4 %collective-permute-start.48 = (bf16[240,640]{1,0:T(8,128)(2,1)S(1)}, bf16[240,640]{1,0:T(8,128)(2,1)S(1)}, u32[]{:S(2)}, u32[]{:S(2)}) collective-permute-start(bf16[240,640]{1,0:T(8,128)(2,1)S(1)} %maximum_select_fusion.7), channel_id=1, source_target_pairs={{0,2},{1,3},{2,0},{3,1},{4,6},{5,7},{6,4},{7,5},{8,10},{9,11},{10,... | collective-permute-start | bytes 921608 | tf_op jit(solution)/shard_map/ppermute | solution.py:556
  510.5 3.0 collective-permute-start.33
  513.4 14.0 %collective-permute-start.34 = (f32[5200]{0:T(1024)S(1)}, f32[5200]{0:T(1024)S(1)}, u32[]{:S(2)}, u32[]{:S(2)}) collective-permute-start(f32[5200]{0:T(1024)S(1)} %add.573), channel_id=1, source_target_pairs={{0,2},{1,3},{2,0},{3,1},{4,6},{5,7},{6,4},{7,5},{8,10},{9,11},{10,... | collective-permute-start | bytes 62408 | tf_op jit(solution)/shard_map/ppermute | solution.py:575
  527.4 8.8 %collective-permute-start.35 = (f32[5200]{0:T(1024)S(1)}, f32[5200]{0:T(1024)S(1)}, u32[]{:S(2)}, u32[]{:S(2)}) collective-permute-start(f32[5200]{0:T(1024)S(1)} %add.574), channel_id=1, source_target_pairs={{0,4},{1,5},{2,6},{3,7},{4,0},{5,1},{6,2},{7,3},{8,12},{9,13},{10,... | collective-permute-start | bytes 62408 | tf_op jit(solution)/shard_map/ppermute | solution.py:575
  527.7 11.9 %collective-permute-start.55 = (bf16[480,640]{1,0:T(8,128)(2,1)S(1)}, bf16[480,640]{1,0:T(8,128)(2,1)S(1)}, u32[]{:S(2)}, u32[]{:S(2)}) collective-permute-start(bf16[480,640]{1,0:T(8,128)(2,1)S(1)} %maximum_select_fusion.5), channel_id=1, source_target_pairs={{0,1},{1,0},{2,3},{3,2},{4,5},{5,4},{6,7},{7,6},{8,9},{9,8},{10,11... | collective-permute-start | bytes 1843208 | tf_op jit(solution)/shard_map/ppermute | solution.py:556
  528.0 39.3 %collective-permute-start.49 = (bf16[480,640]{1,0:T(8,128)(2,1)S(1)}, bf16[480,640]{1,0:T(8,128)(2,1)S(1)}, u32[]{:S(2)}, u32[]{:S(2)}) collective-permute-start(bf16[480,640]{1,0:T(8,128)(2,1)S(1)} %maximum_select_fusion.4), channel_id=1, source_target_pairs={{0,1},{1,0},{2,3},{3,2},{4,5},{5,4},{6,7},{7,6},{8,9},{9,8},{10,11... | collective-permute-start | bytes 1843208 | tf_op jit(solution)/shard_map/ppermute | solution.py:556
  529.9 91.0 %collective-permute-start.61 = (bf16[480,1280]{1,0:T(8,128)(2,1)S(1)}, bf16[480,1280]{1,0:T(8,128)(2,1)}, u32[]{:S(2)}, u32[]{:S(2)}) collective-permute-start(bf16[480,1280]{1,0:T(8,128)(2,1)S(1)} %maximum_select_fusion.3), channel_id=1, source_target_pairs={{0,1},{1,0},{2,3},{3,2},{4,5},{5,4},{6,7},{7,6},{8,9},{9,8},{10,11... | collective-permute-start | bytes 3686408 | tf_op jit(solution)/shard_map/ppermute | solution.py:556
  531.3 60.8 %collective-permute-start.30 = (bf16[256,1280]{1,0:T(8,128)(2,1)}, bf16[256,1280]{1,0:T(8,128)(2,1)}, u32[]{:S(2)}, u32[]{:S(2)}) collective-permute-start(bf16[256,1280]{1,0:T(8,128)(2,1)} %get-tuple-element.147), channel_id=1, source_target_pairs={{6,0},{14,1},{0,2},{8,3},{2,4},{10,5},{4,6},{12,7},{7,8},{15,9},{1... | collective-permute-start | bytes 1966088 | tf_op jit(solution)/shard_map/ppermute | solution.py:618
  536.2 55.9 %collective-permute-start.29 = (bf16[256,1280]{1,0:T(8,128)(2,1)}, bf16[256,1280]{1,0:T(8,128)(2,1)}, u32[]{:S(2)}, u32[]{:S(2)}) collective-permute-start(bf16[256,1280]{1,0:T(8,128)(2,1)} %get-tuple-element.148), channel_id=1, source_target_pairs={{4,0},{12,1},{6,2},{14,3},{0,4},{8,5},{2,6},{10,7},{5,8},{13,9},{7... | collective-permute-start | bytes 1966088 | tf_op jit(solution)/shard_map/ppermute | solution.py:618
  539.6 43.9 %copy-start.31 = (bf16[480,640]{1,0:T(8,128)(2,1)}, bf16[480,640]{1,0:T(8,128)(2,1)S(1)}, u32[]{:S(2)}) copy-start(bf16[480,640]{1,0:T(8,128)(2,1)S(1)} %collective-permute-done.55) | copy-start | bytes 1843204
  539.6 52.5 %collective-permute-start.28 = (bf16[256,1280]{1,0:T(8,128)(2,1)}, bf16[256,1280]{1,0:T(8,128)(2,1)}, u32[]{:S(2)}, u32[]{:S(2)}) collective-permute-start(bf16[256,1280]{1,0:T(8,128)(2,1)} %get-tuple-element.149), channel_id=1, source_target_pairs={{2,0},{10,1},{4,2},{12,3},{6,4},{14,5},{0,6},{8,7},{3,8},{11,9},{5... | collective-permute-start | bytes 1966088 | tf_op jit(solution)/shard_map/ppermute | solution.py:618
  567.3 43.8 %collective-permute-start.27 = (bf16[256,1280]{1,0:T(8,128)(2,1)S(1)}, bf16[256,1280]{1,0:T(8,128)(2,1)}, u32[]{:S(2)}, u32[]{:S(2)}) collective-permute-start(bf16[256,1280]{1,0:T(8,128)(2,1)S(1)} %get-tuple-element.150), channel_id=1, source_target_pairs={{0,0},{8,1},{2,2},{10,3},{4,4},{12,5},{6,6},{14,7},{1,8},{9,9},{3,... | collective-permute-start | bytes 1966088 | tf_op jit(solution)/shard_map/ppermute | solution.py:618
  (51 other events, 504.5 us)

commit v4 on v3

--- a/solution.py
+++ b/solution.py
@@ -537,7 +537,7 @@
     )(*grads, w)
 
 
-def reduce_places(buf, places):
+def reduce_places(buf, places, late=(), hold=()):
     place = lax.axis_index("seq")
     lines, wide = buf.shape
     bits = places.bit_length() - 1
@@ -547,11 +547,15 @@
         halves = buf.reshape(2, -1, wide)
         keep = lax.dynamic_index_in_dim(halves, bit, 0, keepdims=False)
         send = lax.dynamic_index_in_dim(halves, 1 - bit, 0, keepdims=False)
+        if hold and b == 2:
+            send = after(send, *hold)
         yield send
         got = lax.ppermute(send, "seq", [(i, i ^ (1 << b)) for i in range(places)])
         buf = (keep.astype(f32) + got.astype(f32)).astype(bf16)
     for b in reversed(range(bits)):
         bit = (place >> b) & 1
+        if late and b == 0:
+            buf = after(buf, *late)
         yield buf
         got = lax.ppermute(buf, "seq", [(i, i ^ (1 << b)) for i in range(places)])
         buf = jnp.where(
@@ -640,7 +644,7 @@
         lax.ppermute(parts[flip], "dp", team.turn_rows(step, flip)) for step, flip in shifts[2:]
     ]
     near = lax.ppermute(parts[1], "dp", team.swap_core())
-    x_own = spread_done(spread(after(activations, *parts), near))
+    x_blocks = spread(after(activations, *parts), near)
     other_ids = lax.ppermute(segment_ids, "dp", team.swap_core())
     w_half, small = join(
         [parts[0], near] + far,
@@ -651,12 +655,11 @@
     small = small.reshape(team.dp, -1)[:, : 4 * rows_here]
     small = small.reshape(team.dp, 4, rows_here).transpose(1, 0, 2).reshape(4, width).astype(f32)
     gain_in, gain_mid, bias_up, bias_down = (small[i : i + 1] for i in range(4))
-    xs = [x_own] + [lax.ppermute(x_own, axes, team.rotate(-j)) for j in range(1, size)]
     three = after(jnp.concatenate([w_out, w_up, w_down]), *far)
     three = [three] + [
         lax.ppermute(three, "dp", team.turn_rows(step)) for step in range(1, team.rows)
     ]
-    cot_own = spread(after(cotangent, x_own).astype(bf16))
+    cot_own = spread(after(cotangent, *far).astype(bf16))
 
     ids = lax.dynamic_index_in_dim(
         jnp.where(side == core, segment_ids, other_ids), group, 0, keepdims=False
@@ -681,6 +684,8 @@
     unit = jnp.ones((head_size,), f32)
     factor_row = jnp.tile(jnp.concatenate([factor * log2e, unit, unit]), local_heads)[None, :]
 
+    x_own = spread_done(after(x_blocks, w_half, table, starts, factor_row))
+    xs = [x_own] + [lax.ppermute(x_own, axes, team.rotate(-j)) for j in range(1, size)]
     qkv, normed_in = project_qkv(
         xs, gain_in, w_half, factor_row, local_heads, head_size, team.dp, span
     )
@@ -774,7 +779,7 @@
     pair = math.gcd(local_heads, 4)
     grad_in = after(grad_heads, *three_rows)
     chunks, dots, heads_of = [], 0.0, []
-    steps = None
+    steps, hold = None, []
     for c in range(local_heads // pair):
         grads, dot = attend_back(
             c, pair, table, qkv, att, grad_in, lse, starts, factor[:, None]
@@ -787,7 +792,7 @@
         else:
             if steps is None:
                 three_far = after(three_far, grads)
-                steps = reduce_places(add(three_rows[0], *three_far), team.seq)
+                steps = reduce_places(add(three_rows[0], *three_far), team.seq, hold=hold)
             grads = after(grads, next(steps))
         send, keep = head_grad(grads, normed_in, team.rows, row, core)
         near = [lax.ppermute(piece, "dp", team.swap_core()) for piece in send]
@@ -800,7 +805,7 @@
         ]
         heads_of.append((keep[0], near[0], far))
         grad_in = after(grad_in, *send, *keep)
-    steps = steps or reduce_places(add(three_rows[0], *three_far), team.seq)
+    steps = steps or reduce_places(add(three_rows[0], *three_far), team.seq, hold=hold)
     blocks = own // span
     chunks = after(chunks, *send, *keep)
     partial = [
@@ -822,7 +827,11 @@
         scaled_in
         - x_float * rms_in * rms_in * jnp.mean(scaled_in * x_float, axis=-1, keepdims=True)
     )
-    input_grad = unspread_done(unspread(input_grad_own.astype(bf16)), f32)
+    input_grad_own = input_grad_own.astype(bf16)
+    input_grad = unspread(input_grad_own)
+    late = input_grad[seqs // 2 :]
+    hold.append(input_grad_own)
+    input_grad = unspread_done(input_grad, f32)
     result = unspread_done(result, bf16)
 
     three = last(steps).astype(f32)
@@ -835,7 +844,8 @@
             [add(mine, *[f[0] for f in far]), add(theirs, *[f[1] for f in far])]
         )
         total = place_in([(total, member // 2)], team.half) if team.half > 1 else total
-        full.append(last(reduce_places(total.reshape(-1, total.shape[-1]), team.seq)))
+        total = after(total.reshape(-1, total.shape[-1]), input_grad_own)
+        full.append(last(reduce_places(total, team.seq, late)))
     full = unfold(full, team.half, rows_here, core).reshape(heads, 3, head_size, rows_here)
     vectors = sum_everywhere(
         team,

time: 637 us -> 655 us (1.028)
  the two profiles are of different devices: /device:TPU:1 before, /device:TPU:25 now
where the time goes in v4:
time: 655 us; the launch traced here: 645 us
  waiting for transfers between devices  222 us (34%)
  Pallas kernels  183 us (28%)
  starting transfers between devices  95.5 us (15%)
  matrix products  51 us (8%)
  other arithmetic  49.7 us (8%)
  local copies, waits for them, and re-layouts  41.4 us (6%)
    pallas_call x2, Pallas kernels, attend_back(): pl.pallas_call(functools.partial(attend_back_kernel, count, block, pair),...  53.8 us
    ppermute x9, waiting for transfers between devices, reduce_places(): got = lax.ppermute(send, 'seq', [(i, i ^ 1 << b) for i in range(places)])  45.9 us
    dot_general x8, matrix products, mm(): return lax.dot_general(a, b, dims, preferred_element_type=f32)  44.7 us
    ppermute x9, waiting for transfers between devices, reduce_places(): got = lax.ppermute(buf, 'seq', [(i, i ^ 1 << b) for i in range(places)])  39.5 us
    ppermute x2, waiting for transfers between devices, on_device(): lax.ppermute(parts[flip], 'dp', team.turn_rows(step, flip))  37.1 us
    pallas_call x7, Pallas kernels, join(): pl.pallas_call(functools.partial(join_kernel, count, ends), grid_spec=plt...  33.8 us
    ppermute x8, starting transfers between devices, unspread(): lax.ppermute(array[step * span:(step + 1) * span], axes, team.back(step))  30.3 us
    pallas_call x1, Pallas kernels, attend(): pl.pallas_call(functools.partial(attend_kernel, count, block, pair), grid...  26.3 us
  transfers between devices with their start and end apart: 62, of which 19 were waited for; matrix products, arithmetic and copies ran while one was open for 13% of the time, Pallas kernels for 27%

profile of v4, /device:TPU:25, one launch (start us, length us, event | category | flops | bytes accessed | tf_op | source)
XLA Modules:
  0.0 644.9 jit_solution(1339837439363547763)
XLA Ops:
  0.7 2.8 concatenate.90
  9.8 2.5 pad_maximum_fusion.4
  19.8 4.1 convert_reduce_fusion
  24.4 2.4 dynamic-slice_bitcast_fusion.12
  26.8 3.4 collective-permute-start.2
  30.2 13.4 %collective-permute-done.6.refs_3_ = bf16[336,1920]{1,0:T(8,128)(2,1)S(1)} collective-permute-done((bf16[336,1920]{1,0:T(8,128)(2,1)}, bf16[336,1920]{1,0:T(8,128)(2,1)S(1)}, u32[]{:S(2)}, u32[]{:S(2)}) %collective-permute-start.6) | collective-permute-done | bytes 1290272 | tf_op jit(solution)/shard_map/ppermute | solution.py:644
  43.7 3.1 collective-permute-start.1
  47.5 23.7 %collective-permute-done.5.refs_2_ = bf16[336,1920]{1,0:T(8,128)(2,1)} collective-permute-done((bf16[336,1920]{1,0:T(8,128)(2,1)S(1)}, bf16[336,1920]{1,0:T(8,128)(2,1)}, u32[]{:S(2)}, u32[]{:S(2)}) %collective-permute-start.5) | collective-permute-done | bytes 1290272 | tf_op jit(solution)/shard_map/ppermute | solution.py:644
  71.2 6.4 join.7
  78.1 3.9 join.8
  82.5 3.2 pad_maximum_fusion.1.refs_0_
  88.8 2.6 collective-permute-start.10
  93.8 19.7 %qkv.1 = (bf16[8,3,2048,80]{3,2,1,0:T(8,128)(2,1)}, bf16[2,2048,640]{2,1,0:T(8,128)(2,1)}) custom-call(bf16[1024,1280]{1,0:T(8,128)(2,1)} %bitcast.199, bf16[1024,1280]{1,0:T(8,128)(2,1)} %copy-done.15, f32[1,1280]{1,0:T(1,128)} %slice.77.refs_2_, bf16[1280,1920]{1,0:T(8,128)(2,1)} %bitcast.214, f32[1,1920]{1,0:T(1,128)} %broadcast_in_dim_tile.3.refs_4_), custom_call_target="tpu_custom_call" | custom-call | flops 1 | bytes 1 | tf_op jit(solution)/shard_map/qkv/pallas_call | solution.py:163
  113.5 22.9 %collective-permute-done.9.refs_2_ = bf16[256,1280]{1,0:T(8,128)(2,1)} collective-permute-done((bf16[256,1280]{1,0:T(8,128)(2,1)}, bf16[256,1280]{1,0:T(8,128)(2,1)}, u32[]{:S(2)}, u32[]{:S(2)}) %collective-permute-start.9) | collective-permute-done | bytes 655392 | tf_op jit(solution)/shard_map/ppermute | solution.py:614
  136.4 26.3 %attend.1 = (bf16[640,2048]{1,0:T(8,128)(2,1)}, f32[8,1,2048]{2,1,0:T(1,128)}) custom-call(s32[5,8]{1,0:T(8,128)} %stack.83.table, bf16[8,3,2048,80]{3,2,1,0:T(8,128)(2,1)} %get-tuple-element.85.qkv_ref, s32[8,256]{1,0:T(8,128)} %copy-done.28), custom_call_target="tpu_custom_call" | custom-call | flops 1 | bytes 1 | tf_op jit(solution)/shard_map/attend/pallas_call | solution.py:357
  163.4 3.0 fusion.39
  168.3 3.1 collective-permute-start.19
  174.3 3.5 join.9
  177.8 7.9 %join.10 = (bf16[4,320,1280]{2,1,0:T(8,128)(2,1)}, bf16[4,320,1280]{2,1,0:T(8,128)(2,1)}, bf16[4,320,1280]{2,1,0:T(8,128)(2,1)}) custom-call(s32[4]{0:T(128)} %add_add_fusion.1.slots_ref, bf16[960,1280]{1,0:T(8,128)(2,1)} %pad_maximum_fusion.1.refs_0_, bf16[960,1280]{1,0:T(8,128)(2,1)} %collective-permute-done.12.refs_1_, ...), custom_call_target="tpu_custom_call" | custom-call | flops 1 | bytes 1 | tf_op jit(solution)/shard_map/join/pallas_call | solution.py:116
  185.8 6.3 multiply_reduce_fusion.3
  192.1 3.7 fusion.35
  195.9 5.7 add_convert_fusion
  203.0 3.9 join.11
  206.9 10.4 %convert_reduce_fusion.3 = (f32[1280]{0:T(1024)S(1)}, bf16[1024,1280]{1,0:T(8,128)(2,1)}) fusion(f32[1024,1280]{1,0:T(8,128)} %copy-done.39, f32[1280]{0:T(1024)S(1)} %add.541, bf16[1024,1280]{1,0:T(8,128)(2,1)} %bitcast.201, bf16[1280,1280]{1,0:T(8,128)(2,1)} %bitcast.251), kind=kOutput, calls=%fused_computation.19 | convolution fusion | flops 3371170560 | bytes 13772800 | tf_op jit(solution)/shard_map/dot_general | solution.py:25
  217.4 4.1 convolution_convert_fusion.2
  221.5 6.9 %multiply_reduce_fusion = (f32[1280]{0:T(1024)S(1)}, f32[1024]{0:T(1024)S(1)}, f32[1024,1280]{1,0:T(8,128)S(1)}) fusion(f32[1024,1280]{1,0:T(8,128)S(1)} %bitcast.204, f32[1024]{0:T(1024)S(1)} %add_rsqrt_fusion, f32[1280]{0:T(1024)S(1)} %mul.203, bf16[1024,1280]{1,0:T(8,128)(2,1)} %get-tuple-element.195, bf16[1280,1280]{1,0:T(8,128)(2,1)S(1)} %bitcast.250), kind=kOutput, calls=%fused_computation.20 | convolution fusion | flops 3363305216 | bytes 16402432 | tf_op jit(solution)/shard_map/dot_general | solution.py:25
  228.4 5.8 convolution_convert_fusion.1
  237.9 4.2 convolution_convert_fusion
  244.0 3.9 convolution_convert_fusion.3
  261.7 2.7 collective-permute-start.15
  265.8 3.5 pad_maximum_fusion.grad_ref
  269.3 26.8 %attend_back.2 = (bf16[960,2048]{1,0:T(8,128)(2,1)}, f32[80,1]{1,0:T(8,128)}) custom-call(s32[5,8]{1,0:T(8,128)} %stack.83.table, bf16[8,3,2048,80]{3,2,1,0:T(8,128)(2,1)} %get-tuple-element.85.qkv_ref, bf16[640,2048]{1,0:T(8,128)(2,1)} %get-tuple-element.86.att_ref, bf16[640,2048]{1,0:T(8,128)(2,1)} %pad_maximum_fusion.grad_ref, ...), custom_call_target="tpu_custom_call" | custom-call | flops 1 | bytes 1 | tf_op jit(solution)/shard_map/attend_back/pallas_call | solution.py:479
  296.0 21.4 %collective-permute-done.17.refs_2_ = bf16[256,1280]{1,0:T(8,128)(2,1)} collective-permute-done((bf16[256,1280]{1,0:T(8,128)(2,1)}, bf16[256,1280]{1,0:T(8,128)(2,1)}, u32[]{:S(2)}, u32[]{:S(2)}) %collective-permute-start.17) | collective-permute-done | bytes 655392 | tf_op jit(solution)/shard_map/ppermute | solution.py:622
  317.5 12.2 %head_grad.2 = (bf16[480,640]{1,0:T(8,128)(2,1)}, bf16[480,640]{1,0:T(8,128)(2,1)}, bf16[480,640]{1,0:T(8,128)(2,1)}, bf16[480,640]{1,0:T(8,128)(2,1)}) custom-call(s32[3]{0:T(128)} %pad_add_fusion.2.place_ref, bf16[960,2048]{1,0:T(8,128)(2,1)} %get-tuple-element.122.grads_ref.refs_0_, bf16[2,2048,640]{2,1,0:T(8,128)(2,1)} %get-tuple-element.107.normed_ref), custom_call_target="tpu_custom_call" | custom-call | flops 1 | bytes 1 | tf_op jit(solution)/shard_map/head_grad/pallas_call | solution.py:209
  333.4 27.0 %attend_back.3 = (bf16[960,2048]{1,0:T(8,128)(2,1)}, f32[80,1]{1,0:T(8,128)}) custom-call(s32[5,8]{1,0:T(8,128)} %stack.83.table, bf16[8,3,2048,80]{3,2,1,0:T(8,128)(2,1)} %get-tuple-element.85.qkv_ref, bf16[640,2048]{1,0:T(8,128)(2,1)} %get-tuple-element.86.att_ref, bf16[640,2048]{1,0:T(8,128)(2,1)} %pad_maximum_fusion.grad_ref, ...), custom_call_target="tpu_custom_call" | custom-call | flops 1 | bytes 1 | tf_op jit(solution)/shard_map/attend_back/pallas_call | solution.py:479
  366.3 12.2 %head_grad.3 = (bf16[480,640]{1,0:T(8,128)(2,1)}, bf16[480,640]{1,0:T(8,128)(2,1)}, bf16[480,640]{1,0:T(8,128)(2,1)}, bf16[480,640]{1,0:T(8,128)(2,1)}) custom-call(s32[3]{0:T(128)} %pad_add_fusion.2.place_ref, bf16[960,2048]{1,0:T(8,128)(2,1)} %get-tuple-element.123.grads_ref.refs_1_, bf16[2,2048,640]{2,1,0:T(8,128)(2,1)} %get-tuple-element.107.normed_ref), custom_call_target="tpu_custom_call" | custom-call | flops 1 | bytes 1 | tf_op jit(solution)/shard_map/head_grad/pallas_call | solution.py:209
  379.4 9.9 %input_side.2 = bf16[1024,1280]{1,0:T(8,128)(2,1)} custom-call(bf16[960,2048]{1,0:T(8,128)(2,1)} %get-tuple-element.122.grads_ref.refs_0_, bf16[960,2048]{1,0:T(8,128)(2,1)} %get-tuple-element.123.grads_ref.refs_1_, bf16[1280,1920]{1,0:T(8,128)(2,1)} %bitcast.215), custom_call_target="tpu_custom_call" | custom-call | flops 10066329600 | bytes 1 | tf_op jit(solution)/shard_map/input_side/pallas_call | solution.py:525
  389.3 10.0 %input_side.3 = bf16[1024,1280]{1,0:T(8,128)(2,1)} custom-call(bf16[960,2048]{1,0:T(8,128)(2,1)} %get-tuple-element.122.grads_ref.refs_0_, bf16[960,2048]{1,0:T(8,128)(2,1)} %get-tuple-element.123.grads_ref.refs_1_, bf16[1280,1920]{1,0:T(8,128)(2,1)} %bitcast.216), custom_call_target="tpu_custom_call" | custom-call | flops 10066329600 | bytes 1 | tf_op jit(solution)/shard_map/input_side/pallas_call | solution.py:525
  404.4 10.0 %collective-permute-done.41 = bf16[480,640]{1,0:T(8,128)(2,1)S(1)} collective-permute-done((bf16[480,640]{1,0:T(8,128)(2,1)S(1)}, bf16[480,640]{1,0:T(8,128)(2,1)S(1)}, u32[]{:S(2)}, u32[]{:S(2)}) %collective-permute-start.41) | collective-permute-done | bytes 614432 | tf_op jit(solution)/shard_map/ppermute | solution.py:801
  414.5 13.2 %collective-permute-done.43 = bf16[480,640]{1,0:T(8,128)(2,1)S(1)} collective-permute-done((bf16[480,640]{1,0:T(8,128)(2,1)}, bf16[480,640]{1,0:T(8,128)(2,1)S(1)}, u32[]{:S(2)}, u32[]{:S(2)}) %collective-permute-start.43) | collective-permute-done | bytes 614432 | tf_op jit(solution)/shard_map/ppermute | solution.py:801
  432.3 2.7 fusion.8
  435.0 2.7 fusion.5
  445.5 8.4 %collective-permute-done.58 = bf16[120,1280]{1,0:T(8,128)(2,1)S(1)} collective-permute-done((bf16[120,1280]{1,0:T(8,128)(2,1)S(1)}, bf16[120,1280]{1,0:T(8,128)(2,1)S(1)}, u32[]{:S(2)}, u32[]{:S(2)}) %collective-permute-start.58) | collective-permute-done | bytes 307232 | tf_op jit(solution)/shard_map/ppermute | solution.py:553
  455.2 6.0 collective-permute-start.59
  461.4 12.3 %collective-permute-done.50 = bf16[480,640]{1,0:T(8,128)(2,1)S(1)} collective-permute-done((bf16[480,640]{1,0:T(8,128)(2,1)S(1)}, bf16[480,640]{1,0:T(8,128)(2,1)S(1)}, u32[]{:S(2)}, u32[]{:S(2)}) %collective-permute-start.50) | collective-permute-done | bytes 614432 | tf_op jit(solution)/shard_map/ppermute | solution.py:553
  473.7 15.4 %collective-permute-start.45 = (bf16[240,640]{1,0:T(8,128)(2,1)S(1)}, bf16[240,640]{1,0:T(8,128)(2,1)S(1)}, u32[]{:S(2)}, u32[]{:S(2)}) collective-permute-start(bf16[240,640]{1,0:T(8,128)(2,1)S(1)} %dynamic-slice_bitcast_fusion.19), channel_id=1, source_target_pairs={{0,2},{1,3},{2,0},{3,1},{4,6},{5,7},{6,4},{7,5},{8,10},{9,11},{10,... | collective-permute-start | bytes 921608 | tf_op jit(solution)/shard_map/ppermute | solution.py:553
  489.3 19.9 %collective-permute-done.59 = bf16[120,1280]{1,0:T(8,128)(2,1)S(1)} collective-permute-done((bf16[120,1280]{1,0:T(8,128)(2,1)S(1)}, bf16[120,1280]{1,0:T(8,128)(2,1)S(1)}, u32[]{:S(2)}, u32[]{:S(2)}) %collective-permute-start.59) | collective-permute-done | bytes 307232 | tf_op jit(solution)/shard_map/ppermute | solution.py:560
  511.0 6.5 %collective-permute-done.51 = bf16[240,640]{1,0:T(8,128)(2,1)S(1)} collective-permute-done((bf16[240,640]{1,0:T(8,128)(2,1)S(1)}, bf16[240,640]{1,0:T(8,128)(2,1)S(1)}, u32[]{:S(2)}, u32[]{:S(2)}) %collective-permute-start.51) | collective-permute-done | bytes 307232 | tf_op jit(solution)/shard_map/ppermute | solution.py:553
  517.5 2.9 collective-permute-start.46
  520.5 11.5 %collective-permute-done.46 = bf16[120,640]{1,0:T(8,128)(2,1)S(1)} collective-permute-done((bf16[120,640]{1,0:T(8,128)(2,1)S(1)}, bf16[120,640]{1,0:T(8,128)(2,1)S(1)}, u32[]{:S(2)}, u32[]{:S(2)}) %collective-permute-start.46) | collective-permute-done | bytes 153632 | tf_op jit(solution)/shard_map/ppermute | solution.py:553
  532.0 3.1 collective-permute-start.52
  535.2 7.0 %collective-permute-done.52 = bf16[120,640]{1,0:T(8,128)(2,1)S(1)} collective-permute-done((bf16[120,640]{1,0:T(8,128)(2,1)S(1)}, bf16[120,640]{1,0:T(8,128)(2,1)S(1)}, u32[]{:S(2)}, u32[]{:S(2)}) %collective-permute-start.52) | collective-permute-done | bytes 153632 | tf_op jit(solution)/shard_map/ppermute | solution.py:553
  542.3 9.8 %collective-permute-done.47 = bf16[120,640]{1,0:T(8,128)(2,1)S(1)} collective-permute-done((bf16[120,640]{1,0:T(8,128)(2,1)S(1)}, bf16[120,640]{1,0:T(8,128)(2,1)S(1)}, u32[]{:S(2)}, u32[]{:S(2)}) %collective-permute-start.47) | collective-permute-done | bytes 153632 | tf_op jit(solution)/shard_map/ppermute | solution.py:560
  552.7 7.6 %collective-permute-done.53 = bf16[120,640]{1,0:T(8,128)(2,1)S(1)} collective-permute-done((bf16[120,640]{1,0:T(8,128)(2,1)S(1)}, bf16[120,640]{1,0:T(8,128)(2,1)S(1)}, u32[]{:S(2)}, u32[]{:S(2)}) %collective-permute-start.53) | collective-permute-done | bytes 153632 | tf_op jit(solution)/shard_map/ppermute | solution.py:560
  565.4 23.5 %collective-permute-done.33 = f32[5200]{0:T(1024)S(1)} collective-permute-done((f32[5200]{0:T(1024)S(1)}, f32[5200]{0:T(1024)S(1)}, u32[]{:S(2)}, u32[]{:S(2)}) %collective-permute-start.33) | collective-permute-done | bytes 20832 | tf_op jit(solution)/shard_map/ppermute | solution.py:579
  592.0 5.4 collective-permute-start.28
  597.5 17.1 %collective-permute-start.27 = (bf16[256,1280]{1,0:T(8,128)(2,1)S(1)}, bf16[256,1280]{1,0:T(8,128)(2,1)}, u32[]{:S(2)}, u32[]{:S(2)}) collective-permute-start(bf16[256,1280]{1,0:T(8,128)(2,1)S(1)} %get-tuple-element.168), channel_id=1, source_target_pairs={{0,0},{8,1},{2,2},{10,3},{4,4},{12,5},{6,6},{14,7},{1,8},{9,9},{3,... | collective-permute-start | bytes 1966088 | tf_op jit(solution)/shard_map/ppermute | solution.py:622
  615.2 3.7 join.12
  620.1 2.7 maximum_select_fusion.1.refs_0_
  622.8 2.7 maximum_select_fusion.2.refs_1_
  625.5 4.5 collective-permute-done.27.refs_0_
  630.0 4.5 join.13
  634.5 5.4 unfold.1
  642.1 2.4 fusion.36
  (301 shorter events, 93.3 us)
Async XLA Ops:
  12.4 31.3 %collective-permute-start.6 = (bf16[336,1920]{1,0:T(8,128)(2,1)}, bf16[336,1920]{1,0:T(8,128)(2,1)S(1)}, u32[]{:S(2)}, u32[]{:S(2)}) collective-permute-start(bf16[336,1920]{1,0:T(8,128)(2,1)} %get-tuple-element.185), channel_id=1, source_target_pairs={{0,24},{8,16},{16,8},{24,0},{1,25},{9,17},{17,9},{25,1},{2,26},{10... | collective-permute-start | bytes 3870728 | tf_op jit(solution)/shard_map/ppermute | solution.py:644
  14.2 10.2 %collective-permute-start = (bf16[336,1920]{1,0:T(8,128)(2,1)}, bf16[336,1920]{1,0:T(8,128)(2,1)}, u32[]{:S(2)}, u32[]{:S(2)}) collective-permute-start(bf16[336,1920]{1,0:T(8,128)(2,1)} %get-tuple-element.185), channel_id=1, source_target_pairs={{0,8},{8,0},{16,24},{24,16},{1,9},{9,1},{17,25},{25,17},{2,10},{10... | collective-permute-start | bytes 3870728 | tf_op jit(solution)/shard_map/ppermute | solution.py:646
  14.2 5.6 collective-permute-start.7
  14.7 56.5 %collective-permute-start.5 = (bf16[336,1920]{1,0:T(8,128)(2,1)S(1)}, bf16[336,1920]{1,0:T(8,128)(2,1)}, u32[]{:S(2)}, u32[]{:S(2)}) collective-permute-start(bf16[336,1920]{1,0:T(8,128)(2,1)S(1)} %get-tuple-element.186.refs_0_), channel_id=1, source_target_pairs={{0,16},{8,24},{16,0},{24,8},{1,17},{9,25},{17,1},{25,9},{2,18},{10... | collective-permute-start | bytes 3870728 | tf_op jit(solution)/shard_map/ppermute | solution.py:644
  17.1 60.5 %collective-permute-start.4 = (bf16[256,1280]{1,0:T(8,128)(2,1)}, bf16[256,1280]{1,0:T(8,128)(2,1)}, u32[]{:S(2)}, u32[]{:S(2)}) collective-permute-start(bf16[256,1280]{1,0:T(8,128)(2,1)} %get-tuple-element.181), channel_id=1, source_target_pairs={{0,6},{1,14},{2,0},{3,8},{4,2},{5,10},{6,4},{7,12},{8,7},{9,15},{1... | collective-permute-start | bytes 1966088 | tf_op jit(solution)/shard_map/ppermute | solution.py:614
  19.8 57.8 %collective-permute-start.3 = (bf16[256,1280]{1,0:T(8,128)(2,1)S(1)}, bf16[256,1280]{1,0:T(8,128)(2,1)}, u32[]{:S(2)}, u32[]{:S(2)}) collective-permute-start(bf16[256,1280]{1,0:T(8,128)(2,1)S(1)} %get-tuple-element.182), channel_id=1, source_target_pairs={{0,4},{1,12},{2,6},{3,14},{4,0},{5,8},{6,2},{7,10},{8,5},{9,13},{1... | collective-permute-start | bytes 1966088 | tf_op jit(solution)/shard_map/ppermute | solution.py:614
  23.9 53.6 %copy-start.28 = (s32[8,256]{1,0:T(8,128)}, s32[8,256]{1,0:T(8,128)S(1)}, u32[]{:S(2)}) copy-start(s32[8,256]{1,0:T(8,128)S(1)} %reshape.562.start_ref) | copy-start | bytes 24580
  26.8 50.8 %collective-permute-start.2 = (bf16[256,1280]{1,0:T(8,128)(2,1)}, bf16[256,1280]{1,0:T(8,128)(2,1)}, u32[]{:S(2)}, u32[]{:S(2)}) collective-permute-start(bf16[256,1280]{1,0:T(8,128)(2,1)} %get-tuple-element.183), channel_id=1, source_target_pairs={{0,2},{1,10},{2,4},{3,12},{4,6},{5,14},{6,0},{7,8},{8,3},{9,11},{1... | collective-permute-start | bytes 1966088 | tf_op jit(solution)/shard_map/ppermute | solution.py:614
  43.7 33.9 %collective-permute-start.1 = (bf16[256,1280]{1,0:T(8,128)(2,1)}, bf16[256,1280]{1,0:T(8,128)(2,1)}, u32[]{:S(2)}, u32[]{:S(2)}) collective-permute-start(bf16[256,1280]{1,0:T(8,128)(2,1)} %get-tuple-element.184), channel_id=1, source_target_pairs={{0,0},{1,8},{2,2},{3,10},{4,4},{5,12},{6,6},{7,14},{8,1},{9,9},{10... | collective-permute-start | bytes 1966088 | tf_op jit(solution)/shard_map/ppermute | solution.py:614
  82.0 10.3 %collective-permute-start.8 = (bf16[1024,1280]{1,0:T(8,128)(2,1)}, bf16[1024,1280]{1,0:T(8,128)(2,1)S(1)}, u32[]{:S(2)}, u32[]{:S(2)}) collective-permute-start(bf16[1024,1280]{1,0:T(8,128)(2,1)} %bitcast.198), channel_id=1, source_target_pairs={{0,8},{1,9},{2,10},{3,11},{4,12},{5,13},{6,14},{7,15},{8,0},{9,1},... | collective-permute-start | bytes 7864328 | tf_op jit(solution)/shard_map/ppermute | solution.py:688
  85.7 76.9 %collective-permute-start.12 = (bf16[960,1280]{1,0:T(8,128)(2,1)}, bf16[960,1280]{1,0:T(8,128)(2,1)}, u32[]{:S(2)}, u32[]{:S(2)}) collective-permute-start(bf16[960,1280]{1,0:T(8,128)(2,1)} %pad_maximum_fusion.1.refs_0_), channel_id=1, source_target_pairs={{0,16},{8,24},{16,0},{24,8},{1,17},{9,25},{17,1},{25,9},{2,18},{10... | collective-permute-start | bytes 7372808 | tf_op jit(solution)/shard_map/ppermute | solution.py:660
  88.8 24.7 %collective-permute-start.10 = (bf16[256,1280]{1,0:T(8,128)(2,1)}, bf16[256,1280]{1,0:T(8,128)(2,1)}, u32[]{:S(2)}, u32[]{:S(2)}) collective-permute-start(bf16[256,1280]{1,0:T(8,128)(2,1)} %get-tuple-element.173), channel_id=1, source_target_pairs={{0,6},{1,14},{2,0},{3,8},{4,2},{5,10},{6,4},{7,12},{8,7},{9,15},{1... | collective-permute-start | bytes 1966088 | tf_op jit(solution)/shard_map/ppermute | solution.py:614
  91.4 45.0 %collective-permute-start.9 = (bf16[256,1280]{1,0:T(8,128)(2,1)}, bf16[256,1280]{1,0:T(8,128)(2,1)}, u32[]{:S(2)}, u32[]{:S(2)}) collective-permute-start(bf16[256,1280]{1,0:T(8,128)(2,1)} %get-tuple-element.174), channel_id=1, source_target_pairs={{0,4},{1,12},{2,6},{3,14},{4,0},{5,8},{6,2},{7,10},{8,5},{9,13},{1... | collective-permute-start | bytes 1966088 | tf_op jit(solution)/shard_map/ppermute | solution.py:614
  162.7 15.1 %collective-permute-start.13 = (bf16[960,1280]{1,0:T(8,128)(2,1)}, bf16[960,1280]{1,0:T(8,128)(2,1)}, u32[]{:S(2)}, u32[]{:S(2)}) collective-permute-start(bf16[960,1280]{1,0:T(8,128)(2,1)} %pad_maximum_fusion.1.refs_0_), channel_id=1, source_target_pairs={{0,8},{8,0},{16,24},{24,16},{1,9},{9,1},{17,25},{25,17},{2,10},{10... | collective-permute-start | bytes 7372808 | tf_op jit(solution)/shard_map/ppermute | solution.py:696
  163.3 14.5 %collective-permute-start.14 = (bf16[960,1280]{1,0:T(8,128)(2,1)}, bf16[960,1280]{1,0:T(8,128)(2,1)}, u32[]{:S(2)}, u32[]{:S(2)}) collective-permute-start(bf16[960,1280]{1,0:T(8,128)(2,1)} %collective-permute-done.12.refs_1_), channel_id=1, source_target_pairs={{0,8},{8,0},{16,24},{24,16},{1,9},{9,1},{17,25},{25,17},{2,10},{10... | collective-permute-start | bytes 7372808 | tf_op jit(solution)/shard_map/ppermute | solution.py:696
  166.4 6.8 %collective-permute-start.11 = (bf16[640,1024]{1,0:T(8,128)(2,1)S(1)}, bf16[640,1024]{1,0:T(8,128)(2,1)S(1)}, u32[]{:S(2)}, u32[]{:S(2)}) collective-permute-start(bf16[640,1024]{1,0:T(8,128)(2,1)S(1)} %get-tuple-element.179), channel_id=1, source_target_pairs={{0,8},{1,9},{2,10},{3,11},{4,12},{5,13},{6,14},{7,15},{8,0},{9,1},... | collective-permute-start | bytes 3932168 | tf_op jit(solution)/shard_map/ppermute | solution.py:709
  168.3 33.3 %collective-permute-start.20 = (bf16[256,1280]{1,0:T(8,128)(2,1)}, bf16[256,1280]{1,0:T(8,128)(2,1)S(1)}, u32[]{:S(2)}, u32[]{:S(2)}) collective-permute-start(bf16[256,1280]{1,0:T(8,128)(2,1)} %get-tuple-element.171), channel_id=1, source_target_pairs={{0,2},{1,10},{2,4},{3,12},{4,6},{5,14},{6,0},{7,8},{8,3},{9,11},{1... | collective-permute-start | bytes 1966088 | tf_op jit(solution)/shard_map/ppermute | solution.py:614
  168.3 33.3 %collective-permute-start.19 = (bf16[256,1280]{1,0:T(8,128)(2,1)S(1)}, bf16[256,1280]{1,0:T(8,128)(2,1)S(1)}, u32[]{:S(2)}, u32[]{:S(2)}) collective-permute-start(bf16[256,1280]{1,0:T(8,128)(2,1)S(1)} %copy-done.19), channel_id=1, source_target_pairs={{0,0},{1,8},{2,2},{3,10},{4,4},{5,12},{6,6},{7,14},{8,1},{9,9},{10... | collective-permute-start | bytes 1966088 | tf_op jit(solution)/shard_map/ppermute | solution.py:614
  235.5 14.0 %collective-permute-start.22 = (bf16[2,320,1280]{2,1,0:T(8,128)(2,1)}, bf16[2,320,1280]{2,1,0:T(8,128)(2,1)}, u32[]{:S(2)}, u32[]{:S(2)}) collective-permute-start(bf16[2,320,1280]{2,1,0:T(8,128)(2,1)} %dynamic-slice_bitcast_fusion.2), channel_id=1, source_target_pairs={{0,8},{8,0},{16,24},{24,16},{1,9},{9,1},{17,25},{25,17},{2,10},{10... | collective-permute-start | bytes 4915208 | tf_op jit(solution)/shard_map/ppermute | solution.py:751
  242.3 9.9 %collective-permute-start.23 = (bf16[2,320,1280]{2,1,0:T(8,128)(2,1)S(1)}, bf16[2,320,1280]{2,1,0:T(8,128)(2,1)S(1)}, u32[]{:S(2)}, u32[]{:S(2)}) collective-permute-start(bf16[2,320,1280]{2,1,0:T(8,128)(2,1)S(1)} %dynamic-slice_bitcast_fusion.1), channel_id=1, source_target_pairs={{0,8},{8,0},{16,24},{24,16},{1,9},{9,1},{17,25},{25,17},{2,10},{10... | collective-permute-start | bytes 4915208 | tf_op jit(solution)/shard_map/ppermute | solution.py:751
  242.6 11.0 %collective-permute-start.24 = (bf16[2,320,1280]{2,1,0:T(8,128)(2,1)S(1)}, bf16[2,320,1280]{2,1,0:T(8,128)(2,1)S(1)}, u32[]{:S(2)}, u32[]{:S(2)}) collective-permute-start(bf16[2,320,1280]{2,1,0:T(8,128)(2,1)S(1)} %dynamic-slice_bitcast_fusion), channel_id=1, source_target_pairs={{0,8},{8,0},{16,24},{24,16},{1,9},{9,1},{17,25},{25,17},{2,10},{10... | collective-permute-start | bytes 4915208 | tf_op jit(solution)/shard_map/ppermute | solution.py:751
  249.3 12.4 %collective-permute-start.21 = (bf16[640,1024]{1,0:T(8,128)(2,1)S(1)}, bf16[640,1024]{1,0:T(8,128)(2,1)}, u32[]{:S(2)}, u32[]{:S(2)}) collective-permute-start(bf16[640,1024]{1,0:T(8,128)(2,1)S(1)} %get-tuple-element.170), channel_id=1, source_target_pairs={{0,8},{1,9},{2,10},{3,11},{4,12},{5,13},{6,14},{7,15},{8,0},{9,1},... | collective-permute-start | bytes 3932168 | tf_op jit(solution)/shard_map/ppermute | solution.py:743
  256.5 105.7 %collective-permute-start.25 = (bf16[960,1280]{1,0:T(8,128)(2,1)}, bf16[960,1280]{1,0:T(8,128)(2,1)}, u32[]{:S(2)}, u32[]{:S(2)}) collective-permute-start(bf16[960,1280]{1,0:T(8,128)(2,1)} %pad_maximum_fusion.3), channel_id=1, source_target_pairs={{0,16},{8,24},{16,0},{24,8},{1,17},{9,25},{17,1},{25,9},{2,18},{10... | collective-permute-start | bytes 7372808 | tf_op jit(solution)/shard_map/ppermute | solution.py:770
  259.1 37.0 %collective-permute-start.18 = (bf16[256,1280]{1,0:T(8,128)(2,1)}, bf16[256,1280]{1,0:T(8,128)(2,1)}, u32[]{:S(2)}, u32[]{:S(2)}) collective-permute-start(bf16[256,1280]{1,0:T(8,128)(2,1)} %get-tuple-element.175), channel_id=1, source_target_pairs={{6,0},{14,1},{0,2},{8,3},{2,4},{10,5},{4,6},{12,7},{7,8},{15,9},{1... | collective-permute-start | bytes 1966088 | tf_op jit(solution)/shard_map/ppermute | solution.py:622
  259.1 58.4 %collective-permute-start.17 = (bf16[256,1280]{1,0:T(8,128)(2,1)}, bf16[256,1280]{1,0:T(8,128)(2,1)}, u32[]{:S(2)}, u32[]{:S(2)}) collective-permute-start(bf16[256,1280]{1,0:T(8,128)(2,1)} %get-tuple-element.176), channel_id=1, source_target_pairs={{4,0},{12,1},{6,2},{14,3},{0,4},{8,5},{2,6},{10,7},{5,8},{13,9},{7... | collective-permute-start | bytes 1966088 | tf_op jit(solution)/shard_map/ppermute | solution.py:622
  261.0 56.5 %collective-permute-start.16 = (bf16[256,1280]{1,0:T(8,128)(2,1)}, bf16[256,1280]{1,0:T(8,128)(2,1)}, u32[]{:S(2)}, u32[]{:S(2)}) collective-permute-start(bf16[256,1280]{1,0:T(8,128)(2,1)} %get-tuple-element.177), channel_id=1, source_target_pairs={{2,0},{10,1},{4,2},{12,3},{6,4},{14,5},{0,6},{8,7},{3,8},{11,9},{5... | collective-permute-start | bytes 1966088 | tf_op jit(solution)/shard_map/ppermute | solution.py:622
  261.7 55.8 %collective-permute-start.15 = (bf16[256,1280]{1,0:T(8,128)(2,1)}, bf16[256,1280]{1,0:T(8,128)(2,1)}, u32[]{:S(2)}, u32[]{:S(2)}) collective-permute-start(bf16[256,1280]{1,0:T(8,128)(2,1)} %get-tuple-element.178), channel_id=1, source_target_pairs={{0,0},{8,1},{2,2},{10,3},{4,4},{12,5},{6,6},{14,7},{1,8},{9,9},{3,... | collective-permute-start | bytes 1966088 | tf_op jit(solution)/shard_map/ppermute | solution.py:622
  329.7 31.6 %collective-permute-start.38 = (bf16[480,640]{1,0:T(8,128)(2,1)}, bf16[480,640]{1,0:T(8,128)(2,1)}, u32[]{:S(2)}, u32[]{:S(2)}) collective-permute-start(bf16[480,640]{1,0:T(8,128)(2,1)} %get-tuple-element.109), channel_id=1, source_target_pairs={{0,8},{8,0},{16,24},{24,16},{1,9},{9,1},{17,25},{25,17},{2,10},{10... | collective-permute-start | bytes 1843208 | tf_op jit(solution)/shard_map/ppermute | solution.py:798
  331.8 67.5 %collective-permute-start.36 = (bf16[480,640]{1,0:T(8,128)(2,1)}, bf16[480,640]{1,0:T(8,128)(2,1)S(1)}, u32[]{:S(2)}, u32[]{:S(2)}) collective-permute-start(bf16[480,640]{1,0:T(8,128)(2,1)} %get-tuple-element.108), channel_id=1, source_target_pairs={{0,8},{8,0},{16,24},{24,16},{1,9},{9,1},{17,25},{25,17},{2,10},{10... | collective-permute-start | bytes 1843208 | tf_op jit(solution)/shard_map/ppermute | solution.py:798
  332.8 66.6 %collective-permute-start.37 = (bf16[480,640]{1,0:T(8,128)(2,1)}, bf16[480,640]{1,0:T(8,128)(2,1)}, u32[]{:S(2)}, u32[]{:S(2)}) collective-permute-start(bf16[480,640]{1,0:T(8,128)(2,1)} %get-tuple-element.111), channel_id=1, source_target_pairs={{0,16},{8,24},{16,0},{24,8},{1,17},{9,25},{17,1},{25,9},{2,18},{10... | collective-permute-start | bytes 1843208 | tf_op jit(solution)/shard_map/ppermute | solution.py:801
  361.3 43.0 %collective-permute-start.39 = (bf16[480,640]{1,0:T(8,128)(2,1)}, bf16[480,640]{1,0:T(8,128)(2,1)}, u32[]{:S(2)}, u32[]{:S(2)}) collective-permute-start(bf16[480,640]{1,0:T(8,128)(2,1)} %collective-permute-done.38), channel_id=1, source_target_pairs={{0,16},{8,24},{16,0},{24,8},{1,17},{9,25},{17,1},{25,9},{2,18},{10... | collective-permute-start | bytes 1843208 | tf_op jit(solution)/shard_map/ppermute | solution.py:801
  365.6 34.3 %collective-permute-start.56 = (bf16[480,1280]{1,0:T(8,128)(2,1)}, bf16[480,1280]{1,0:T(8,128)(2,1)S(1)}, u32[]{:S(2)}, u32[]{:S(2)}) collective-permute-start(bf16[480,1280]{1,0:T(8,128)(2,1)} %dynamic-slice_bitcast_fusion.5), channel_id=1, source_target_pairs={{0,1},{1,0},{2,3},{3,2},{4,5},{5,4},{6,7},{7,6},{8,9},{9,8},{10,11... | collective-permute-start | bytes 3686408 | tf_op jit(solution)/shard_map/ppermute | solution.py:553
  378.5 21.0 %collective-permute-start.42 = (bf16[480,640]{1,0:T(8,128)(2,1)}, bf16[480,640]{1,0:T(8,128)(2,1)}, u32[]{:S(2)}, u32[]{:S(2)}) collective-permute-start(bf16[480,640]{1,0:T(8,128)(2,1)} %get-tuple-element.117), channel_id=1, source_target_pairs={{0,8},{8,0},{16,24},{24,16},{1,9},{9,1},{17,25},{25,17},{2,10},{10... | collective-permute-start | bytes 1843208 | tf_op jit(solution)/shard_map/ppermute | solution.py:798
  399.3 5.1 collective-permute-start.40
  399.4 15.1 %collective-permute-start.41 = (bf16[480,640]{1,0:T(8,128)(2,1)S(1)}, bf16[480,640]{1,0:T(8,128)(2,1)S(1)}, u32[]{:S(2)}, u32[]{:S(2)}) collective-permute-start(bf16[480,640]{1,0:T(8,128)(2,1)S(1)} %copy-done.38), channel_id=1, source_target_pairs={{0,16},{8,24},{16,0},{24,8},{1,17},{9,25},{17,1},{25,9},{2,18},{10... | collective-permute-start | bytes 1843208 | tf_op jit(solution)/shard_map/ppermute | solution.py:801
  399.5 31.6 %collective-permute-start.26 = (bf16[1024,1280]{1,0:T(8,128)(2,1)}, bf16[1024,1280]{1,0:T(8,128)(2,1)S(1)}, u32[]{:S(2)}, u32[]{:S(2)}) collective-permute-start(bf16[1024,1280]{1,0:T(8,128)(2,1)} %input_side.2), channel_id=1, source_target_pairs={{0,8},{1,9},{2,10},{3,11},{4,12},{5,13},{6,14},{7,15},{8,0},{9,1},... | collective-permute-start | bytes 7864328 | tf_op jit(solution)/shard_map/ppermute | solution.py:818
  401.0 26.6 %collective-permute-start.43 = (bf16[480,640]{1,0:T(8,128)(2,1)}, bf16[480,640]{1,0:T(8,128)(2,1)S(1)}, u32[]{:S(2)}, u32[]{:S(2)}) collective-permute-start(bf16[480,640]{1,0:T(8,128)(2,1)} %collective-permute-done.42), channel_id=1, source_target_pairs={{0,16},{8,24},{16,0},{24,8},{1,17},{9,25},{17,1},{25,9},{2,18},{10... | collective-permute-start | bytes 1843208 | tf_op jit(solution)/shard_map/ppermute | solution.py:801
  404.3 26.5 %collective-permute-start.57 = (bf16[240,1280]{1,0:T(8,128)(2,1)S(1)}, bf16[240,1280]{1,0:T(8,128)(2,1)S(1)}, u32[]{:S(2)}, u32[]{:S(2)}) collective-permute-start(bf16[240,1280]{1,0:T(8,128)(2,1)S(1)} %dynamic-slice_bitcast_fusion.14), channel_id=1, source_target_pairs={{0,2},{1,3},{2,0},{3,1},{4,6},{5,7},{6,4},{7,5},{8,10},{9,11},{10,... | collective-permute-start | bytes 1843208 | tf_op jit(solution)/shard_map/ppermute | solution.py:553
  438.7 15.2 %collective-permute-start.58 = (bf16[120,1280]{1,0:T(8,128)(2,1)S(1)}, bf16[120,1280]{1,0:T(8,128)(2,1)S(1)}, u32[]{:S(2)}, u32[]{:S(2)}) collective-permute-start(bf16[120,1280]{1,0:T(8,128)(2,1)S(1)} %dynamic-slice_bitcast_fusion.17), channel_id=1, source_target_pairs={{0,4},{1,5},{2,6},{3,7},{4,0},{5,1},{6,2},{7,3},{8,12},{9,13},{10,... | collective-permute-start | bytes 921608 | tf_op jit(solution)/shard_map/ppermute | solution.py:553
  439.0 16.2 %collective-permute-start.44 = (bf16[480,640]{1,0:T(8,128)(2,1)S(1)}, bf16[480,640]{1,0:T(8,128)(2,1)S(1)}, u32[]{:S(2)}, u32[]{:S(2)}) collective-permute-start(bf16[480,640]{1,0:T(8,128)(2,1)S(1)} %dynamic-slice_bitcast_fusion.16), channel_id=1, source_target_pairs={{0,1},{1,0},{2,3},{3,2},{4,5},{5,4},{6,7},{7,6},{8,9},{9,8},{10,11... | collective-permute-start | bytes 1843208 | tf_op jit(solution)/shard_map/ppermute | solution.py:553
  440.9 2.9 collective-permute-start.31
  442.9 30.9 %collective-permute-start.50 = (bf16[480,640]{1,0:T(8,128)(2,1)S(1)}, bf16[480,640]{1,0:T(8,128)(2,1)S(1)}, u32[]{:S(2)}, u32[]{:S(2)}) collective-permute-start(bf16[480,640]{1,0:T(8,128)(2,1)S(1)} %dynamic-slice_bitcast_fusion.15), channel_id=1, source_target_pairs={{0,1},{1,0},{2,3},{3,2},{4,5},{5,4},{6,7},{7,6},{8,9},{9,8},{10,11... | collective-permute-start | bytes 1843208 | tf_op jit(solution)/shard_map/ppermute | solution.py:553
  443.0 121.9 %collective-permute-start.30 = (bf16[256,1280]{1,0:T(8,128)(2,1)S(1)}, bf16[256,1280]{1,0:T(8,128)(2,1)S(1)}, u32[]{:S(2)}, u32[]{:S(2)}) collective-permute-start(bf16[256,1280]{1,0:T(8,128)(2,1)S(1)} %get-tuple-element.165), channel_id=1, source_target_pairs={{6,0},{14,1},{0,2},{8,3},{2,4},{10,5},{4,6},{12,7},{7,8},{15,9},{1... | collective-permute-start | bytes 1966088 | tf_op jit(solution)/shard_map/ppermute | solution.py:622
  443.8 121.1 %collective-permute-start.29 = (bf16[256,1280]{1,0:T(8,128)(2,1)S(1)}, bf16[256,1280]{1,0:T(8,128)(2,1)S(1)}, u32[]{:S(2)}, u32[]{:S(2)}) collective-permute-start(bf16[256,1280]{1,0:T(8,128)(2,1)S(1)} %get-tuple-element.166), channel_id=1, source_target_pairs={{4,0},{12,1},{6,2},{14,3},{0,4},{8,5},{2,6},{10,7},{5,8},{13,9},{7... | collective-permute-start | bytes 1966088 | tf_op jit(solution)/shard_map/ppermute | solution.py:622
  453.9 107.4 %collective-permute-start.32 = (f32[5200]{0:T(1024)S(1)}, f32[5200]{0:T(1024)S(1)}, u32[]{:S(2)}, u32[]{:S(2)}) collective-permute-start(f32[5200]{0:T(1024)S(1)} %add.571), channel_id=1, source_target_pairs={{0,16},{8,24},{16,0},{24,8},{1,17},{9,25},{17,1},{25,9},{2,18},{10... | collective-permute-start | bytes 62408 | tf_op jit(solution)/shard_map/ppermute | solution.py:577
  455.2 54.0 %collective-permute-start.59 = (bf16[120,1280]{1,0:T(8,128)(2,1)S(1)}, bf16[120,1280]{1,0:T(8,128)(2,1)S(1)}, u32[]{:S(2)}, u32[]{:S(2)}) collective-permute-start(bf16[120,1280]{1,0:T(8,128)(2,1)S(1)} %fusion.23), channel_id=1, source_target_pairs={{0,4},{1,5},{2,6},{3,7},{4,0},{5,1},{6,2},{7,3},{8,12},{9,13},{10,... | collective-permute-start | bytes 921608 | tf_op jit(solution)/shard_map/ppermute | solution.py:560
  473.7 35.6 %collective-permute-start.45 = (bf16[240,640]{1,0:T(8,128)(2,1)S(1)}, bf16[240,640]{1,0:T(8,128)(2,1)S(1)}, u32[]{:S(2)}, u32[]{:S(2)}) collective-permute-start(bf16[240,640]{1,0:T(8,128)(2,1)S(1)} %dynamic-slice_bitcast_fusion.19), channel_id=1, source_target_pairs={{0,2},{1,3},{2,0},{3,1},{4,6},{5,7},{6,4},{7,5},{8,10},{9,11},{10,... | collective-permute-start | bytes 921608 | tf_op jit(solution)/shard_map/ppermute | solution.py:553
  509.2 8.3 %collective-permute-start.51 = (bf16[240,640]{1,0:T(8,128)(2,1)S(1)}, bf16[240,640]{1,0:T(8,128)(2,1)S(1)}, u32[]{:S(2)}, u32[]{:S(2)}) collective-permute-start(bf16[240,640]{1,0:T(8,128)(2,1)S(1)} %dynamic-slice_bitcast_fusion.18), channel_id=1, source_target_pairs={{0,2},{1,3},{2,0},{3,1},{4,6},{5,7},{6,4},{7,5},{8,10},{9,11},{10,... | collective-permute-start | bytes 921608 | tf_op jit(solution)/shard_map/ppermute | solution.py:553
  509.3 42.8 %collective-permute-start.60 = (bf16[240,1280]{1,0:T(8,128)(2,1)S(1)}, bf16[240,1280]{1,0:T(8,128)(2,1)S(1)}, u32[]{:S(2)}, u32[]{:S(2)}) collective-permute-start(bf16[240,1280]{1,0:T(8,128)(2,1)S(1)} %maximum_select_fusion.6), channel_id=1, source_target_pairs={{0,2},{1,3},{2,0},{3,1},{4,6},{5,7},{6,4},{7,5},{8,10},{9,11},{10,... | collective-permute-start | bytes 1843208 | tf_op jit(solution)/shard_map/ppermute | solution.py:560
  517.5 14.5 %collective-permute-start.46 = (bf16[120,640]{1,0:T(8,128)(2,1)S(1)}, bf16[120,640]{1,0:T(8,128)(2,1)S(1)}, u32[]{:S(2)}, u32[]{:S(2)}) collective-permute-start(bf16[120,640]{1,0:T(8,128)(2,1)S(1)} %dynamic-slice_bitcast_fusion.21), channel_id=1, source_target_pairs={{0,4},{1,5},{2,6},{3,7},{4,0},{5,1},{6,2},{7,3},{8,12},{9,13},{10,... | collective-permute-start | bytes 460808 | tf_op jit(solution)/shard_map/ppermute | solution.py:553
  532.0 10.2 %collective-permute-start.52 = (bf16[120,640]{1,0:T(8,128)(2,1)S(1)}, bf16[120,640]{1,0:T(8,128)(2,1)S(1)}, u32[]{:S(2)}, u32[]{:S(2)}) collective-permute-start(bf16[120,640]{1,0:T(8,128)(2,1)S(1)} %dynamic-slice_bitcast_fusion.20), channel_id=1, source_target_pairs={{0,4},{1,5},{2,6},{3,7},{4,0},{5,1},{6,2},{7,3},{8,12},{9,13},{10,... | collective-permute-start | bytes 460808 | tf_op jit(solution)/shard_map/ppermute | solution.py:553
  542.2 9.8 %collective-permute-start.47 = (bf16[120,640]{1,0:T(8,128)(2,1)S(1)}, bf16[120,640]{1,0:T(8,128)(2,1)S(1)}, u32[]{:S(2)}, u32[]{:S(2)}) collective-permute-start(bf16[120,640]{1,0:T(8,128)(2,1)S(1)} %fusion.27), channel_id=1, source_target_pairs={{0,4},{1,5},{2,6},{3,7},{4,0},{5,1},{6,2},{7,3},{8,12},{9,13},{10,... | collective-permute-start | bytes 460808 | tf_op jit(solution)/shard_map/ppermute | solution.py:560
  552.1 8.2 %collective-permute-start.53 = (bf16[120,640]{1,0:T(8,128)(2,1)S(1)}, bf16[120,640]{1,0:T(8,128)(2,1)S(1)}, u32[]{:S(2)}, u32[]{:S(2)}) collective-permute-start(bf16[120,640]{1,0:T(8,128)(2,1)S(1)} %fusion.26), channel_id=1, source_target_pairs={{0,4},{1,5},{2,6},{3,7},{4,0},{5,1},{6,2},{7,3},{8,12},{9,13},{10,... | collective-permute-start | bytes 460808 | tf_op jit(solution)/shard_map/ppermute | solution.py:560
  552.2 11.5 %collective-permute-start.48 = (bf16[240,640]{1,0:T(8,128)(2,1)S(1)}, bf16[240,640]{1,0:T(8,128)(2,1)S(1)}, u32[]{:S(2)}, u32[]{:S(2)}) collective-permute-start(bf16[240,640]{1,0:T(8,128)(2,1)S(1)} %maximum_select_fusion.7), channel_id=1, source_target_pairs={{0,2},{1,3},{2,0},{3,1},{4,6},{5,7},{6,4},{7,5},{8,10},{9,11},{10,... | collective-permute-start | bytes 921608 | tf_op jit(solution)/shard_map/ppermute | solution.py:560
  560.3 79.7 %collective-permute-start.61 = (bf16[480,1280]{1,0:T(8,128)(2,1)S(1)}, bf16[480,1280]{1,0:T(8,128)(2,1)}, u32[]{:S(2)}, u32[]{:S(2)}) collective-permute-start(bf16[480,1280]{1,0:T(8,128)(2,1)S(1)} %maximum_select_fusion.3), channel_id=1, source_target_pairs={{0,1},{1,0},{2,3},{3,2},{4,5},{5,4},{6,7},{7,6},{8,9},{9,8},{10,11... | collective-permute-start | bytes 3686408 | tf_op jit(solution)/shard_map/ppermute | solution.py:560
  561.3 27.7 %collective-permute-start.54 = (bf16[240,640]{1,0:T(8,128)(2,1)S(1)}, bf16[240,640]{1,0:T(8,128)(2,1)S(1)}, u32[]{:S(2)}, u32[]{:S(2)}) collective-permute-start(bf16[240,640]{1,0:T(8,128)(2,1)S(1)} %maximum_select_fusion.8), channel_id=1, source_target_pairs={{0,2},{1,3},{2,0},{3,1},{4,6},{5,7},{6,4},{7,5},{8,10},{9,11},{10,... | collective-permute-start | bytes 921608 | tf_op jit(solution)/shard_map/ppermute | solution.py:560
  563.6 25.3 %collective-permute-start.33 = (f32[5200]{0:T(1024)S(1)}, f32[5200]{0:T(1024)S(1)}, u32[]{:S(2)}, u32[]{:S(2)}) collective-permute-start(f32[5200]{0:T(1024)S(1)} %add.572), channel_id=1, source_target_pairs={{0,1},{1,0},{2,3},{3,2},{4,5},{5,4},{6,7},{7,6},{8,9},{9,8},{10,11... | collective-permute-start | bytes 62408 | tf_op jit(solution)/shard_map/ppermute | solution.py:579
  564.9 49.6 %copy-start.20 = (bf16[256,1280]{1,0:T(8,128)(2,1)}, bf16[256,1280]{1,0:T(8,128)(2,1)S(1)}, u32[]{:S(2)}) copy-start(bf16[256,1280]{1,0:T(8,128)(2,1)S(1)} %collective-permute-done.30.refs_3_) | copy-start | bytes 1966084
  564.9 55.2 %collective-permute-start.49 = (bf16[480,640]{1,0:T(8,128)(2,1)S(1)}, bf16[480,640]{1,0:T(8,128)(2,1)}, u32[]{:S(2)}, u32[]{:S(2)}) collective-permute-start(bf16[480,640]{1,0:T(8,128)(2,1)S(1)} %maximum_select_fusion.4), channel_id=1, source_target_pairs={{0,1},{1,0},{2,3},{3,2},{4,5},{5,4},{6,7},{7,6},{8,9},{9,8},{10,11... | collective-permute-start | bytes 1843208 | tf_op jit(solution)/shard_map/ppermute | solution.py:560
  588.9 3.1 collective-permute-start.34
  589.2 33.6 %collective-permute-start.55 = (bf16[480,640]{1,0:T(8,128)(2,1)S(1)}, bf16[480,640]{1,0:T(8,128)(2,1)}, u32[]{:S(2)}, u32[]{:S(2)}) collective-permute-start(bf16[480,640]{1,0:T(8,128)(2,1)S(1)} %maximum_select_fusion.5), channel_id=1, source_target_pairs={{0,1},{1,0},{2,3},{3,2},{4,5},{5,4},{6,7},{7,6},{8,9},{9,8},{10,11... | collective-permute-start | bytes 1843208 | tf_op jit(solution)/shard_map/ppermute | solution.py:560
  592.0 5.4 collective-permute-start.35
  592.0 33.5 %collective-permute-start.28 = (bf16[256,1280]{1,0:T(8,128)(2,1)}, bf16[256,1280]{1,0:T(8,128)(2,1)}, u32[]{:S(2)}, u32[]{:S(2)}) collective-permute-start(bf16[256,1280]{1,0:T(8,128)(2,1)} %get-tuple-element.167), channel_id=1, source_target_pairs={{2,0},{10,1},{4,2},{12,3},{6,4},{14,5},{0,6},{8,7},{3,8},{11,9},{5... | collective-permute-start | bytes 1966088 | tf_op jit(solution)/shard_map/ppermute | solution.py:622
  597.5 32.6 %collective-permute-start.27 = (bf16[256,1280]{1,0:T(8,128)(2,1)S(1)}, bf16[256,1280]{1,0:T(8,128)(2,1)}, u32[]{:S(2)}, u32[]{:S(2)}) collective-permute-start(bf16[256,1280]{1,0:T(8,128)(2,1)S(1)} %get-tuple-element.168), channel_id=1, source_target_pairs={{0,0},{8,1},{2,2},{10,3},{4,4},{12,5},{6,6},{14,7},{1,8},{9,9},{3,... | collective-permute-start | bytes 1966088 | tf_op jit(solution)/shard_map/ppermute | solution.py:622
  (45 other events, 440.5 us)

commit v5 on v3

--- a/solution.py
+++ b/solution.py
@@ -547,8 +547,9 @@
         halves = buf.reshape(2, -1, wide)
         keep = lax.dynamic_index_in_dim(halves, bit, 0, keepdims=False)
         send = lax.dynamic_index_in_dim(halves, 1 - bit, 0, keepdims=False)
-        yield send
+        first = yield send
         got = lax.ppermute(send, "seq", [(i, i ^ (1 << b)) for i in range(places)])
+        got = after(got, first) if first is not None else got
         buf = (keep.astype(f32) + got.astype(f32)).astype(bf16)
     for b in reversed(range(bits)):
         bit = (place >> b) & 1
@@ -640,7 +641,7 @@
         lax.ppermute(parts[flip], "dp", team.turn_rows(step, flip)) for step, flip in shifts[2:]
     ]
     near = lax.ppermute(parts[1], "dp", team.swap_core())
-    x_own = spread_done(spread(after(activations, *parts), near))
+    x_blocks = spread(after(activations, *parts), near)
     other_ids = lax.ppermute(segment_ids, "dp", team.swap_core())
     w_half, small = join(
         [parts[0], near] + far,
@@ -651,12 +652,11 @@
     small = small.reshape(team.dp, -1)[:, : 4 * rows_here]
     small = small.reshape(team.dp, 4, rows_here).transpose(1, 0, 2).reshape(4, width).astype(f32)
     gain_in, gain_mid, bias_up, bias_down = (small[i : i + 1] for i in range(4))
-    xs = [x_own] + [lax.ppermute(x_own, axes, team.rotate(-j)) for j in range(1, size)]
     three = after(jnp.concatenate([w_out, w_up, w_down]), *far)
     three = [three] + [
         lax.ppermute(three, "dp", team.turn_rows(step)) for step in range(1, team.rows)
     ]
-    cot_own = spread(after(cotangent, x_own).astype(bf16))
+    cot_own = spread(after(cotangent, *far).astype(bf16))
 
     ids = lax.dynamic_index_in_dim(
         jnp.where(side == core, segment_ids, other_ids), group, 0, keepdims=False
@@ -681,11 +681,12 @@
     unit = jnp.ones((head_size,), f32)
     factor_row = jnp.tile(jnp.concatenate([factor * log2e, unit, unit]), local_heads)[None, :]
 
+    x_own = spread_done(after(x_blocks, w_half, table, starts, factor_row))
+    xs = [x_own] + [lax.ppermute(x_own, axes, team.rotate(-j)) for j in range(1, size)]
     qkv, normed_in = project_qkv(
         xs, gain_in, w_half, factor_row, local_heads, head_size, team.dp, span
     )
-    early = seqs // 2
-    qkv, cot_own[early:] = after((qkv, cot_own[early:]), *cot_own[early:])
+    qkv, cot_own[1::2] = after((qkv, cot_own[1::2]), *cot_own[1::2])
     att, lse = attend(table, qkv, starts)
     three = after(three, att)
     swapped = [lax.ppermute(piece, "dp", team.swap_core()) for piece in three]
@@ -774,7 +775,6 @@
     pair = math.gcd(local_heads, 4)
     grad_in = after(grad_heads, *three_rows)
     chunks, dots, heads_of = [], 0.0, []
-    steps = None
     for c in range(local_heads // pair):
         grads, dot = attend_back(
             c, pair, table, qkv, att, grad_in, lse, starts, factor[:, None]
@@ -785,10 +785,7 @@
             result = after(result, grads)
             grads = after(grads, *result)
         else:
-            if steps is None:
-                three_far = after(three_far, grads)
-                steps = reduce_places(add(three_rows[0], *three_far), team.seq)
-            grads = after(grads, next(steps))
+            grads = after(grads, steps.send(grads))
         send, keep = head_grad(grads, normed_in, team.rows, row, core)
         near = [lax.ppermute(piece, "dp", team.swap_core()) for piece in send]
         far = [
@@ -799,10 +796,13 @@
             for step in range(1, team.rows)
         ]
         heads_of.append((keep[0], near[0], far))
+        if c == 0:
+            three_far = after(three_far, *send)
+            steps = reduce_places(add(three_rows[0], *three_far), team.seq)
+            grad_in = after(grad_in, next(steps))
         grad_in = after(grad_in, *send, *keep)
-    steps = steps or reduce_places(add(three_rows[0], *three_far), team.seq)
     blocks = own // span
-    chunks = after(chunks, *send, *keep)
+    chunks = after(chunks, steps.send(send), *send, *keep)
     partial = [
         input_side(chunks, w_half, span, j * blocks, blocks) for j in range(1, size)
     ]

time: 637 us -> 617 us (0.969)
  the two profiles are of different devices: /device:TPU:1 before, /device:TPU:12 now
where the time goes in v5:
time: 617 us; the launch traced here: 607 us
  waiting for transfers between devices  202 us (33%)
  Pallas kernels  174 us (28%)
  starting transfers between devices  86.3 us (14%)
  matrix products  52.1 us (8%)
  other arithmetic  46.2 us (7%)
  local copies, waits for them, and re-layouts  43.7 us (7%)
    ppermute x8, waiting for transfers between devices, unspread(): lax.ppermute(array[step * span:(step + 1) * span], axes, team.back(step))  65.1 us
    pallas_call x2, Pallas kernels, attend_back(): pl.pallas_call(functools.partial(attend_back_kernel, count, block, pair),...  47.1 us
    dot_general x8, matrix products, mm(): return lax.dot_general(a, b, dims, preferred_element_type=f32)  45.8 us
    ppermute x9, waiting for transfers between devices, reduce_places(): got = lax.ppermute(send, 'seq', [(i, i ^ 1 << b) for i in range(places)])  41.4 us
    pallas_call x7, Pallas kernels, join(): pl.pallas_call(functools.partial(join_kernel, count, ends), grid_spec=plt...  33.7 us
    ppermute x2, waiting for transfers between devices, on_device(): lax.ppermute(parts[flip], 'dp', team.turn_rows(step, flip))  33.1 us
    pallas_call x2, Pallas kernels, head_grad(): pl.pallas_call(functools.partial(head_grad_kernel, rows, fold), grid_spec...  24.5 us
    pallas_call x1, Pallas kernels, attend(): pl.pallas_call(functools.partial(attend_kernel, count, block, pair), grid...  23.6 us
  transfers between devices with their start and end apart: 62, of which 22 were waited for; matrix products, arithmetic and copies ran while one was open for 14% of the time, Pallas kernels for 27%

profile of v5, /device:TPU:12, one launch (start us, length us, event | category | flops | bytes accessed | tf_op | source)
XLA Modules:
  0.0 606.8 jit_solution(13409957896364441909)
XLA Ops:
  0.7 2.8 concatenate.90
  9.8 2.5 pad_maximum_fusion.4
  18.5 2.6 collective-permute-start.3
  21.1 4.1 convert_reduce_fusion
  28.2 2.5 collective-permute-start.2
  30.6 12.5 %collective-permute-done.6.refs_3_ = bf16[336,1920]{1,0:T(8,128)(2,1)S(1)} collective-permute-done((bf16[336,1920]{1,0:T(8,128)(2,1)}, bf16[336,1920]{1,0:T(8,128)(2,1)S(1)}, u32[]{:S(2)}, u32[]{:S(2)}) %collective-permute-start.6) | collective-permute-done | bytes 1290272 | tf_op jit(solution)/shard_map/ppermute | solution.py:641
  43.2 6.5 %collective-permute-start.1 = (bf16[256,1280]{1,0:T(8,128)(2,1)}, bf16[256,1280]{1,0:T(8,128)(2,1)}, u32[]{:S(2)}, u32[]{:S(2)}) collective-permute-start(bf16[256,1280]{1,0:T(8,128)(2,1)} %get-tuple-element.180), channel_id=1, source_target_pairs={{0,0},{1,8},{2,2},{3,10},{4,4},{5,12},{6,6},{7,14},{8,1},{9,9},{10... | collective-permute-start | bytes 1966088 | tf_op jit(solution)/shard_map/ppermute | solution.py:611
  50.4 20.6 %collective-permute-done.5.refs_2_ = bf16[336,1920]{1,0:T(8,128)(2,1)} collective-permute-done((bf16[336,1920]{1,0:T(8,128)(2,1)S(1)}, bf16[336,1920]{1,0:T(8,128)(2,1)}, u32[]{:S(2)}, u32[]{:S(2)}) %collective-permute-start.5) | collective-permute-done | bytes 1290272 | tf_op jit(solution)/shard_map/ppermute | solution.py:641
  71.0 6.4 %join.7 = (bf16[4,320,1920]{2,1,0:T(8,128)(2,1)}, bf16[4,16,1920]{2,1,0:T(8,128)(2,1)}) custom-call(s32[4]{0:T(128)} %add_add_fusion.slots_ref, bf16[336,1920]{1,0:T(8,128)(2,1)} %copy-done.9, bf16[336,1920]{1,0:T(8,128)(2,1)} %collective-permute-done.refs_1_, bf16[336,1920]{1,0:T(8,128)(2,1)} %collective-permute-done.5.refs_2_, bf16[336,1920]{1,0:T(8,128)(2,1)} %copy-done.22), custom_call_target="tpu_custom_call" | custom-call | flops 1 | bytes 1 | tf_op jit(solution)/shard_map/join/pallas_call | solution.py:116
  78.3 3.9 join.8
  82.4 3.2 pad_maximum_fusion.1.refs_0_
  92.8 19.7 %qkv.1 = (bf16[8,3,2048,80]{3,2,1,0:T(8,128)(2,1)}, bf16[2,2048,640]{2,1,0:T(8,128)(2,1)}) custom-call(bf16[1024,1280]{1,0:T(8,128)(2,1)} %bitcast.199, bf16[1024,1280]{1,0:T(8,128)(2,1)} %copy-done.20, f32[1,1280]{1,0:T(1,128)} %slice.77.refs_2_, bf16[1280,1920]{1,0:T(8,128)(2,1)} %bitcast.216, f32[1,1920]{1,0:T(1,128)} %broadcast_in_dim_tile.3.refs_4_), custom_call_target="tpu_custom_call" | custom-call | flops 1 | bytes 1 | tf_op jit(solution)/shard_map/qkv/pallas_call | solution.py:163
  112.4 8.7 %collective-permute-done.9.refs_1_ = bf16[256,1280]{1,0:T(8,128)(2,1)} collective-permute-done((bf16[256,1280]{1,0:T(8,128)(2,1)}, bf16[256,1280]{1,0:T(8,128)(2,1)}, u32[]{:S(2)}, u32[]{:S(2)}) %collective-permute-start.9) | collective-permute-done | bytes 655392 | tf_op jit(solution)/shard_map/ppermute | solution.py:611
  121.1 23.6 %attend.1 = (bf16[640,2048]{1,0:T(8,128)(2,1)}, f32[8,1,2048]{2,1,0:T(1,128)}) custom-call(s32[5,8]{1,0:T(8,128)} %stack.83.table, bf16[8,3,2048,80]{3,2,1,0:T(8,128)(2,1)} %get-tuple-element.83.qkv_ref, s32[8,256]{1,0:T(8,128)} %copy-done.33), custom_call_target="tpu_custom_call" | custom-call | flops 1 | bytes 1 | tf_op jit(solution)/shard_map/attend/pallas_call | solution.py:357
  145.3 3.0 fusion.39
  150.2 4.9 collective-permute-start.20
  156.9 3.5 join.9
  160.4 7.9 %join.10 = (bf16[4,320,1280]{2,1,0:T(8,128)(2,1)}, bf16[4,320,1280]{2,1,0:T(8,128)(2,1)}, bf16[4,320,1280]{2,1,0:T(8,128)(2,1)}) custom-call(s32[4]{0:T(128)} %add_add_fusion.1.slots_ref, bf16[960,1280]{1,0:T(8,128)(2,1)} %pad_maximum_fusion.1.refs_0_, bf16[960,1280]{1,0:T(8,128)(2,1)} %collective-permute-done.12.refs_1_, ...), custom_call_target="tpu_custom_call" | custom-call | flops 1 | bytes 1 | tf_op jit(solution)/shard_map/join/pallas_call | solution.py:116
  168.4 6.3 %multiply_reduce_fusion.3 = (f32[1024]{0:T(1024)S(1)}, f32[1024,1280]{1,0:T(8,128)S(1)}) fusion(bf16[1280,1024]{1,0:T(8,128)(2,1)S(1)} %bitcast.209, bf16[1280,1280]{1,0:T(8,128)(2,1)} %bitcast.225, bf16[1024,1280]{1,0:T(8,128)(2,1)S(1)} %bitcast.200), kind=kOutput, calls=%fused_computation.30 | convolution fusion | flops 3360685056 | bytes 13766656 | tf_op jit(solution)/shard_map/dot_general | solution.py:711
  174.7 3.7 fusion.35
  178.5 5.7 add_convert_fusion
  185.6 3.9 join.11
  189.5 11.0 %convert_reduce_fusion.3 = (f32[1280]{0:T(1024)}, bf16[1024,1280]{1,0:T(8,128)(2,1)}) fusion(f32[1024,1280]{1,0:T(8,128)} %copy-done.48, f32[1280]{0:T(1024)S(1)} %add.541, bf16[1024,1280]{1,0:T(8,128)(2,1)} %bitcast.201, bf16[1280,1280]{1,0:T(8,128)(2,1)} %bitcast.253), kind=kOutput, calls=%fused_computation.19 | convolution fusion | flops 3371170560 | bytes 13772800 | tf_op jit(solution)/shard_map/dot_general | solution.py:25
  200.5 4.0 convolution_convert_fusion.2
  204.6 7.5 %multiply_reduce_fusion = (f32[1280]{0:T(1024)}, f32[1024]{0:T(1024)S(1)}, f32[1024,1280]{1,0:T(8,128)S(1)}) fusion(f32[1024,1280]{1,0:T(8,128)S(1)} %bitcast.204, f32[1024]{0:T(1024)S(1)} %add_rsqrt_fusion, f32[1280]{0:T(1024)S(1)} %mul.203, bf16[1024,1280]{1,0:T(8,128)(2,1)} %get-tuple-element.191, bf16[1280,1280]{1,0:T(8,128)(2,1)S(1)} %bitcast.252), kind=kOutput, calls=%fused_computation.20 | convolution fusion | flops 3363305216 | bytes 16402432 | tf_op jit(solution)/shard_map/dot_general | solution.py:25
  212.1 5.8 convolution_convert_fusion.1
  219.3 2.8 collective-permute-start.22
  224.1 4.2 convolution_convert_fusion
  234.5 2.9 fusion.16
  237.5 2.8 fusion.15
  243.4 3.9 convolution_convert_fusion.3
  255.0 6.5 %collective-permute-start.15 = (bf16[256,1280]{1,0:T(8,128)(2,1)}, bf16[256,1280]{1,0:T(8,128)(2,1)}, u32[]{:S(2)}, u32[]{:S(2)}) collective-permute-start(bf16[256,1280]{1,0:T(8,128)(2,1)} %get-tuple-element.174), channel_id=1, source_target_pairs={{0,0},{8,1},{2,2},{10,3},{4,4},{12,5},{6,6},{14,7},{1,8},{9,9},{3,... | collective-permute-start | bytes 1966088 | tf_op jit(solution)/shard_map/ppermute | solution.py:619
  262.8 3.5 pad_maximum_fusion.grad_ref
  266.3 23.4 %attend_back.2 = (bf16[960,2048]{1,0:T(8,128)(2,1)}, f32[80,1]{1,0:T(8,128)}) custom-call(s32[5,8]{1,0:T(8,128)} %stack.83.table, bf16[8,3,2048,80]{3,2,1,0:T(8,128)(2,1)} %get-tuple-element.83.qkv_ref, bf16[640,2048]{1,0:T(8,128)(2,1)} %get-tuple-element.84.att_ref, bf16[640,2048]{1,0:T(8,128)(2,1)} %pad_maximum_fusion.grad_ref, ...), custom_call_target="tpu_custom_call" | custom-call | flops 1 | bytes 1 | tf_op jit(solution)/shard_map/attend_back/pallas_call | solution.py:479
  289.7 19.0 %collective-permute-done.17.refs_2_ = bf16[256,1280]{1,0:T(8,128)(2,1)} collective-permute-done((bf16[256,1280]{1,0:T(8,128)(2,1)}, bf16[256,1280]{1,0:T(8,128)(2,1)}, u32[]{:S(2)}, u32[]{:S(2)}) %collective-permute-start.17) | collective-permute-done | bytes 655392 | tf_op jit(solution)/shard_map/ppermute | solution.py:619
  308.7 2.8 collective-permute-done.16.refs_1_
  311.5 12.3 %head_grad.2 = (bf16[480,640]{1,0:T(8,128)(2,1)}, bf16[480,640]{1,0:T(8,128)(2,1)}, bf16[480,640]{1,0:T(8,128)(2,1)}, bf16[480,640]{1,0:T(8,128)(2,1)}) custom-call(s32[3]{0:T(128)} %pad_add_fusion.2.place_ref, bf16[960,2048]{1,0:T(8,128)(2,1)} %get-tuple-element.123.grads_ref.refs_0_, bf16[2,2048,640]{2,1,0:T(8,128)(2,1)} %get-tuple-element.105.normed_ref), custom_call_target="tpu_custom_call" | custom-call | flops 1 | bytes 1 | tf_op jit(solution)/shard_map/head_grad/pallas_call | solution.py:209
  330.9 23.7 %attend_back.3 = (bf16[960,2048]{1,0:T(8,128)(2,1)}, f32[80,1]{1,0:T(8,128)}) custom-call(s32[5,8]{1,0:T(8,128)} %stack.83.table, bf16[8,3,2048,80]{3,2,1,0:T(8,128)(2,1)} %get-tuple-element.83.qkv_ref, bf16[640,2048]{1,0:T(8,128)(2,1)} %get-tuple-element.84.att_ref, bf16[640,2048]{1,0:T(8,128)(2,1)} %pad_maximum_fusion.grad_ref, ...), custom_call_target="tpu_custom_call" | custom-call | flops 1 | bytes 1 | tf_op jit(solution)/shard_map/attend_back/pallas_call | solution.py:479
  354.6 3.5 collective-permute-done.26
  363.4 3.5 join.12
  367.6 12.2 %head_grad.3 = (bf16[480,640]{1,0:T(8,128)(2,1)}, bf16[480,640]{1,0:T(8,128)(2,1)}, bf16[480,640]{1,0:T(8,128)(2,1)}, bf16[480,640]{1,0:T(8,128)(2,1)}) custom-call(s32[3]{0:T(128)} %pad_add_fusion.2.place_ref, bf16[960,2048]{1,0:T(8,128)(2,1)} %get-tuple-element.124.grads_ref.refs_1_, bf16[2,2048,640]{2,1,0:T(8,128)(2,1)} %get-tuple-element.105.normed_ref), custom_call_target="tpu_custom_call" | custom-call | flops 1 | bytes 1 | tf_op jit(solution)/shard_map/head_grad/pallas_call | solution.py:209
  381.4 9.9 %input_side.2 = bf16[1024,1280]{1,0:T(8,128)(2,1)} custom-call(bf16[960,2048]{1,0:T(8,128)(2,1)} %get-tuple-element.123.grads_ref.refs_0_, bf16[960,2048]{1,0:T(8,128)(2,1)} %get-tuple-element.124.grads_ref.refs_1_, bf16[1280,1920]{1,0:T(8,128)(2,1)} %bitcast.217), custom_call_target="tpu_custom_call" | custom-call | flops 10066329600 | bytes 1 | tf_op jit(solution)/shard_map/input_side/pallas_call | solution.py:525
  396.5 10.1 %input_side.3 = bf16[1024,1280]{1,0:T(8,128)(2,1)} custom-call(bf16[960,2048]{1,0:T(8,128)(2,1)} %get-tuple-element.123.grads_ref.refs_0_, bf16[960,2048]{1,0:T(8,128)(2,1)} %get-tuple-element.124.grads_ref.refs_1_, bf16[1280,1920]{1,0:T(8,128)(2,1)} %bitcast.218), custom_call_target="tpu_custom_call" | custom-call | flops 10066329600 | bytes 1 | tf_op jit(solution)/shard_map/input_side/pallas_call | solution.py:525
  406.8 3.4 collective-permute-start.59
  410.2 10.5 %collective-permute-done.45 = bf16[480,640]{1,0:T(8,128)(2,1)S(1)} collective-permute-done((bf16[480,640]{1,0:T(8,128)(2,1)}, bf16[480,640]{1,0:T(8,128)(2,1)S(1)}, u32[]{:S(2)}, u32[]{:S(2)}) %collective-permute-start.45) | collective-permute-done | bytes 614432 | tf_op jit(solution)/shard_map/ppermute | solution.py:793
  426.3 11.7 %collective-permute-done.52 = bf16[480,640]{1,0:T(8,128)(2,1)S(1)} collective-permute-done((bf16[480,640]{1,0:T(8,128)(2,1)S(1)}, bf16[480,640]{1,0:T(8,128)(2,1)S(1)}, u32[]{:S(2)}, u32[]{:S(2)}) %collective-permute-start.52) | collective-permute-done | bytes 614432 | tf_op jit(solution)/shard_map/ppermute | solution.py:551
  439.2 10.3 %collective-permute-done.46 = bf16[480,640]{1,0:T(8,128)(2,1)S(1)} collective-permute-done((bf16[480,640]{1,0:T(8,128)(2,1)S(1)}, bf16[480,640]{1,0:T(8,128)(2,1)S(1)}, u32[]{:S(2)}, u32[]{:S(2)}) %collective-permute-start.46) | collective-permute-done | bytes 614432 | tf_op jit(solution)/shard_map/ppermute | solution.py:551
  452.5 6.5 %collective-permute-done.47 = bf16[240,640]{1,0:T(8,128)(2,1)S(1)} collective-permute-done((bf16[240,640]{1,0:T(8,128)(2,1)S(1)}, bf16[240,640]{1,0:T(8,128)(2,1)S(1)}, u32[]{:S(2)}, u32[]{:S(2)}) %collective-permute-start.47) | collective-permute-done | bytes 307232 | tf_op jit(solution)/shard_map/ppermute | solution.py:551
  459.1 3.1 collective-permute-start.48
  462.4 7.2 %collective-permute-done.48 = bf16[120,640]{1,0:T(8,128)(2,1)S(1)} collective-permute-done((bf16[120,640]{1,0:T(8,128)(2,1)S(1)}, bf16[120,640]{1,0:T(8,128)(2,1)S(1)}, u32[]{:S(2)}, u32[]{:S(2)}) %collective-permute-start.48) | collective-permute-done | bytes 153632 | tf_op jit(solution)/shard_map/ppermute | solution.py:551
  469.6 3.4 collective-permute-start.49
  473.1 3.0 collective-permute-done.55
  476.2 3.7 collective-permute-start.56
  482.5 5.0 collective-permute-done.56
  488.8 2.7 fusion.8
  495.5 14.7 %collective-permute-done.61 = bf16[480,1280]{1,0:T(8,128)(2,1)S(1)} collective-permute-done((bf16[480,1280]{1,0:T(8,128)(2,1)S(1)}, bf16[480,1280]{1,0:T(8,128)(2,1)S(1)}, u32[]{:S(2)}, u32[]{:S(2)}) %collective-permute-start.61) | collective-permute-done | bytes 1228832 | tf_op jit(solution)/shard_map/ppermute | solution.py:557
  511.9 19.9 %collective-permute-done.35 = f32[5200]{0:T(1024)S(1)} collective-permute-done((f32[5200]{0:T(1024)S(1)}, f32[5200]{0:T(1024)S(1)}, u32[]{:S(2)}, u32[]{:S(2)}) %collective-permute-start.35) | collective-permute-done | bytes 20832 | tf_op jit(solution)/shard_map/ppermute | solution.py:576
  532.6 2.5 fusion.5
  535.6 4.6 collective-permute-start.37
  540.5 3.6 collective-permute-start.31
  551.5 5.4 unfold.1
  558.1 39.1 %collective-permute-done.31.refs_2_ = bf16[256,1280]{1,0:T(8,128)(2,1)S(1)} collective-permute-done((bf16[256,1280]{1,0:T(8,128)(2,1)S(1)}, bf16[256,1280]{1,0:T(8,128)(2,1)S(1)}, u32[]{:S(2)}, u32[]{:S(2)}) %collective-permute-start.31) | collective-permute-done | bytes 655392 | tf_op jit(solution)/shard_map/ppermute | solution.py:619
  597.2 3.0 collective-permute-done.30.refs_1_
  601.9 4.5 join.13
  (324 shorter events, 102.7 us)
Async XLA Ops:
  12.4 30.8 %collective-permute-start.6 = (bf16[336,1920]{1,0:T(8,128)(2,1)}, bf16[336,1920]{1,0:T(8,128)(2,1)S(1)}, u32[]{:S(2)}, u32[]{:S(2)}) collective-permute-start(bf16[336,1920]{1,0:T(8,128)(2,1)} %get-tuple-element.181), channel_id=1, source_target_pairs={{0,24},{8,16},{16,8},{24,0},{1,25},{9,17},{17,9},{25,1},{2,26},{10... | collective-permute-start | bytes 3870728 | tf_op jit(solution)/shard_map/ppermute | solution.py:641
  12.4 13.4 %collective-permute-start = (bf16[336,1920]{1,0:T(8,128)(2,1)}, bf16[336,1920]{1,0:T(8,128)(2,1)}, u32[]{:S(2)}, u32[]{:S(2)}) collective-permute-start(bf16[336,1920]{1,0:T(8,128)(2,1)} %get-tuple-element.181), channel_id=1, source_target_pairs={{0,8},{8,0},{16,24},{24,16},{1,9},{9,1},{17,25},{25,17},{2,10},{10... | collective-permute-start | bytes 3870728 | tf_op jit(solution)/shard_map/ppermute | solution.py:643
  13.0 5.5 collective-permute-start.7
  13.0 58.0 %collective-permute-start.5 = (bf16[336,1920]{1,0:T(8,128)(2,1)S(1)}, bf16[336,1920]{1,0:T(8,128)(2,1)}, u32[]{:S(2)}, u32[]{:S(2)}) collective-permute-start(bf16[336,1920]{1,0:T(8,128)(2,1)S(1)} %get-tuple-element.182.refs_0_), channel_id=1, source_target_pairs={{0,16},{8,24},{16,0},{24,8},{1,17},{9,25},{17,1},{25,9},{2,18},{10... | collective-permute-start | bytes 3870728 | tf_op jit(solution)/shard_map/ppermute | solution.py:641
  16.7 60.7 %collective-permute-start.4 = (bf16[256,1280]{1,0:T(8,128)(2,1)}, bf16[256,1280]{1,0:T(8,128)(2,1)}, u32[]{:S(2)}, u32[]{:S(2)}) collective-permute-start(bf16[256,1280]{1,0:T(8,128)(2,1)} %get-tuple-element.177), channel_id=1, source_target_pairs={{0,6},{1,14},{2,0},{3,8},{4,2},{5,10},{6,4},{7,12},{8,7},{9,15},{1... | collective-permute-start | bytes 1966088 | tf_op jit(solution)/shard_map/ppermute | solution.py:611
  18.5 58.9 %collective-permute-start.3 = (bf16[256,1280]{1,0:T(8,128)(2,1)S(1)}, bf16[256,1280]{1,0:T(8,128)(2,1)}, u32[]{:S(2)}, u32[]{:S(2)}) collective-permute-start(bf16[256,1280]{1,0:T(8,128)(2,1)S(1)} %get-tuple-element.178), channel_id=1, source_target_pairs={{0,4},{1,12},{2,6},{3,14},{4,0},{5,8},{6,2},{7,10},{8,5},{9,13},{1... | collective-permute-start | bytes 1966088 | tf_op jit(solution)/shard_map/ppermute | solution.py:611
  25.3 52.1 %copy-start.33 = (s32[8,256]{1,0:T(8,128)}, s32[8,256]{1,0:T(8,128)S(1)}, u32[]{:S(2)}) copy-start(s32[8,256]{1,0:T(8,128)S(1)} %reshape.562.start_ref) | copy-start | bytes 24580
  28.2 49.6 %collective-permute-start.2 = (bf16[256,1280]{1,0:T(8,128)(2,1)}, bf16[256,1280]{1,0:T(8,128)(2,1)}, u32[]{:S(2)}, u32[]{:S(2)}) collective-permute-start(bf16[256,1280]{1,0:T(8,128)(2,1)} %get-tuple-element.179), channel_id=1, source_target_pairs={{0,2},{1,10},{2,4},{3,12},{4,6},{5,14},{6,0},{7,8},{8,3},{9,11},{1... | collective-permute-start | bytes 1966088 | tf_op jit(solution)/shard_map/ppermute | solution.py:611
  43.2 34.6 %collective-permute-start.1 = (bf16[256,1280]{1,0:T(8,128)(2,1)}, bf16[256,1280]{1,0:T(8,128)(2,1)}, u32[]{:S(2)}, u32[]{:S(2)}) collective-permute-start(bf16[256,1280]{1,0:T(8,128)(2,1)} %get-tuple-element.180), channel_id=1, source_target_pairs={{0,0},{1,8},{2,2},{3,10},{4,4},{5,12},{6,6},{7,14},{8,1},{9,9},{10... | collective-permute-start | bytes 1966088 | tf_op jit(solution)/shard_map/ppermute | solution.py:611
  82.3 9.0 %collective-permute-start.8 = (bf16[1024,1280]{1,0:T(8,128)(2,1)}, bf16[1024,1280]{1,0:T(8,128)(2,1)S(1)}, u32[]{:S(2)}, u32[]{:S(2)}) collective-permute-start(bf16[1024,1280]{1,0:T(8,128)(2,1)} %bitcast.198), channel_id=1, source_target_pairs={{0,8},{1,9},{2,10},{3,11},{4,12},{5,13},{6,14},{7,15},{8,0},{9,1},... | collective-permute-start | bytes 7864328 | tf_op jit(solution)/shard_map/ppermute | solution.py:685
  85.6 59.1 %collective-permute-start.12 = (bf16[960,1280]{1,0:T(8,128)(2,1)}, bf16[960,1280]{1,0:T(8,128)(2,1)}, u32[]{:S(2)}, u32[]{:S(2)}) collective-permute-start(bf16[960,1280]{1,0:T(8,128)(2,1)} %pad_maximum_fusion.1.refs_0_), channel_id=1, source_target_pairs={{0,16},{8,24},{16,0},{24,8},{1,17},{9,25},{17,1},{25,9},{2,18},{10... | collective-permute-start | bytes 7372808 | tf_op jit(solution)/shard_map/ppermute | solution.py:657
  87.9 24.5 %collective-permute-start.10 = (bf16[256,1280]{1,0:T(8,128)(2,1)}, bf16[256,1280]{1,0:T(8,128)(2,1)}, u32[]{:S(2)}, u32[]{:S(2)}) collective-permute-start(bf16[256,1280]{1,0:T(8,128)(2,1)} %get-tuple-element.169), channel_id=1, source_target_pairs={{0,6},{1,14},{2,0},{3,8},{4,2},{5,10},{6,4},{7,12},{8,7},{9,15},{1... | collective-permute-start | bytes 1966088 | tf_op jit(solution)/shard_map/ppermute | solution.py:611
  88.2 32.9 %collective-permute-start.9 = (bf16[256,1280]{1,0:T(8,128)(2,1)}, bf16[256,1280]{1,0:T(8,128)(2,1)}, u32[]{:S(2)}, u32[]{:S(2)}) collective-permute-start(bf16[256,1280]{1,0:T(8,128)(2,1)} %get-tuple-element.170), channel_id=1, source_target_pairs={{0,2},{1,10},{2,4},{3,12},{4,6},{5,14},{6,0},{7,8},{8,3},{9,11},{1... | collective-permute-start | bytes 1966088 | tf_op jit(solution)/shard_map/ppermute | solution.py:611
  144.7 15.7 %collective-permute-start.13 = (bf16[960,1280]{1,0:T(8,128)(2,1)}, bf16[960,1280]{1,0:T(8,128)(2,1)}, u32[]{:S(2)}, u32[]{:S(2)}) collective-permute-start(bf16[960,1280]{1,0:T(8,128)(2,1)} %pad_maximum_fusion.1.refs_0_), channel_id=1, source_target_pairs={{0,8},{8,0},{16,24},{24,16},{1,9},{9,1},{17,25},{25,17},{2,10},{10... | collective-permute-start | bytes 7372808 | tf_op jit(solution)/shard_map/ppermute | solution.py:692
  145.1 15.3 %collective-permute-start.14 = (bf16[960,1280]{1,0:T(8,128)(2,1)}, bf16[960,1280]{1,0:T(8,128)(2,1)}, u32[]{:S(2)}, u32[]{:S(2)}) collective-permute-start(bf16[960,1280]{1,0:T(8,128)(2,1)} %collective-permute-done.12.refs_1_), channel_id=1, source_target_pairs={{0,8},{8,0},{16,24},{24,16},{1,9},{9,1},{17,25},{25,17},{2,10},{10... | collective-permute-start | bytes 7372808 | tf_op jit(solution)/shard_map/ppermute | solution.py:692
  148.3 7.5 %collective-permute-start.11 = (bf16[640,1024]{1,0:T(8,128)(2,1)S(1)}, bf16[640,1024]{1,0:T(8,128)(2,1)S(1)}, u32[]{:S(2)}, u32[]{:S(2)}) collective-permute-start(bf16[640,1024]{1,0:T(8,128)(2,1)S(1)} %get-tuple-element.175), channel_id=1, source_target_pairs={{0,8},{1,9},{2,10},{3,11},{4,12},{5,13},{6,14},{7,15},{8,0},{9,1},... | collective-permute-start | bytes 3932168 | tf_op jit(solution)/shard_map/ppermute | solution.py:705
  150.2 34.0 %collective-permute-start.20 = (bf16[256,1280]{1,0:T(8,128)(2,1)}, bf16[256,1280]{1,0:T(8,128)(2,1)S(1)}, u32[]{:S(2)}, u32[]{:S(2)}) collective-permute-start(bf16[256,1280]{1,0:T(8,128)(2,1)} %get-tuple-element.167), channel_id=1, source_target_pairs={{0,4},{1,12},{2,6},{3,14},{4,0},{5,8},{6,2},{7,10},{8,5},{9,13},{1... | collective-permute-start | bytes 1966088 | tf_op jit(solution)/shard_map/ppermute | solution.py:611
  155.1 29.1 %collective-permute-start.19 = (bf16[256,1280]{1,0:T(8,128)(2,1)S(1)}, bf16[256,1280]{1,0:T(8,128)(2,1)S(1)}, u32[]{:S(2)}, u32[]{:S(2)}) collective-permute-start(bf16[256,1280]{1,0:T(8,128)(2,1)S(1)} %copy-done.23), channel_id=1, source_target_pairs={{0,0},{1,8},{2,2},{3,10},{4,4},{5,12},{6,6},{7,14},{8,1},{9,9},{10... | collective-permute-start | bytes 1966088 | tf_op jit(solution)/shard_map/ppermute | solution.py:611
  219.3 12.3 %collective-permute-start.22 = (bf16[2,320,1280]{2,1,0:T(8,128)(2,1)}, bf16[2,320,1280]{2,1,0:T(8,128)(2,1)}, u32[]{:S(2)}, u32[]{:S(2)}) collective-permute-start(bf16[2,320,1280]{2,1,0:T(8,128)(2,1)} %dynamic-slice_bitcast_fusion.2), channel_id=1, source_target_pairs={{0,8},{8,0},{16,24},{24,16},{1,9},{9,1},{17,25},{25,17},{2,10},{10... | collective-permute-start | bytes 4915208 | tf_op jit(solution)/shard_map/ppermute | solution.py:747
  229.8 4.2 collective-permute-start.23
  231.2 6.3 %collective-permute-start.24 = (bf16[2,320,1280]{2,1,0:T(8,128)(2,1)}, bf16[2,320,1280]{2,1,0:T(8,128)(2,1)}, u32[]{:S(2)}, u32[]{:S(2)}) collective-permute-start(bf16[2,320,1280]{2,1,0:T(8,128)(2,1)} %dynamic-slice_bitcast_fusion), channel_id=1, source_target_pairs={{0,8},{8,0},{16,24},{24,16},{1,9},{9,1},{17,25},{25,17},{2,10},{10... | collective-permute-start | bytes 4915208 | tf_op jit(solution)/shard_map/ppermute | solution.py:747
  241.9 81.8 %collective-permute-start.25 = (bf16[960,1280]{1,0:T(8,128)(2,1)}, bf16[960,1280]{1,0:T(8,128)(2,1)}, u32[]{:S(2)}, u32[]{:S(2)}) collective-permute-start(bf16[960,1280]{1,0:T(8,128)(2,1)} %pad_maximum_fusion.3), channel_id=1, source_target_pairs={{0,16},{8,24},{16,0},{24,8},{1,17},{9,25},{17,1},{25,9},{2,18},{10... | collective-permute-start | bytes 7372808 | tf_op jit(solution)/shard_map/ppermute | solution.py:766
  248.7 6.3 %collective-permute-start.21 = (bf16[640,1024]{1,0:T(8,128)(2,1)S(1)}, bf16[640,1024]{1,0:T(8,128)(2,1)}, u32[]{:S(2)}, u32[]{:S(2)}) collective-permute-start(bf16[640,1024]{1,0:T(8,128)(2,1)S(1)} %get-tuple-element.166), channel_id=1, source_target_pairs={{0,8},{1,9},{2,10},{3,11},{4,12},{5,13},{6,14},{7,15},{8,0},{9,1},... | collective-permute-start | bytes 3932168 | tf_op jit(solution)/shard_map/ppermute | solution.py:739
  251.2 38.5 %collective-permute-start.18 = (bf16[256,1280]{1,0:T(8,128)(2,1)}, bf16[256,1280]{1,0:T(8,128)(2,1)}, u32[]{:S(2)}, u32[]{:S(2)}) collective-permute-start(bf16[256,1280]{1,0:T(8,128)(2,1)} %get-tuple-element.171), channel_id=1, source_target_pairs={{6,0},{14,1},{0,2},{8,3},{2,4},{10,5},{4,6},{12,7},{7,8},{15,9},{1... | collective-permute-start | bytes 1966088 | tf_op jit(solution)/shard_map/ppermute | solution.py:619
  251.6 57.0 %collective-permute-start.17 = (bf16[256,1280]{1,0:T(8,128)(2,1)}, bf16[256,1280]{1,0:T(8,128)(2,1)}, u32[]{:S(2)}, u32[]{:S(2)}) collective-permute-start(bf16[256,1280]{1,0:T(8,128)(2,1)} %get-tuple-element.172), channel_id=1, source_target_pairs={{4,0},{12,1},{6,2},{14,3},{0,4},{8,5},{2,6},{10,7},{5,8},{13,9},{7... | collective-permute-start | bytes 1966088 | tf_op jit(solution)/shard_map/ppermute | solution.py:619
  253.4 58.1 %collective-permute-start.16 = (bf16[256,1280]{1,0:T(8,128)(2,1)}, bf16[256,1280]{1,0:T(8,128)(2,1)}, u32[]{:S(2)}, u32[]{:S(2)}) collective-permute-start(bf16[256,1280]{1,0:T(8,128)(2,1)} %get-tuple-element.173), channel_id=1, source_target_pairs={{2,0},{10,1},{4,2},{12,3},{6,4},{14,5},{0,6},{8,7},{3,8},{11,9},{5... | collective-permute-start | bytes 1966088 | tf_op jit(solution)/shard_map/ppermute | solution.py:619
  255.0 56.5 %collective-permute-start.15 = (bf16[256,1280]{1,0:T(8,128)(2,1)}, bf16[256,1280]{1,0:T(8,128)(2,1)}, u32[]{:S(2)}, u32[]{:S(2)}) collective-permute-start(bf16[256,1280]{1,0:T(8,128)(2,1)} %get-tuple-element.174), channel_id=1, source_target_pairs={{0,0},{8,1},{2,2},{10,3},{4,4},{12,5},{6,6},{14,7},{1,8},{9,9},{3,... | collective-permute-start | bytes 1966088 | tf_op jit(solution)/shard_map/ppermute | solution.py:619
  328.7 29.4 %collective-permute-start.26 = (bf16[480,1280]{1,0:T(8,128)(2,1)}, bf16[480,1280]{1,0:T(8,128)(2,1)}, u32[]{:S(2)}, u32[]{:S(2)}) collective-permute-start(bf16[480,1280]{1,0:T(8,128)(2,1)} %dynamic-slice_bitcast_fusion.5), channel_id=1, source_target_pairs={{0,1},{1,0},{2,3},{3,2},{4,5},{5,4},{6,7},{7,6},{8,9},{9,8},{10,11... | collective-permute-start | bytes 3686408 | tf_op jit(solution)/shard_map/ppermute | solution.py:551
  330.9 36.0 %collective-permute-start.40 = (bf16[480,640]{1,0:T(8,128)(2,1)}, bf16[480,640]{1,0:T(8,128)(2,1)}, u32[]{:S(2)}, u32[]{:S(2)}) collective-permute-start(bf16[480,640]{1,0:T(8,128)(2,1)} %get-tuple-element.107), channel_id=1, source_target_pairs={{0,8},{8,0},{16,24},{24,16},{1,9},{9,1},{17,25},{25,17},{2,10},{10... | collective-permute-start | bytes 1843208 | tf_op jit(solution)/shard_map/ppermute | solution.py:790
  359.8 20.3 %collective-permute-start.27 = (bf16[240,1280]{1,0:T(8,128)(2,1)S(1)}, bf16[240,1280]{1,0:T(8,128)(2,1)S(1)}, u32[]{:S(2)}, u32[]{:S(2)}) collective-permute-start(bf16[240,1280]{1,0:T(8,128)(2,1)S(1)} %dynamic-slice_bitcast_fusion.16), channel_id=1, source_target_pairs={{0,2},{1,3},{2,0},{3,1},{4,6},{5,7},{6,4},{7,5},{8,10},{9,11},{10,... | collective-permute-start | bytes 1843208 | tf_op jit(solution)/shard_map/ppermute | solution.py:551
  361.9 29.5 %collective-permute-start.39 = (bf16[480,640]{1,0:T(8,128)(2,1)S(1)}, bf16[480,640]{1,0:T(8,128)(2,1)S(1)}, u32[]{:S(2)}, u32[]{:S(2)}) collective-permute-start(bf16[480,640]{1,0:T(8,128)(2,1)S(1)} %copy-done.47), channel_id=1, source_target_pairs={{0,16},{8,24},{16,0},{24,8},{1,17},{9,25},{17,1},{25,9},{2,18},{10... | collective-permute-start | bytes 1843208 | tf_op jit(solution)/shard_map/ppermute | solution.py:793
  363.4 43.3 %collective-permute-start.38 = (bf16[480,640]{1,0:T(8,128)(2,1)}, bf16[480,640]{1,0:T(8,128)(2,1)S(1)}, u32[]{:S(2)}, u32[]{:S(2)}) collective-permute-start(bf16[480,640]{1,0:T(8,128)(2,1)} %get-tuple-element.106), channel_id=1, source_target_pairs={{0,8},{8,0},{16,24},{24,16},{1,9},{9,1},{17,25},{25,17},{2,10},{10... | collective-permute-start | bytes 1843208 | tf_op jit(solution)/shard_map/ppermute | solution.py:790
  366.9 39.9 %collective-permute-start.41 = (bf16[480,640]{1,0:T(8,128)(2,1)}, bf16[480,640]{1,0:T(8,128)(2,1)S(1)}, u32[]{:S(2)}, u32[]{:S(2)}) collective-permute-start(bf16[480,640]{1,0:T(8,128)(2,1)} %collective-permute-done.40), channel_id=1, source_target_pairs={{0,16},{8,24},{16,0},{24,8},{1,17},{9,25},{17,1},{25,9},{2,18},{10... | collective-permute-start | bytes 1843208 | tf_op jit(solution)/shard_map/ppermute | solution.py:793
  379.8 13.1 %collective-permute-start.44 = (bf16[480,640]{1,0:T(8,128)(2,1)}, bf16[480,640]{1,0:T(8,128)(2,1)}, u32[]{:S(2)}, u32[]{:S(2)}) collective-permute-start(bf16[480,640]{1,0:T(8,128)(2,1)} %get-tuple-element.117), channel_id=1, source_target_pairs={{0,8},{8,0},{16,24},{24,16},{1,9},{9,1},{17,25},{25,17},{2,10},{10... | collective-permute-start | bytes 1843208 | tf_op jit(solution)/shard_map/ppermute | solution.py:790
  380.2 14.9 %collective-permute-start.58 = (bf16[120,1280]{1,0:T(8,128)(2,1)S(1)}, bf16[120,1280]{1,0:T(8,128)(2,1)S(1)}, u32[]{:S(2)}, u32[]{:S(2)}) collective-permute-start(bf16[120,1280]{1,0:T(8,128)(2,1)S(1)} %dynamic-slice_bitcast_fusion.19), channel_id=1, source_target_pairs={{0,4},{1,5},{2,6},{3,7},{4,0},{5,1},{6,2},{7,3},{8,12},{9,13},{10,... | collective-permute-start | bytes 921608 | tf_op jit(solution)/shard_map/ppermute | solution.py:551
  391.4 18.9 %collective-permute-start.43 = (bf16[480,640]{1,0:T(8,128)(2,1)}, bf16[480,640]{1,0:T(8,128)(2,1)S(1)}, u32[]{:S(2)}, u32[]{:S(2)}) collective-permute-start(bf16[480,640]{1,0:T(8,128)(2,1)} %get-tuple-element.120), channel_id=1, source_target_pairs={{0,16},{8,24},{16,0},{24,8},{1,17},{9,25},{17,1},{25,9},{2,18},{10... | collective-permute-start | bytes 1843208 | tf_op jit(solution)/shard_map/ppermute | solution.py:793
  392.9 17.3 %collective-permute-start.42 = (bf16[480,640]{1,0:T(8,128)(2,1)}, bf16[480,640]{1,0:T(8,128)(2,1)S(1)}, u32[]{:S(2)}, u32[]{:S(2)}) collective-permute-start(bf16[480,640]{1,0:T(8,128)(2,1)} %get-tuple-element.116), channel_id=1, source_target_pairs={{0,8},{8,0},{16,24},{24,16},{1,9},{9,1},{17,25},{25,17},{2,10},{10... | collective-permute-start | bytes 1843208 | tf_op jit(solution)/shard_map/ppermute | solution.py:790
  395.1 25.6 %collective-permute-start.45 = (bf16[480,640]{1,0:T(8,128)(2,1)}, bf16[480,640]{1,0:T(8,128)(2,1)S(1)}, u32[]{:S(2)}, u32[]{:S(2)}) collective-permute-start(bf16[480,640]{1,0:T(8,128)(2,1)} %collective-permute-done.44), channel_id=1, source_target_pairs={{0,16},{8,24},{16,0},{24,8},{1,17},{9,25},{17,1},{25,9},{2,18},{10... | collective-permute-start | bytes 1843208 | tf_op jit(solution)/shard_map/ppermute | solution.py:793
  406.7 82.0 %collective-permute-start.28 = (bf16[1024,1280]{1,0:T(8,128)(2,1)}, bf16[1024,1280]{1,0:T(8,128)(2,1)S(1)}, u32[]{:S(2)}, u32[]{:S(2)}) collective-permute-start(bf16[1024,1280]{1,0:T(8,128)(2,1)} %input_side.2), channel_id=1, source_target_pairs={{0,8},{1,9},{2,10},{3,11},{4,12},{5,13},{6,14},{7,15},{8,0},{9,1},... | collective-permute-start | bytes 7864328 | tf_op jit(solution)/shard_map/ppermute | solution.py:813
  406.8 17.1 %collective-permute-start.59 = (bf16[120,1280]{1,0:T(8,128)(2,1)S(1)}, bf16[120,1280]{1,0:T(8,128)(2,1)S(1)}, u32[]{:S(2)}, u32[]{:S(2)}) collective-permute-start(bf16[120,1280]{1,0:T(8,128)(2,1)S(1)} %fusion.23), channel_id=1, source_target_pairs={{0,4},{1,5},{2,6},{3,7},{4,0},{5,1},{6,2},{7,3},{8,12},{9,13},{10,... | collective-permute-start | bytes 921608 | tf_op jit(solution)/shard_map/ppermute | solution.py:557
  421.2 16.8 %collective-permute-start.52 = (bf16[480,640]{1,0:T(8,128)(2,1)S(1)}, bf16[480,640]{1,0:T(8,128)(2,1)S(1)}, u32[]{:S(2)}, u32[]{:S(2)}) collective-permute-start(bf16[480,640]{1,0:T(8,128)(2,1)S(1)} %dynamic-slice_bitcast_fusion.14), channel_id=1, source_target_pairs={{0,1},{1,0},{2,3},{3,2},{4,5},{5,4},{6,7},{7,6},{8,9},{9,8},{10,11... | collective-permute-start | bytes 1843208 | tf_op jit(solution)/shard_map/ppermute | solution.py:551
  422.5 27.0 %collective-permute-start.46 = (bf16[480,640]{1,0:T(8,128)(2,1)S(1)}, bf16[480,640]{1,0:T(8,128)(2,1)S(1)}, u32[]{:S(2)}, u32[]{:S(2)}) collective-permute-start(bf16[480,640]{1,0:T(8,128)(2,1)S(1)} %dynamic-slice_bitcast_fusion.15), channel_id=1, source_target_pairs={{0,1},{1,0},{2,3},{3,2},{4,5},{5,4},{6,7},{7,6},{8,9},{9,8},{10,11... | collective-permute-start | bytes 1843208 | tf_op jit(solution)/shard_map/ppermute | solution.py:551
  424.0 55.9 %collective-permute-start.60 = (bf16[240,1280]{1,0:T(8,128)(2,1)S(1)}, bf16[240,1280]{1,0:T(8,128)(2,1)S(1)}, u32[]{:S(2)}, u32[]{:S(2)}) collective-permute-start(bf16[240,1280]{1,0:T(8,128)(2,1)S(1)} %maximum_select_fusion.6), channel_id=1, source_target_pairs={{0,2},{1,3},{2,0},{3,1},{4,6},{5,7},{6,4},{7,5},{8,10},{9,11},{10,... | collective-permute-start | bytes 1843208 | tf_op jit(solution)/shard_map/ppermute | solution.py:557
  438.2 12.3 %collective-permute-start.53 = (bf16[240,640]{1,0:T(8,128)(2,1)S(1)}, bf16[240,640]{1,0:T(8,128)(2,1)S(1)}, u32[]{:S(2)}, u32[]{:S(2)}) collective-permute-start(bf16[240,640]{1,0:T(8,128)(2,1)S(1)} %dynamic-slice_bitcast_fusion.17), channel_id=1, source_target_pairs={{0,2},{1,3},{2,0},{3,1},{4,6},{5,7},{6,4},{7,5},{8,10},{9,11},{10,... | collective-permute-start | bytes 921608 | tf_op jit(solution)/shard_map/ppermute | solution.py:551
  449.7 9.3 %collective-permute-start.47 = (bf16[240,640]{1,0:T(8,128)(2,1)S(1)}, bf16[240,640]{1,0:T(8,128)(2,1)S(1)}, u32[]{:S(2)}, u32[]{:S(2)}) collective-permute-start(bf16[240,640]{1,0:T(8,128)(2,1)S(1)} %dynamic-slice_bitcast_fusion.18), channel_id=1, source_target_pairs={{0,2},{1,3},{2,0},{3,1},{4,6},{5,7},{6,4},{7,5},{8,10},{9,11},{10,... | collective-permute-start | bytes 921608 | tf_op jit(solution)/shard_map/ppermute | solution.py:551
  450.7 11.6 %collective-permute-start.54 = (bf16[120,640]{1,0:T(8,128)(2,1)S(1)}, bf16[120,640]{1,0:T(8,128)(2,1)S(1)}, u32[]{:S(2)}, u32[]{:S(2)}) collective-permute-start(bf16[120,640]{1,0:T(8,128)(2,1)S(1)} %dynamic-slice_bitcast_fusion.20), channel_id=1, source_target_pairs={{0,4},{1,5},{2,6},{3,7},{4,0},{5,1},{6,2},{7,3},{8,12},{9,13},{10,... | collective-permute-start | bytes 460808 | tf_op jit(solution)/shard_map/ppermute | solution.py:551
  459.1 10.5 %collective-permute-start.48 = (bf16[120,640]{1,0:T(8,128)(2,1)S(1)}, bf16[120,640]{1,0:T(8,128)(2,1)S(1)}, u32[]{:S(2)}, u32[]{:S(2)}) collective-permute-start(bf16[120,640]{1,0:T(8,128)(2,1)S(1)} %dynamic-slice_bitcast_fusion.21), channel_id=1, source_target_pairs={{0,4},{1,5},{2,6},{3,7},{4,0},{5,1},{6,2},{7,3},{8,12},{9,13},{10,... | collective-permute-start | bytes 460808 | tf_op jit(solution)/shard_map/ppermute | solution.py:551
  462.3 13.8 %collective-permute-start.55 = (bf16[120,640]{1,0:T(8,128)(2,1)S(1)}, bf16[120,640]{1,0:T(8,128)(2,1)S(1)}, u32[]{:S(2)}, u32[]{:S(2)}) collective-permute-start(bf16[120,640]{1,0:T(8,128)(2,1)S(1)} %fusion.26), channel_id=1, source_target_pairs={{0,4},{1,5},{2,6},{3,7},{4,0},{5,1},{6,2},{7,3},{8,12},{9,13},{10,... | collective-permute-start | bytes 460808 | tf_op jit(solution)/shard_map/ppermute | solution.py:557
  469.6 11.7 %collective-permute-start.49 = (bf16[120,640]{1,0:T(8,128)(2,1)S(1)}, bf16[120,640]{1,0:T(8,128)(2,1)S(1)}, u32[]{:S(2)}, u32[]{:S(2)}) collective-permute-start(bf16[120,640]{1,0:T(8,128)(2,1)S(1)} %fusion.27), channel_id=1, source_target_pairs={{0,4},{1,5},{2,6},{3,7},{4,0},{5,1},{6,2},{7,3},{8,12},{9,13},{10,... | collective-permute-start | bytes 460808 | tf_op jit(solution)/shard_map/ppermute | solution.py:557
  476.2 11.3 %collective-permute-start.56 = (bf16[240,640]{1,0:T(8,128)(2,1)S(1)}, bf16[240,640]{1,0:T(8,128)(2,1)S(1)}, u32[]{:S(2)}, u32[]{:S(2)}) collective-permute-start(bf16[240,640]{1,0:T(8,128)(2,1)S(1)} %maximum_select_fusion.8), channel_id=1, source_target_pairs={{0,2},{1,3},{2,0},{3,1},{4,6},{5,7},{6,4},{7,5},{8,10},{9,11},{10,... | collective-permute-start | bytes 921608 | tf_op jit(solution)/shard_map/ppermute | solution.py:557
  480.3 30.0 %collective-permute-start.61 = (bf16[480,1280]{1,0:T(8,128)(2,1)S(1)}, bf16[480,1280]{1,0:T(8,128)(2,1)S(1)}, u32[]{:S(2)}, u32[]{:S(2)}) collective-permute-start(bf16[480,1280]{1,0:T(8,128)(2,1)S(1)} %maximum_select_fusion.3), channel_id=1, source_target_pairs={{0,1},{1,0},{2,3},{3,2},{4,5},{5,4},{6,7},{7,6},{8,9},{9,8},{10,11... | collective-permute-start | bytes 3686408 | tf_op jit(solution)/shard_map/ppermute | solution.py:557
  481.4 10.4 %collective-permute-start.50 = (bf16[240,640]{1,0:T(8,128)(2,1)S(1)}, bf16[240,640]{1,0:T(8,128)(2,1)S(1)}, u32[]{:S(2)}, u32[]{:S(2)}) collective-permute-start(bf16[240,640]{1,0:T(8,128)(2,1)S(1)} %maximum_select_fusion.7), channel_id=1, source_target_pairs={{0,2},{1,3},{2,0},{3,1},{4,6},{5,7},{6,4},{7,5},{8,10},{9,11},{10,... | collective-permute-start | bytes 921608 | tf_op jit(solution)/shard_map/ppermute | solution.py:557
  487.7 56.4 %collective-permute-start.57 = (bf16[480,640]{1,0:T(8,128)(2,1)S(1)}, bf16[480,640]{1,0:T(8,128)(2,1)S(1)}, u32[]{:S(2)}, u32[]{:S(2)}) collective-permute-start(bf16[480,640]{1,0:T(8,128)(2,1)S(1)} %maximum_select_fusion.5), channel_id=1, source_target_pairs={{0,1},{1,0},{2,3},{3,2},{4,5},{5,4},{6,7},{7,6},{8,9},{9,8},{10,11... | collective-permute-start | bytes 1843208 | tf_op jit(solution)/shard_map/ppermute | solution.py:557
  488.8 43.9 %slice-start.4 = ((s8[5242880]{0:T(1024)(128)(4,1)}), s8[4194304]{0:T(1024)(128)(4,1)S(1)}, s32[]{:S(2)}) async-start(s8[5242880]{0:T(1024)(128)(4,1)} %bitcast.207), calls=%async_computation.4 | async-start | bytes 8388608
  491.6 2.4 collective-permute-start.33
  492.0 57.3 %collective-permute-start.51 = (bf16[480,640]{1,0:T(8,128)(2,1)S(1)}, bf16[480,640]{1,0:T(8,128)(2,1)S(1)}, u32[]{:S(2)}, u32[]{:S(2)}) collective-permute-start(bf16[480,640]{1,0:T(8,128)(2,1)S(1)} %maximum_select_fusion.4), channel_id=1, source_target_pairs={{0,1},{1,0},{2,3},{3,2},{4,5},{5,4},{6,7},{7,6},{8,9},{9,8},{10,11... | collective-permute-start | bytes 1843208 | tf_op jit(solution)/shard_map/ppermute | solution.py:557
  494.0 16.8 %collective-permute-start.34 = (f32[5200]{0:T(1024)S(1)}, f32[5200]{0:T(1024)S(1)}, u32[]{:S(2)}, u32[]{:S(2)}) collective-permute-start(f32[5200]{0:T(1024)S(1)} %add.577), channel_id=1, source_target_pairs={{0,16},{8,24},{16,0},{24,8},{1,17},{9,25},{17,1},{25,9},{2,18},{10... | collective-permute-start | bytes 62408 | tf_op jit(solution)/shard_map/ppermute | solution.py:574
  510.9 20.9 %collective-permute-start.35 = (f32[5200]{0:T(1024)S(1)}, f32[5200]{0:T(1024)S(1)}, u32[]{:S(2)}, u32[]{:S(2)}) collective-permute-start(f32[5200]{0:T(1024)S(1)} %add.578), channel_id=1, source_target_pairs={{0,1},{1,0},{2,3},{3,2},{4,5},{5,4},{6,7},{7,6},{8,9},{9,8},{10,11... | collective-permute-start | bytes 62408 | tf_op jit(solution)/shard_map/ppermute | solution.py:576
  531.8 3.8 collective-permute-start.36
  535.6 8.5 %collective-permute-start.37 = (f32[5200]{0:T(1024)S(1)}, f32[5200]{0:T(1024)S(1)}, u32[]{:S(2)}, u32[]{:S(2)}) collective-permute-start(f32[5200]{0:T(1024)S(1)} %add.580), channel_id=1, source_target_pairs={{0,4},{1,5},{2,6},{3,7},{4,0},{5,1},{6,2},{7,3},{8,12},{9,13},{10,... | collective-permute-start | bytes 62408 | tf_op jit(solution)/shard_map/ppermute | solution.py:576
  540.4 17.7 %collective-permute-start.32 = (bf16[256,1280]{1,0:T(8,128)(2,1)S(1)}, bf16[256,1280]{1,0:T(8,128)(2,1)S(1)}, u32[]{:S(2)}, u32[]{:S(2)}) collective-permute-start(bf16[256,1280]{1,0:T(8,128)(2,1)S(1)} %get-tuple-element.161), channel_id=1, source_target_pairs={{6,0},{14,1},{0,2},{8,3},{2,4},{10,5},{4,6},{12,7},{7,8},{15,9},{1... | collective-permute-start | bytes 1966088 | tf_op jit(solution)/shard_map/ppermute | solution.py:619
  540.5 56.7 %collective-permute-start.31 = (bf16[256,1280]{1,0:T(8,128)(2,1)S(1)}, bf16[256,1280]{1,0:T(8,128)(2,1)S(1)}, u32[]{:S(2)}, u32[]{:S(2)}) collective-permute-start(bf16[256,1280]{1,0:T(8,128)(2,1)S(1)} %get-tuple-element.162), channel_id=1, source_target_pairs={{4,0},{12,1},{6,2},{14,3},{0,4},{8,5},{2,6},{10,7},{5,8},{13,9},{7... | collective-permute-start | bytes 1966088 | tf_op jit(solution)/shard_map/ppermute | solution.py:619
  544.1 56.1 %collective-permute-start.30 = (bf16[256,1280]{1,0:T(8,128)(2,1)S(1)}, bf16[256,1280]{1,0:T(8,128)(2,1)S(1)}, u32[]{:S(2)}, u32[]{:S(2)}) collective-permute-start(bf16[256,1280]{1,0:T(8,128)(2,1)S(1)} %get-tuple-element.163), channel_id=1, source_target_pairs={{2,0},{10,1},{4,2},{12,3},{6,4},{14,5},{0,6},{8,7},{3,8},{11,9},{5... | collective-permute-start | bytes 1966088 | tf_op jit(solution)/shard_map/ppermute | solution.py:619
  544.1 56.1 %collective-permute-start.29 = (bf16[256,1280]{1,0:T(8,128)(2,1)S(1)}, bf16[256,1280]{1,0:T(8,128)(2,1)S(1)}, u32[]{:S(2)}, u32[]{:S(2)}) collective-permute-start(bf16[256,1280]{1,0:T(8,128)(2,1)S(1)} %get-tuple-element.164), channel_id=1, source_target_pairs={{0,0},{8,1},{2,2},{10,3},{4,4},{12,5},{6,6},{14,7},{1,8},{9,9},{3,... | collective-permute-start | bytes 1966088 | tf_op jit(solution)/shard_map/ppermute | solution.py:619
  (56 other events, 470.7 us)

commit v6 on v5

--- a/solution.py
+++ b/solution.py
@@ -537,7 +537,7 @@
     )(*grads, w)
 
 
-def reduce_places(buf, places):
+def reduce_places(buf, places, late=()):
     place = lax.axis_index("seq")
     lines, wide = buf.shape
     bits = places.bit_length() - 1
@@ -553,6 +553,8 @@
         buf = (keep.astype(f32) + got.astype(f32)).astype(bf16)
     for b in reversed(range(bits)):
         bit = (place >> b) & 1
+        if late and b == 0:
+            buf = after(buf, *late)
         yield buf
         got = lax.ppermute(buf, "seq", [(i, i ^ (1 << b)) for i in range(places)])
         buf = jnp.where(
@@ -822,7 +824,8 @@
         scaled_in
         - x_float * rms_in * rms_in * jnp.mean(scaled_in * x_float, axis=-1, keepdims=True)
     )
-    input_grad = unspread_done(unspread(input_grad_own.astype(bf16)), f32)
+    input_grad_own = input_grad_own.astype(bf16)
+    input_grad = unspread_done(unspread(input_grad_own), f32)
     result = unspread_done(result, bf16)
 
     three = last(steps).astype(f32)
@@ -835,7 +838,7 @@
             [add(mine, *[f[0] for f in far]), add(theirs, *[f[1] for f in far])]
         )
         total = place_in([(total, member // 2)], team.half) if team.half > 1 else total
-        full.append(last(reduce_places(total.reshape(-1, total.shape[-1]), team.seq)))
+        full.append(last(reduce_places(total.reshape(-1, total.shape[-1]), team.seq, (input_grad_own,))))
     full = unfold(full, team.half, rows_here, core).reshape(heads, 3, head_size, rows_here)
     vectors = sum_everywhere(
         team,

time: 617 us -> 597 us (0.968)
  waiting for transfers between devices: 202 us -> 186 us
  starting transfers between devices: 86.3 us -> 77.1 us
    ppermute x8, waiting for transfers between devices: 65.1 us -> 46.9 us  [unspread(): lax.ppermute(array[step * span:(step + 1) * span], axes, team.back(step))]
    ppermute x3, waiting for transfers between devices: 20.4 us -> 12.6 us  [sum_everywhere(): lax.ppermute(total, 'seq', [(i, i ^ 1 << b) for i in range(team.seq)])]
    unnamed x124 -> x128, local copies, waits for them, and re-layouts: 13.5 us -> 14.6 us
  transfers between devices with their start and end apart: 62 -> 62, of which waited for: 22 -> 25; matrix products, arithmetic and copies ran while one was open for 14% -> 14% of each run, Pallas kernels for 27% -> 28%
where the time goes in v6:
time: 597 us; the launch traced here: 587 us
  waiting for transfers between devices  186 us (31%)
  Pallas kernels  178 us (30%)
  starting transfers between devices  77.1 us (13%)
  matrix products  52.1 us (9%)
  other arithmetic  47.2 us (8%)
  local copies, waits for them, and re-layouts  44.7 us (7%)
    pallas_call x2, Pallas kernels, attend_back(): pl.pallas_call(functools.partial(attend_back_kernel, count, block, pair),...  50.2 us
    ppermute x8, waiting for transfers between devices, unspread(): lax.ppermute(array[step * span:(step + 1) * span], axes, team.back(step))  46.9 us
    dot_general x8, matrix products, mm(): return lax.dot_general(a, b, dims, preferred_element_type=f32)  45.8 us
    ppermute x9, waiting for transfers between devices, reduce_places(): got = lax.ppermute(send, 'seq', [(i, i ^ 1 << b) for i in range(places)])  40.2 us
    pallas_call x7, Pallas kernels, join(): pl.pallas_call(functools.partial(join_kernel, count, ends), grid_spec=plt...  33.7 us
    ppermute x2, waiting for transfers between devices, on_device(): lax.ppermute(parts[flip], 'dp', team.turn_rows(step, flip))  33.1 us
    ppermute x9, waiting for transfers between devices, reduce_places(): got = lax.ppermute(buf, 'seq', [(i, i ^ 1 << b) for i in range(places)])  27.6 us
    pallas_call x1, Pallas kernels, attend(): pl.pallas_call(functools.partial(attend_kernel, count, block, pair), grid...  24.8 us
  transfers between devices with their start and end apart: 62, of which 25 were waited for; matrix products, arithmetic and copies ran while one was open for 14% of the time, Pallas kernels for 28%

profile of v6, /device:TPU:12, one launch (start us, length us, event | category | flops | bytes accessed | tf_op | source)
XLA Modules:
  0.0 587.3 jit_solution(6906507780751309413)
XLA Ops:
  0.7 2.8 concatenate.90
  9.8 2.5 pad_maximum_fusion.4
  18.5 2.6 collective-permute-start.3
  21.1 4.1 convert_reduce_fusion
  28.2 2.5 collective-permute-start.2
  30.7 12.5 %collective-permute-done.6.refs_3_ = bf16[336,1920]{1,0:T(8,128)(2,1)S(1)} collective-permute-done((bf16[336,1920]{1,0:T(8,128)(2,1)}, bf16[336,1920]{1,0:T(8,128)(2,1)S(1)}, u32[]{:S(2)}, u32[]{:S(2)}) %collective-permute-start.6) | collective-permute-done | bytes 1290272 | tf_op jit(solution)/shard_map/ppermute | solution.py:643
  43.2 6.6 %collective-permute-start.1 = (bf16[256,1280]{1,0:T(8,128)(2,1)}, bf16[256,1280]{1,0:T(8,128)(2,1)}, u32[]{:S(2)}, u32[]{:S(2)}) collective-permute-start(bf16[256,1280]{1,0:T(8,128)(2,1)} %get-tuple-element.184), channel_id=1, source_target_pairs={{0,0},{1,8},{2,2},{3,10},{4,4},{5,12},{6,6},{7,14},{8,1},{9,9},{10... | collective-permute-start | bytes 1966088 | tf_op jit(solution)/shard_map/ppermute | solution.py:613
  50.4 20.6 %collective-permute-done.5.refs_2_ = bf16[336,1920]{1,0:T(8,128)(2,1)} collective-permute-done((bf16[336,1920]{1,0:T(8,128)(2,1)S(1)}, bf16[336,1920]{1,0:T(8,128)(2,1)}, u32[]{:S(2)}, u32[]{:S(2)}) %collective-permute-start.5) | collective-permute-done | bytes 1290272 | tf_op jit(solution)/shard_map/ppermute | solution.py:643
  71.0 6.4 %join.7 = (bf16[4,320,1920]{2,1,0:T(8,128)(2,1)}, bf16[4,16,1920]{2,1,0:T(8,128)(2,1)}) custom-call(s32[4]{0:T(128)} %add_add_fusion.slots_ref, bf16[336,1920]{1,0:T(8,128)(2,1)} %copy-done.9, bf16[336,1920]{1,0:T(8,128)(2,1)} %collective-permute-done.refs_1_, bf16[336,1920]{1,0:T(8,128)(2,1)} %collective-permute-done.5.refs_2_, bf16[336,1920]{1,0:T(8,128)(2,1)} %copy-done.22), custom_call_target="tpu_custom_call" | custom-call | flops 1 | bytes 1 | tf_op jit(solution)/shard_map/join/pallas_call | solution.py:116
  78.3 3.9 join.8
  82.4 3.2 pad_maximum_fusion.1.refs_0_
  92.8 19.7 %qkv.1 = (bf16[8,3,2048,80]{3,2,1,0:T(8,128)(2,1)}, bf16[2,2048,640]{2,1,0:T(8,128)(2,1)}) custom-call(bf16[1024,1280]{1,0:T(8,128)(2,1)} %bitcast.199, bf16[1024,1280]{1,0:T(8,128)(2,1)} %copy-done.20, f32[1,1280]{1,0:T(1,128)} %slice.77.refs_2_, bf16[1280,1920]{1,0:T(8,128)(2,1)} %bitcast.216, f32[1,1920]{1,0:T(1,128)} %broadcast_in_dim_tile.3.refs_4_), custom_call_target="tpu_custom_call" | custom-call | flops 1 | bytes 1 | tf_op jit(solution)/shard_map/qkv/pallas_call | solution.py:163
  112.4 8.7 %collective-permute-done.9.refs_1_ = bf16[256,1280]{1,0:T(8,128)(2,1)} collective-permute-done((bf16[256,1280]{1,0:T(8,128)(2,1)}, bf16[256,1280]{1,0:T(8,128)(2,1)}, u32[]{:S(2)}, u32[]{:S(2)}) %collective-permute-start.9) | collective-permute-done | bytes 655392 | tf_op jit(solution)/shard_map/ppermute | solution.py:613
  121.2 24.8 %attend.1 = (bf16[640,2048]{1,0:T(8,128)(2,1)}, f32[8,1,2048]{2,1,0:T(1,128)}) custom-call(s32[5,8]{1,0:T(8,128)} %stack.83.table, bf16[8,3,2048,80]{3,2,1,0:T(8,128)(2,1)} %get-tuple-element.85.qkv_ref, s32[8,256]{1,0:T(8,128)} %copy-done.33), custom_call_target="tpu_custom_call" | custom-call | flops 1 | bytes 1 | tf_op jit(solution)/shard_map/attend/pallas_call | solution.py:357
  146.5 3.0 fusion.39
  153.0 3.2 collective-permute-done.11.refs_1_
  157.3 3.5 join.9
  160.9 8.0 %join.10 = (bf16[4,320,1280]{2,1,0:T(8,128)(2,1)}, bf16[4,320,1280]{2,1,0:T(8,128)(2,1)}, bf16[4,320,1280]{2,1,0:T(8,128)(2,1)}) custom-call(s32[4]{0:T(128)} %add_add_fusion.1.slots_ref, bf16[960,1280]{1,0:T(8,128)(2,1)} %pad_maximum_fusion.1.refs_0_, bf16[960,1280]{1,0:T(8,128)(2,1)} %collective-permute-done.12.refs_1_, ...), custom_call_target="tpu_custom_call" | custom-call | flops 1 | bytes 1 | tf_op jit(solution)/shard_map/join/pallas_call | solution.py:116
  168.9 6.3 %multiply_reduce_fusion.3 = (f32[1024]{0:T(1024)S(1)}, f32[1024,1280]{1,0:T(8,128)S(1)}) fusion(bf16[1280,1024]{1,0:T(8,128)(2,1)S(1)} %bitcast.209, bf16[1280,1280]{1,0:T(8,128)(2,1)} %bitcast.225, bf16[1024,1280]{1,0:T(8,128)(2,1)S(1)} %bitcast.200), kind=kOutput, calls=%fused_computation.30 | convolution fusion | flops 3360685056 | bytes 13766656 | tf_op jit(solution)/shard_map/dot_general | solution.py:713
  175.2 3.7 fusion.35
  179.0 5.7 add_convert_fusion
  186.1 3.9 join.11
  190.0 11.0 %convert_reduce_fusion.3 = (f32[1280]{0:T(1024)}, bf16[1024,1280]{1,0:T(8,128)(2,1)}) fusion(f32[1024,1280]{1,0:T(8,128)} %copy-done.50, f32[1280]{0:T(1024)S(1)} %add.541, bf16[1024,1280]{1,0:T(8,128)(2,1)} %bitcast.201, bf16[1280,1280]{1,0:T(8,128)(2,1)} %bitcast.253), kind=kOutput, calls=%fused_computation.19 | convolution fusion | flops 3371170560 | bytes 13772800 | tf_op jit(solution)/shard_map/dot_general | solution.py:25
  201.1 4.0 convolution_convert_fusion.2
  205.1 7.5 %multiply_reduce_fusion = (f32[1280]{0:T(1024)}, f32[1024]{0:T(1024)S(1)}, f32[1024,1280]{1,0:T(8,128)S(1)}) fusion(f32[1024,1280]{1,0:T(8,128)S(1)} %bitcast.204, f32[1024]{0:T(1024)S(1)} %add_rsqrt_fusion, f32[1280]{0:T(1024)S(1)} %mul.203, bf16[1024,1280]{1,0:T(8,128)(2,1)} %get-tuple-element.195, bf16[1280,1280]{1,0:T(8,128)(2,1)S(1)} %bitcast.252), kind=kOutput, calls=%fused_computation.20 | convolution fusion | flops 3363305216 | bytes 16402432 | tf_op jit(solution)/shard_map/dot_general | solution.py:25
  212.6 5.8 convolution_convert_fusion.1
  223.7 4.2 convolution_convert_fusion
  234.1 2.9 fusion.16
  237.0 2.8 fusion.15
  242.7 3.9 convolution_convert_fusion.3
  253.2 6.6 %collective-permute-start.15 = (bf16[256,1280]{1,0:T(8,128)(2,1)}, bf16[256,1280]{1,0:T(8,128)(2,1)}, u32[]{:S(2)}, u32[]{:S(2)}) collective-permute-start(bf16[256,1280]{1,0:T(8,128)(2,1)} %get-tuple-element.178), channel_id=1, source_target_pairs={{0,0},{8,1},{2,2},{10,3},{4,4},{12,5},{6,6},{14,7},{1,8},{9,9},{3,... | collective-permute-start | bytes 1966088 | tf_op jit(solution)/shard_map/ppermute | solution.py:621
  261.0 3.5 pad_maximum_fusion.grad_ref
  264.5 24.9 %attend_back.2 = (bf16[960,2048]{1,0:T(8,128)(2,1)}, f32[80,1]{1,0:T(8,128)}) custom-call(s32[5,8]{1,0:T(8,128)} %stack.83.table, bf16[8,3,2048,80]{3,2,1,0:T(8,128)(2,1)} %get-tuple-element.85.qkv_ref, bf16[640,2048]{1,0:T(8,128)(2,1)} %get-tuple-element.86.att_ref, bf16[640,2048]{1,0:T(8,128)(2,1)} %pad_maximum_fusion.grad_ref, ...), custom_call_target="tpu_custom_call" | custom-call | flops 1 | bytes 1 | tf_op jit(solution)/shard_map/attend_back/pallas_call | solution.py:479
  289.4 19.2 %collective-permute-done.17.refs_2_ = bf16[256,1280]{1,0:T(8,128)(2,1)} collective-permute-done((bf16[256,1280]{1,0:T(8,128)(2,1)}, bf16[256,1280]{1,0:T(8,128)(2,1)}, u32[]{:S(2)}, u32[]{:S(2)}) %collective-permute-start.17) | collective-permute-done | bytes 655392 | tf_op jit(solution)/shard_map/ppermute | solution.py:621
  308.6 2.6 collective-permute-done.16.refs_1_
  311.2 12.3 %head_grad.2 = (bf16[480,640]{1,0:T(8,128)(2,1)}, bf16[480,640]{1,0:T(8,128)(2,1)}, bf16[480,640]{1,0:T(8,128)(2,1)}, bf16[480,640]{1,0:T(8,128)(2,1)}) custom-call(s32[3]{0:T(128)} %pad_add_fusion.2.place_ref, bf16[960,2048]{1,0:T(8,128)(2,1)} %get-tuple-element.125.grads_ref.refs_0_, bf16[2,2048,640]{2,1,0:T(8,128)(2,1)} %get-tuple-element.107.normed_ref), custom_call_target="tpu_custom_call" | custom-call | flops 1 | bytes 1 | tf_op jit(solution)/shard_map/head_grad/pallas_call | solution.py:209
  330.7 25.3 %attend_back.3 = (bf16[960,2048]{1,0:T(8,128)(2,1)}, f32[80,1]{1,0:T(8,128)}) custom-call(s32[5,8]{1,0:T(8,128)} %stack.83.table, bf16[8,3,2048,80]{3,2,1,0:T(8,128)(2,1)} %get-tuple-element.85.qkv_ref, bf16[640,2048]{1,0:T(8,128)(2,1)} %get-tuple-element.86.att_ref, bf16[640,2048]{1,0:T(8,128)(2,1)} %pad_maximum_fusion.grad_ref, ...), custom_call_target="tpu_custom_call" | custom-call | flops 1 | bytes 1 | tf_op jit(solution)/shard_map/attend_back/pallas_call | solution.py:479
  363.7 3.5 join.12
  368.6 12.2 %head_grad.3 = (bf16[480,640]{1,0:T(8,128)(2,1)}, bf16[480,640]{1,0:T(8,128)(2,1)}, bf16[480,640]{1,0:T(8,128)(2,1)}, bf16[480,640]{1,0:T(8,128)(2,1)}) custom-call(s32[3]{0:T(128)} %pad_add_fusion.2.place_ref, bf16[960,2048]{1,0:T(8,128)(2,1)} %get-tuple-element.126.grads_ref.refs_1_, bf16[2,2048,640]{2,1,0:T(8,128)(2,1)} %get-tuple-element.107.normed_ref), custom_call_target="tpu_custom_call" | custom-call | flops 1 | bytes 1 | tf_op jit(solution)/shard_map/head_grad/pallas_call | solution.py:209
  382.5 9.9 %input_side.2 = bf16[1024,1280]{1,0:T(8,128)(2,1)} custom-call(bf16[960,2048]{1,0:T(8,128)(2,1)} %get-tuple-element.125.grads_ref.refs_0_, bf16[960,2048]{1,0:T(8,128)(2,1)} %get-tuple-element.126.grads_ref.refs_1_, bf16[1280,1920]{1,0:T(8,128)(2,1)} %bitcast.217), custom_call_target="tpu_custom_call" | custom-call | flops 10066329600 | bytes 1 | tf_op jit(solution)/shard_map/input_side/pallas_call | solution.py:525
  397.5 10.1 %input_side.3 = bf16[1024,1280]{1,0:T(8,128)(2,1)} custom-call(bf16[960,2048]{1,0:T(8,128)(2,1)} %get-tuple-element.125.grads_ref.refs_0_, bf16[960,2048]{1,0:T(8,128)(2,1)} %get-tuple-element.126.grads_ref.refs_1_, bf16[1280,1920]{1,0:T(8,128)(2,1)} %bitcast.218), custom_call_target="tpu_custom_call" | custom-call | flops 10066329600 | bytes 1 | tf_op jit(solution)/shard_map/input_side/pallas_call | solution.py:525
  407.8 3.4 collective-permute-start.59
  411.2 10.3 %collective-permute-done.45 = bf16[480,640]{1,0:T(8,128)(2,1)S(1)} collective-permute-done((bf16[480,640]{1,0:T(8,128)(2,1)}, bf16[480,640]{1,0:T(8,128)(2,1)S(1)}, u32[]{:S(2)}, u32[]{:S(2)}) %collective-permute-start.45) | collective-permute-done | bytes 614432 | tf_op jit(solution)/shard_map/ppermute | solution.py:795
  427.3 11.6 %collective-permute-done.52 = bf16[480,640]{1,0:T(8,128)(2,1)S(1)} collective-permute-done((bf16[480,640]{1,0:T(8,128)(2,1)S(1)}, bf16[480,640]{1,0:T(8,128)(2,1)S(1)}, u32[]{:S(2)}, u32[]{:S(2)}) %collective-permute-start.52) | collective-permute-done | bytes 614432 | tf_op jit(solution)/shard_map/ppermute | solution.py:551
  440.2 10.0 %collective-permute-done.46 = bf16[480,640]{1,0:T(8,128)(2,1)S(1)} collective-permute-done((bf16[480,640]{1,0:T(8,128)(2,1)S(1)}, bf16[480,640]{1,0:T(8,128)(2,1)S(1)}, u32[]{:S(2)}, u32[]{:S(2)}) %collective-permute-start.46) | collective-permute-done | bytes 614432 | tf_op jit(solution)/shard_map/ppermute | solution.py:551
  453.5 6.4 %collective-permute-done.47 = bf16[240,640]{1,0:T(8,128)(2,1)S(1)} collective-permute-done((bf16[240,640]{1,0:T(8,128)(2,1)S(1)}, bf16[240,640]{1,0:T(8,128)(2,1)S(1)}, u32[]{:S(2)}, u32[]{:S(2)}) %collective-permute-start.47) | collective-permute-done | bytes 307232 | tf_op jit(solution)/shard_map/ppermute | solution.py:551
  460.0 3.2 collective-permute-start.48
  463.3 8.0 %collective-permute-done.48 = bf16[120,640]{1,0:T(8,128)(2,1)S(1)} collective-permute-done((bf16[120,640]{1,0:T(8,128)(2,1)S(1)}, bf16[120,640]{1,0:T(8,128)(2,1)S(1)}, u32[]{:S(2)}, u32[]{:S(2)}) %collective-permute-start.48) | collective-permute-done | bytes 153632 | tf_op jit(solution)/shard_map/ppermute | solution.py:551
  471.4 3.4 collective-permute-start.49
  474.9 3.1 collective-permute-done.55
  478.0 3.0 collective-permute-start.56
  483.5 5.3 collective-permute-done.56
  489.0 2.7 fusion.8
  495.5 2.5 collective-permute-done.34
  498.8 2.5 fusion.5
  502.6 9.4 %collective-permute-done.35 = f32[5200]{0:T(1024)S(1)} collective-permute-done((f32[5200]{0:T(1024)S(1)}, f32[5200]{0:T(1024)S(1)}, u32[]{:S(2)}, u32[]{:S(2)}) %collective-permute-start.35) | collective-permute-done | bytes 20832 | tf_op jit(solution)/shard_map/ppermute | solution.py:578
  512.6 3.2 collective-permute-done.36
  516.5 3.3 collective-permute-start.57
  519.8 4.1 collective-permute-start.32
  531.9 16.0 %collective-permute-done.57 = bf16[480,640]{1,0:T(8,128)(2,1)S(1)} collective-permute-done((bf16[480,640]{1,0:T(8,128)(2,1)S(1)}, bf16[480,640]{1,0:T(8,128)(2,1)S(1)}, u32[]{:S(2)}, u32[]{:S(2)}) %collective-permute-start.57) | collective-permute-done | bytes 614432 | tf_op jit(solution)/shard_map/ppermute | solution.py:559
  550.1 5.4 unfold.1
  555.5 11.6 %collective-permute-done.32.refs_3_ = bf16[256,1280]{1,0:T(8,128)(2,1)S(1)} collective-permute-done((bf16[256,1280]{1,0:T(8,128)(2,1)S(1)}, bf16[256,1280]{1,0:T(8,128)(2,1)S(1)}, u32[]{:S(2)}, u32[]{:S(2)}) %collective-permute-start.32) | collective-permute-done | bytes 655392 | tf_op jit(solution)/shard_map/ppermute | solution.py:621
  567.1 13.0 %collective-permute-done.31.refs_2_ = bf16[256,1280]{1,0:T(8,128)(2,1)S(1)} collective-permute-done((bf16[256,1280]{1,0:T(8,128)(2,1)S(1)}, bf16[256,1280]{1,0:T(8,128)(2,1)S(1)}, u32[]{:S(2)}, u32[]{:S(2)}) %collective-permute-start.31) | collective-permute-done | bytes 655392 | tf_op jit(solution)/shard_map/ppermute | solution.py:621
  582.4 4.5 join.13
  (328 shorter events, 108.7 us)
Async XLA Ops:
  12.4 30.8 %collective-permute-start.6 = (bf16[336,1920]{1,0:T(8,128)(2,1)}, bf16[336,1920]{1,0:T(8,128)(2,1)S(1)}, u32[]{:S(2)}, u32[]{:S(2)}) collective-permute-start(bf16[336,1920]{1,0:T(8,128)(2,1)} %get-tuple-element.185), channel_id=1, source_target_pairs={{0,24},{8,16},{16,8},{24,0},{1,25},{9,17},{17,9},{25,1},{2,26},{10... | collective-permute-start | bytes 3870728 | tf_op jit(solution)/shard_map/ppermute | solution.py:643
  12.4 13.4 %collective-permute-start = (bf16[336,1920]{1,0:T(8,128)(2,1)}, bf16[336,1920]{1,0:T(8,128)(2,1)}, u32[]{:S(2)}, u32[]{:S(2)}) collective-permute-start(bf16[336,1920]{1,0:T(8,128)(2,1)} %get-tuple-element.185), channel_id=1, source_target_pairs={{0,8},{8,0},{16,24},{24,16},{1,9},{9,1},{17,25},{25,17},{2,10},{10... | collective-permute-start | bytes 3870728 | tf_op jit(solution)/shard_map/ppermute | solution.py:645
  13.0 5.6 collective-permute-start.7
  13.0 58.0 %collective-permute-start.5 = (bf16[336,1920]{1,0:T(8,128)(2,1)S(1)}, bf16[336,1920]{1,0:T(8,128)(2,1)}, u32[]{:S(2)}, u32[]{:S(2)}) collective-permute-start(bf16[336,1920]{1,0:T(8,128)(2,1)S(1)} %get-tuple-element.186.refs_0_), channel_id=1, source_target_pairs={{0,16},{8,24},{16,0},{24,8},{1,17},{9,25},{17,1},{25,9},{2,18},{10... | collective-permute-start | bytes 3870728 | tf_op jit(solution)/shard_map/ppermute | solution.py:643
  16.7 60.7 %collective-permute-start.4 = (bf16[256,1280]{1,0:T(8,128)(2,1)}, bf16[256,1280]{1,0:T(8,128)(2,1)}, u32[]{:S(2)}, u32[]{:S(2)}) collective-permute-start(bf16[256,1280]{1,0:T(8,128)(2,1)} %get-tuple-element.181), channel_id=1, source_target_pairs={{0,6},{1,14},{2,0},{3,8},{4,2},{5,10},{6,4},{7,12},{8,7},{9,15},{1... | collective-permute-start | bytes 1966088 | tf_op jit(solution)/shard_map/ppermute | solution.py:613
  18.5 58.9 %collective-permute-start.3 = (bf16[256,1280]{1,0:T(8,128)(2,1)S(1)}, bf16[256,1280]{1,0:T(8,128)(2,1)}, u32[]{:S(2)}, u32[]{:S(2)}) collective-permute-start(bf16[256,1280]{1,0:T(8,128)(2,1)S(1)} %get-tuple-element.182), channel_id=1, source_target_pairs={{0,4},{1,12},{2,6},{3,14},{4,0},{5,8},{6,2},{7,10},{8,5},{9,13},{1... | collective-permute-start | bytes 1966088 | tf_op jit(solution)/shard_map/ppermute | solution.py:613
  25.3 52.1 %copy-start.33 = (s32[8,256]{1,0:T(8,128)}, s32[8,256]{1,0:T(8,128)S(1)}, u32[]{:S(2)}) copy-start(s32[8,256]{1,0:T(8,128)S(1)} %reshape.562.start_ref) | copy-start | bytes 24580
  28.2 49.6 %collective-permute-start.2 = (bf16[256,1280]{1,0:T(8,128)(2,1)}, bf16[256,1280]{1,0:T(8,128)(2,1)}, u32[]{:S(2)}, u32[]{:S(2)}) collective-permute-start(bf16[256,1280]{1,0:T(8,128)(2,1)} %get-tuple-element.183), channel_id=1, source_target_pairs={{0,2},{1,10},{2,4},{3,12},{4,6},{5,14},{6,0},{7,8},{8,3},{9,11},{1... | collective-permute-start | bytes 1966088 | tf_op jit(solution)/shard_map/ppermute | solution.py:613
  43.2 34.6 %collective-permute-start.1 = (bf16[256,1280]{1,0:T(8,128)(2,1)}, bf16[256,1280]{1,0:T(8,128)(2,1)}, u32[]{:S(2)}, u32[]{:S(2)}) collective-permute-start(bf16[256,1280]{1,0:T(8,128)(2,1)} %get-tuple-element.184), channel_id=1, source_target_pairs={{0,0},{1,8},{2,2},{3,10},{4,4},{5,12},{6,6},{7,14},{8,1},{9,9},{10... | collective-permute-start | bytes 1966088 | tf_op jit(solution)/shard_map/ppermute | solution.py:613
  82.3 9.0 %collective-permute-start.8 = (bf16[1024,1280]{1,0:T(8,128)(2,1)}, bf16[1024,1280]{1,0:T(8,128)(2,1)S(1)}, u32[]{:S(2)}, u32[]{:S(2)}) collective-permute-start(bf16[1024,1280]{1,0:T(8,128)(2,1)} %bitcast.198), channel_id=1, source_target_pairs={{0,8},{1,9},{2,10},{3,11},{4,12},{5,13},{6,14},{7,15},{8,0},{9,1},... | collective-permute-start | bytes 7864328 | tf_op jit(solution)/shard_map/ppermute | solution.py:687
  85.6 60.3 %collective-permute-start.12 = (bf16[960,1280]{1,0:T(8,128)(2,1)}, bf16[960,1280]{1,0:T(8,128)(2,1)}, u32[]{:S(2)}, u32[]{:S(2)}) collective-permute-start(bf16[960,1280]{1,0:T(8,128)(2,1)} %pad_maximum_fusion.1.refs_0_), channel_id=1, source_target_pairs={{0,16},{8,24},{16,0},{24,8},{1,17},{9,25},{17,1},{25,9},{2,18},{10... | collective-permute-start | bytes 7372808 | tf_op jit(solution)/shard_map/ppermute | solution.py:659
  88.0 24.5 %collective-permute-start.10 = (bf16[256,1280]{1,0:T(8,128)(2,1)}, bf16[256,1280]{1,0:T(8,128)(2,1)}, u32[]{:S(2)}, u32[]{:S(2)}) collective-permute-start(bf16[256,1280]{1,0:T(8,128)(2,1)} %get-tuple-element.173), channel_id=1, source_target_pairs={{0,6},{1,14},{2,0},{3,8},{4,2},{5,10},{6,4},{7,12},{8,7},{9,15},{1... | collective-permute-start | bytes 1966088 | tf_op jit(solution)/shard_map/ppermute | solution.py:613
  88.3 32.9 %collective-permute-start.9 = (bf16[256,1280]{1,0:T(8,128)(2,1)}, bf16[256,1280]{1,0:T(8,128)(2,1)}, u32[]{:S(2)}, u32[]{:S(2)}) collective-permute-start(bf16[256,1280]{1,0:T(8,128)(2,1)} %get-tuple-element.174), channel_id=1, source_target_pairs={{0,2},{1,10},{2,4},{3,12},{4,6},{5,14},{6,0},{7,8},{8,3},{9,11},{1... | collective-permute-start | bytes 1966088 | tf_op jit(solution)/shard_map/ppermute | solution.py:613
  145.9 14.9 %collective-permute-start.13 = (bf16[960,1280]{1,0:T(8,128)(2,1)}, bf16[960,1280]{1,0:T(8,128)(2,1)}, u32[]{:S(2)}, u32[]{:S(2)}) collective-permute-start(bf16[960,1280]{1,0:T(8,128)(2,1)} %pad_maximum_fusion.1.refs_0_), channel_id=1, source_target_pairs={{0,8},{8,0},{16,24},{24,16},{1,9},{9,1},{17,25},{25,17},{2,10},{10... | collective-permute-start | bytes 7372808 | tf_op jit(solution)/shard_map/ppermute | solution.py:694
  146.3 14.6 %collective-permute-start.14 = (bf16[960,1280]{1,0:T(8,128)(2,1)}, bf16[960,1280]{1,0:T(8,128)(2,1)}, u32[]{:S(2)}, u32[]{:S(2)}) collective-permute-start(bf16[960,1280]{1,0:T(8,128)(2,1)} %collective-permute-done.12.refs_1_), channel_id=1, source_target_pairs={{0,8},{8,0},{16,24},{24,16},{1,9},{9,1},{17,25},{25,17},{2,10},{10... | collective-permute-start | bytes 7372808 | tf_op jit(solution)/shard_map/ppermute | solution.py:694
  149.5 6.8 %collective-permute-start.11 = (bf16[640,1024]{1,0:T(8,128)(2,1)S(1)}, bf16[640,1024]{1,0:T(8,128)(2,1)S(1)}, u32[]{:S(2)}, u32[]{:S(2)}) collective-permute-start(bf16[640,1024]{1,0:T(8,128)(2,1)S(1)} %get-tuple-element.179), channel_id=1, source_target_pairs={{0,8},{1,9},{2,10},{3,11},{4,12},{5,13},{6,14},{7,15},{8,0},{9,1},... | collective-permute-start | bytes 3932168 | tf_op jit(solution)/shard_map/ppermute | solution.py:707
  151.4 33.3 %collective-permute-start.20 = (bf16[256,1280]{1,0:T(8,128)(2,1)}, bf16[256,1280]{1,0:T(8,128)(2,1)S(1)}, u32[]{:S(2)}, u32[]{:S(2)}) collective-permute-start(bf16[256,1280]{1,0:T(8,128)(2,1)} %get-tuple-element.171), channel_id=1, source_target_pairs={{0,4},{1,12},{2,6},{3,14},{4,0},{5,8},{6,2},{7,10},{8,5},{9,13},{1... | collective-permute-start | bytes 1966088 | tf_op jit(solution)/shard_map/ppermute | solution.py:613
  152.3 32.3 %collective-permute-start.19 = (bf16[256,1280]{1,0:T(8,128)(2,1)S(1)}, bf16[256,1280]{1,0:T(8,128)(2,1)S(1)}, u32[]{:S(2)}, u32[]{:S(2)}) collective-permute-start(bf16[256,1280]{1,0:T(8,128)(2,1)S(1)} %copy-done.23), channel_id=1, source_target_pairs={{0,0},{1,8},{2,2},{3,10},{4,4},{5,12},{6,6},{7,14},{8,1},{9,9},{10... | collective-permute-start | bytes 1966088 | tf_op jit(solution)/shard_map/ppermute | solution.py:613
  219.8 11.4 %collective-permute-start.22 = (bf16[2,320,1280]{2,1,0:T(8,128)(2,1)}, bf16[2,320,1280]{2,1,0:T(8,128)(2,1)}, u32[]{:S(2)}, u32[]{:S(2)}) collective-permute-start(bf16[2,320,1280]{2,1,0:T(8,128)(2,1)} %dynamic-slice_bitcast_fusion.2), channel_id=1, source_target_pairs={{0,8},{8,0},{16,24},{24,16},{1,9},{9,1},{17,25},{25,17},{2,10},{10... | collective-permute-start | bytes 4915208 | tf_op jit(solution)/shard_map/ppermute | solution.py:749
  229.4 4.2 collective-permute-start.23
  230.8 6.3 %collective-permute-start.24 = (bf16[2,320,1280]{2,1,0:T(8,128)(2,1)}, bf16[2,320,1280]{2,1,0:T(8,128)(2,1)}, u32[]{:S(2)}, u32[]{:S(2)}) collective-permute-start(bf16[2,320,1280]{2,1,0:T(8,128)(2,1)} %dynamic-slice_bitcast_fusion), channel_id=1, source_target_pairs={{0,8},{8,0},{16,24},{24,16},{1,9},{9,1},{17,25},{25,17},{2,10},{10... | collective-permute-start | bytes 4915208 | tf_op jit(solution)/shard_map/ppermute | solution.py:749
  241.5 82.0 %collective-permute-start.25 = (bf16[960,1280]{1,0:T(8,128)(2,1)}, bf16[960,1280]{1,0:T(8,128)(2,1)}, u32[]{:S(2)}, u32[]{:S(2)}) collective-permute-start(bf16[960,1280]{1,0:T(8,128)(2,1)} %pad_maximum_fusion.3), channel_id=1, source_target_pairs={{0,16},{8,24},{16,0},{24,8},{1,17},{9,25},{17,1},{25,9},{2,18},{10... | collective-permute-start | bytes 7372808 | tf_op jit(solution)/shard_map/ppermute | solution.py:768
  247.9 5.3 collective-permute-start.21
  250.4 39.0 %collective-permute-start.18 = (bf16[256,1280]{1,0:T(8,128)(2,1)}, bf16[256,1280]{1,0:T(8,128)(2,1)}, u32[]{:S(2)}, u32[]{:S(2)}) collective-permute-start(bf16[256,1280]{1,0:T(8,128)(2,1)} %get-tuple-element.175), channel_id=1, source_target_pairs={{6,0},{14,1},{0,2},{8,3},{2,4},{10,5},{4,6},{12,7},{7,8},{15,9},{1... | collective-permute-start | bytes 1966088 | tf_op jit(solution)/shard_map/ppermute | solution.py:621
  251.6 57.0 %collective-permute-start.17 = (bf16[256,1280]{1,0:T(8,128)(2,1)}, bf16[256,1280]{1,0:T(8,128)(2,1)}, u32[]{:S(2)}, u32[]{:S(2)}) collective-permute-start(bf16[256,1280]{1,0:T(8,128)(2,1)} %get-tuple-element.176), channel_id=1, source_target_pairs={{4,0},{12,1},{6,2},{14,3},{0,4},{8,5},{2,6},{10,7},{5,8},{13,9},{7... | collective-permute-start | bytes 1966088 | tf_op jit(solution)/shard_map/ppermute | solution.py:621
  253.2 58.0 %collective-permute-start.16 = (bf16[256,1280]{1,0:T(8,128)(2,1)}, bf16[256,1280]{1,0:T(8,128)(2,1)}, u32[]{:S(2)}, u32[]{:S(2)}) collective-permute-start(bf16[256,1280]{1,0:T(8,128)(2,1)} %get-tuple-element.177), channel_id=1, source_target_pairs={{2,0},{10,1},{4,2},{12,3},{6,4},{14,5},{0,6},{8,7},{3,8},{11,9},{5... | collective-permute-start | bytes 1966088 | tf_op jit(solution)/shard_map/ppermute | solution.py:621
  253.2 58.0 %collective-permute-start.15 = (bf16[256,1280]{1,0:T(8,128)(2,1)}, bf16[256,1280]{1,0:T(8,128)(2,1)}, u32[]{:S(2)}, u32[]{:S(2)}) collective-permute-start(bf16[256,1280]{1,0:T(8,128)(2,1)} %get-tuple-element.178), channel_id=1, source_target_pairs={{0,0},{8,1},{2,2},{10,3},{4,4},{12,5},{6,6},{14,7},{1,8},{9,9},{3,... | collective-permute-start | bytes 1966088 | tf_op jit(solution)/shard_map/ppermute | solution.py:621
  328.5 29.6 %collective-permute-start.26 = (bf16[480,1280]{1,0:T(8,128)(2,1)}, bf16[480,1280]{1,0:T(8,128)(2,1)}, u32[]{:S(2)}, u32[]{:S(2)}) collective-permute-start(bf16[480,1280]{1,0:T(8,128)(2,1)} %dynamic-slice_bitcast_fusion.5), channel_id=1, source_target_pairs={{0,1},{1,0},{2,3},{3,2},{4,5},{5,4},{6,7},{7,6},{8,9},{9,8},{10,11... | collective-permute-start | bytes 3686408 | tf_op jit(solution)/shard_map/ppermute | solution.py:551
  330.7 36.5 %collective-permute-start.40 = (bf16[480,640]{1,0:T(8,128)(2,1)}, bf16[480,640]{1,0:T(8,128)(2,1)}, u32[]{:S(2)}, u32[]{:S(2)}) collective-permute-start(bf16[480,640]{1,0:T(8,128)(2,1)} %get-tuple-element.109), channel_id=1, source_target_pairs={{0,8},{8,0},{16,24},{24,16},{1,9},{9,1},{17,25},{25,17},{2,10},{10... | collective-permute-start | bytes 1843208 | tf_op jit(solution)/shard_map/ppermute | solution.py:792
  359.7 21.3 %collective-permute-start.27 = (bf16[240,1280]{1,0:T(8,128)(2,1)S(1)}, bf16[240,1280]{1,0:T(8,128)(2,1)S(1)}, u32[]{:S(2)}, u32[]{:S(2)}) collective-permute-start(bf16[240,1280]{1,0:T(8,128)(2,1)S(1)} %dynamic-slice_bitcast_fusion.16), channel_id=1, source_target_pairs={{0,2},{1,3},{2,0},{3,1},{4,6},{5,7},{6,4},{7,5},{8,10},{9,11},{10,... | collective-permute-start | bytes 1843208 | tf_op jit(solution)/shard_map/ppermute | solution.py:551
  362.4 30.0 %collective-permute-start.39 = (bf16[480,640]{1,0:T(8,128)(2,1)S(1)}, bf16[480,640]{1,0:T(8,128)(2,1)S(1)}, u32[]{:S(2)}, u32[]{:S(2)}) collective-permute-start(bf16[480,640]{1,0:T(8,128)(2,1)S(1)} %copy-done.49), channel_id=1, source_target_pairs={{0,16},{8,24},{16,0},{24,8},{1,17},{9,25},{17,1},{25,9},{2,18},{10... | collective-permute-start | bytes 1843208 | tf_op jit(solution)/shard_map/ppermute | solution.py:795
  363.7 44.1 %collective-permute-start.38 = (bf16[480,640]{1,0:T(8,128)(2,1)}, bf16[480,640]{1,0:T(8,128)(2,1)S(1)}, u32[]{:S(2)}, u32[]{:S(2)}) collective-permute-start(bf16[480,640]{1,0:T(8,128)(2,1)} %get-tuple-element.108), channel_id=1, source_target_pairs={{0,8},{8,0},{16,24},{24,16},{1,9},{9,1},{17,25},{25,17},{2,10},{10... | collective-permute-start | bytes 1843208 | tf_op jit(solution)/shard_map/ppermute | solution.py:792
  367.2 40.6 %collective-permute-start.41 = (bf16[480,640]{1,0:T(8,128)(2,1)}, bf16[480,640]{1,0:T(8,128)(2,1)S(1)}, u32[]{:S(2)}, u32[]{:S(2)}) collective-permute-start(bf16[480,640]{1,0:T(8,128)(2,1)} %collective-permute-done.40), channel_id=1, source_target_pairs={{0,16},{8,24},{16,0},{24,8},{1,17},{9,25},{17,1},{25,9},{2,18},{10... | collective-permute-start | bytes 1843208 | tf_op jit(solution)/shard_map/ppermute | solution.py:795
  380.8 13.1 %collective-permute-start.44 = (bf16[480,640]{1,0:T(8,128)(2,1)}, bf16[480,640]{1,0:T(8,128)(2,1)}, u32[]{:S(2)}, u32[]{:S(2)}) collective-permute-start(bf16[480,640]{1,0:T(8,128)(2,1)} %get-tuple-element.119), channel_id=1, source_target_pairs={{0,8},{8,0},{16,24},{24,16},{1,9},{9,1},{17,25},{25,17},{2,10},{10... | collective-permute-start | bytes 1843208 | tf_op jit(solution)/shard_map/ppermute | solution.py:792
  381.2 14.8 %collective-permute-start.58 = (bf16[120,1280]{1,0:T(8,128)(2,1)S(1)}, bf16[120,1280]{1,0:T(8,128)(2,1)S(1)}, u32[]{:S(2)}, u32[]{:S(2)}) collective-permute-start(bf16[120,1280]{1,0:T(8,128)(2,1)S(1)} %dynamic-slice_bitcast_fusion.19), channel_id=1, source_target_pairs={{0,4},{1,5},{2,6},{3,7},{4,0},{5,1},{6,2},{7,3},{8,12},{9,13},{10,... | collective-permute-start | bytes 921608 | tf_op jit(solution)/shard_map/ppermute | solution.py:551
  392.4 29.2 %copy-start.31 = (bf16[480,640]{1,0:T(8,128)(2,1)S(1)}, bf16[480,640]{1,0:T(8,128)(2,1)}, u32[]{:S(2)}) copy-start(bf16[480,640]{1,0:T(8,128)(2,1)} %get-tuple-element.134) | copy-start | bytes 1843204
  392.4 18.9 %collective-permute-start.43 = (bf16[480,640]{1,0:T(8,128)(2,1)}, bf16[480,640]{1,0:T(8,128)(2,1)S(1)}, u32[]{:S(2)}, u32[]{:S(2)}) collective-permute-start(bf16[480,640]{1,0:T(8,128)(2,1)} %get-tuple-element.122), channel_id=1, source_target_pairs={{0,16},{8,24},{16,0},{24,8},{1,17},{9,25},{17,1},{25,9},{2,18},{10... | collective-permute-start | bytes 1843208 | tf_op jit(solution)/shard_map/ppermute | solution.py:795
  393.9 17.3 %collective-permute-start.42 = (bf16[480,640]{1,0:T(8,128)(2,1)}, bf16[480,640]{1,0:T(8,128)(2,1)S(1)}, u32[]{:S(2)}, u32[]{:S(2)}) collective-permute-start(bf16[480,640]{1,0:T(8,128)(2,1)} %get-tuple-element.118), channel_id=1, source_target_pairs={{0,8},{8,0},{16,24},{24,16},{1,9},{9,1},{17,25},{25,17},{2,10},{10... | collective-permute-start | bytes 1843208 | tf_op jit(solution)/shard_map/ppermute | solution.py:792
  396.0 25.6 %collective-permute-start.45 = (bf16[480,640]{1,0:T(8,128)(2,1)}, bf16[480,640]{1,0:T(8,128)(2,1)S(1)}, u32[]{:S(2)}, u32[]{:S(2)}) collective-permute-start(bf16[480,640]{1,0:T(8,128)(2,1)} %collective-permute-done.44), channel_id=1, source_target_pairs={{0,16},{8,24},{16,0},{24,8},{1,17},{9,25},{17,1},{25,9},{2,18},{10... | collective-permute-start | bytes 1843208 | tf_op jit(solution)/shard_map/ppermute | solution.py:795
  407.7 81.2 %collective-permute-start.28 = (bf16[1024,1280]{1,0:T(8,128)(2,1)}, bf16[1024,1280]{1,0:T(8,128)(2,1)S(1)}, u32[]{:S(2)}, u32[]{:S(2)}) collective-permute-start(bf16[1024,1280]{1,0:T(8,128)(2,1)} %input_side.2), channel_id=1, source_target_pairs={{0,8},{1,9},{2,10},{3,11},{4,12},{5,13},{6,14},{7,15},{8,0},{9,1},... | collective-permute-start | bytes 7864328 | tf_op jit(solution)/shard_map/ppermute | solution.py:815
  407.8 17.0 %collective-permute-start.59 = (bf16[120,1280]{1,0:T(8,128)(2,1)S(1)}, bf16[120,1280]{1,0:T(8,128)(2,1)S(1)}, u32[]{:S(2)}, u32[]{:S(2)}) collective-permute-start(bf16[120,1280]{1,0:T(8,128)(2,1)S(1)} %fusion.23), channel_id=1, source_target_pairs={{0,4},{1,5},{2,6},{3,7},{4,0},{5,1},{6,2},{7,3},{8,12},{9,13},{10,... | collective-permute-start | bytes 921608 | tf_op jit(solution)/shard_map/ppermute | solution.py:559
  422.1 16.8 %collective-permute-start.52 = (bf16[480,640]{1,0:T(8,128)(2,1)S(1)}, bf16[480,640]{1,0:T(8,128)(2,1)S(1)}, u32[]{:S(2)}, u32[]{:S(2)}) collective-permute-start(bf16[480,640]{1,0:T(8,128)(2,1)S(1)} %dynamic-slice_bitcast_fusion.14), channel_id=1, source_target_pairs={{0,1},{1,0},{2,3},{3,2},{4,5},{5,4},{6,7},{7,6},{8,9},{9,8},{10,11... | collective-permute-start | bytes 1843208 | tf_op jit(solution)/shard_map/ppermute | solution.py:551
  423.5 26.7 %collective-permute-start.46 = (bf16[480,640]{1,0:T(8,128)(2,1)S(1)}, bf16[480,640]{1,0:T(8,128)(2,1)S(1)}, u32[]{:S(2)}, u32[]{:S(2)}) collective-permute-start(bf16[480,640]{1,0:T(8,128)(2,1)S(1)} %dynamic-slice_bitcast_fusion.15), channel_id=1, source_target_pairs={{0,1},{1,0},{2,3},{3,2},{4,5},{5,4},{6,7},{7,6},{8,9},{9,8},{10,11... | collective-permute-start | bytes 1843208 | tf_op jit(solution)/shard_map/ppermute | solution.py:551
  424.9 56.2 %collective-permute-start.60 = (bf16[240,1280]{1,0:T(8,128)(2,1)S(1)}, bf16[240,1280]{1,0:T(8,128)(2,1)S(1)}, u32[]{:S(2)}, u32[]{:S(2)}) collective-permute-start(bf16[240,1280]{1,0:T(8,128)(2,1)S(1)} %maximum_select_fusion.6), channel_id=1, source_target_pairs={{0,2},{1,3},{2,0},{3,1},{4,6},{5,7},{6,4},{7,5},{8,10},{9,11},{10,... | collective-permute-start | bytes 1843208 | tf_op jit(solution)/shard_map/ppermute | solution.py:559
  439.1 12.5 %collective-permute-start.53 = (bf16[240,640]{1,0:T(8,128)(2,1)S(1)}, bf16[240,640]{1,0:T(8,128)(2,1)S(1)}, u32[]{:S(2)}, u32[]{:S(2)}) collective-permute-start(bf16[240,640]{1,0:T(8,128)(2,1)S(1)} %dynamic-slice_bitcast_fusion.17), channel_id=1, source_target_pairs={{0,2},{1,3},{2,0},{3,1},{4,6},{5,7},{6,4},{7,5},{8,10},{9,11},{10,... | collective-permute-start | bytes 921608 | tf_op jit(solution)/shard_map/ppermute | solution.py:551
  450.4 9.4 %collective-permute-start.47 = (bf16[240,640]{1,0:T(8,128)(2,1)S(1)}, bf16[240,640]{1,0:T(8,128)(2,1)S(1)}, u32[]{:S(2)}, u32[]{:S(2)}) collective-permute-start(bf16[240,640]{1,0:T(8,128)(2,1)S(1)} %dynamic-slice_bitcast_fusion.18), channel_id=1, source_target_pairs={{0,2},{1,3},{2,0},{3,1},{4,6},{5,7},{6,4},{7,5},{8,10},{9,11},{10,... | collective-permute-start | bytes 921608 | tf_op jit(solution)/shard_map/ppermute | solution.py:551
  451.7 11.5 %collective-permute-start.54 = (bf16[120,640]{1,0:T(8,128)(2,1)S(1)}, bf16[120,640]{1,0:T(8,128)(2,1)S(1)}, u32[]{:S(2)}, u32[]{:S(2)}) collective-permute-start(bf16[120,640]{1,0:T(8,128)(2,1)S(1)} %dynamic-slice_bitcast_fusion.20), channel_id=1, source_target_pairs={{0,4},{1,5},{2,6},{3,7},{4,0},{5,1},{6,2},{7,3},{8,12},{9,13},{10,... | collective-permute-start | bytes 460808 | tf_op jit(solution)/shard_map/ppermute | solution.py:551
  460.0 11.4 %collective-permute-start.48 = (bf16[120,640]{1,0:T(8,128)(2,1)S(1)}, bf16[120,640]{1,0:T(8,128)(2,1)S(1)}, u32[]{:S(2)}, u32[]{:S(2)}) collective-permute-start(bf16[120,640]{1,0:T(8,128)(2,1)S(1)} %dynamic-slice_bitcast_fusion.21), channel_id=1, source_target_pairs={{0,4},{1,5},{2,6},{3,7},{4,0},{5,1},{6,2},{7,3},{8,12},{9,13},{10,... | collective-permute-start | bytes 460808 | tf_op jit(solution)/shard_map/ppermute | solution.py:551
  463.2 14.7 %collective-permute-start.55 = (bf16[120,640]{1,0:T(8,128)(2,1)S(1)}, bf16[120,640]{1,0:T(8,128)(2,1)S(1)}, u32[]{:S(2)}, u32[]{:S(2)}) collective-permute-start(bf16[120,640]{1,0:T(8,128)(2,1)S(1)} %fusion.26), channel_id=1, source_target_pairs={{0,4},{1,5},{2,6},{3,7},{4,0},{5,1},{6,2},{7,3},{8,12},{9,13},{10,... | collective-permute-start | bytes 460808 | tf_op jit(solution)/shard_map/ppermute | solution.py:559
  471.4 10.9 %collective-permute-start.49 = (bf16[120,640]{1,0:T(8,128)(2,1)S(1)}, bf16[120,640]{1,0:T(8,128)(2,1)S(1)}, u32[]{:S(2)}, u32[]{:S(2)}) collective-permute-start(bf16[120,640]{1,0:T(8,128)(2,1)S(1)} %fusion.27), channel_id=1, source_target_pairs={{0,4},{1,5},{2,6},{3,7},{4,0},{5,1},{6,2},{7,3},{8,12},{9,13},{10,... | collective-permute-start | bytes 460808 | tf_op jit(solution)/shard_map/ppermute | solution.py:559
  478.0 10.7 %collective-permute-start.56 = (bf16[240,640]{1,0:T(8,128)(2,1)S(1)}, bf16[240,640]{1,0:T(8,128)(2,1)S(1)}, u32[]{:S(2)}, u32[]{:S(2)}) collective-permute-start(bf16[240,640]{1,0:T(8,128)(2,1)S(1)} %maximum_select_fusion.8), channel_id=1, source_target_pairs={{0,2},{1,3},{2,0},{3,1},{4,6},{5,7},{6,4},{7,5},{8,10},{9,11},{10,... | collective-permute-start | bytes 921608 | tf_op jit(solution)/shard_map/ppermute | solution.py:559
  481.5 30.5 %collective-permute-start.61 = (bf16[480,1280]{1,0:T(8,128)(2,1)S(1)}, bf16[480,1280]{1,0:T(8,128)(2,1)S(1)}, u32[]{:S(2)}, u32[]{:S(2)}) collective-permute-start(bf16[480,1280]{1,0:T(8,128)(2,1)S(1)} %maximum_select_fusion.3), channel_id=1, source_target_pairs={{0,1},{1,0},{2,3},{3,2},{4,5},{5,4},{6,7},{7,6},{8,9},{9,8},{10,11... | collective-permute-start | bytes 3686408 | tf_op jit(solution)/shard_map/ppermute | solution.py:559
  482.4 11.5 %collective-permute-start.50 = (bf16[240,640]{1,0:T(8,128)(2,1)S(1)}, bf16[240,640]{1,0:T(8,128)(2,1)S(1)}, u32[]{:S(2)}, u32[]{:S(2)}) collective-permute-start(bf16[240,640]{1,0:T(8,128)(2,1)S(1)} %maximum_select_fusion.7), channel_id=1, source_target_pairs={{0,2},{1,3},{2,0},{3,1},{4,6},{5,7},{6,4},{7,5},{8,10},{9,11},{10,... | collective-permute-start | bytes 921608 | tf_op jit(solution)/shard_map/ppermute | solution.py:559
  491.8 2.3 collective-permute-start.33
  494.2 3.9 collective-permute-start.34
  498.1 13.9 %collective-permute-start.35 = (f32[5200]{0:T(1024)S(1)}, f32[5200]{0:T(1024)S(1)}, u32[]{:S(2)}, u32[]{:S(2)}) collective-permute-start(f32[5200]{0:T(1024)S(1)} %add.578), channel_id=1, source_target_pairs={{0,1},{1,0},{2,3},{3,2},{4,5},{5,4},{6,7},{7,6},{8,9},{9,8},{10,11... | collective-permute-start | bytes 62408 | tf_op jit(solution)/shard_map/ppermute | solution.py:578
  501.3 25.4 %collective-permute-start.51 = (bf16[480,640]{1,0:T(8,128)(2,1)S(1)}, bf16[480,640]{1,0:T(8,128)(2,1)S(1)}, u32[]{:S(2)}, u32[]{:S(2)}) collective-permute-start(bf16[480,640]{1,0:T(8,128)(2,1)S(1)} %maximum_select_fusion.4), channel_id=1, source_target_pairs={{0,1},{1,0},{2,3},{3,2},{4,5},{5,4},{6,7},{7,6},{8,9},{9,8},{10,11... | collective-permute-start | bytes 1843208 | tf_op jit(solution)/shard_map/ppermute | solution.py:559
  512.0 3.8 collective-permute-start.36
  515.8 9.0 %collective-permute-start.37 = (f32[5200]{0:T(1024)S(1)}, f32[5200]{0:T(1024)S(1)}, u32[]{:S(2)}, u32[]{:S(2)}) collective-permute-start(f32[5200]{0:T(1024)S(1)} %add.580), channel_id=1, source_target_pairs={{0,4},{1,5},{2,6},{3,7},{4,0},{5,1},{6,2},{7,3},{8,12},{9,13},{10,... | collective-permute-start | bytes 62408 | tf_op jit(solution)/shard_map/ppermute | solution.py:578
  516.5 31.4 %collective-permute-start.57 = (bf16[480,640]{1,0:T(8,128)(2,1)S(1)}, bf16[480,640]{1,0:T(8,128)(2,1)S(1)}, u32[]{:S(2)}, u32[]{:S(2)}) collective-permute-start(bf16[480,640]{1,0:T(8,128)(2,1)S(1)} %maximum_select_fusion.5), channel_id=1, source_target_pairs={{0,1},{1,0},{2,3},{3,2},{4,5},{5,4},{6,7},{7,6},{8,9},{9,8},{10,11... | collective-permute-start | bytes 1843208 | tf_op jit(solution)/shard_map/ppermute | solution.py:559
  519.8 47.3 %collective-permute-start.32 = (bf16[256,1280]{1,0:T(8,128)(2,1)S(1)}, bf16[256,1280]{1,0:T(8,128)(2,1)S(1)}, u32[]{:S(2)}, u32[]{:S(2)}) collective-permute-start(bf16[256,1280]{1,0:T(8,128)(2,1)S(1)} %get-tuple-element.165), channel_id=1, source_target_pairs={{6,0},{14,1},{0,2},{8,3},{2,4},{10,5},{4,6},{12,7},{7,8},{15,9},{1... | collective-permute-start | bytes 1966088 | tf_op jit(solution)/shard_map/ppermute | solution.py:621
  523.9 56.2 %collective-permute-start.31 = (bf16[256,1280]{1,0:T(8,128)(2,1)S(1)}, bf16[256,1280]{1,0:T(8,128)(2,1)S(1)}, u32[]{:S(2)}, u32[]{:S(2)}) collective-permute-start(bf16[256,1280]{1,0:T(8,128)(2,1)S(1)} %get-tuple-element.166), channel_id=1, source_target_pairs={{4,0},{12,1},{6,2},{14,3},{0,4},{8,5},{2,6},{10,7},{5,8},{13,9},{7... | collective-permute-start | bytes 1966088 | tf_op jit(solution)/shard_map/ppermute | solution.py:621
  524.8 55.9 %collective-permute-start.30 = (bf16[256,1280]{1,0:T(8,128)(2,1)S(1)}, bf16[256,1280]{1,0:T(8,128)(2,1)S(1)}, u32[]{:S(2)}, u32[]{:S(2)}) collective-permute-start(bf16[256,1280]{1,0:T(8,128)(2,1)S(1)} %get-tuple-element.167), channel_id=1, source_target_pairs={{2,0},{10,1},{4,2},{12,3},{6,4},{14,5},{0,6},{8,7},{3,8},{11,9},{5... | collective-permute-start | bytes 1966088 | tf_op jit(solution)/shard_map/ppermute | solution.py:621
  526.7 54.1 %collective-permute-start.29 = (bf16[256,1280]{1,0:T(8,128)(2,1)S(1)}, bf16[256,1280]{1,0:T(8,128)(2,1)S(1)}, u32[]{:S(2)}, u32[]{:S(2)}) collective-permute-start(bf16[256,1280]{1,0:T(8,128)(2,1)S(1)} %get-tuple-element.168), channel_id=1, source_target_pairs={{0,0},{8,1},{2,2},{10,3},{4,4},{12,5},{6,6},{14,7},{1,8},{9,9},{3,... | collective-permute-start | bytes 1966088 | tf_op jit(solution)/shard_map/ppermute | solution.py:621
  (58 other events, 387.3 us)
